TPU v7x, 256 devices: a whole 4x4x8 slice. The times are simulated.
256 devices in a mesh: gx: 32 (over y, x, core), gy: 8 (over z).
Axes of the slice: x: 4, y: 4, z: 8, core: 2. Of those that a mesh axis runs over, the one named last changes fastest.
Arguments:
- atmos: float32 [5, 48, 256, 1024], P(None, None, 'gx', 'gy'), may hold values from -4 to 4
- level_set: float32 [2048, 8192], P('gx', 'gy'), may hold values from -8 to 8
- fuel_left: float32 [2048, 8192], P('gx', 'gy'), may hold values from 0.3 to 1
- fuel_map: int32 [2048, 8192], P('gx', 'gy'), may hold values from 0 to 12
- spread_rate: float32 [13], replicated, may hold values from 0.04 to 0.15
- wind_factor: float32 [13], replicated, may hold values from 0.1 to 0.5
- burn_time: float32 [13], replicated, may hold values from 3 to 20
- heat_yield: float32 [13], replicated, may hold values from 1 to 4
- burn_tiles: int32 [32, 8, 16], P('gx', 'gy'), may hold values from 0 to 15, as said below
- burn_count: int32 [32, 8], P('gx', 'gy'), may hold values from 1 to 16, as said below
- substep_count: int32 [32, 128], P('gx', 'gy'), may hold values from 1 to 8, as said below
Outputs:
- atmos_next: float32 [5, 48, 256, 1024], P(None, None, 'gx', 'gy')
- level_next: float32 [2048, 8192], P('gx', 'gy')
- fuel_next: float32 [2048, 8192], P('gx', 'gy')
Inputs may be any that keep to these rules, and one draw needn't show every extreme that they name: `burn_tiles`: each device's 16 entries are distinct local tile numbers; some device has all 16 entries valid. `burn_count`: some device has 16 burning tiles. `substep_count`: some tile takes 8 substeps.
All inputs are finite; a program needn't handle non-finite values.
Results may differ from a plain program's by a relative error of at most 0.000075.
Values sent between devices are 32-bit elements; how exact they have to be, the bound alone decides.
A program may use at most 64 MiB of HBM per device.

v0:
```python
import jax
import jax.numpy as jnp
from jax import lax
from jax.sharding import PartitionSpec as P

RF = 8
TILE = 64
SUBSTEPS = 8


COURANT = 0.2
DIFFUSE = 0.05


def extended(cells, sides, width):
    for axis, dim in sides:
        count = lax.axis_size(axis)
        ends = count - 1
        head = lax.slice_in_dim(cells, 0, width, axis=dim)
        tail = lax.slice_in_dim(cells, cells.shape[dim] - width, cells.shape[dim], axis=dim)
        cells = jnp.concatenate(
            [
                lax.ppermute(tail, axis, [(i, (i + 1) % count) for i in range(ends)]),
                cells,
                lax.ppermute(head, axis, [((i + 1) % count, i) for i in range(ends)]),
            ],
            axis=dim,
        )
    return cells


def advance(
    padded, level, remaining, heating, spread, gain, burnout, yields, wind_u, wind_v, active
):
    back_x = level - padded[..., 1:-3, 2:-2]
    ahead_x = padded[..., 3:-1, 2:-2] - level
    back_y = level - padded[..., 2:-2, 1:-3]
    ahead_y = padded[..., 2:-2, 3:-1] - level
    upwind = jnp.sqrt(
        jnp.maximum(back_x, 0.0) ** 2
        + jnp.minimum(ahead_x, 0.0) ** 2
        + jnp.maximum(back_y, 0.0) ** 2
        + jnp.minimum(ahead_y, 0.0) ** 2
    )
    slope_x = (
        padded[..., :-4, 2:-2]
        - 8.0 * padded[..., 1:-3, 2:-2]
        + 8.0 * padded[..., 3:-1, 2:-2]
        - padded[..., 4:, 2:-2]
    ) / 12.0
    slope_y = (
        padded[..., 2:-2, :-4]
        - 8.0 * padded[..., 2:-2, 1:-3]
        + 8.0 * padded[..., 2:-2, 3:-1]
        - padded[..., 2:-2, 4:]
    ) / 12.0
    pushing = jnp.maximum(wind_u * slope_x + wind_v * slope_y, 0.0)
    advanced = level - spread * (upwind + gain * pushing)
    burned = remaining / (1.0 + jnp.exp(advanced)) / burnout
    return (
        jnp.where(active, advanced, level),
        jnp.where(active, remaining - burned, remaining),
        heating + jnp.where(active, yields * burned, 0.0),
    )


def atmos_step(padded, heat_atm):
    width_x = padded.shape[2] - 6
    width_y = padded.shape[3] - 6

    def shifted(along_x, along_y):
        return padded[
            :, :, 3 + along_x : 3 + along_x + width_x, 3 + along_y : 3 + along_y + width_y
        ]

    centre = shifted(0, 0)
    deriv_x = (
        shifted(3, 0)
        - 9.0 * shifted(2, 0)
        + 45.0 * shifted(1, 0)
        - 45.0 * shifted(-1, 0)
        + 9.0 * shifted(-2, 0)
        - shifted(-3, 0)
    ) / 60.0
    deriv_y = (
        shifted(0, 3)
        - 9.0 * shifted(0, 2)
        + 45.0 * shifted(0, 1)
        - 45.0 * shifted(0, -1)
        + 9.0 * shifted(0, -2)
        - shifted(0, -3)
    ) / 60.0
    laplace = shifted(1, 0) + shifted(-1, 0) + shifted(0, 1) + shifted(0, -1) - 4.0 * centre
    updated = centre - COURANT * (centre[0:1] * deriv_x + centre[1:2] * deriv_y) + DIFFUSE * laplace
    depth = padded.shape[1]
    profile = jnp.exp(-4.0 * jnp.arange(depth).astype(jnp.float32) / depth)
    return updated.at[3].add(heat_atm[None, :, :] * profile[:, None, None])


def interp_table(count, ratio, extra):
    indices = jnp.arange(count + 2 * extra) - extra
    coarse = indices // ratio
    within = indices % ratio
    lower = jnp.where(within < ratio // 2, coarse, coarse + 1) + 2
    weight = (within.astype(jnp.float32) + 0.5) / ratio + jnp.where(within < ratio // 2, 0.5, -0.5)
    columns = jnp.arange(count // ratio + 6)
    return (1.0 - weight)[:, None] * (columns[None, :] == lower[:, None]) + weight[:, None] * (
        columns[None, :] == lower[:, None] + 1
    )


def surface_winds(surface, fire_rows, fire_cols, extra):
    table_x = interp_table(fire_rows, RF, extra)
    table_y = interp_table(fire_cols, RF, extra)
    along = jnp.einsum("ia,kab->kib", table_x, surface, precision=lax.Precision.HIGHEST)
    return jnp.einsum("kib,jb->kij", along, table_y, precision=lax.Precision.HIGHEST)


def fire_halo(level):
    return extended(level, (("gx", 0), ("gy", 1)), 2)


def shards(
    atmos,
    level_set,
    fuel_left,
    fuel_map,
    spread_rate,
    wind_factor,
    burn_time,
    heat_yield,
    burn_tiles,
    burn_count,
    substep_count,
):
    fire_rows, fire_cols = level_set.shape
    atmos_rows, atmos_cols = (atmos.shape[2], atmos.shape[3])
    padded_atm = extended(atmos, (("gx", 2), ("gy", 3)), 3)
    surface = padded_atm[0:2, 0]
    spread = jnp.zeros(level_set.shape, jnp.float32)
    gain = jnp.zeros(level_set.shape, jnp.float32)
    burnout = jnp.ones(level_set.shape, jnp.float32)
    yields = jnp.zeros(level_set.shape, jnp.float32)
    for category in range(spread_rate.shape[0]):
        picked = fuel_map == category
        spread = jnp.where(picked, spread_rate[category], spread)
        gain = jnp.where(picked, wind_factor[category], gain)
        burnout = jnp.where(picked, burn_time[category], burnout)
        yields = jnp.where(picked, heat_yield[category], yields)
    slots = burn_tiles.reshape(-1)
    listed = burn_count.reshape(())
    tiles_dev = substep_count.size
    slot_valid = jnp.arange(slots.shape[0]) < listed
    tile_on = jnp.any(
        (slots[:, None] == jnp.arange(tiles_dev)[None, :]) & slot_valid[:, None], axis=0
    )
    tile_on = tile_on.reshape(substep_count.shape)
    tiles_x, tiles_y = substep_count.shape
    winds = surface_winds(surface, fire_rows, fire_cols, 0)
    level, remaining = (level_set, fuel_left)
    heating = jnp.zeros_like(level_set)
    for substep in range(SUBSTEPS):
        tile_active = tile_on & (substep < substep_count)
        active = jnp.broadcast_to(
            tile_active[:, None, :, None], (tiles_x, TILE, tiles_y, TILE)
        ).reshape(fire_rows, fire_cols)
        padded = fire_halo(level)
        level, remaining, heating = advance(
            padded,
            level,
            remaining,
            heating,
            spread,
            gain,
            burnout,
            yields,
            winds[0],
            winds[1],
            active,
        )
    heat_atm = heating.reshape(atmos_rows, RF, atmos_cols, RF).sum(axis=(1, 3)) / (RF * RF)
    return (atmos_step(padded_atm, heat_atm), level, remaining)


def solution(mesh):
    return jax.shard_map(
        shards,
        mesh=mesh,
        in_specs=(
            P(None, None, "gx", "gy"),
            P("gx", "gy"),
            P("gx", "gy"),
            P("gx", "gy"),
            P(),
            P(),
            P(),
            P(),
            P("gx", "gy", None),
            P("gx", "gy"),
            P("gx", "gy"),
        ),
        out_specs=(P(None, None, "gx", "gy"), P("gx", "gy"), P("gx", "gy")),
        check_vma=False,
    )
```

profile of v0, /device:TPU:120, one launch (start us, length us, event | category | flops | bytes accessed | tf_op | source)
XLA Modules:
  0.0 283.8 jit_solution(16115186287746265816)
XLA Ops:
  6.0 5.9 %collective-permute-start = (f32[5,48,3,128]{3,1,2,0:T(8,128)}, f32[5,48,3,128]{3,1,2,0:T(8,128)}, u32[]{:S(2)}, u32[]{:S(2)}) collective-permute-start(f32[5,48,3,128]{3,1,2,0:T(8,128)} %copy.50), channel_id=1, source_target_pairs={{8,0},{16,8},{24,16},{32,24},{40,32},{48,40},{56,48},{64,56},{72,6... | collective-permute-start | bytes 1105928 | tf_op jit(solution)/shard_map/ppermute | solution.py:25
  11.9 1.9 collective-permute-start.5
  13.9 2.4 collective-permute-start.4
  22.6 5.0 %collective-permute-start.6 = (f32[68,2]{1,0:T(8,128)}, f32[68,2]{1,0:T(8,128)S(1)}, u32[]{:S(2)}, u32[]{:S(2)}) collective-permute-start(f32[68,2]{1,0:T(8,128)} %get-tuple-element.92), channel_id=1, source_target_pairs={{0,1},{1,2},{2,3},{3,4},{4,5},{5,6},{6,7},{8,9},{9,10},{10,11},{11... | collective-permute-start | bytes 1640 | tf_op jit(solution)/shard_map/ppermute | solution.py:23
  34.5 2.5 fusion.204
  37.1 2.5 copy.43
  39.5 5.1 %collective-permute-start.3 = (f32[5,48,14,3]{1,2,3,0:T(8,128)S(1)}, f32[5,48,14,3]{1,2,3,0:T(8,128)S(1)}, u32[]{:S(2)}, u32[]{:S(2)}) collective-permute-start(f32[5,48,14,3]{1,2,3,0:T(8,128)S(1)} %copy.43), channel_id=1, source_target_pairs={{0,1},{1,2},{2,3},{3,4},{4,5},{5,6},{6,7},{8,9},{9,10},{10,11},{11... | collective-permute-start | bytes 120968 | tf_op jit(solution)/shard_map/ppermute | solution.py:23
  49.4 4.1 %collective-permute-done.2 = f32[5,48,14,3]{1,2,3,0:T(8,128)S(1)} collective-permute-done((f32[5,48,14,3]{1,2,3,0:T(8,128)S(1)}, f32[5,48,14,3]{1,2,3,0:T(8,128)S(1)}, u32[]{:S(2)}, u32[]{:S(2)}) %collective-permute-start.2) | collective-permute-done | bytes 40352 | tf_op jit(solution)/shard_map/ppermute | solution.py:25
  53.5 2.1 copy.42
  57.6 18.3 %broadcast_select_fusion.7 = (f32[64,1024]{1,0:T(8,128)S(1)}, f32[64,1024]{1,0:T(8,128)}, f32[64,1024]{1,0:T(8,128)S(1)}, f32[64,1024]{1,0:T(8,128)S(1)}, pred[6...) fusion(f32[64,1024]{1,0:T(8,128)S(1)} %copy-done.11, ...), kind=kLoop, calls=%fused_computation.298 | loop fusion | flops 5046272 | bytes 4531304 | tf_op jit(solution)/shard_map/jit(_where)/select_n | solution.py:61
  76.0 3.5 %collective-permute-start.9 = (f32[2,1024]{1,0:T(2,128)S(1)}, f32[2,1024]{1,0:T(2,128)S(1)}, u32[]{:S(2)}, u32[]{:S(2)}) collective-permute-start(f32[2,1024]{1,0:T(2,128)S(1)} %get-tuple-element.107), channel_id=1, source_target_pairs={{8,0},{16,8},{24,16},{32,24},{40,32},{48,40},{56,48},{64,56},{72,6... | collective-permute-start | bytes 24584 | tf_op jit(solution)/shard_map/ppermute | solution.py:25
  79.5 1.9 collective-permute-start.8
  81.4 5.1 %collective-permute-done.8 = f32[2,1024]{1,0:T(2,128)S(1)} collective-permute-done((f32[2,1024]{1,0:T(2,128)S(1)}, f32[2,1024]{1,0:T(2,128)S(1)}, u32[]{:S(2)}, u32[]{:S(2)}) %collective-permute-start.8) | collective-permute-done | bytes 8224 | tf_op jit(solution)/shard_map/ppermute | solution.py:23
  89.2 3.9 %collective-permute-start.11 = (f32[68,2]{1,0:T(8,128)}, f32[68,2]{1,0:T(8,128)}, u32[]{:S(2)}, u32[]{:S(2)}) collective-permute-start(f32[68,2]{1,0:T(8,128)} %get-tuple-element.89), channel_id=1, source_target_pairs={{1,0},{2,1},{3,2},{4,3},{5,4},{6,5},{7,6},{9,8},{10,9},{11,10},{12... | collective-permute-start | bytes 1640 | tf_op jit(solution)/shard_map/ppermute | solution.py:25
  93.4 3.1 %collective-permute-done.11 = f32[68,2]{1,0:T(8,128)} collective-permute-done((f32[68,2]{1,0:T(8,128)}, f32[68,2]{1,0:T(8,128)}, u32[]{:S(2)}, u32[]{:S(2)}) %collective-permute-start.11) | collective-permute-done | bytes 576 | tf_op jit(solution)/shard_map/ppermute | solution.py:25
  97.8 2.7 broadcast_select_fusion.6
  102.5 2.4 collective-permute-start.12
  104.9 4.7 %collective-permute-done.12 = f32[2,1024]{1,0:T(2,128)S(1)} collective-permute-done((f32[2,1024]{1,0:T(2,128)S(1)}, f32[2,1024]{1,0:T(2,128)S(1)}, u32[]{:S(2)}, u32[]{:S(2)}) %collective-permute-start.12) | collective-permute-done | bytes 8224 | tf_op jit(solution)/shard_map/ppermute | solution.py:23
  112.2 3.9 %collective-permute-start.15 = (f32[68,2]{1,0:T(8,128)}, f32[68,2]{1,0:T(8,128)}, u32[]{:S(2)}, u32[]{:S(2)}) collective-permute-start(f32[68,2]{1,0:T(8,128)} %get-tuple-element.85), channel_id=1, source_target_pairs={{1,0},{2,1},{3,2},{4,3},{5,4},{6,5},{7,6},{9,8},{10,9},{11,10},{12... | collective-permute-start | bytes 1640 | tf_op jit(solution)/shard_map/ppermute | solution.py:25
  116.4 3.1 %collective-permute-done.15 = f32[68,2]{1,0:T(8,128)} collective-permute-done((f32[68,2]{1,0:T(8,128)}, f32[68,2]{1,0:T(8,128)}, u32[]{:S(2)}, u32[]{:S(2)}) %collective-permute-start.15) | collective-permute-done | bytes 576 | tf_op jit(solution)/shard_map/ppermute | solution.py:25
  120.7 2.8 broadcast_select_fusion.5
  125.4 2.4 collective-permute-start.16
  127.9 4.7 %collective-permute-done.16 = f32[2,1024]{1,0:T(2,128)S(1)} collective-permute-done((f32[2,1024]{1,0:T(2,128)S(1)}, f32[2,1024]{1,0:T(2,128)S(1)}, u32[]{:S(2)}, u32[]{:S(2)}) %collective-permute-start.16) | collective-permute-done | bytes 8224 | tf_op jit(solution)/shard_map/ppermute | solution.py:23
  135.1 3.9 %collective-permute-start.19 = (f32[68,2]{1,0:T(8,128)}, f32[68,2]{1,0:T(8,128)}, u32[]{:S(2)}, u32[]{:S(2)}) collective-permute-start(f32[68,2]{1,0:T(8,128)} %get-tuple-element.81), channel_id=1, source_target_pairs={{1,0},{2,1},{3,2},{4,3},{5,4},{6,5},{7,6},{9,8},{10,9},{11,10},{12... | collective-permute-start | bytes 1640 | tf_op jit(solution)/shard_map/ppermute | solution.py:25
  139.4 3.1 %collective-permute-done.19 = f32[68,2]{1,0:T(8,128)} collective-permute-done((f32[68,2]{1,0:T(8,128)}, f32[68,2]{1,0:T(8,128)}, u32[]{:S(2)}, u32[]{:S(2)}) %collective-permute-start.19) | collective-permute-done | bytes 576 | tf_op jit(solution)/shard_map/ppermute | solution.py:25
  143.7 2.7 broadcast_select_fusion.4
  148.4 2.6 collective-permute-start.20
  151.0 4.7 %collective-permute-done.20 = f32[2,1024]{1,0:T(2,128)S(1)} collective-permute-done((f32[2,1024]{1,0:T(2,128)S(1)}, f32[2,1024]{1,0:T(2,128)S(1)}, u32[]{:S(2)}, u32[]{:S(2)}) %collective-permute-start.20) | collective-permute-done | bytes 8224 | tf_op jit(solution)/shard_map/ppermute | solution.py:23
  158.3 3.9 %collective-permute-start.23 = (f32[68,2]{1,0:T(8,128)}, f32[68,2]{1,0:T(8,128)}, u32[]{:S(2)}, u32[]{:S(2)}) collective-permute-start(f32[68,2]{1,0:T(8,128)} %get-tuple-element.77), channel_id=1, source_target_pairs={{1,0},{2,1},{3,2},{4,3},{5,4},{6,5},{7,6},{9,8},{10,9},{11,10},{12... | collective-permute-start | bytes 1640 | tf_op jit(solution)/shard_map/ppermute | solution.py:25
  162.5 3.1 %collective-permute-done.23 = f32[68,2]{1,0:T(8,128)} collective-permute-done((f32[68,2]{1,0:T(8,128)}, f32[68,2]{1,0:T(8,128)}, u32[]{:S(2)}, u32[]{:S(2)}) %collective-permute-start.23) | collective-permute-done | bytes 576 | tf_op jit(solution)/shard_map/ppermute | solution.py:25
  166.9 2.8 broadcast_select_fusion.3
  171.6 2.4 collective-permute-start.24
  174.0 4.7 %collective-permute-done.24 = f32[2,1024]{1,0:T(2,128)S(1)} collective-permute-done((f32[2,1024]{1,0:T(2,128)S(1)}, f32[2,1024]{1,0:T(2,128)S(1)}, u32[]{:S(2)}, u32[]{:S(2)}) %collective-permute-start.24) | collective-permute-done | bytes 8224 | tf_op jit(solution)/shard_map/ppermute | solution.py:23
  181.3 3.9 %collective-permute-start.27 = (f32[68,2]{1,0:T(8,128)}, f32[68,2]{1,0:T(8,128)}, u32[]{:S(2)}, u32[]{:S(2)}) collective-permute-start(f32[68,2]{1,0:T(8,128)} %get-tuple-element.73), channel_id=1, source_target_pairs={{1,0},{2,1},{3,2},{4,3},{5,4},{6,5},{7,6},{9,8},{10,9},{11,10},{12... | collective-permute-start | bytes 1640 | tf_op jit(solution)/shard_map/ppermute | solution.py:25
  189.9 2.8 broadcast_select_fusion.2
  194.6 2.4 collective-permute-start.28
  197.7 3.9 %collective-permute-done.28 = f32[2,1024]{1,0:T(2,128)S(1)} collective-permute-done((f32[2,1024]{1,0:T(2,128)S(1)}, f32[2,1024]{1,0:T(2,128)S(1)}, u32[]{:S(2)}, u32[]{:S(2)}) %collective-permute-start.28) | collective-permute-done | bytes 8224 | tf_op jit(solution)/shard_map/ppermute | solution.py:23
  204.3 3.9 %collective-permute-start.31 = (f32[68,2]{1,0:T(8,128)}, f32[68,2]{1,0:T(8,128)}, u32[]{:S(2)}, u32[]{:S(2)}) collective-permute-start(f32[68,2]{1,0:T(8,128)} %get-tuple-element.69), channel_id=1, source_target_pairs={{1,0},{2,1},{3,2},{4,3},{5,4},{6,5},{7,6},{9,8},{10,9},{11,10},{12... | collective-permute-start | bytes 1640 | tf_op jit(solution)/shard_map/ppermute | solution.py:25
  209.1 2.6 collective-permute-done.31
  212.9 2.8 broadcast_select_fusion.1
  218.9 2.4 collective-permute-start.32
  223.2 2.9 %collective-permute-done.32 = f32[2,1024]{1,0:T(2,128)S(1)} collective-permute-done((f32[2,1024]{1,0:T(2,128)}, f32[2,1024]{1,0:T(2,128)S(1)}, u32[]{:S(2)}, u32[]{:S(2)}) %collective-permute-start.32) | collective-permute-done | bytes 8224 | tf_op jit(solution)/shard_map/ppermute | solution.py:23
  229.0 3.9 %collective-permute-start.35 = (f32[68,2]{1,0:T(8,128)S(1)}, f32[68,2]{1,0:T(8,128)S(1)}, u32[]{:S(2)}, u32[]{:S(2)}) collective-permute-start(f32[68,2]{1,0:T(8,128)S(1)} %get-tuple-element.65), channel_id=1, source_target_pairs={{1,0},{2,1},{3,2},{4,3},{5,4},{6,5},{7,6},{9,8},{10,9},{11,10},{12... | collective-permute-start | bytes 1640 | tf_op jit(solution)/shard_map/ppermute | solution.py:25
  233.1 14.7 %fusion.8 = f32[5,48,8,128]{3,2,0,1:T(8,128)} fusion(f32[5,48,8,128]{3,2,0,1:T(8,128)} %copy-done, f32[5,48,3,128]{3,2,0,1:T(4,128)S(1)} %copy.36, f32[5,48,14,3]{3,2,0,1:T(8,128)S(1)} %copy.44, f32[5,48,3,128]{3,2,0,1:T(4,128)} %copy-done.3, f32[5,48,14,3]{3,2,0,1:T(8,128)} %copy.42, f32[5,48,11,128]{3,2,0,1:T(8,128)} %copy-done.1, ...), kind=kLoop, calls=%fused_computation.14 | loop fusion | flops 12533760 | bytes 6126336 | tf_op jit(solution)/shard_map/add | solution.py:94
  248.2 10.1 %subtract_select_fusion = (f32[64,1024]{1,0:T(8,128)}, f32[64,1024]{1,0:T(8,128)S(1)}) fusion(pred[1024]{0:T(1024)(128)(4,1)S(1)} %broadcast_in_dim.374, f32[64,1024]{1,0:T(8,128)S(1)} %copy-done.24, pred[1024]{0:T(1024)(128)(4,1)S(1)} %broadcast_in_dim.370, f32[64,1024]{1,0:T(8,128)S(1)} %copy-done.23, f32[64,1024]{1,0:T(8,128)S(1)} %copy-done.22, ...), kind=kLoop, calls=%fused_computation.43 | loop fusion | flops 6029312 | bytes 5857332 | tf_op jit(solution)/shard_map/jit(_where)/select_n | solution.py:62
  259.1 17.3 %select_add_fusion = f32[64,1024]{1,0:T(8,128)S(1)} fusion(pred[64,1024]{1,0:T(8,128)(4,1)S(1)} %copy-done.41, pred[64,1024]{1,0:T(8,128)(4,1)S(1)} %copy-done.40, pred[64,1024]{1,0:T(8,128)(4,1)S(1)} %copy-done.39, pred[64,1024]{1,0:T(8,128)(4,1)S(1)} %copy-done.38, pred[64,1024]{1,0:T(8,128)(4,1)S(1)} %copy-done.37, pred[64,1024]{1,0:T(8,128)(4,1)S(1)} %copy-done.36, ...), kind=kLoop, calls=%fused_computation.262 | loop fusion | flops 5701632 | bytes 3481704 | tf_op jit(solution)/shard_map/add | solution.py:63
  276.4 3.6 %reshape.188 = f32[8,8,128,8]{3,2,1,0:T(8,128)} reshape(f32[64,1024]{1,0:T(8,128)S(1)} %select_add_fusion) | data formatting | bytes 524288 | tf_op jit(solution)/shard_map/reshape | solution.py:181
  280.0 2.6 reduce_sum.9
  (233 shorter events, 73.2 us)
Async XLA Ops:
  0.6 15.6 %copy-start.7 = (f32[5,48,8,128]{3,2,1,0:T(8,128)S(1)}, f32[5,48,8,128]{3,2,1,0:T(8,128)}, u32[]{:S(2)}) copy-start(f32[5,48,8,128]{3,2,1,0:T(8,128)} %param.13) | copy-start | bytes 2949124
  3.3 26.9 %collective-permute-start.1 = (f32[5,48,3,128]{3,1,2,0:T(8,128)}, f32[5,48,3,128]{3,1,2,0:T(8,128)}, u32[]{:S(2)}, u32[]{:S(2)}) collective-permute-start(f32[5,48,3,128]{3,1,2,0:T(8,128)} %copy.51), channel_id=1, source_target_pairs={{0,8},{8,16},{16,24},{24,32},{32,40},{40,48},{48,56},{56,64},{64,7... | collective-permute-start | bytes 1105928 | tf_op jit(solution)/shard_map/ppermute | solution.py:23
  6.0 25.3 %collective-permute-start = (f32[5,48,3,128]{3,1,2,0:T(8,128)}, f32[5,48,3,128]{3,1,2,0:T(8,128)}, u32[]{:S(2)}, u32[]{:S(2)}) collective-permute-start(f32[5,48,3,128]{3,1,2,0:T(8,128)} %copy.50), channel_id=1, source_target_pairs={{8,0},{16,8},{24,16},{32,24},{40,32},{48,40},{56,48},{64,56},{72,6... | collective-permute-start | bytes 1105928 | tf_op jit(solution)/shard_map/ppermute | solution.py:25
  11.9 10.0 %collective-permute-start.5 = (f32[2,1024]{1,0:T(2,128)S(1)}, f32[2,1024]{1,0:T(2,128)S(1)}, u32[]{:S(2)}, u32[]{:S(2)}) collective-permute-start(f32[2,1024]{1,0:T(2,128)S(1)} %get-tuple-element.109), channel_id=1, source_target_pairs={{8,0},{16,8},{24,16},{32,24},{40,32},{48,40},{56,48},{64,56},{72,6... | collective-permute-start | bytes 24584 | tf_op jit(solution)/shard_map/ppermute | solution.py:25
  13.9 8.0 %collective-permute-start.4 = (f32[2,1024]{1,0:T(2,128)S(1)}, f32[2,1024]{1,0:T(2,128)S(1)}, u32[]{:S(2)}, u32[]{:S(2)}) collective-permute-start(f32[2,1024]{1,0:T(2,128)S(1)} %get-tuple-element.108), channel_id=1, source_target_pairs={{0,8},{8,16},{16,24},{24,32},{32,40},{40,48},{48,56},{56,64},{64,7... | collective-permute-start | bytes 24584 | tf_op jit(solution)/shard_map/ppermute | solution.py:23
  16.4 18.1 %copy-start = (f32[5,48,8,128]{3,2,0,1:T(8,128)}, f32[5,48,8,128]{3,2,0,1:T(8,128)S(1)}, u32[]{:S(2)}) copy-start(f32[5,48,8,128]{3,2,0,1:T(8,128)S(1)} %get-tuple-element.57) | copy-start | bytes 2949124
  22.6 24.8 %collective-permute-start.6 = (f32[68,2]{1,0:T(8,128)}, f32[68,2]{1,0:T(8,128)S(1)}, u32[]{:S(2)}, u32[]{:S(2)}) collective-permute-start(f32[68,2]{1,0:T(8,128)} %get-tuple-element.92), channel_id=1, source_target_pairs={{0,1},{1,2},{2,3},{3,4},{4,5},{5,6},{6,7},{8,9},{9,10},{10,11},{11... | collective-permute-start | bytes 1640 | tf_op jit(solution)/shard_map/ppermute | solution.py:23
  27.6 19.8 %collective-permute-start.7 = (f32[68,2]{1,0:T(8,128)}, f32[68,2]{1,0:T(8,128)S(1)}, u32[]{:S(2)}, u32[]{:S(2)}) collective-permute-start(f32[68,2]{1,0:T(8,128)} %get-tuple-element.93), channel_id=1, source_target_pairs={{1,0},{2,1},{3,2},{4,3},{5,4},{6,5},{7,6},{9,8},{10,9},{11,10},{12... | collective-permute-start | bytes 1640 | tf_op jit(solution)/shard_map/ppermute | solution.py:25
  39.5 8.9 %collective-permute-start.3 = (f32[5,48,14,3]{1,2,3,0:T(8,128)S(1)}, f32[5,48,14,3]{1,2,3,0:T(8,128)S(1)}, u32[]{:S(2)}, u32[]{:S(2)}) collective-permute-start(f32[5,48,14,3]{1,2,3,0:T(8,128)S(1)} %copy.43), channel_id=1, source_target_pairs={{0,1},{1,2},{2,3},{3,4},{4,5},{5,6},{6,7},{8,9},{9,10},{10,11},{11... | collective-permute-start | bytes 120968 | tf_op jit(solution)/shard_map/ppermute | solution.py:23
  45.5 8.0 %collective-permute-start.2 = (f32[5,48,14,3]{1,2,3,0:T(8,128)S(1)}, f32[5,48,14,3]{1,2,3,0:T(8,128)S(1)}, u32[]{:S(2)}, u32[]{:S(2)}) collective-permute-start(f32[5,48,14,3]{1,2,3,0:T(8,128)S(1)} %copy.41), channel_id=1, source_target_pairs={{1,0},{2,1},{3,2},{4,3},{5,4},{6,5},{7,6},{9,8},{10,9},{11,10},{12... | collective-permute-start | bytes 120968 | tf_op jit(solution)/shard_map/ppermute | solution.py:25
  57.6 35.5 %copy-start.54 = (pred[16]{0:T(512)(128)(4,1)S(1)}, pred[16]{0:T(512)(128)(4,1)}, u32[]{:S(2)}) copy-start(pred[16]{0:T(512)(128)(4,1)} %get-tuple-element.111) | copy-start | bytes 52
  76.0 5.4 %collective-permute-start.9 = (f32[2,1024]{1,0:T(2,128)S(1)}, f32[2,1024]{1,0:T(2,128)S(1)}, u32[]{:S(2)}, u32[]{:S(2)}) collective-permute-start(f32[2,1024]{1,0:T(2,128)S(1)} %get-tuple-element.107), channel_id=1, source_target_pairs={{8,0},{16,8},{24,16},{32,24},{40,32},{48,40},{56,48},{64,56},{72,6... | collective-permute-start | bytes 24584 | tf_op jit(solution)/shard_map/ppermute | solution.py:25
  79.5 7.1 %collective-permute-start.8 = (f32[2,1024]{1,0:T(2,128)S(1)}, f32[2,1024]{1,0:T(2,128)S(1)}, u32[]{:S(2)}, u32[]{:S(2)}) collective-permute-start(f32[2,1024]{1,0:T(2,128)S(1)} %get-tuple-element.106), channel_id=1, source_target_pairs={{0,8},{8,16},{16,24},{24,32},{32,40},{40,48},{48,56},{56,64},{64,7... | collective-permute-start | bytes 24584 | tf_op jit(solution)/shard_map/ppermute | solution.py:23
  87.3 6.2 %collective-permute-start.10 = (f32[68,2]{1,0:T(8,128)}, f32[68,2]{1,0:T(8,128)}, u32[]{:S(2)}, u32[]{:S(2)}) collective-permute-start(f32[68,2]{1,0:T(8,128)} %get-tuple-element.88), channel_id=1, source_target_pairs={{0,1},{1,2},{2,3},{3,4},{4,5},{5,6},{6,7},{8,9},{9,10},{10,11},{11... | collective-permute-start | bytes 1640 | tf_op jit(solution)/shard_map/ppermute | solution.py:23
  89.2 7.4 %collective-permute-start.11 = (f32[68,2]{1,0:T(8,128)}, f32[68,2]{1,0:T(8,128)}, u32[]{:S(2)}, u32[]{:S(2)}) collective-permute-start(f32[68,2]{1,0:T(8,128)} %get-tuple-element.89), channel_id=1, source_target_pairs={{1,0},{2,1},{3,2},{4,3},{5,4},{6,5},{7,6},{9,8},{10,9},{11,10},{12... | collective-permute-start | bytes 1640 | tf_op jit(solution)/shard_map/ppermute | solution.py:25
  93.3 22.8 %copy-start.53 = (pred[16]{0:T(512)(128)(4,1)S(1)}, pred[16]{0:T(512)(128)(4,1)}, u32[]{:S(2)}) copy-start(pred[16]{0:T(512)(128)(4,1)} %get-tuple-element.112) | copy-start | bytes 52
  100.5 4.3 %collective-permute-start.13 = (f32[2,1024]{1,0:T(2,128)S(1)}, f32[2,1024]{1,0:T(2,128)S(1)}, u32[]{:S(2)}, u32[]{:S(2)}) collective-permute-start(f32[2,1024]{1,0:T(2,128)S(1)} %get-tuple-element.105), channel_id=1, source_target_pairs={{8,0},{16,8},{24,16},{32,24},{40,32},{48,40},{56,48},{64,56},{72,6... | collective-permute-start | bytes 24584 | tf_op jit(solution)/shard_map/ppermute | solution.py:25
  102.5 7.1 %collective-permute-start.12 = (f32[2,1024]{1,0:T(2,128)S(1)}, f32[2,1024]{1,0:T(2,128)S(1)}, u32[]{:S(2)}, u32[]{:S(2)}) collective-permute-start(f32[2,1024]{1,0:T(2,128)S(1)} %get-tuple-element.104), channel_id=1, source_target_pairs={{0,8},{8,16},{16,24},{24,32},{32,40},{40,48},{48,56},{56,64},{64,7... | collective-permute-start | bytes 24584 | tf_op jit(solution)/shard_map/ppermute | solution.py:23
  110.2 6.2 %collective-permute-start.14 = (f32[68,2]{1,0:T(8,128)}, f32[68,2]{1,0:T(8,128)}, u32[]{:S(2)}, u32[]{:S(2)}) collective-permute-start(f32[68,2]{1,0:T(8,128)} %get-tuple-element.84), channel_id=1, source_target_pairs={{0,1},{1,2},{2,3},{3,4},{4,5},{5,6},{6,7},{8,9},{9,10},{10,11},{11... | collective-permute-start | bytes 1640 | tf_op jit(solution)/shard_map/ppermute | solution.py:23
  112.2 7.4 %collective-permute-start.15 = (f32[68,2]{1,0:T(8,128)}, f32[68,2]{1,0:T(8,128)}, u32[]{:S(2)}, u32[]{:S(2)}) collective-permute-start(f32[68,2]{1,0:T(8,128)} %get-tuple-element.85), channel_id=1, source_target_pairs={{1,0},{2,1},{3,2},{4,3},{5,4},{6,5},{7,6},{9,8},{10,9},{11,10},{12... | collective-permute-start | bytes 1640 | tf_op jit(solution)/shard_map/ppermute | solution.py:25
  116.3 22.8 %copy-start.52 = (pred[16]{0:T(512)(128)(4,1)S(1)}, pred[16]{0:T(512)(128)(4,1)}, u32[]{:S(2)}) copy-start(pred[16]{0:T(512)(128)(4,1)} %get-tuple-element.113) | copy-start | bytes 52
  123.5 4.3 %collective-permute-start.17 = (f32[2,1024]{1,0:T(2,128)S(1)}, f32[2,1024]{1,0:T(2,128)S(1)}, u32[]{:S(2)}, u32[]{:S(2)}) collective-permute-start(f32[2,1024]{1,0:T(2,128)S(1)} %get-tuple-element.103), channel_id=1, source_target_pairs={{8,0},{16,8},{24,16},{32,24},{40,32},{48,40},{56,48},{64,56},{72,6... | collective-permute-start | bytes 24584 | tf_op jit(solution)/shard_map/ppermute | solution.py:25
  125.4 7.1 %collective-permute-start.16 = (f32[2,1024]{1,0:T(2,128)S(1)}, f32[2,1024]{1,0:T(2,128)S(1)}, u32[]{:S(2)}, u32[]{:S(2)}) collective-permute-start(f32[2,1024]{1,0:T(2,128)S(1)} %get-tuple-element.102), channel_id=1, source_target_pairs={{0,8},{8,16},{16,24},{24,32},{32,40},{40,48},{48,56},{56,64},{64,7... | collective-permute-start | bytes 24584 | tf_op jit(solution)/shard_map/ppermute | solution.py:23
  133.2 6.2 %collective-permute-start.18 = (f32[68,2]{1,0:T(8,128)}, f32[68,2]{1,0:T(8,128)}, u32[]{:S(2)}, u32[]{:S(2)}) collective-permute-start(f32[68,2]{1,0:T(8,128)} %get-tuple-element.80), channel_id=1, source_target_pairs={{0,1},{1,2},{2,3},{3,4},{4,5},{5,6},{6,7},{8,9},{9,10},{10,11},{11... | collective-permute-start | bytes 1640 | tf_op jit(solution)/shard_map/ppermute | solution.py:23
  135.1 7.4 %collective-permute-start.19 = (f32[68,2]{1,0:T(8,128)}, f32[68,2]{1,0:T(8,128)}, u32[]{:S(2)}, u32[]{:S(2)}) collective-permute-start(f32[68,2]{1,0:T(8,128)} %get-tuple-element.81), channel_id=1, source_target_pairs={{1,0},{2,1},{3,2},{4,3},{5,4},{6,5},{7,6},{9,8},{10,9},{11,10},{12... | collective-permute-start | bytes 1640 | tf_op jit(solution)/shard_map/ppermute | solution.py:25
  139.2 23.0 %copy-start.51 = (pred[16]{0:T(512)(128)(4,1)S(1)}, pred[16]{0:T(512)(128)(4,1)}, u32[]{:S(2)}) copy-start(pred[16]{0:T(512)(128)(4,1)} %get-tuple-element.114) | copy-start | bytes 52
  146.5 4.5 %collective-permute-start.21 = (f32[2,1024]{1,0:T(2,128)S(1)}, f32[2,1024]{1,0:T(2,128)S(1)}, u32[]{:S(2)}, u32[]{:S(2)}) collective-permute-start(f32[2,1024]{1,0:T(2,128)S(1)} %get-tuple-element.101), channel_id=1, source_target_pairs={{8,0},{16,8},{24,16},{32,24},{40,32},{48,40},{56,48},{64,56},{72,6... | collective-permute-start | bytes 24584 | tf_op jit(solution)/shard_map/ppermute | solution.py:25
  148.4 7.3 %collective-permute-start.20 = (f32[2,1024]{1,0:T(2,128)S(1)}, f32[2,1024]{1,0:T(2,128)S(1)}, u32[]{:S(2)}, u32[]{:S(2)}) collective-permute-start(f32[2,1024]{1,0:T(2,128)S(1)} %get-tuple-element.100), channel_id=1, source_target_pairs={{0,8},{8,16},{16,24},{24,32},{32,40},{40,48},{48,56},{56,64},{64,7... | collective-permute-start | bytes 24584 | tf_op jit(solution)/shard_map/ppermute | solution.py:23
  156.4 6.2 %collective-permute-start.22 = (f32[68,2]{1,0:T(8,128)}, f32[68,2]{1,0:T(8,128)}, u32[]{:S(2)}, u32[]{:S(2)}) collective-permute-start(f32[68,2]{1,0:T(8,128)} %get-tuple-element.76), channel_id=1, source_target_pairs={{0,1},{1,2},{2,3},{3,4},{4,5},{5,6},{6,7},{8,9},{9,10},{10,11},{11... | collective-permute-start | bytes 1640 | tf_op jit(solution)/shard_map/ppermute | solution.py:23
  158.3 7.4 %collective-permute-start.23 = (f32[68,2]{1,0:T(8,128)}, f32[68,2]{1,0:T(8,128)}, u32[]{:S(2)}, u32[]{:S(2)}) collective-permute-start(f32[68,2]{1,0:T(8,128)} %get-tuple-element.77), channel_id=1, source_target_pairs={{1,0},{2,1},{3,2},{4,3},{5,4},{6,5},{7,6},{9,8},{10,9},{11,10},{12... | collective-permute-start | bytes 1640 | tf_op jit(solution)/shard_map/ppermute | solution.py:25
  166.9 20.2 %copy-start.50 = (pred[16]{0:T(512)(128)(4,1)S(1)}, pred[16]{0:T(512)(128)(4,1)}, u32[]{:S(2)}) copy-start(pred[16]{0:T(512)(128)(4,1)} %get-tuple-element.115) | copy-start | bytes 52
  169.7 4.3 %collective-permute-start.25 = (f32[2,1024]{1,0:T(2,128)S(1)}, f32[2,1024]{1,0:T(2,128)S(1)}, u32[]{:S(2)}, u32[]{:S(2)}) collective-permute-start(f32[2,1024]{1,0:T(2,128)S(1)} %get-tuple-element.99), channel_id=1, source_target_pairs={{8,0},{16,8},{24,16},{32,24},{40,32},{48,40},{56,48},{64,56},{72,6... | collective-permute-start | bytes 24584 | tf_op jit(solution)/shard_map/ppermute | solution.py:25
  171.6 7.1 %collective-permute-start.24 = (f32[2,1024]{1,0:T(2,128)S(1)}, f32[2,1024]{1,0:T(2,128)S(1)}, u32[]{:S(2)}, u32[]{:S(2)}) collective-permute-start(f32[2,1024]{1,0:T(2,128)S(1)} %get-tuple-element.98), channel_id=1, source_target_pairs={{0,8},{8,16},{16,24},{24,32},{32,40},{40,48},{48,56},{56,64},{64,7... | collective-permute-start | bytes 24584 | tf_op jit(solution)/shard_map/ppermute | solution.py:23
  179.4 7.9 %collective-permute-start.26 = (f32[68,2]{1,0:T(8,128)}, f32[68,2]{1,0:T(8,128)}, u32[]{:S(2)}, u32[]{:S(2)}) collective-permute-start(f32[68,2]{1,0:T(8,128)} %get-tuple-element.72), channel_id=1, source_target_pairs={{0,1},{1,2},{2,3},{3,4},{4,5},{5,6},{6,7},{8,9},{9,10},{10,11},{11... | collective-permute-start | bytes 1640 | tf_op jit(solution)/shard_map/ppermute | solution.py:23
  181.3 7.4 %collective-permute-start.27 = (f32[68,2]{1,0:T(8,128)}, f32[68,2]{1,0:T(8,128)}, u32[]{:S(2)}, u32[]{:S(2)}) collective-permute-start(f32[68,2]{1,0:T(8,128)} %get-tuple-element.73), channel_id=1, source_target_pairs={{1,0},{2,1},{3,2},{4,3},{5,4},{6,5},{7,6},{9,8},{10,9},{11,10},{12... | collective-permute-start | bytes 1640 | tf_op jit(solution)/shard_map/ppermute | solution.py:25
  187.2 21.0 %copy-start.46 = (f32[13]{0:T(128)S(1)}, f32[13]{0:T(128)}, u32[]{:S(2)}) copy-start(f32[13]{0:T(128)} %param.20) | copy-start | bytes 160
  187.2 21.7 %copy-start.49 = (pred[16]{0:T(512)(128)(4,1)S(1)}, pred[16]{0:T(512)(128)(4,1)}, u32[]{:S(2)}) copy-start(pred[16]{0:T(512)(128)(4,1)} %get-tuple-element.116) | copy-start | bytes 52
  192.7 5.1 %collective-permute-start.29 = (f32[2,1024]{1,0:T(2,128)S(1)}, f32[2,1024]{1,0:T(2,128)S(1)}, u32[]{:S(2)}, u32[]{:S(2)}) collective-permute-start(f32[2,1024]{1,0:T(2,128)S(1)} %get-tuple-element.97), channel_id=1, source_target_pairs={{8,0},{16,8},{24,16},{32,24},{40,32},{48,40},{56,48},{64,56},{72,6... | collective-permute-start | bytes 24584 | tf_op jit(solution)/shard_map/ppermute | solution.py:25
  194.6 7.1 %collective-permute-start.28 = (f32[2,1024]{1,0:T(2,128)S(1)}, f32[2,1024]{1,0:T(2,128)S(1)}, u32[]{:S(2)}, u32[]{:S(2)}) collective-permute-start(f32[2,1024]{1,0:T(2,128)S(1)} %get-tuple-element.96), channel_id=1, source_target_pairs={{0,8},{8,16},{16,24},{24,32},{32,40},{40,48},{48,56},{56,64},{64,7... | collective-permute-start | bytes 24584 | tf_op jit(solution)/shard_map/ppermute | solution.py:23
  202.4 6.7 %collective-permute-start.30 = (f32[68,2]{1,0:T(8,128)}, f32[68,2]{1,0:T(8,128)}, u32[]{:S(2)}, u32[]{:S(2)}) collective-permute-start(f32[68,2]{1,0:T(8,128)} %get-tuple-element.68), channel_id=1, source_target_pairs={{0,1},{1,2},{2,3},{3,4},{4,5},{5,6},{6,7},{8,9},{9,10},{10,11},{11... | collective-permute-start | bytes 1640 | tf_op jit(solution)/shard_map/ppermute | solution.py:23
  204.3 7.4 %collective-permute-start.31 = (f32[68,2]{1,0:T(8,128)}, f32[68,2]{1,0:T(8,128)}, u32[]{:S(2)}, u32[]{:S(2)}) collective-permute-start(f32[68,2]{1,0:T(8,128)} %get-tuple-element.69), channel_id=1, source_target_pairs={{1,0},{2,1},{3,2},{4,3},{5,4},{6,5},{7,6},{9,8},{10,9},{11,10},{12... | collective-permute-start | bytes 1640 | tf_op jit(solution)/shard_map/ppermute | solution.py:25
  217.0 6.3 %collective-permute-start.33 = (f32[2,1024]{1,0:T(2,128)}, f32[2,1024]{1,0:T(2,128)S(1)}, u32[]{:S(2)}, u32[]{:S(2)}) collective-permute-start(f32[2,1024]{1,0:T(2,128)} %get-tuple-element.95), channel_id=1, source_target_pairs={{8,0},{16,8},{24,16},{32,24},{40,32},{48,40},{56,48},{64,56},{72,6... | collective-permute-start | bytes 24584 | tf_op jit(solution)/shard_map/ppermute | solution.py:25
  218.9 7.3 %collective-permute-start.32 = (f32[2,1024]{1,0:T(2,128)}, f32[2,1024]{1,0:T(2,128)S(1)}, u32[]{:S(2)}, u32[]{:S(2)}) collective-permute-start(f32[2,1024]{1,0:T(2,128)} %get-tuple-element.94), channel_id=1, source_target_pairs={{0,8},{8,16},{16,24},{24,32},{32,40},{40,48},{48,56},{56,64},{64,7... | collective-permute-start | bytes 24584 | tf_op jit(solution)/shard_map/ppermute | solution.py:23
  227.0 20.7 %collective-permute-start.34 = (f32[68,2]{1,0:T(8,128)S(1)}, f32[68,2]{1,0:T(8,128)S(1)}, u32[]{:S(2)}, u32[]{:S(2)}) collective-permute-start(f32[68,2]{1,0:T(8,128)S(1)} %get-tuple-element.64), channel_id=1, source_target_pairs={{0,1},{1,2},{2,3},{3,4},{4,5},{5,6},{6,7},{8,9},{9,10},{10,11},{11... | collective-permute-start | bytes 1640 | tf_op jit(solution)/shard_map/ppermute | solution.py:23
  229.0 18.8 %collective-permute-start.35 = (f32[68,2]{1,0:T(8,128)S(1)}, f32[68,2]{1,0:T(8,128)S(1)}, u32[]{:S(2)}, u32[]{:S(2)}) collective-permute-start(f32[68,2]{1,0:T(8,128)S(1)} %get-tuple-element.65), channel_id=1, source_target_pairs={{1,0},{2,1},{3,2},{4,3},{5,4},{6,5},{7,6},{9,8},{10,9},{11,10},{12... | collective-permute-start | bytes 1640 | tf_op jit(solution)/shard_map/ppermute | solution.py:25
  232.9 15.1 %copy-start.18 = (f32[64,1024]{1,0:T(8,128)S(1)}, f32[64,1024]{1,0:T(8,128)}, u32[]{:S(2)}) copy-start(f32[64,1024]{1,0:T(8,128)} %get-tuple-element.36) | copy-start | bytes 786436
  232.9 15.1 %copy-start.19 = (f32[64,1024]{1,0:T(8,128)S(1)}, f32[64,1024]{1,0:T(8,128)}, u32[]{:S(2)}) copy-start(f32[64,1024]{1,0:T(8,128)} %get-tuple-element.34) | copy-start | bytes 786436
  232.9 15.1 %copy-start.20 = (f32[64,1024]{1,0:T(8,128)S(1)}, f32[64,1024]{1,0:T(8,128)}, u32[]{:S(2)}) copy-start(f32[64,1024]{1,0:T(8,128)} %get-tuple-element.32) | copy-start | bytes 786436
  (50 other events, 503.2 us)
where the time goes:
time: 287 us; the launch traced here: 284 us
  other arithmetic  99.8 us (35%)
  starting transfers between devices  98.5 us (34%)
  waiting for transfers between devices  51.9 us (18%)
  local copies, waits for them, and re-layouts  29.3 us (10%)
    ppermute x18, starting transfers between devices, extended(): lax.ppermute(head, axis, [((i + 1) % count, i) for i in range(ends)])  54.1 us
    ppermute x18, starting transfers between devices, extended(): lax.ppermute(tail, axis, [(i, (i + 1) % count) for i in range(ends)])  44.4 us
    select_n x8, other arithmetic, advance(): jnp.where(active, advanced, level)  35.6 us
    ppermute x18, waiting for transfers between devices, extended(): lax.ppermute(tail, axis, [(i, (i + 1) % count) for i in range(ends)])  31.2 us
    ppermute x18, waiting for transfers between devices, extended(): lax.ppermute(head, axis, [((i + 1) % count, i) for i in range(ends)])  20.7 us
    add x1, other arithmetic, advance(): heating + jnp.where(active, yields * burned, 0.0)  17.3 us
    add x1, other arithmetic, atmos_step(): centre - COURANT * (centre[0:1] * deriv_x + centre[1:2] * deriv_y)  14.7 us
    select_n x1, other arithmetic, advance(): jnp.where(active, remaining - burned, remaining)  10.1 us
  transfers between devices with their start and end apart: 36, of which 18 were waited for; matrix products, arithmetic and copies ran while one was open for 14% of the time, Pallas kernels for 0%

commit v1 on v0

--- a/solution.py
+++ b/solution.py
@@ -62,6 +62,33 @@
         jnp.where(active, remaining - burned, remaining),
         heating + jnp.where(active, yields * burned, 0.0),
     )
+
+
+def spread_level(padded, level, spread, gain, wind_u, wind_v):
+    back_x = level - padded[..., 1:-3, 2:-2]
+    ahead_x = padded[..., 3:-1, 2:-2] - level
+    back_y = level - padded[..., 2:-2, 1:-3]
+    ahead_y = padded[..., 2:-2, 3:-1] - level
+    upwind = jnp.sqrt(
+        jnp.maximum(back_x, 0.0) ** 2
+        + jnp.minimum(ahead_x, 0.0) ** 2
+        + jnp.maximum(back_y, 0.0) ** 2
+        + jnp.minimum(ahead_y, 0.0) ** 2
+    )
+    slope_x = (
+        padded[..., :-4, 2:-2]
+        - 8.0 * padded[..., 1:-3, 2:-2]
+        + 8.0 * padded[..., 3:-1, 2:-2]
+        - padded[..., 4:, 2:-2]
+    ) / 12.0
+    slope_y = (
+        padded[..., 2:-2, :-4]
+        - 8.0 * padded[..., 2:-2, 1:-3]
+        + 8.0 * padded[..., 2:-2, 3:-1]
+        - padded[..., 2:-2, 4:]
+    ) / 12.0
+    pushing = jnp.maximum(wind_u * slope_x + wind_v * slope_y, 0.0)
+    return level - spread * (upwind + gain * pushing)
 
 
 def atmos_step(padded, heat_atm):
@@ -156,28 +183,31 @@
     )
     tile_on = tile_on.reshape(substep_count.shape)
     tiles_x, tiles_y = substep_count.shape
-    winds = surface_winds(surface, fire_rows, fire_cols, 0)
-    level, remaining = (level_set, fuel_left)
+    halo = 2 * SUBSTEPS
+    nsteps = jnp.where(tile_on, substep_count, 0).astype(jnp.float32)
+    nsteps = jnp.broadcast_to(nsteps[:, None, :, None], (tiles_x, TILE, tiles_y, TILE)).reshape(
+        fire_rows, fire_cols
+    )
+    stacked = extended(
+        jnp.stack([level_set, spread, gain, nsteps]), (("gx", 1), ("gy", 2)), halo
+    )
+    level, spread_ext, gain_ext, nsteps_ext = stacked[0], stacked[1], stacked[2], stacked[3]
+    winds = surface_winds(surface, fire_rows, fire_cols, halo)
+    inner = (slice(halo, halo + fire_rows), slice(halo, halo + fire_cols))
+    remaining = fuel_left
     heating = jnp.zeros_like(level_set)
     for substep in range(SUBSTEPS):
-        tile_active = tile_on & (substep < substep_count)
-        active = jnp.broadcast_to(
-            tile_active[:, None, :, None], (tiles_x, TILE, tiles_y, TILE)
-        ).reshape(fire_rows, fire_cols)
-        padded = fire_halo(level)
-        level, remaining, heating = advance(
-            padded,
-            level,
-            remaining,
-            heating,
-            spread,
-            gain,
-            burnout,
-            yields,
-            winds[0],
-            winds[1],
-            active,
+        active_ext = substep < nsteps_ext
+        padded = jnp.pad(level, 2)
+        moved = spread_level(padded, level, spread_ext, gain_ext, winds[0], winds[1])
+        burned = remaining / (1.0 + jnp.exp(moved[inner])) / burnout
+        active = active_ext[inner]
+        remaining, heating = (
+            jnp.where(active, remaining - burned, remaining),
+            heating + jnp.where(active, yields * burned, 0.0),
         )
+        level = jnp.where(active_ext, moved, level)
+    level = level[inner]
     heat_atm = heating.reshape(atmos_rows, RF, atmos_cols, RF).sum(axis=(1, 3)) / (RF * RF)
     return (atmos_step(padded_atm, heat_atm), level, remaining)
 

time: 287 us -> 145 us (0.51)
  starting transfers between devices: 98.5 us -> 25.1 us
  waiting for transfers between devices: 51.9 us -> 10.7 us
  other arithmetic: 99.8 us -> 69.1 us
  local copies, waits for them, and re-layouts: 29.3 us -> 34.6 us
    ppermute x18 -> x4, starting transfers between devices: 54.1 us -> 13.7 us  [extended(): lax.ppermute(head, axis, [((i + 1) % count, i) for i in range(ends)])]
    ppermute x18 -> x4, starting transfers between devices: 44.4 us -> 11.4 us  [extended(): lax.ppermute(tail, axis, [(i, (i + 1) % count) for i in range(ends)])]
    select_n x9, other arithmetic: 45.8 us -> 17.2 us  [the longest x1 10 us: shards(): jnp.where(active, remaining - burned, remaining)]
    ppermute x18 -> x4, waiting for transfers between devices: 31.2 us -> 4.63 us  [extended(): lax.ppermute(tail, axis, [(i, (i + 1) % count) for i in range(ends)])]
    another operation x0 -> x2, other arithmetic: none -> 17.2 us  [shards(): jnp.stack([level_set, spread, gain, nsteps])]
    ppermute x18 -> x4, waiting for transfers between devices: 20.7 us -> 6.03 us  [extended(): lax.ppermute(head, axis, [((i + 1) % count, i) for i in range(ends)])]
    concatenate x9 -> x2, other arithmetic: 8.7 us -> 0.53 us  [extended(): jnp.concatenate([lax.ppermute(tail, axis, [(i, (i + 1) % count) for i in...]
    slice x8 -> x1, other arithmetic: 5.74 us -> 0.04 us  [extended(): lax.slice_in_dim(cells, cells.shape[dim] - width, cells.shape[dim], axis=...]
  transfers between devices with their start and end apart: 36 -> 8, of which waited for: 18 -> 4; matrix products, arithmetic and copies ran while one was open for 14% -> 24% of each run, Pallas kernels for 0% -> 0%
where the time goes in v1:
time: 145 us; the launch traced here: 144 us
  other arithmetic  69.1 us (48%)
  local copies, waits for them, and re-layouts  34.6 us (24%)
  starting transfers between devices  25.1 us (17%)
  waiting for transfers between devices  10.7 us (7%)
  matrix products  2.35 us (2%)
  between operations  1.88 us (1%)
    add x1, other arithmetic, shards(): heating + jnp.where(active, yields * burned, 0.0)  17.9 us
    another operation x2, other arithmetic, shards(): jnp.stack([level_set, spread, gain, nsteps])  17.2 us
    ppermute x4, starting transfers between devices, extended(): lax.ppermute(head, axis, [((i + 1) % count, i) for i in range(ends)])  13.7 us
    ppermute x4, starting transfers between devices, extended(): lax.ppermute(tail, axis, [(i, (i + 1) % count) for i in range(ends)])  11.4 us
    add x1, other arithmetic, atmos_step(): centre - COURANT * (centre[0:1] * deriv_x + centre[1:2] * deriv_y)  10.4 us
    select_n x1, other arithmetic, shards(): jnp.where(active, remaining - burned, remaining)  10 us
    slice x4, local copies, waits for them, and re-layouts, extended(): head = lax.slice_in_dim(cells, 0, width, axis=dim)  7.41 us
    select_n x8, other arithmetic, shards(): level = jnp.where(active_ext, moved, level)  7.21 us
  transfers between devices with their start and end apart: 8, of which 4 were waited for; matrix products, arithmetic and copies ran while one was open for 24% of the time, Pallas kernels for 0%

profile of v1, /device:TPU:120, one launch (start us, length us, event | category | flops | bytes accessed | tf_op | source)
XLA Modules:
  0.0 143.6 jit_solution(15685591393694792971)
XLA Ops:
  0.7 1.7 %fusion.125 = (f32[5,48,3,128]{3,2,1,0:T(4,128)S(1)}, f32[5,48,3,128]{3,2,1,0:T(4,128)S(1)}) fusion(f32[5,48,8,128]{3,2,1,0:T(8,128)} %param.13), kind=kLoop, calls=%fused_computation.291 | loop fusion | bytes 1474560 | tf_op jit(solution)/shard_map/slice | solution.py:19
  2.4 0.8 copy.51
  3.2 2.0 %collective-permute-start.1 = (f32[5,48,3,128]{3,1,2,0:T(8,128)}, f32[5,48,3,128]{3,1,2,0:T(8,128)}, u32[]{:S(2)}, u32[]{:S(2)}) collective-permute-start(f32[5,48,3,128]{3,1,2,0:T(8,128)} %copy.51), channel_id=1, source_target_pairs={{0,8},{8,16},{16,24},{24,32},{32,40},{40,48},{48,56},{56,64},{64,7... | collective-permute-start | bytes 1105928 | tf_op jit(solution)/shard_map/ppermute | solution.py:23
  5.2 0.8 copy.50
  6.0 5.7 %collective-permute-start = (f32[5,48,3,128]{3,1,2,0:T(8,128)}, f32[5,48,3,128]{3,1,2,0:T(8,128)}, u32[]{:S(2)}, u32[]{:S(2)}) collective-permute-start(f32[5,48,3,128]{3,1,2,0:T(8,128)} %copy.50), channel_id=1, source_target_pairs={{8,0},{16,8},{24,16},{32,24},{40,32},{48,40},{56,48},{64,56},{72,6... | collective-permute-start | bytes 1105928 | tf_op jit(solution)/shard_map/ppermute | solution.py:25
  11.7 0.7 fusion.129
  13.4 0.7 fusion.128
  14.1 8.8 %select_bitcast_fusion.1 = (f32[1,64,1024]{2,1,0:T(8,128)S(1)}, pred[64,1024]{1,0:T(8,128)(4,1)S(1)}, pred[64,1024]{1,0:T(8,128)(4,1)S(1)}, pred[64,1024]{1,0:T(...) fusion(f32[]{:T(128)} %bitcast.15, f32[]{:T(128)} %bitcast.14, ...), kind=kLoop, calls=%fused_computation.203 | loop fusion | flops 1703936 | bytes 1376308 | tf_op jit(solution)/shard_map/stack | solution.py:192
  23.6 8.4 %select_bitcast_fusion = f32[1,64,1024]{2,1,0:T(8,128)S(1)} fusion(pred[64,1024]{1,0:T(8,128)(4,1)S(1)} %get-tuple-element.55, pred[64,1024]{1,0:T(8,128)(4,1)S(1)} %get-tuple-element.54, pred[64,1024]{1,0:T(8,128)(4,1)S(1)} %get-tuple-element.53, pred[64,1024]{1,0:T(8,128)(4,1)S(1)} %get-tuple-element.52, pred[64,1024]{1,0:T(8,128)(4,1)S(1)} %get-tuple-element.51, ...), kind=kLoop, calls=%fused_computation.202 | loop fusion | flops 851968 | bytes 1114164 | tf_op jit(solution)/shard_map/stack | solution.py:192
  32.1 1.9 %collective-permute-start.5 = (f32[4,16,1024]{2,1,0:T(8,128)S(1)}, f32[4,16,1024]{2,1,0:T(8,128)S(1)}, u32[]{:S(2)}, u32[]{:S(2)}) collective-permute-start(f32[4,16,1024]{2,1,0:T(8,128)S(1)} %get-tuple-element.61), channel_id=1, source_target_pairs={{8,0},{16,8},{24,16},{32,24},{40,32},{48,40},{56,48},{64,56},{72,6... | collective-permute-start | bytes 786440 | tf_op jit(solution)/shard_map/ppermute | solution.py:25
  34.0 2.4 %collective-permute-start.4 = (f32[4,16,1024]{2,1,0:T(8,128)S(1)}, f32[4,16,1024]{2,1,0:T(8,128)S(1)}, u32[]{:S(2)}, u32[]{:S(2)}) collective-permute-start(f32[4,16,1024]{2,1,0:T(8,128)S(1)} %get-tuple-element.60), channel_id=1, source_target_pairs={{0,8},{8,16},{16,24},{24,32},{32,40},{40,48},{48,56},{56,64},{64,7... | collective-permute-start | bytes 786440 | tf_op jit(solution)/shard_map/ppermute | solution.py:23
  36.4 1.1 constant_dynamic-update-slice_fusion.1
  38.3 0.7 fusion.126
  39.6 0.8 multiply_bitcast_fusion.1
  40.4 3.4 %collective-permute-done.4 = f32[4,16,1024]{2,1,0:T(8,128)S(1)} collective-permute-done((f32[4,16,1024]{2,1,0:T(8,128)S(1)}, f32[4,16,1024]{2,1,0:T(8,128)S(1)}, u32[]{:S(2)}, u32[]{:S(2)}) %collective-permute-start.4) | collective-permute-done | bytes 262176 | tf_op jit(solution)/shard_map/ppermute | solution.py:23
  44.1 5.0 %collective-permute-start.6 = (f32[4,96,16]{2,1,0:T(8,128)S(1)}, f32[4,96,16]{2,1,0:T(8,128)S(1)}, u32[]{:S(2)}, u32[]{:S(2)}) collective-permute-start(f32[4,96,16]{2,1,0:T(8,128)S(1)} %get-tuple-element.59), channel_id=1, source_target_pairs={{0,1},{1,2},{2,3},{3,4},{4,5},{5,6},{6,7},{8,9},{9,10},{10,11},{11... | collective-permute-start | bytes 73736 | tf_op jit(solution)/shard_map/ppermute | solution.py:23
  49.1 1.9 %collective-permute-start.7 = (f32[4,96,16]{2,1,0:T(8,128)S(1)}, f32[4,96,16]{2,1,0:T(8,128)S(1)}, u32[]{:S(2)}, u32[]{:S(2)}) collective-permute-start(f32[4,96,16]{2,1,0:T(8,128)S(1)} %get-tuple-element.58), channel_id=1, source_target_pairs={{1,0},{2,1},{3,2},{4,3},{5,4},{6,5},{7,6},{9,8},{10,9},{11,10},{12... | collective-permute-start | bytes 73736 | tf_op jit(solution)/shard_map/ppermute | solution.py:25
  51.1 1.2 collective-permute-done.6
  52.3 5.6 %collective-permute-done.7 = f32[4,96,16]{2,1,0:T(8,128)S(1)} collective-permute-done((f32[4,96,16]{2,1,0:T(8,128)S(1)}, f32[4,96,16]{2,1,0:T(8,128)S(1)}, u32[]{:S(2)}, u32[]{:S(2)}) %collective-permute-start.7) | collective-permute-done | bytes 24608 | tf_op jit(solution)/shard_map/ppermute | solution.py:25
  57.9 2.1 %concatenate.40 = f32[4,96,1056]{2,1,0:T(8,128)S(1)} concatenate(f32[4,96,16]{2,1,0:T(8,128)S(1)} %collective-permute-done.6, f32[4,96,1024]{2,1,0:T(8,128)} %copy-done.1, f32[4,96,16]{2,1,0:T(8,128)S(1)} %collective-permute-done.7), dimensions={2} | concatenate | bytes 3244032 | tf_op jit(solution)/shard_map/concatenate | solution.py:21
  60.0 0.8 slice_bitcast_fusion.4
  60.9 1.2 copy.36
  62.0 2.1 %constant_dynamic-update-slice_fusion = (f32[5,48,11,128]{3,2,0,1:T(8,128)}, f32[5,48,3,128]{3,2,0,1:T(4,128)S(1)}) fusion(f32[5,48,11,128]{3,2,0,1:T(8,128)} %get-tuple-element.64, f32[5,48,3,128]{3,1,2,0:T(8,128)} %collective-permute-done), kind=kLoop, calls=%fused_computation.250 | loop fusion | bytes 1228800 | tf_op jit(solution)/shard_map/concatenate | solution.py:21
  64.1 0.8 copy-done.2
  65.3 2.6 %fusion.123 = (f32[5,48,14,3]{3,2,0,1:T(8,128)}, f32[5,48,14,3]{3,2,0,1:T(8,128)}) fusion(f32[5,48,14,128]{3,2,0,1:T(8,128)S(1)} %pad_maximum_fusion), kind=kLoop, calls=%fused_computation.289 | loop fusion | bytes 161280 | tf_op jit(solution)/shard_map/slice | solution.py:19
  67.9 3.0 %copy.43 = f32[5,48,14,3]{1,2,3,0:T(8,128)} copy(f32[5,48,14,3]{3,2,0,1:T(8,128)} %get-tuple-element.57) | data formatting | bytes 80640 | tf_op jit(solution)/shard_map/slice | solution.py:20
  70.8 1.9 %collective-permute-start.3 = (f32[5,48,14,3]{1,2,3,0:T(8,128)}, f32[5,48,14,3]{1,2,3,0:T(8,128)}, u32[]{:S(2)}, u32[]{:S(2)}) collective-permute-start(f32[5,48,14,3]{1,2,3,0:T(8,128)} %copy.43), channel_id=1, source_target_pairs={{0,1},{1,2},{2,3},{3,4},{4,5},{5,6},{6,7},{8,9},{9,10},{10,11},{11... | collective-permute-start | bytes 120968 | tf_op jit(solution)/shard_map/ppermute | solution.py:23
  72.8 3.0 %copy.41 = f32[5,48,14,3]{1,2,3,0:T(8,128)} copy(f32[5,48,14,3]{3,2,0,1:T(8,128)} %get-tuple-element.56) | data formatting | bytes 80640 | tf_op jit(solution)/shard_map/slice | solution.py:19
  75.7 4.1 %collective-permute-start.2 = (f32[5,48,14,3]{1,2,3,0:T(8,128)}, f32[5,48,14,3]{1,2,3,0:T(8,128)}, u32[]{:S(2)}, u32[]{:S(2)}) collective-permute-start(f32[5,48,14,3]{1,2,3,0:T(8,128)} %copy.41), channel_id=1, source_target_pairs={{1,0},{2,1},{3,2},{4,3},{5,4},{6,5},{7,6},{9,8},{10,9},{11,10},{12... | collective-permute-start | bytes 120968 | tf_op jit(solution)/shard_map/ppermute | solution.py:25
  80.6 3.1 %copy.44 = f32[5,48,14,3]{3,2,0,1:T(8,128)} copy(f32[5,48,14,3]{1,2,3,0:T(8,128)} %collective-permute-done.3) | data formatting | bytes 80640 | tf_op jit(solution)/shard_map/ppermute | solution.py:23
  84.0 3.0 %copy.42 = f32[5,48,14,3]{3,2,0,1:T(8,128)} copy(f32[5,48,14,3]{1,2,3,0:T(8,128)} %collective-permute-done.2) | data formatting | bytes 80640 | tf_op jit(solution)/shard_map/ppermute | solution.py:25
  87.0 1.3 convolution_bitcast_fusion
  88.3 1.1 fusion.19
  89.4 0.9 fusion.116
  90.3 0.9 fusion.122
  91.2 0.9 fusion.121
  92.1 0.9 fusion.120
  93.0 0.9 fusion.119
  93.9 0.9 fusion.118
  94.8 0.9 fusion.117
  95.8 0.8 multiply_subtract_fusion
  96.6 1.0 slice_select_fusion
  97.7 10.0 %subtract_select_fusion = f32[64,1024]{1,0:T(8,128)} fusion(f32[96,1056]{1,0:T(8,128)S(1)} %multiply_subtract_fusion, pred[96,1056]{1,0:T(8,128)(4,1)S(1)} %get-tuple-element.23, f32[96,1056]{1,0:T(8,128)S(1)} %get-tuple-element.22, pred[96,1056]{1,0:T(8,128)(4,1)S(1)} %get-tuple-element.26, pred[96,1056]{1,0:T(8,128)(4,1)S(1)} %copy-done.25, ...), kind=kLoop, calls=%fused_computation.153 | loop fusion | flops 3473408 | bytes 3997748 | tf_op jit(solution)/shard_map/jit(_where)/select_n | solution.py:206
  107.7 17.9 %select_add_fusion = f32[64,1024]{1,0:T(8,128)S(1)} fusion(pred[64,1024]{1,0:T(8,128)(4,1)S(1)} %copy-done.22, pred[64,1024]{1,0:T(8,128)(4,1)S(1)} %copy-done.20, pred[64,1024]{1,0:T(8,128)(4,1)S(1)} %copy-done.18, pred[64,1024]{1,0:T(8,128)(4,1)S(1)} %copy-done.16, pred[64,1024]{1,0:T(8,128)(4,1)S(1)} %copy-done.14, pred[64,1024]{1,0:T(8,128)(4,1)S(1)} %copy-done.12, ...), kind=kLoop, calls=%fused_computation.199 | loop fusion | flops 5701632 | bytes 3997800 | tf_op jit(solution)/shard_map/add | solution.py:207
  125.6 3.7 %reshape.188 = f32[8,8,128,8]{3,2,1,0:T(8,128)} reshape(f32[64,1024]{1,0:T(8,128)S(1)} %select_add_fusion) | data formatting | bytes 524288 | tf_op jit(solution)/shard_map/reshape | solution.py:211
  129.3 2.7 %reduce_sum.9 = f32[8,128]{1,0:T(8,128)S(1)} reduce(f32[8,8,128,8]{3,2,1,0:T(8,128)} %reshape.188, f32[]{:T(128)} %constant.172.clone.1), dimensions={1,3}, to_apply=%region_1.2 | reduce | flops 64512 | bytes 266244 | tf_op jit(solution)/shard_map/reduce_sum | solution.py:211
  132.1 10.4 %fusion.8 = f32[5,48,8,128]{3,2,0,1:T(8,128)S(1)} fusion(f32[5,48,8,128]{3,2,0,1:T(8,128)S(1)} %get-tuple-element.65, f32[5,48,3,128]{3,2,0,1:T(4,128)S(1)} %copy.36, f32[5,48,14,3]{3,2,0,1:T(8,128)S(1)} %copy-done, f32[5,48,3,128]{3,2,0,1:T(4,128)} %copy-done.2, f32[5,48,14,3]{3,2,0,1:T(8,128)} %copy.42, f32[5,48,11,128]{3,2,0,1:T(8,128)} %get-tuple-element.68, ...), kind=kLoop, calls=%fused_computation.15 | loop fusion | flops 12533760 | bytes 6126336 | tf_op jit(solution)/shard_map/add | solution.py:121
  142.6 1.0 copy.49
  (89 shorter events, 4.4 us)
Async XLA Ops:
  0.6 11.1 %copy-start.27 = (f32[13]{0:T(128)S(1)}, f32[13]{0:T(128)}, u32[]{:S(2)}) copy-start(f32[13]{0:T(128)} %param.17) | copy-start | bytes 160
  0.6 12.5 %copy-start.31 = (s32[1,1,16]{2,1,0:T(1,128)S(1)}, s32[1,1,16]{2,1,0:T(1,128)}, u32[]{:S(2)}) copy-start(s32[1,1,16]{2,1,0:T(1,128)} %param.21) | copy-start | bytes 196
  0.7 12.5 %copy-start.32 = (s32[1,16]{1,0:T(1,128)S(1)}, s32[1,16]{1,0:T(1,128)}, u32[]{:S(2)}) copy-start(s32[1,16]{1,0:T(1,128)} %param.23) | copy-start | bytes 196
  0.7 12.7 %copy-start.28 = (f32[13]{0:T(128)S(1)}, f32[13]{0:T(128)}, u32[]{:S(2)}) copy-start(f32[13]{0:T(128)} %param.18) | copy-start | bytes 160
  0.7 13.4 %copy-start.26 = (s32[64,1024]{1,0:T(8,128)S(1)}, s32[64,1024]{1,0:T(8,128)}, u32[]{:S(2)}) copy-start(s32[64,1024]{1,0:T(8,128)} %param.16) | copy-start | bytes 786436
  3.2 28.8 %copy-start.23 = (f32[64,1024]{1,0:T(8,128)S(1)}, f32[64,1024]{1,0:T(8,128)}, u32[]{:S(2)}) copy-start(f32[64,1024]{1,0:T(8,128)} %param.14) | copy-start | bytes 786436
  3.2 57.7 %collective-permute-start.1 = (f32[5,48,3,128]{3,1,2,0:T(8,128)}, f32[5,48,3,128]{3,1,2,0:T(8,128)}, u32[]{:S(2)}, u32[]{:S(2)}) collective-permute-start(f32[5,48,3,128]{3,1,2,0:T(8,128)} %copy.51), channel_id=1, source_target_pairs={{0,8},{8,16},{16,24},{24,32},{32,40},{40,48},{48,56},{56,64},{64,7... | collective-permute-start | bytes 1105928 | tf_op jit(solution)/shard_map/ppermute | solution.py:23
  6.0 56.1 %collective-permute-start = (f32[5,48,3,128]{3,1,2,0:T(8,128)}, f32[5,48,3,128]{3,1,2,0:T(8,128)}, u32[]{:S(2)}, u32[]{:S(2)}) collective-permute-start(f32[5,48,3,128]{3,1,2,0:T(8,128)} %copy.50), channel_id=1, source_target_pairs={{8,0},{16,8},{24,16},{32,24},{40,32},{48,40},{56,48},{64,56},{72,6... | collective-permute-start | bytes 1105928 | tf_op jit(solution)/shard_map/ppermute | solution.py:25
  14.1 22.3 %copy-start.3 = (f32[5,48,8,128]{3,2,1,0:T(8,128)S(1)}, f32[5,48,8,128]{3,2,1,0:T(8,128)}, u32[]{:S(2)}) copy-start(f32[5,48,8,128]{3,2,1,0:T(8,128)} %param.13) | copy-start | bytes 2949124
  22.9 0.6 copy-start.5
  22.9 0.6 copy-start.7
  22.9 0.6 copy-start.9
  22.9 0.7 copy-start.11
  22.9 14.6 %copy-start.13 = (pred[64,1024]{1,0:T(8,128)(4,1)}, pred[64,1024]{1,0:T(8,128)(4,1)S(1)}, u32[]{:S(2)}) copy-start(pred[64,1024]{1,0:T(8,128)(4,1)S(1)} %get-tuple-element.51) | copy-start | bytes 196612
  22.9 14.6 %copy-start.15 = (pred[64,1024]{1,0:T(8,128)(4,1)}, pred[64,1024]{1,0:T(8,128)(4,1)S(1)}, u32[]{:S(2)}) copy-start(pred[64,1024]{1,0:T(8,128)(4,1)S(1)} %get-tuple-element.52) | copy-start | bytes 196612
  22.9 14.6 %copy-start.17 = (pred[64,1024]{1,0:T(8,128)(4,1)}, pred[64,1024]{1,0:T(8,128)(4,1)S(1)}, u32[]{:S(2)}) copy-start(pred[64,1024]{1,0:T(8,128)(4,1)S(1)} %get-tuple-element.53) | copy-start | bytes 196612
  22.9 14.6 %copy-start.19 = (pred[64,1024]{1,0:T(8,128)(4,1)}, pred[64,1024]{1,0:T(8,128)(4,1)S(1)}, u32[]{:S(2)}) copy-start(pred[64,1024]{1,0:T(8,128)(4,1)S(1)} %get-tuple-element.54) | copy-start | bytes 196612
  23.0 14.6 %copy-start.21 = (pred[64,1024]{1,0:T(8,128)(4,1)}, pred[64,1024]{1,0:T(8,128)(4,1)S(1)}, u32[]{:S(2)}) copy-start(pred[64,1024]{1,0:T(8,128)(4,1)S(1)} %get-tuple-element.55) | copy-start | bytes 196612
  32.0 5.7 %copy-start.29 = (f32[13]{0:T(128)S(1)}, f32[13]{0:T(128)}, u32[]{:S(2)}) copy-start(f32[13]{0:T(128)} %param.20) | copy-start | bytes 160
  32.0 6.3 %copy-start.30 = (f32[13]{0:T(128)S(1)}, f32[13]{0:T(128)}, u32[]{:S(2)}) copy-start(f32[13]{0:T(128)} %param.19) | copy-start | bytes 160
  32.1 8.3 %collective-permute-start.5 = (f32[4,16,1024]{2,1,0:T(8,128)S(1)}, f32[4,16,1024]{2,1,0:T(8,128)S(1)}, u32[]{:S(2)}, u32[]{:S(2)}) collective-permute-start(f32[4,16,1024]{2,1,0:T(8,128)S(1)} %get-tuple-element.61), channel_id=1, source_target_pairs={{8,0},{16,8},{24,16},{32,24},{40,32},{48,40},{56,48},{64,56},{72,6... | collective-permute-start | bytes 786440 | tf_op jit(solution)/shard_map/ppermute | solution.py:25
  34.0 9.8 %collective-permute-start.4 = (f32[4,16,1024]{2,1,0:T(8,128)S(1)}, f32[4,16,1024]{2,1,0:T(8,128)S(1)}, u32[]{:S(2)}, u32[]{:S(2)}) collective-permute-start(f32[4,16,1024]{2,1,0:T(8,128)S(1)} %get-tuple-element.60), channel_id=1, source_target_pairs={{0,8},{8,16},{16,24},{24,32},{32,40},{40,48},{48,56},{56,64},{64,7... | collective-permute-start | bytes 786440 | tf_op jit(solution)/shard_map/ppermute | solution.py:23
  44.0 8.3 %copy-start.1 = (f32[4,96,1024]{2,1,0:T(8,128)}, f32[4,96,1024]{2,1,0:T(8,128)S(1)}, u32[]{:S(2)}) copy-start(f32[4,96,1024]{2,1,0:T(8,128)S(1)} %pad_maximum_fusion.1) | copy-start | bytes 4718596
  44.1 8.2 %collective-permute-start.6 = (f32[4,96,16]{2,1,0:T(8,128)S(1)}, f32[4,96,16]{2,1,0:T(8,128)S(1)}, u32[]{:S(2)}, u32[]{:S(2)}) collective-permute-start(f32[4,96,16]{2,1,0:T(8,128)S(1)} %get-tuple-element.59), channel_id=1, source_target_pairs={{0,1},{1,2},{2,3},{3,4},{4,5},{5,6},{6,7},{8,9},{9,10},{10,11},{11... | collective-permute-start | bytes 73736 | tf_op jit(solution)/shard_map/ppermute | solution.py:23
  49.1 8.8 %collective-permute-start.7 = (f32[4,96,16]{2,1,0:T(8,128)S(1)}, f32[4,96,16]{2,1,0:T(8,128)S(1)}, u32[]{:S(2)}, u32[]{:S(2)}) collective-permute-start(f32[4,96,16]{2,1,0:T(8,128)S(1)} %get-tuple-element.58), channel_id=1, source_target_pairs={{1,0},{2,1},{3,2},{4,3},{5,4},{6,5},{7,6},{9,8},{10,9},{11,10},{12... | collective-permute-start | bytes 73736 | tf_op jit(solution)/shard_map/ppermute | solution.py:25
  64.1 0.8 copy-start.2
  70.8 9.7 %collective-permute-start.3 = (f32[5,48,14,3]{1,2,3,0:T(8,128)}, f32[5,48,14,3]{1,2,3,0:T(8,128)}, u32[]{:S(2)}, u32[]{:S(2)}) collective-permute-start(f32[5,48,14,3]{1,2,3,0:T(8,128)} %copy.43), channel_id=1, source_target_pairs={{0,1},{1,2},{2,3},{3,4},{4,5},{5,6},{6,7},{8,9},{9,10},{10,11},{11... | collective-permute-start | bytes 120968 | tf_op jit(solution)/shard_map/ppermute | solution.py:23
  75.7 8.3 %collective-permute-start.2 = (f32[5,48,14,3]{1,2,3,0:T(8,128)}, f32[5,48,14,3]{1,2,3,0:T(8,128)}, u32[]{:S(2)}, u32[]{:S(2)}) collective-permute-start(f32[5,48,14,3]{1,2,3,0:T(8,128)} %copy.41), channel_id=1, source_target_pairs={{1,0},{2,1},{3,2},{4,3},{5,4},{6,5},{7,6},{9,8},{10,9},{11,10},{12... | collective-permute-start | bytes 120968 | tf_op jit(solution)/shard_map/ppermute | solution.py:25
  87.0 2.4 %copy-start.4 = (f32[96,1056]{1,0:T(8,128)S(1)}, f32[96,1056]{1,0:T(8,128)}, u32[]{:S(2)}) copy-start(f32[96,1056]{1,0:T(8,128)} %slice_bitcast_fusion.4) | copy-start | bytes 1216516
  95.7 1.0 copy-start.25
  95.7 1.9 %copy-start.6 = (pred[64,1024]{1,0:T(8,128)(4,1)S(1)}, pred[64,1024]{1,0:T(8,128)(4,1)}, u32[]{:S(2)}) copy-start(pred[64,1024]{1,0:T(8,128)(4,1)} %copy-done.5) | copy-start | bytes 196612
  95.7 1.9 %copy-start.8 = (pred[64,1024]{1,0:T(8,128)(4,1)S(1)}, pred[64,1024]{1,0:T(8,128)(4,1)}, u32[]{:S(2)}) copy-start(pred[64,1024]{1,0:T(8,128)(4,1)} %copy-done.7) | copy-start | bytes 196612
  95.7 1.9 %copy-start.10 = (pred[64,1024]{1,0:T(8,128)(4,1)S(1)}, pred[64,1024]{1,0:T(8,128)(4,1)}, u32[]{:S(2)}) copy-start(pred[64,1024]{1,0:T(8,128)(4,1)} %copy-done.9) | copy-start | bytes 196612
  95.7 1.9 %copy-start.12 = (pred[64,1024]{1,0:T(8,128)(4,1)S(1)}, pred[64,1024]{1,0:T(8,128)(4,1)}, u32[]{:S(2)}) copy-start(pred[64,1024]{1,0:T(8,128)(4,1)} %copy-done.11) | copy-start | bytes 196612
  95.7 1.9 %copy-start.14 = (pred[64,1024]{1,0:T(8,128)(4,1)S(1)}, pred[64,1024]{1,0:T(8,128)(4,1)}, u32[]{:S(2)}) copy-start(pred[64,1024]{1,0:T(8,128)(4,1)} %copy-done.13) | copy-start | bytes 196612
  95.7 1.9 %copy-start.16 = (pred[64,1024]{1,0:T(8,128)(4,1)S(1)}, pred[64,1024]{1,0:T(8,128)(4,1)}, u32[]{:S(2)}) copy-start(pred[64,1024]{1,0:T(8,128)(4,1)} %copy-done.15) | copy-start | bytes 196612
  95.7 1.9 %copy-start.18 = (pred[64,1024]{1,0:T(8,128)(4,1)S(1)}, pred[64,1024]{1,0:T(8,128)(4,1)}, u32[]{:S(2)}) copy-start(pred[64,1024]{1,0:T(8,128)(4,1)} %copy-done.17) | copy-start | bytes 196612
  95.8 1.9 %copy-start.20 = (pred[64,1024]{1,0:T(8,128)(4,1)S(1)}, pred[64,1024]{1,0:T(8,128)(4,1)}, u32[]{:S(2)}) copy-start(pred[64,1024]{1,0:T(8,128)(4,1)} %copy-done.19) | copy-start | bytes 196612
  95.8 1.9 %copy-start.22 = (pred[64,1024]{1,0:T(8,128)(4,1)S(1)}, pred[64,1024]{1,0:T(8,128)(4,1)}, u32[]{:S(2)}) copy-start(pred[64,1024]{1,0:T(8,128)(4,1)} %copy-done.21) | copy-start | bytes 196612
  95.8 1.9 %copy-start.24 = (f32[64,1024]{1,0:T(8,128)S(1)}, f32[64,1024]{1,0:T(8,128)}, u32[]{:S(2)}) copy-start(f32[64,1024]{1,0:T(8,128)} %param.15) | copy-start | bytes 786436
  129.3 2.8 %copy-start = (f32[5,48,14,3]{3,2,0,1:T(8,128)S(1)}, f32[5,48,14,3]{3,2,0,1:T(8,128)}, u32[]{:S(2)}) copy-start(f32[5,48,14,3]{3,2,0,1:T(8,128)} %copy.44) | copy-start | bytes 120964

commit v2 on v1

--- a/solution.py
+++ b/solution.py
@@ -2,6 +2,8 @@
 import jax.numpy as jnp
 from jax import lax
 from jax.sharding import PartitionSpec as P
+from jax.experimental import pallas as pl
+from jax.experimental.pallas import tpu as pltpu
 
 RF = 8
 TILE = 64
@@ -136,11 +138,88 @@
     )
 
 
-def surface_winds(surface, fire_rows, fire_cols, extra):
-    table_x = interp_table(fire_rows, RF, extra)
-    table_y = interp_table(fire_cols, RF, extra)
+def surface_winds(surface, fire_rows, fire_cols, extra_x, extra_y):
+    table_x = interp_table(fire_rows, RF, extra_x)
+    table_y = interp_table(fire_cols, RF, extra_y)
     along = jnp.einsum("ia,kab->kib", table_x, surface, precision=lax.Precision.HIGHEST)
     return jnp.einsum("kib,jb->kij", along, table_y, precision=lax.Precision.HIGHEST)
+
+
+HALO_Y = 128
+
+
+def shift(a, d, axis):
+    return pltpu.roll(a, (-d) % a.shape[axis], axis)
+
+
+def lookup(tab_ref, cat, row, default):
+    ncat = tab_ref.shape[0] // 4
+    out = jnp.full(cat.shape, default, jnp.float32)
+    for category in range(ncat):
+        out = jnp.where(cat == float(category), tab_ref[row * ncat + category], out)
+    return out
+
+
+def fire_kernel(tab_ref, ext_ref, wind_ref, fuel_ref, level_out, fuel_out, heat_out):
+    rows, cols = fuel_ref.shape
+    hx = (ext_ref.shape[1] - rows) // 2
+    hy = (ext_ref.shape[2] - cols) // 2
+    inner = (slice(hx, hx + rows), slice(hy, hy + cols))
+    level = ext_ref[0]
+    cat = ext_ref[1]
+    nsteps = ext_ref[2]
+    spread = lookup(tab_ref, cat, 0, 0.0)
+    gain = lookup(tab_ref, cat, 1, 0.0)
+    cat_in = cat[inner]
+    burnout = lookup(tab_ref, cat_in, 2, 1.0)
+    yields = lookup(tab_ref, cat_in, 3, 0.0)
+    nsteps_in = nsteps[inner]
+    wind_u = wind_ref[0]
+    wind_v = wind_ref[1]
+    remaining = fuel_ref[...]
+    heating = jnp.zeros_like(remaining)
+    for substep in range(SUBSTEPS):
+        xm1 = shift(level, -1, 0)
+        xp1 = shift(level, 1, 0)
+        ym1 = shift(level, -1, 1)
+        yp1 = shift(level, 1, 1)
+        back_x = level - xm1
+        ahead_x = xp1 - level
+        back_y = level - ym1
+        ahead_y = yp1 - level
+        upwind = jnp.sqrt(
+            jnp.maximum(back_x, 0.0) ** 2
+            + jnp.minimum(ahead_x, 0.0) ** 2
+            + jnp.maximum(back_y, 0.0) ** 2
+            + jnp.minimum(ahead_y, 0.0) ** 2
+        )
+        slope_x = (shift(level, -2, 0) - 8.0 * xm1 + 8.0 * xp1 - shift(level, 2, 0)) / 12.0
+        slope_y = (shift(level, -2, 1) - 8.0 * ym1 + 8.0 * yp1 - shift(level, 2, 1)) / 12.0
+        pushing = jnp.maximum(wind_u * slope_x + wind_v * slope_y, 0.0)
+        moved = level - spread * (upwind + gain * pushing)
+        burned = remaining / (1.0 + jnp.exp(moved[inner])) / burnout
+        active = float(substep) < nsteps_in
+        remaining = jnp.where(active, remaining - burned, remaining)
+        heating = heating + jnp.where(active, yields * burned, 0.0)
+        level = jnp.where(float(substep) < nsteps, moved, level)
+    level_out[...] = level[inner]
+    fuel_out[...] = remaining
+    heat_out[...] = heating.reshape(rows // RF, RF, cols).sum(axis=1)
+
+
+def fire_step(tables, ext, winds, fuel_left):
+    rows, cols = fuel_left.shape
+    vmem = pl.BlockSpec(memory_space=pltpu.VMEM)
+    return pl.pallas_call(
+        fire_kernel,
+        out_shape=(
+            jax.ShapeDtypeStruct((rows, cols), jnp.float32),
+            jax.ShapeDtypeStruct((rows, cols), jnp.float32),
+            jax.ShapeDtypeStruct((rows // RF, cols), jnp.float32),
+        ),
+        in_specs=[pl.BlockSpec(memory_space=pltpu.SMEM), vmem, vmem, vmem],
+        out_specs=(vmem, vmem, vmem),
+    )(tables, ext, winds, fuel_left)
 
 
 def fire_halo(level):
@@ -164,16 +243,6 @@
     atmos_rows, atmos_cols = (atmos.shape[2], atmos.shape[3])
     padded_atm = extended(atmos, (("gx", 2), ("gy", 3)), 3)
     surface = padded_atm[0:2, 0]
-    spread = jnp.zeros(level_set.shape, jnp.float32)
-    gain = jnp.zeros(level_set.shape, jnp.float32)
-    burnout = jnp.ones(level_set.shape, jnp.float32)
-    yields = jnp.zeros(level_set.shape, jnp.float32)
-    for category in range(spread_rate.shape[0]):
-        picked = fuel_map == category
-        spread = jnp.where(picked, spread_rate[category], spread)
-        gain = jnp.where(picked, wind_factor[category], gain)
-        burnout = jnp.where(picked, burn_time[category], burnout)
-        yields = jnp.where(picked, heat_yield[category], yields)
     slots = burn_tiles.reshape(-1)
     listed = burn_count.reshape(())
     tiles_dev = substep_count.size
@@ -188,27 +257,14 @@
     nsteps = jnp.broadcast_to(nsteps[:, None, :, None], (tiles_x, TILE, tiles_y, TILE)).reshape(
         fire_rows, fire_cols
     )
-    stacked = extended(
-        jnp.stack([level_set, spread, gain, nsteps]), (("gx", 1), ("gy", 2)), halo
-    )
-    level, spread_ext, gain_ext, nsteps_ext = stacked[0], stacked[1], stacked[2], stacked[3]
-    winds = surface_winds(surface, fire_rows, fire_cols, halo)
-    inner = (slice(halo, halo + fire_rows), slice(halo, halo + fire_cols))
-    remaining = fuel_left
-    heating = jnp.zeros_like(level_set)
-    for substep in range(SUBSTEPS):
-        active_ext = substep < nsteps_ext
-        padded = jnp.pad(level, 2)
-        moved = spread_level(padded, level, spread_ext, gain_ext, winds[0], winds[1])
-        burned = remaining / (1.0 + jnp.exp(moved[inner])) / burnout
-        active = active_ext[inner]
-        remaining, heating = (
-            jnp.where(active, remaining - burned, remaining),
-            heating + jnp.where(active, yields * burned, 0.0),
-        )
-        level = jnp.where(active_ext, moved, level)
-    level = level[inner]
-    heat_atm = heating.reshape(atmos_rows, RF, atmos_cols, RF).sum(axis=(1, 3)) / (RF * RF)
+    stacked = jnp.stack([level_set, fuel_map.astype(jnp.float32), nsteps])
+    stacked = extended(stacked, (("gx", 1), ("gy", 2)), halo)
+    room = jnp.zeros(stacked.shape[:2] + (HALO_Y - halo,), jnp.float32)
+    stacked = jnp.concatenate([room, stacked, room], axis=2)
+    winds = surface_winds(surface, fire_rows, fire_cols, halo, HALO_Y)
+    tables = jnp.concatenate([spread_rate, wind_factor, burn_time, heat_yield]).astype(jnp.float32)
+    level, remaining, heat_rows = fire_step(tables, stacked, winds, fuel_left)
+    heat_atm = heat_rows.reshape(atmos_rows, atmos_cols, RF).sum(axis=2) / (RF * RF)
     return (atmos_step(padded_atm, heat_atm), level, remaining)
 
 

time: 145 us -> 87.5 us (0.60)
  other arithmetic: 69.1 us -> 14.5 us
  local copies, waits for them, and re-layouts: 34.6 us -> 22.2 us
  Pallas kernels: 0 us -> 11.9 us
  waiting for transfers between devices: 10.7 us -> 7.18 us
    add x1 -> x0, other arithmetic: 17.9 us -> none  [shards(): heating + jnp.where(active, yields * burned, 0.0)]
    select_n x9 -> x0, other arithmetic: 17.2 us -> none  [the longest x1 10 us: shards(): jnp.where(active, remaining - burned, remaining)]
    another operation x2 -> x1, other arithmetic: 17.2 us -> 0.97 us  [shards(): stacked = jnp.stack([level_set, fuel_map.astype(jnp.float32), nsteps])]
    pallas_call x0 -> x1, Pallas kernels: none -> 11.9 us  [fire_step(): pl.pallas_call(fire_kernel, out_shape=(jax.ShapeDtypeStruct((rows, cols),...]
    ppermute x4, waiting for transfers between devices: 6.03 us -> 1.51 us  [extended(): lax.ppermute(head, axis, [((i + 1) % count, i) for i in range(ends)])]
    concatenate x2 -> x1, local copies, waits for them, and re-layouts: 4.19 us -> 0.34 us  [extended(): jnp.concatenate([lax.ppermute(tail, axis, [(i, (i + 1) % count) for i in...]
    ppermute x4, starting transfers between devices: 11.4 us -> 14.6 us  [extended(): lax.ppermute(tail, axis, [(i, (i + 1) % count) for i in range(ends)])]
    slice x4 -> x0, local copies, waits for them, and re-layouts: 2.81 us -> none  [the longest x1 0.71 us: shards(): gain = jnp.where(picked, wind_factor[category], gain)]
  transfers between devices with their start and end apart: 8 -> 8, of which waited for: 4 -> 2; matrix products, arithmetic and copies ran while one was open for 24% -> 19% of each run, Pallas kernels for 0% -> 0%
where the time goes in v2:
time: 87.5 us; the launch traced here: 86.8 us
  starting transfers between devices  26.1 us (30%)
  local copies, waits for them, and re-layouts  22.2 us (25%)
  other arithmetic  14.5 us (17%)
  Pallas kernels  11.9 us (14%)
  waiting for transfers between devices  7.18 us (8%)
  matrix products  3.23 us (4%)
  between operations  1.64 us (2%)
    ppermute x4, starting transfers between devices, extended(): lax.ppermute(tail, axis, [(i, (i + 1) % count) for i in range(ends)])  14.6 us
    pallas_call x1, Pallas kernels, fire_step(): pl.pallas_call(fire_kernel, out_shape=(jax.ShapeDtypeStruct((rows, cols),...  11.9 us
    ppermute x4, starting transfers between devices, extended(): lax.ppermute(head, axis, [((i + 1) % count, i) for i in range(ends)])  11.5 us
    add x1, other arithmetic, atmos_step(): centre - COURANT * (centre[0:1] * deriv_x + centre[1:2] * deriv_y)  10.1 us
    slice x4, local copies, waits for them, and re-layouts, extended(): head = lax.slice_in_dim(cells, 0, width, axis=dim)  6 us
    ppermute x4, waiting for transfers between devices, extended(): lax.ppermute(tail, axis, [(i, (i + 1) % count) for i in range(ends)])  5.68 us
    unnamed x26, local copies, waits for them, and re-layouts  3.39 us
    slice x1, local copies, waits for them, and re-layouts, extended(): lax.slice_in_dim(cells, cells.shape[dim] - width, cells.shape[dim], axis=...  3.04 us
  transfers between devices with their start and end apart: 8, of which 2 were waited for; matrix products, arithmetic and copies ran while one was open for 19% of the time, Pallas kernels for 0%

profile of v2, /device:TPU:120, one launch (start us, length us, event | category | flops | bytes accessed | tf_op | source)
XLA Modules:
  0.0 86.8 jit_solution(6365453351351549829)
XLA Ops:
  0.7 1.7 %fusion.57 = (f32[5,48,3,128]{3,2,1,0:T(4,128)S(1)}, f32[5,48,3,128]{3,2,1,0:T(4,128)S(1)}) fusion(f32[5,48,8,128]{3,2,1,0:T(8,128)} %param.13), kind=kLoop, calls=%fused_computation.121 | loop fusion | bytes 1474560 | tf_op jit(solution)/shard_map/slice | solution.py:21
  2.4 0.0 copy-start.3
  2.4 2.1 %collective-permute-start.1 = (f32[5,48,3,128]{3,1,2,0:T(8,128)S(1)}, f32[5,48,3,128]{3,1,2,0:T(8,128)S(1)}, u32[]{:S(2)}, u32[]{:S(2)}) collective-permute-start(f32[5,48,3,128]{3,1,2,0:T(8,128)S(1)} %copy.51), channel_id=1, source_target_pairs={{0,8},{8,16},{16,24},{24,32},{32,40},{40,48},{48,56},{56,64},{64,7... | collective-permute-start | bytes 1105928 | tf_op jit(solution)/shard_map/ppermute | solution.py:25
  4.5 0.8 copy.50
  5.2 5.7 %collective-permute-start = (f32[5,48,3,128]{3,1,2,0:T(8,128)}, f32[5,48,3,128]{3,1,2,0:T(8,128)S(1)}, u32[]{:S(2)}, u32[]{:S(2)}) collective-permute-start(f32[5,48,3,128]{3,1,2,0:T(8,128)} %copy.50), channel_id=1, source_target_pairs={{8,0},{16,8},{24,16},{32,24},{40,32},{48,40},{56,48},{64,56},{72,6... | collective-permute-start | bytes 1105928 | tf_op jit(solution)/shard_map/ppermute | solution.py:27
  11.7 0.1 fusion.43
  11.8 0.0 copy-done.10
  11.8 0.1 broadcast_in_dim.29
  11.8 0.1 broadcast_in_dim.30
  11.9 1.0 %convert_bitcast_fusion = f32[1,64,1024]{2,1,0:T(8,128)S(1)} fusion(s32[64,1024]{1,0:T(8,128)} %param.16), kind=kLoop, calls=%fused_computation.49 | loop fusion | flops 65536 | bytes 524288 | tf_op jit(solution)/shard_map/stack | solution.py:260
  13.0 1.9 %collective-permute-start.5 = (f32[3,16,1024]{2,1,0:T(8,128)S(1)}, f32[3,16,1024]{2,1,0:T(8,128)S(1)}, u32[]{:S(2)}, u32[]{:S(2)}) collective-permute-start(f32[3,16,1024]{2,1,0:T(8,128)S(1)} %get-tuple-element.38), channel_id=1, source_target_pairs={{8,0},{16,8},{24,16},{32,24},{40,32},{48,40},{56,48},{64,56},{72,6... | collective-permute-start | bytes 589832 | tf_op jit(solution)/shard_map/ppermute | solution.py:27
  14.9 2.4 %collective-permute-start.4 = (f32[3,16,1024]{2,1,0:T(8,128)S(1)}, f32[3,16,1024]{2,1,0:T(8,128)S(1)}, u32[]{:S(2)}, u32[]{:S(2)}) collective-permute-start(f32[3,16,1024]{2,1,0:T(8,128)S(1)} %get-tuple-element.37), channel_id=1, source_target_pairs={{0,8},{8,16},{16,24},{24,32},{32,40},{40,48},{48,56},{56,64},{64,7... | collective-permute-start | bytes 589832 | tf_op jit(solution)/shard_map/ppermute | solution.py:25
  17.3 0.1 constant_dynamic-update-slice_fusion.1
  17.5 0.8 multiply_bitcast_fusion.1
  18.3 0.0 collective-permute-done.5
  18.3 5.7 %collective-permute-done.4 = f32[3,16,1024]{2,1,0:T(8,128)S(1)} collective-permute-done((f32[3,16,1024]{2,1,0:T(8,128)S(1)}, f32[3,16,1024]{2,1,0:T(8,128)S(1)}, u32[]{:S(2)}, u32[]{:S(2)}) %collective-permute-start.4) | collective-permute-done | bytes 196640 | tf_op jit(solution)/shard_map/ppermute | solution.py:25
  24.0 0.1 pad_maximum_fusion.1
  24.1 0.9 %fusion.56 = (f32[3,96,16]{2,1,0:T(8,128)}, f32[3,96,16]{2,1,0:T(8,128)}) fusion(f32[3,96,1024]{2,1,0:T(8,128)S(1)} %pad_maximum_fusion.1), kind=kLoop, calls=%fused_computation.120 | loop fusion | bytes 73728 | tf_op jit(solution)/shard_map/slice | solution.py:21
  25.0 5.0 %collective-permute-start.6 = (f32[3,96,16]{2,1,0:T(8,128)}, f32[3,96,16]{2,1,0:T(8,128)}, u32[]{:S(2)}, u32[]{:S(2)}) collective-permute-start(f32[3,96,16]{2,1,0:T(8,128)} %get-tuple-element.30), channel_id=1, source_target_pairs={{0,1},{1,2},{2,3},{3,4},{4,5},{5,6},{6,7},{8,9},{9,10},{10,11},{11... | collective-permute-start | bytes 55304 | tf_op jit(solution)/shard_map/ppermute | solution.py:25
  30.0 1.9 %collective-permute-start.7 = (f32[3,96,16]{2,1,0:T(8,128)}, f32[3,96,16]{2,1,0:T(8,128)}, u32[]{:S(2)}, u32[]{:S(2)}) collective-permute-start(f32[3,96,16]{2,1,0:T(8,128)} %get-tuple-element.29), channel_id=1, source_target_pairs={{1,0},{2,1},{3,2},{4,3},{5,4},{6,5},{7,6},{9,8},{10,9},{11,10},{12... | collective-permute-start | bytes 55304 | tf_op jit(solution)/shard_map/ppermute | solution.py:27
  32.0 0.0 collective-permute-done.1
  32.0 0.2 copy.36
  32.2 0.0 collective-permute-done
  32.2 0.3 constant_dynamic-update-slice_fusion
  32.6 1.3 %copy-done = f32[5,48,11,128]{3,2,0,1:T(8,128)} copy-done((f32[5,48,11,128]{3,2,0,1:T(8,128)}, f32[5,48,11,128]{3,2,0,1:T(8,128)S(1)}, u32[]{:S(2)}) %copy-start) | copy-done | bytes 1351704
  33.8 0.1 copy-done.1
  34.0 0.4 pad_maximum_fusion
  34.3 1.9 %fusion.55 = (f32[5,48,14,3]{3,2,0,1:T(8,128)S(1)}, f32[5,48,14,3]{3,2,0,1:T(8,128)}) fusion(f32[5,48,14,128]{3,2,0,1:T(8,128)S(1)} %pad_maximum_fusion), kind=kLoop, calls=%fused_computation.119 | loop fusion | bytes 161280 | tf_op jit(solution)/shard_map/slice | solution.py:21
  36.3 3.0 %copy.43 = f32[5,48,14,3]{1,2,3,0:T(8,128)} copy(f32[5,48,14,3]{3,2,0,1:T(8,128)} %get-tuple-element.28) | data formatting | bytes 80640 | tf_op jit(solution)/shard_map/slice | solution.py:22
  39.3 5.1 %collective-permute-start.3 = (f32[5,48,14,3]{1,2,3,0:T(8,128)}, f32[5,48,14,3]{1,2,3,0:T(8,128)}, u32[]{:S(2)}, u32[]{:S(2)}) collective-permute-start(f32[5,48,14,3]{1,2,3,0:T(8,128)} %copy.43), channel_id=1, source_target_pairs={{0,1},{1,2},{2,3},{3,4},{4,5},{5,6},{6,7},{8,9},{9,10},{10,11},{11... | collective-permute-start | bytes 120968 | tf_op jit(solution)/shard_map/ppermute | solution.py:25
  44.4 1.5 %copy.41 = f32[5,48,14,3]{1,2,3,0:T(8,128)} copy(f32[5,48,14,3]{3,2,0,1:T(8,128)S(1)} %get-tuple-element.27) | data formatting | bytes 80640 | tf_op jit(solution)/shard_map/slice | solution.py:21
  45.9 1.9 %collective-permute-start.2 = (f32[5,48,14,3]{1,2,3,0:T(8,128)}, f32[5,48,14,3]{1,2,3,0:T(8,128)}, u32[]{:S(2)}, u32[]{:S(2)}) collective-permute-start(f32[5,48,14,3]{1,2,3,0:T(8,128)} %copy.41), channel_id=1, source_target_pairs={{1,0},{2,1},{3,2},{4,3},{5,4},{6,5},{7,6},{9,8},{10,9},{11,10},{12... | collective-permute-start | bytes 120968 | tf_op jit(solution)/shard_map/ppermute | solution.py:27
  47.9 0.6 pad_maximum_fusion.20.tab_ref
  48.5 0.0 collective-permute-done.6
  48.5 0.0 collective-permute-done.7
  48.5 2.4 %concatenate.44.ext_ref = f32[3,96,1280]{2,1,0:T(8,128)} concatenate(f32[3,96,112]{2,1,0:T(8,128)S(1)} %broadcast_in_dim.26, f32[3,96,16]{2,1,0:T(8,128)} %collective-permute-done.6, f32[3,96,1024]{2,1,0:T(8,128)} %copy-done.2, f32[3,96,16]{2,1,0:T(8,128)} %collective-permute-done.7, f32[3,96,112]{2,1,0:T(8,128)S(1)} %broadcast_in_dim.26), dimensions={2} | concatenate | bytes 2949120 | tf_op jit(solution)/shard_map/concatenate | solution.py:263
  50.9 0.0 collective-permute-done.3
  50.9 1.8 %copy.44 = f32[5,48,14,3]{3,2,0,1:T(8,128)S(1)} copy(f32[5,48,14,3]{1,2,3,0:T(8,128)} %collective-permute-done.3) | data formatting | bytes 80640 | tf_op jit(solution)/shard_map/ppermute | solution.py:25
  52.7 1.5 %collective-permute-done.2 = f32[5,48,14,3]{1,2,3,0:T(8,128)} collective-permute-done((f32[5,48,14,3]{1,2,3,0:T(8,128)}, f32[5,48,14,3]{1,2,3,0:T(8,128)}, u32[]{:S(2)}, u32[]{:S(2)}) %collective-permute-start.2) | collective-permute-done | bytes 40352 | tf_op jit(solution)/shard_map/ppermute | solution.py:27
  54.2 3.0 %copy.42 = f32[5,48,14,3]{3,2,0,1:T(8,128)} copy(f32[5,48,14,3]{1,2,3,0:T(8,128)} %collective-permute-done.2) | data formatting | bytes 80640 | tf_op jit(solution)/shard_map/ppermute | solution.py:27
  57.2 1.2 %convolution_bitcast_fusion = f32[2,96,134]{1,2,0:T(8,128)S(1)} fusion(f32[5,48,14,3]{3,2,0,1:T(8,128)} %copy.42, f32[5,48,14,3]{3,2,0,1:T(8,128)S(1)} %copy.44, f32[5,48,3,128]{3,2,0,1:T(4,128)} %copy-done.1, f32[5,48,8,128]{3,2,0,1:T(8,128)S(1)} %get-tuple-element.34, f32[5,48,3,128]{3,2,0,1:T(4,128)S(1)} %copy.36, f32[96]{0:T(128)S(1)} %get-tuple-element.41, ...), kind=kOutput, calls=%fused_computation.6 | convolution fusion | flops 4344032 | bytes 1905408 | tf_op jit(solution)/shard_map/ia,kab->kib/dot_general | solution.py:144
  58.5 2.0 %fusion.19.wind_ref = f32[2,96,1280]{2,1,0:T(8,128)} fusion(f32[2,96,134]{1,2,0:T(8,128)S(1)} %convolution_bitcast_fusion, f32[1280]{0:T(1024)S(1)} %get-tuple-element.45, s32[1280]{0:T(1024)S(1)} %get-tuple-element.48, f32[1280]{0:T(1024)S(1)} %get-tuple-element.46, s32[1280]{0:T(1024)S(1)} %get-tuple-element.47), kind=kOutput, calls=%fused_computation.39 | convolution fusion | flops 396039680 | bytes 1106432 | tf_op jit(solution)/shard_map/kib,jb->kij/dot_general | solution.py:145
  60.5 11.9 %shard_map.130 = (f32[64,1024]{1,0:T(8,128)}, f32[64,1024]{1,0:T(8,128)}, f32[8,1024]{1,0:T(8,128)}) custom-call(f32[52]{0:T(128)} %pad_maximum_fusion.20.tab_ref, f32[3,96,1280]{2,1,0:T(8,128)} %concatenate.44.ext_ref, f32[2,96,1280]{2,1,0:T(8,128)} %fusion.19.wind_ref, f32[64,1024]{1,0:T(8,128)} %fuel_ref.1), custom_call_target="tpu_custom_call" | custom-call | tf_op jit(solution)/shard_map/pallas_call | solution.py:213
  72.4 1.9 %reshape.172 = f32[8,128,8]{2,1,0:T(8,128)} reshape(f32[8,1024]{1,0:T(8,128)} %get-tuple-element.18) | data formatting | bytes 65536 | tf_op jit(solution)/shard_map/reshape | solution.py:267
  74.3 1.2 %reduce_sum.9 = f32[8,128]{1,0:T(8,128)S(1)} reduce(f32[8,128,8]{2,1,0:T(8,128)} %reshape.172, f32[]{:T(128)} %constant.118.clone.1), dimensions={2}, to_apply=%region_1.2 | reduce | flops 7168 | bytes 36868 | tf_op jit(solution)/shard_map/reduce_sum | solution.py:267
  75.5 10.1 %fusion.8 = f32[5,48,8,128]{3,2,0,1:T(8,128)S(1)} fusion(f32[5,48,8,128]{3,2,0,1:T(8,128)S(1)} %get-tuple-element.34, f32[5,48,3,128]{3,2,0,1:T(4,128)S(1)} %copy.36, f32[5,48,14,3]{3,2,0,1:T(8,128)S(1)} %copy.44, f32[5,48,3,128]{3,2,0,1:T(4,128)} %copy-done.1, f32[5,48,14,3]{3,2,0,1:T(8,128)} %copy.42, f32[5,48,11,128]{3,2,0,1:T(8,128)} %copy-done, ...), kind=kLoop, calls=%fused_computation.17 | loop fusion | flops 12533760 | bytes 6126336 | tf_op jit(solution)/shard_map/add | solution.py:123
  85.7 0.1 fusion.29
  85.8 1.0 %copy.49 = f32[5,48,8,128]{3,2,1,0:T(8,128)} copy(f32[5,48,8,128]{3,2,0,1:T(8,128)S(1)} %fusion.29) | data formatting | bytes 1966080
  (30 shorter events, 0.2 us)
Async XLA Ops:
  0.6 11.0 %copy-start.9 = (s32[1,1,16]{2,1,0:T(1,128)S(1)}, s32[1,1,16]{2,1,0:T(1,128)}, u32[]{:S(2)}) copy-start(s32[1,1,16]{2,1,0:T(1,128)} %param.21) | copy-start | bytes 196
  0.6 11.1 %copy-start.10 = (s32[1,16]{1,0:T(1,128)S(1)}, s32[1,16]{1,0:T(1,128)}, u32[]{:S(2)}) copy-start(s32[1,16]{1,0:T(1,128)} %param.23) | copy-start | bytes 196
  0.7 12.3 %copy-start.4 = (f32[64,1024]{1,0:T(8,128)S(1)}, f32[64,1024]{1,0:T(8,128)}, u32[]{:S(2)}) copy-start(f32[64,1024]{1,0:T(8,128)} %param.14) | copy-start | bytes 786436
  2.4 14.9 %copy-start.3 = (f32[5,48,8,128]{3,2,1,0:T(8,128)S(1)}, f32[5,48,8,128]{3,2,1,0:T(8,128)}, u32[]{:S(2)}) copy-start(f32[5,48,8,128]{3,2,1,0:T(8,128)} %param.13) | copy-start | bytes 2949124
  2.4 29.5 %collective-permute-start.1 = (f32[5,48,3,128]{3,1,2,0:T(8,128)S(1)}, f32[5,48,3,128]{3,1,2,0:T(8,128)S(1)}, u32[]{:S(2)}, u32[]{:S(2)}) collective-permute-start(f32[5,48,3,128]{3,1,2,0:T(8,128)S(1)} %copy.51), channel_id=1, source_target_pairs={{0,8},{8,16},{16,24},{24,32},{32,40},{40,48},{48,56},{56,64},{64,7... | collective-permute-start | bytes 1105928 | tf_op jit(solution)/shard_map/ppermute | solution.py:25
  5.2 26.9 %collective-permute-start = (f32[5,48,3,128]{3,1,2,0:T(8,128)}, f32[5,48,3,128]{3,1,2,0:T(8,128)S(1)}, u32[]{:S(2)}, u32[]{:S(2)}) collective-permute-start(f32[5,48,3,128]{3,1,2,0:T(8,128)} %copy.50), channel_id=1, source_target_pairs={{8,0},{16,8},{24,16},{32,24},{40,32},{48,40},{56,48},{64,56},{72,6... | collective-permute-start | bytes 1105928 | tf_op jit(solution)/shard_map/ppermute | solution.py:27
  13.0 5.4 %collective-permute-start.5 = (f32[3,16,1024]{2,1,0:T(8,128)S(1)}, f32[3,16,1024]{2,1,0:T(8,128)S(1)}, u32[]{:S(2)}, u32[]{:S(2)}) collective-permute-start(f32[3,16,1024]{2,1,0:T(8,128)S(1)} %get-tuple-element.38), channel_id=1, source_target_pairs={{8,0},{16,8},{24,16},{32,24},{40,32},{48,40},{56,48},{64,56},{72,6... | collective-permute-start | bytes 589832 | tf_op jit(solution)/shard_map/ppermute | solution.py:27
  14.9 9.1 %collective-permute-start.4 = (f32[3,16,1024]{2,1,0:T(8,128)S(1)}, f32[3,16,1024]{2,1,0:T(8,128)S(1)}, u32[]{:S(2)}, u32[]{:S(2)}) collective-permute-start(f32[3,16,1024]{2,1,0:T(8,128)S(1)} %get-tuple-element.37), channel_id=1, source_target_pairs={{0,8},{8,16},{16,24},{24,32},{32,40},{40,48},{48,56},{56,64},{64,7... | collective-permute-start | bytes 589832 | tf_op jit(solution)/shard_map/ppermute | solution.py:25
  24.1 8.1 %copy-start.2 = (f32[3,96,1024]{2,1,0:T(8,128)}, f32[3,96,1024]{2,1,0:T(8,128)S(1)}, u32[]{:S(2)}) copy-start(f32[3,96,1024]{2,1,0:T(8,128)S(1)} %pad_maximum_fusion.1) | copy-start | bytes 3538948
  25.0 23.5 %collective-permute-start.6 = (f32[3,96,16]{2,1,0:T(8,128)}, f32[3,96,16]{2,1,0:T(8,128)}, u32[]{:S(2)}, u32[]{:S(2)}) collective-permute-start(f32[3,96,16]{2,1,0:T(8,128)} %get-tuple-element.30), channel_id=1, source_target_pairs={{0,1},{1,2},{2,3},{3,4},{4,5},{5,6},{6,7},{8,9},{9,10},{10,11},{11... | collective-permute-start | bytes 55304 | tf_op jit(solution)/shard_map/ppermute | solution.py:25
  30.0 18.5 %collective-permute-start.7 = (f32[3,96,16]{2,1,0:T(8,128)}, f32[3,96,16]{2,1,0:T(8,128)}, u32[]{:S(2)}, u32[]{:S(2)}) collective-permute-start(f32[3,96,16]{2,1,0:T(8,128)} %get-tuple-element.29), channel_id=1, source_target_pairs={{1,0},{2,1},{3,2},{4,3},{5,4},{6,5},{7,6},{9,8},{10,9},{11,10},{12... | collective-permute-start | bytes 55304 | tf_op jit(solution)/shard_map/ppermute | solution.py:27
  32.5 1.3 %copy-start = (f32[5,48,11,128]{3,2,0,1:T(8,128)}, f32[5,48,11,128]{3,2,0,1:T(8,128)S(1)}, u32[]{:S(2)}) copy-start(f32[5,48,11,128]{3,2,0,1:T(8,128)S(1)} %get-tuple-element.39) | copy-start | bytes 4055044
  32.5 1.4 %copy-start.1 = (f32[5,48,3,128]{3,2,0,1:T(4,128)}, f32[5,48,3,128]{3,2,0,1:T(4,128)S(1)}, u32[]{:S(2)}) copy-start(f32[5,48,3,128]{3,2,0,1:T(4,128)S(1)} %get-tuple-element.40) | copy-start | bytes 1105924
  36.3 11.6 %copy-start.5 = (f32[13]{0:T(128)S(1)}, f32[13]{0:T(128)}, u32[]{:S(2)}) copy-start(f32[13]{0:T(128)} %param.20) | copy-start | bytes 160
  36.3 11.6 %copy-start.6 = (f32[13]{0:T(128)S(1)}, f32[13]{0:T(128)}, u32[]{:S(2)}) copy-start(f32[13]{0:T(128)} %param.19) | copy-start | bytes 160
  36.3 11.6 %copy-start.7 = (f32[13]{0:T(128)S(1)}, f32[13]{0:T(128)}, u32[]{:S(2)}) copy-start(f32[13]{0:T(128)} %param.18) | copy-start | bytes 160
  36.3 11.6 %copy-start.8 = (f32[13]{0:T(128)S(1)}, f32[13]{0:T(128)}, u32[]{:S(2)}) copy-start(f32[13]{0:T(128)} %param.17) | copy-start | bytes 160
  39.3 11.6 %collective-permute-start.3 = (f32[5,48,14,3]{1,2,3,0:T(8,128)}, f32[5,48,14,3]{1,2,3,0:T(8,128)}, u32[]{:S(2)}, u32[]{:S(2)}) collective-permute-start(f32[5,48,14,3]{1,2,3,0:T(8,128)} %copy.43), channel_id=1, source_target_pairs={{0,1},{1,2},{2,3},{3,4},{4,5},{5,6},{6,7},{8,9},{9,10},{10,11},{11... | collective-permute-start | bytes 120968 | tf_op jit(solution)/shard_map/ppermute | solution.py:25
  45.9 8.3 %collective-permute-start.2 = (f32[5,48,14,3]{1,2,3,0:T(8,128)}, f32[5,48,14,3]{1,2,3,0:T(8,128)}, u32[]{:S(2)}, u32[]{:S(2)}) collective-permute-start(f32[5,48,14,3]{1,2,3,0:T(8,128)} %copy.41), channel_id=1, source_target_pairs={{1,0},{2,1},{3,2},{4,3},{5,4},{6,5},{7,6},{9,8},{10,9},{11,10},{12... | collective-permute-start | bytes 120968 | tf_op jit(solution)/shard_map/ppermute | solution.py:27

commit v3 on v2

--- a/solution.py
+++ b/solution.py
@@ -29,6 +29,29 @@
             axis=dim,
         )
     return cells
+
+
+def swap_ends(groups, axis):
+    count = lax.axis_size(axis)
+    ends = count - 1
+    heads = [lax.slice_in_dim(a, 0, w, axis=d) for a, d, w in groups]
+    tails = [lax.slice_in_dim(a, a.shape[d] - w, a.shape[d], axis=d) for a, d, w in groups]
+
+    def pack(parts):
+        return jnp.concatenate([p.reshape(-1) for p in parts])
+
+    def unpack(flat, parts):
+        out, at = [], 0
+        for p in parts:
+            out.append(flat[at : at + p.size].reshape(p.shape))
+            at += p.size
+        return out
+
+    below = unpack(lax.ppermute(pack(tails), axis, [(i, i + 1) for i in range(ends)]), tails)
+    above = unpack(lax.ppermute(pack(heads), axis, [(i + 1, i) for i in range(ends)]), heads)
+    return [
+        jnp.concatenate([lo, a, hi], axis=d) for (a, d, w), lo, hi in zip(groups, below, above)
+    ]
 
 
 def advance(
@@ -241,8 +264,6 @@
 ):
     fire_rows, fire_cols = level_set.shape
     atmos_rows, atmos_cols = (atmos.shape[2], atmos.shape[3])
-    padded_atm = extended(atmos, (("gx", 2), ("gy", 3)), 3)
-    surface = padded_atm[0:2, 0]
     slots = burn_tiles.reshape(-1)
     listed = burn_count.reshape(())
     tiles_dev = substep_count.size
@@ -258,7 +279,9 @@
         fire_rows, fire_cols
     )
     stacked = jnp.stack([level_set, fuel_map.astype(jnp.float32), nsteps])
-    stacked = extended(stacked, (("gx", 1), ("gy", 2)), halo)
+    stacked, padded_atm = swap_ends(((stacked, 1, halo), (atmos, 2, 3)), "gx")
+    stacked, padded_atm = swap_ends(((stacked, 2, halo), (padded_atm, 3, 3)), "gy")
+    surface = padded_atm[0:2, 0]
     room = jnp.zeros(stacked.shape[:2] + (HALO_Y - halo,), jnp.float32)
     stacked = jnp.concatenate([room, stacked, room], axis=2)
     winds = surface_winds(surface, fire_rows, fire_cols, halo, HALO_Y)

time: 87.5 us -> 94.4 us (1.079)
  starting transfers between devices: 26.1 us -> 13.1 us
  other arithmetic: 14.5 us -> 27 us
  local copies, waits for them, and re-layouts: 22.2 us -> 26.4 us
  waiting for transfers between devices: 7.18 us -> 10.1 us
    ppermute x8 -> x4, starting transfers between devices: 26.1 us -> 13.1 us  [the longest x2 6.93 us: swap_ends(): lax.ppermute(pack(tails), axis, [(i, i + 1) for i in range(ends)])]
    reshape x0 -> x14, local copies, waits for them, and re-layouts: none -> 9.08 us  [the longest x6 4.68 us: pack(): return jnp.concatenate([p.reshape(-1) for p in parts])]
    add x1, other arithmetic: 10.1 us -> 2.53 us  [atmos_step(): centre - COURANT * (centre[0:1] * deriv_x + centre[1:2] * deriv_y)]
    slice x1, other arithmetic: 0.03 us -> 7.52 us  [shifted(): padded[:, :, 3 + along_x:3 + along_x + width_x, 3 + along_y:3 + along_y +...]
    concatenate x2 -> x7, other arithmetic: 0.46 us -> 7.8 us  [the longest x3 5.35 us: swap_ends(): jnp.concatenate([lo, a, hi], axis=d)]
    ppermute x3 -> x0, local copies, waits for them, and re-layouts: 5.01 us -> none  [the longest x1 3.03 us: extended(): lax.ppermute(head, axis, [((i + 1) % count, i) for i in range(ends)])]
    ppermute x8 -> x4, waiting for transfers between devices: 7.18 us -> 10.1 us  [the longest x2 5.3 us: swap_ends(): lax.ppermute(pack(heads), axis, [(i + 1, i) for i in range(ends)])]
    slice x5 -> x12, local copies, waits for them, and re-layouts: 9.04 us -> 7.01 us  [the longest x8 3.96 us: unpack(): out.append(flat[at:at + p.size].reshape(p.shape))]
  transfers between devices with their start and end apart: 8 -> 4, of which waited for: 2 -> 3; matrix products, arithmetic and copies ran while one was open for 19% -> 9% of each run, Pallas kernels for 0% -> 0%
where the time goes in v3:
time: 94.4 us; the launch traced here: 93.6 us
  other arithmetic  27 us (29%)
  local copies, waits for them, and re-layouts  26.4 us (28%)
  starting transfers between devices  13.1 us (14%)
  Pallas kernels  11.9 us (13%)
  waiting for transfers between devices  10.1 us (11%)
  matrix products  3.28 us (3%)
  between operations  1.82 us (2%)
    pallas_call x1, Pallas kernels, fire_step(): pl.pallas_call(fire_kernel, out_shape=(jax.ShapeDtypeStruct((rows, cols),...  11.9 us
    slice x1, other arithmetic, shifted(): padded[:, :, 3 + along_x:3 + along_x + width_x, 3 + along_y:3 + along_y +...  7.52 us
    ppermute x2, starting transfers between devices, swap_ends(): lax.ppermute(pack(tails), axis, [(i, i + 1) for i in range(ends)])  6.93 us
    ppermute x2, starting transfers between devices, swap_ends(): lax.ppermute(pack(heads), axis, [(i + 1, i) for i in range(ends)])  6.2 us
    concatenate x3, other arithmetic, swap_ends(): jnp.concatenate([lo, a, hi], axis=d)  5.35 us
    ppermute x2, waiting for transfers between devices, swap_ends(): lax.ppermute(pack(heads), axis, [(i + 1, i) for i in range(ends)])  5.3 us
    unnamed x49, local copies, waits for them, and re-layouts  4.9 us
    ppermute x2, waiting for transfers between devices, swap_ends(): lax.ppermute(pack(tails), axis, [(i, i + 1) for i in range(ends)])  4.79 us
  transfers between devices with their start and end apart: 4, of which 3 were waited for; matrix products, arithmetic and copies ran while one was open for 9% of the time, Pallas kernels for 0%

profile of v3, /device:TPU:120, one launch (start us, length us, event | category | flops | bytes accessed | tf_op | source)
XLA Modules:
  0.0 93.6 jit_solution(9029684826598822066)
XLA Ops:
  1.4 0.7 fusion.40
  2.1 0.7 fusion.48
  2.9 1.0 %convert_bitcast_fusion = f32[1,64,1024]{2,1,0:T(8,128)S(1)} fusion(s32[64,1024]{1,0:T(8,128)} %param.16), kind=kLoop, calls=%fused_computation.54 | loop fusion | flops 65536 | bytes 524288 | tf_op jit(solution)/shard_map/stack | solution.py:281
  3.9 0.9 pad_maximum_fusion.15
  5.2 0.8 pad_maximum_fusion.13
  6.1 4.3 %collective-permute-start = (f32[141312]{0:T(1024)}, f32[141312]{0:T(1024)}, u32[]{:S(2)}, u32[]{:S(2)}) collective-permute-start(f32[141312]{0:T(1024)} %pad_maximum_fusion.13), channel_id=1, source_target_pairs={{8,0},{16,8},{24,16},{32,24},{40,32},{48,40},{56,48},{64,56},{72,6... | collective-permute-start | bytes 1695752 | tf_op jit(solution)/shard_map/ppermute | solution.py:51
  10.6 0.9 pad_maximum_fusion.14
  11.4 1.9 %collective-permute-start.1 = (f32[141312]{0:T(1024)}, f32[141312]{0:T(1024)}, u32[]{:S(2)}, u32[]{:S(2)}) collective-permute-start(f32[141312]{0:T(1024)} %pad_maximum_fusion.14), channel_id=1, source_target_pairs={{0,8},{8,16},{16,24},{24,32},{32,40},{40,48},{48,56},{56,64},{64,7... | collective-permute-start | bytes 1695752 | tf_op jit(solution)/shard_map/ppermute | solution.py:50
  13.4 0.6 broadcast_add_fusion.2
  14.0 0.6 fusion.46
  14.6 0.6 broadcast_add_fusion
  15.2 0.6 select_add_fusion
  15.8 0.8 multiply_bitcast_fusion.1
  16.6 1.2 %collective-permute-done = f32[141312]{0:T(1024)} collective-permute-done((f32[141312]{0:T(1024)}, f32[141312]{0:T(1024)}, u32[]{:S(2)}, u32[]{:S(2)}) %collective-permute-start) | collective-permute-done | bytes 565280 | tf_op jit(solution)/shard_map/ppermute | solution.py:51
  17.8 0.9 %slice.178 = f32[49152]{0:T(1024)S(1)} slice(f32[141312]{0:T(1024)} %collective-permute-done), slice={[0:49152]} | slice | bytes 393216 | tf_op jit(solution)/shard_map/slice | solution.py:46
  18.8 1.1 %slice.168 = f32[92160]{0:T(1024)S(1)} slice(f32[141312]{0:T(1024)} %collective-permute-done), slice={[49152:141312]} | slice | bytes 737280 | tf_op jit(solution)/shard_map/slice | solution.py:46
  20.0 4.8 %collective-permute-done.1 = f32[141312]{0:T(1024)} collective-permute-done((f32[141312]{0:T(1024)}, f32[141312]{0:T(1024)}, u32[]{:S(2)}, u32[]{:S(2)}) %collective-permute-start.1) | collective-permute-done | bytes 565280 | tf_op jit(solution)/shard_map/ppermute | solution.py:50
  24.8 0.9 %slice.177 = f32[49152]{0:T(1024)S(1)} slice(f32[141312]{0:T(1024)} %collective-permute-done.1), slice={[0:49152]} | slice | bytes 393216 | tf_op jit(solution)/shard_map/slice | solution.py:46
  25.8 1.0 %slice.172 = f32[92160]{0:T(1024)S(1)} slice(f32[141312]{0:T(1024)} %collective-permute-done.1), slice={[49152:141312]} | slice | bytes 737280 | tf_op jit(solution)/shard_map/slice | solution.py:46
  27.1 1.1 %copy-done.5 = f32[3,96,1024]{2,1,0:T(8,128)} copy-done((f32[3,96,1024]{2,1,0:T(8,128)}, f32[3,96,1024]{2,1,0:T(8,128)S(1)}, u32[]{:S(2)}) %copy-start.5) | copy-done | bytes 1179672
  28.4 0.7 reshape.231
  29.1 0.3 pad_maximum_fusion
  29.4 2.5 %fusion.53 = (f32[5,48,14,3]{3,2,1,0:T(8,128)}, f32[5,48,14,3]{3,2,1,0:T(8,128)}) fusion(f32[5,48,14,128]{3,2,1,0:T(8,128)S(1)} %pad_maximum_fusion), kind=kLoop, calls=%fused_computation.127 | loop fusion | bytes 161280 | tf_op jit(solution)/shard_map/slice | solution.py:37
  31.9 2.6 %reshape.229 = f32[10080]{0:T(1024)S(1)} reshape(f32[5,48,14,3]{3,2,1,0:T(8,128)} %get-tuple-element.33) | data formatting | bytes 80640 | tf_op jit(solution)/shard_map/reshape | solution.py:41
  34.5 0.9 reshape.232
  35.5 0.7 pad_maximum_fusion.19
  36.2 5.0 %collective-permute-start.3 = (f32[14688]{0:T(1024)S(1)}, f32[14688]{0:T(1024)S(1)}, u32[]{:S(2)}, u32[]{:S(2)}) collective-permute-start(f32[14688]{0:T(1024)S(1)} %pad_maximum_fusion.19), channel_id=1, source_target_pairs={{0,1},{1,2},{2,3},{3,4},{4,5},{5,6},{6,7},{8,9},{9,10},{10,11},{11... | collective-permute-start | bytes 176264 | tf_op jit(solution)/shard_map/ppermute | solution.py:50
  41.3 1.9 %collective-permute-start.2 = (f32[14688]{0:T(1024)S(1)}, f32[14688]{0:T(1024)S(1)}, u32[]{:S(2)}, u32[]{:S(2)}) collective-permute-start(f32[14688]{0:T(1024)S(1)} %pad_maximum_fusion.18), channel_id=1, source_target_pairs={{1,0},{2,1},{3,2},{4,3},{5,4},{6,5},{7,6},{9,8},{10,9},{11,10},{12... | collective-permute-start | bytes 176264 | tf_op jit(solution)/shard_map/ppermute | solution.py:51
  43.2 1.3 %pad_maximum_fusion.27.tab_ref = f32[52]{0:T(128)} fusion(f32[13]{0:T(128)} %param.20, f32[13]{0:T(128)} %param.19, f32[13]{0:T(128)} %param.18, f32[13]{0:T(128)} %param.17), kind=kLoop, calls=%fused_computation.116 | loop fusion | flops 156 | bytes 416 | tf_op jit(solution)/shard_map/concatenate | solution.py:288
  44.5 4.1 %collective-permute-done.2 = f32[14688]{0:T(1024)S(1)} collective-permute-done((f32[14688]{0:T(1024)S(1)}, f32[14688]{0:T(1024)S(1)}, u32[]{:S(2)}, u32[]{:S(2)}) %collective-permute-start.2) | collective-permute-done | bytes 58784 | tf_op jit(solution)/shard_map/ppermute | solution.py:51
  48.6 0.8 reshape.235
  49.3 0.8 reshape.234
  50.1 0.6 reshape.230
  51.0 1.9 %reshape.233 = f32[5,48,14,3]{3,2,1,0:T(8,128)} reshape(f32[10080]{0:T(1024)S(1)} %slice.184) | data formatting | bytes 80640 | tf_op jit(solution)/shard_map/reshape | solution.py:46
  52.9 7.5 %pad_maximum_fusion.6 = (f32[5,48,8,128]{3,2,1,0:T(8,128)}, f32[5,48,8,128]{3,2,1,0:T(8,128)}, f32[5,48,8,128]{3,2,1,0:T(8,128)}, f32[5,48,8,128]{3,2,1,0:T(8,128)}) fusion(f32[5,48,14,3]{3,2,1,0:T(8,128)} %reshape.233, f32[5,48,3,128]{3,2,1,0:T(4,128)S(1)} %reshape.222, f32[5,48,8,128]{3,2,1,0:T(8,128)S(1)} %copy-done, f32[5,48,3,128]{3,2,1,0:T(4,128)} %copy-done.1), kind=kLoop, calls=%fused_computation.15 | loop fusion | flops 2457600 | bytes 5692800 | tf_op jit(solution)/shard_map/slice | solution.py:124
  60.4 4.9 %pad_maximum_fusion.7 = (f32[5,48,8,128]{3,2,1,0:T(8,128)}, f32[5,48,8,128]{3,2,1,0:T(8,128)}, f32[5,48,8,128]{3,2,1,0:T(8,128)}, f32[5,48,8,128]{3,2,1,0:T(8,12...) fusion(f32[5,48,14,3]{3,2,1,0:T(8,128)S(1)} %reshape.230, f32[5,48,3,128]{3,2,1,0:T(4,128)S(1)} %reshape.222, ...), kind=kLoop, calls=%fused_computation.16 | loop fusion | flops 2703359 | bytes 7658880 | tf_op jit(solution)/shard_map/concatenate | solution.py:53
  65.3 0.7 broadcast_in_dim.52
  66.0 2.5 %concatenate.60.ext_ref = f32[3,96,1280]{2,1,0:T(8,128)} concatenate(f32[3,96,112]{2,1,0:T(8,128)} %broadcast_in_dim.52, f32[3,96,16]{2,1,0:T(8,128)} %reshape.234, f32[3,96,1024]{2,1,0:T(8,128)} %copy-done.5, f32[3,96,16]{2,1,0:T(8,128)} %reshape.235, f32[3,96,112]{2,1,0:T(8,128)} %broadcast_in_dim.52), dimensions={2} | concatenate | bytes 2949120 | tf_op jit(solution)/shard_map/concatenate | solution.py:286
  68.6 1.2 %convolution_bitcast_fusion = f32[2,96,134]{1,2,0:T(8,128)S(1)} fusion(f32[5,48,14,3]{3,2,1,0:T(8,128)S(1)} %reshape.230, f32[5,48,14,3]{3,2,1,0:T(8,128)} %reshape.233, f32[5,48,3,128]{3,2,1,0:T(4,128)S(1)} %reshape.222, f32[5,48,8,128]{3,2,1,0:T(8,128)S(1)} %copy-done, f32[5,48,3,128]{3,2,1,0:T(4,128)} %copy-done.1, f32[96]{0:T(128)S(1)} %copy-done.21, ...), kind=kOutput, calls=%fused_computation.6 | convolution fusion | flops 4344032 | bytes 1905408 | tf_op jit(solution)/shard_map/ia,kab->kib/dot_general | solution.py:167
  69.9 2.1 %fusion.16.wind_ref = f32[2,96,1280]{2,1,0:T(8,128)} fusion(f32[2,96,134]{1,2,0:T(8,128)S(1)} %convolution_bitcast_fusion, f32[1280]{0:T(1024)S(1)} %copy-done.17, s32[1280]{0:T(1024)S(1)} %copy-done.16, f32[1280]{0:T(1024)S(1)} %copy-done.18, s32[1280]{0:T(1024)S(1)} %get-tuple-element.53), kind=kOutput, calls=%fused_computation.42 | convolution fusion | flops 396039680 | bytes 1106432 | tf_op jit(solution)/shard_map/kib,jb->kij/dot_general | solution.py:168
  71.9 11.9 %shard_map.130 = (f32[64,1024]{1,0:T(8,128)}, f32[64,1024]{1,0:T(8,128)}, f32[8,1024]{1,0:T(8,128)}) custom-call(f32[52]{0:T(128)} %pad_maximum_fusion.27.tab_ref, f32[3,96,1280]{2,1,0:T(8,128)} %concatenate.60.ext_ref, f32[2,96,1280]{2,1,0:T(8,128)} %fusion.16.wind_ref, f32[64,1024]{1,0:T(8,128)} %fuel_ref.1), custom_call_target="tpu_custom_call" | custom-call | tf_op jit(solution)/shard_map/pallas_call | solution.py:236
  83.8 1.9 %reshape.236 = f32[8,128,8]{2,1,0:T(8,128)} reshape(f32[8,1024]{1,0:T(8,128)} %get-tuple-element.18) | data formatting | bytes 65536 | tf_op jit(solution)/shard_map/reshape | solution.py:290
  85.7 1.2 %reduce_sum.9 = f32[8,128]{1,0:T(8,128)S(1)} reduce(f32[8,128,8]{2,1,0:T(8,128)} %reshape.236, f32[]{:T(128)} %constant.120.clone.1), dimensions={2}, to_apply=%region_1.2 | reduce | flops 7168 | bytes 36868 | tf_op jit(solution)/shard_map/reduce_sum | solution.py:290
  87.5 0.7 copy-done.12
  88.1 0.3 copy-done.6
  89.4 0.3 copy-done.10
  90.0 2.5 %fusion.6 = f32[5,48,8,128]{3,2,0,1:T(8,128)S(1)} fusion(f32[5,48,8,128]{3,2,1,0:T(8,128)S(1)} %copy-done.8, f32[5,48,8,128]{3,2,1,0:T(8,128)S(1)} %copy-done.7, f32[5,48,8,128]{3,2,1,0:T(8,128)S(1)} %copy-done.11, f32[5,48,8,128]{3,2,1,0:T(8,128)S(1)} %copy-done.12, f32[5,48,8,128]{3,2,1,0:T(8,128)} %get-tuple-element.36, ...), kind=kLoop, calls=%fused_computation.27 | loop fusion | flops 7372800 | bytes 14155776 | tf_op jit(solution)/shard_map/add | solution.py:146
  92.6 1.0 %copy.29 = f32[5,48,8,128]{3,2,1,0:T(8,128)} copy(f32[5,48,8,128]{3,2,0,1:T(8,128)S(1)} %fusion.26) | data formatting | bytes 1966080
  (69 shorter events, 3.5 us)
Async XLA Ops:
  0.6 4.3 %copy-start = (f32[5,48,8,128]{3,2,1,0:T(8,128)S(1)}, f32[5,48,8,128]{3,2,1,0:T(8,128)}, u32[]{:S(2)}) copy-start(f32[5,48,8,128]{3,2,1,0:T(8,128)} %param.13) | copy-start | bytes 2949124
  6.1 11.7 %collective-permute-start = (f32[141312]{0:T(1024)}, f32[141312]{0:T(1024)}, u32[]{:S(2)}, u32[]{:S(2)}) collective-permute-start(f32[141312]{0:T(1024)} %pad_maximum_fusion.13), channel_id=1, source_target_pairs={{8,0},{16,8},{24,16},{32,24},{40,32},{48,40},{56,48},{64,56},{72,6... | collective-permute-start | bytes 1695752 | tf_op jit(solution)/shard_map/ppermute | solution.py:51
  11.4 13.4 %collective-permute-start.1 = (f32[141312]{0:T(1024)}, f32[141312]{0:T(1024)}, u32[]{:S(2)}, u32[]{:S(2)}) collective-permute-start(f32[141312]{0:T(1024)} %pad_maximum_fusion.14), channel_id=1, source_target_pairs={{0,8},{8,16},{16,24},{24,32},{32,40},{40,48},{48,56},{56,64},{64,7... | collective-permute-start | bytes 1695752 | tf_op jit(solution)/shard_map/ppermute | solution.py:50
  18.8 8.2 %copy-start.13 = (f32[64,1024]{1,0:T(8,128)S(1)}, f32[64,1024]{1,0:T(8,128)}, u32[]{:S(2)}) copy-start(f32[64,1024]{1,0:T(8,128)} %param.14) | copy-start | bytes 786436
  27.0 2.4 %copy-start.1 = (f32[5,48,3,128]{3,2,1,0:T(4,128)}, f32[5,48,3,128]{3,2,1,0:T(4,128)S(1)}, u32[]{:S(2)}) copy-start(f32[5,48,3,128]{3,2,1,0:T(4,128)S(1)} %reshape.225) | copy-start | bytes 1105924
  27.1 1.1 %copy-start.5 = (f32[3,96,1024]{2,1,0:T(8,128)}, f32[3,96,1024]{2,1,0:T(8,128)S(1)}, u32[]{:S(2)}) copy-start(f32[3,96,1024]{2,1,0:T(8,128)S(1)} %pad_maximum_fusion.1) | copy-start | bytes 3538948
  31.9 2.6 %copy-start.4 = (f32[5,48,14,3]{3,2,1,0:T(8,128)S(1)}, f32[5,48,14,3]{3,2,1,0:T(8,128)}, u32[]{:S(2)}) copy-start(f32[5,48,14,3]{3,2,1,0:T(8,128)} %get-tuple-element.34) | copy-start | bytes 120964
  36.2 13.1 %collective-permute-start.3 = (f32[14688]{0:T(1024)S(1)}, f32[14688]{0:T(1024)S(1)}, u32[]{:S(2)}, u32[]{:S(2)}) collective-permute-start(f32[14688]{0:T(1024)S(1)} %pad_maximum_fusion.19), channel_id=1, source_target_pairs={{0,1},{1,2},{2,3},{3,4},{4,5},{5,6},{6,7},{8,9},{9,10},{10,11},{11... | collective-permute-start | bytes 176264 | tf_op jit(solution)/shard_map/ppermute | solution.py:50
  41.3 7.3 %collective-permute-start.2 = (f32[14688]{0:T(1024)S(1)}, f32[14688]{0:T(1024)S(1)}, u32[]{:S(2)}, u32[]{:S(2)}) collective-permute-start(f32[14688]{0:T(1024)S(1)} %pad_maximum_fusion.18), channel_id=1, source_target_pairs={{1,0},{2,1},{3,2},{4,3},{5,4},{6,5},{7,6},{9,8},{10,9},{11,10},{12... | collective-permute-start | bytes 176264 | tf_op jit(solution)/shard_map/ppermute | solution.py:51
  49.3 0.8 copy-start.14
  50.1 0.8 copy-start.15
  52.9 7.5 %copy-start.2 = (f32[5,48,3,128]{3,2,1,0:T(4,128)S(1)}, f32[5,48,3,128]{3,2,1,0:T(4,128)}, u32[]{:S(2)}) copy-start(f32[5,48,3,128]{3,2,1,0:T(4,128)} %copy-done.1) | copy-start | bytes 1105924
  65.3 3.2 %copy-start.19 = (s32[96]{0:T(128)S(1)}, s32[96]{0:T(128)}, u32[]{:S(2)}) copy-start(s32[96]{0:T(128)} %get-tuple-element.49) | copy-start | bytes 1156
  65.3 3.2 %copy-start.20 = (s32[96]{0:T(128)S(1)}, s32[96]{0:T(128)}, u32[]{:S(2)}) copy-start(s32[96]{0:T(128)} %get-tuple-element.50) | copy-start | bytes 1156
  65.3 3.2 %copy-start.21 = (f32[96]{0:T(128)S(1)}, f32[96]{0:T(128)}, u32[]{:S(2)}) copy-start(f32[96]{0:T(128)} %get-tuple-element.47) | copy-start | bytes 1156
  65.3 3.2 %copy-start.22 = (f32[96]{0:T(128)S(1)}, f32[96]{0:T(128)}, u32[]{:S(2)}) copy-start(f32[96]{0:T(128)} %get-tuple-element.48) | copy-start | bytes 1156
  68.6 1.3 %copy-start.16 = (s32[1280]{0:T(1024)S(1)}, s32[1280]{0:T(1024)}, u32[]{:S(2)}) copy-start(s32[1280]{0:T(1024)} %get-tuple-element.54) | copy-start | bytes 15364
  68.6 1.3 %copy-start.17 = (f32[1280]{0:T(1024)S(1)}, f32[1280]{0:T(1024)}, u32[]{:S(2)}) copy-start(f32[1280]{0:T(1024)} %get-tuple-element.51) | copy-start | bytes 15364
  68.6 1.3 %copy-start.18 = (f32[1280]{0:T(1024)S(1)}, f32[1280]{0:T(1024)}, u32[]{:S(2)}) copy-start(f32[1280]{0:T(1024)} %get-tuple-element.52) | copy-start | bytes 15364
  71.9 15.0 %copy-start.3 = (f32[5,48,11,128]{3,2,1,0:T(8,128)S(1)}, f32[5,48,11,128]{3,2,1,0:T(8,128)}, u32[]{:S(2)}) copy-start(f32[5,48,11,128]{3,2,1,0:T(8,128)} %get-tuple-element.42) | copy-start | bytes 4055044
  86.9 1.2 %copy-start.12 = (f32[5,48,8,128]{3,2,1,0:T(8,128)S(1)}, f32[5,48,8,128]{3,2,1,0:T(8,128)}, u32[]{:S(2)}) copy-start(f32[5,48,8,128]{3,2,1,0:T(8,128)} %get-tuple-element.26) | copy-start | bytes 2949124
  87.1 1.4 %copy-start.6 = (f32[5,48,8,128]{3,2,1,0:T(8,128)S(1)}, f32[5,48,8,128]{3,2,1,0:T(8,128)}, u32[]{:S(2)}) copy-start(f32[5,48,8,128]{3,2,1,0:T(8,128)} %get-tuple-element.27) | copy-start | bytes 2949124
  87.1 1.6 %copy-start.7 = (f32[5,48,8,128]{3,2,1,0:T(8,128)S(1)}, f32[5,48,8,128]{3,2,1,0:T(8,128)}, u32[]{:S(2)}) copy-start(f32[5,48,8,128]{3,2,1,0:T(8,128)} %get-tuple-element.28) | copy-start | bytes 2949124
  87.1 1.9 %copy-start.8 = (f32[5,48,8,128]{3,2,1,0:T(8,128)S(1)}, f32[5,48,8,128]{3,2,1,0:T(8,128)}, u32[]{:S(2)}) copy-start(f32[5,48,8,128]{3,2,1,0:T(8,128)} %get-tuple-element.29) | copy-start | bytes 2949124
  87.1 2.2 %copy-start.9 = (f32[5,48,8,128]{3,2,1,0:T(8,128)S(1)}, f32[5,48,8,128]{3,2,1,0:T(8,128)}, u32[]{:S(2)}) copy-start(f32[5,48,8,128]{3,2,1,0:T(8,128)} %get-tuple-element.35) | copy-start | bytes 2949124
  87.2 2.5 %copy-start.10 = (f32[5,48,8,128]{3,2,1,0:T(8,128)S(1)}, f32[5,48,8,128]{3,2,1,0:T(8,128)}, u32[]{:S(2)}) copy-start(f32[5,48,8,128]{3,2,1,0:T(8,128)} %get-tuple-element.24) | copy-start | bytes 2949124
  87.2 2.8 %copy-start.11 = (f32[5,48,8,128]{3,2,1,0:T(8,128)S(1)}, f32[5,48,8,128]{3,2,1,0:T(8,128)}, u32[]{:S(2)}) copy-start(f32[5,48,8,128]{3,2,1,0:T(8,128)} %get-tuple-element.25) | copy-start | bytes 2949124

commit v4 on v2

--- a/solution.py
+++ b/solution.py
@@ -204,7 +204,13 @@
         level = jnp.where(float(substep) < nsteps, moved, level)
     level_out[...] = level[inner]
     fuel_out[...] = remaining
-    heat_out[...] = heating.reshape(rows // RF, RF, cols).sum(axis=1)
+    heat_rows = heating.reshape(rows // RF, RF, cols).sum(axis=1)
+    lane_in = lax.broadcasted_iota(jnp.int32, (cols, cols // RF), 0) // RF
+    lane_out = lax.broadcasted_iota(jnp.int32, (cols, cols // RF), 1)
+    blocks = (lane_in == lane_out).astype(jnp.float32)
+    heat_out[...] = jnp.dot(
+        heat_rows, blocks, precision=lax.Precision.HIGHEST, preferred_element_type=jnp.float32
+    ) / (RF * RF)
 
 
 def fire_step(tables, ext, winds, fuel_left):
@@ -215,11 +221,65 @@
         out_shape=(
             jax.ShapeDtypeStruct((rows, cols), jnp.float32),
             jax.ShapeDtypeStruct((rows, cols), jnp.float32),
-            jax.ShapeDtypeStruct((rows // RF, cols), jnp.float32),
+            jax.ShapeDtypeStruct((rows // RF, cols // RF), jnp.float32),
         ),
         in_specs=[pl.BlockSpec(memory_space=pltpu.SMEM), vmem, vmem, vmem],
         out_specs=(vmem, vmem, vmem),
     )(tables, ext, winds, fuel_left)
+
+
+def atmos_kernel(q_ref, u_ref, v_ref, h_ref, o_ref):
+    rows, cols = o_ref.shape[2], o_ref.shape[3]
+    width = q_ref.shape[3]
+
+    def at(ref, dx, dy):
+        band = ref[0, :, 3 + dx : 3 + dx + rows, :]
+        return pltpu.roll(band, (width - 3 - dy) % width, 2)[:, :, :cols]
+
+    centre = at(q_ref, 0, 0)
+    deriv_x = (
+        at(q_ref, 3, 0)
+        - 9.0 * at(q_ref, 2, 0)
+        + 45.0 * at(q_ref, 1, 0)
+        - 45.0 * at(q_ref, -1, 0)
+        + 9.0 * at(q_ref, -2, 0)
+        - at(q_ref, -3, 0)
+    ) / 60.0
+    deriv_y = (
+        at(q_ref, 0, 3)
+        - 9.0 * at(q_ref, 0, 2)
+        + 45.0 * at(q_ref, 0, 1)
+        - 45.0 * at(q_ref, 0, -1)
+        + 9.0 * at(q_ref, 0, -2)
+        - at(q_ref, 0, -3)
+    ) / 60.0
+    laplace = at(q_ref, 1, 0) + at(q_ref, -1, 0) + at(q_ref, 0, 1) + at(q_ref, 0, -1) - 4.0 * centre
+    updated = (
+        centre
+        - COURANT * (at(u_ref, 0, 0) * deriv_x + at(v_ref, 0, 0) * deriv_y)
+        + DIFFUSE * laplace
+    )
+    o_ref[0] = jnp.where(pl.program_id(0) == 3, updated + h_ref[...], updated)
+
+
+def atmos_call(padded, heat_atm):
+    fields, depth, ext_rows, width = padded.shape
+    rows, cols = heat_atm.shape
+    profile = jnp.exp(-4.0 * jnp.arange(depth).astype(jnp.float32) / depth)
+    heat = heat_atm[None, :, :] * profile[:, None, None]
+    block = (1, depth, ext_rows, width)
+    return pl.pallas_call(
+        atmos_kernel,
+        grid=(fields,),
+        out_shape=jax.ShapeDtypeStruct((fields, depth, rows, cols), jnp.float32),
+        in_specs=[
+            pl.BlockSpec(block, lambda f: (f, 0, 0, 0)),
+            pl.BlockSpec(block, lambda f: (0, 0, 0, 0)),
+            pl.BlockSpec(block, lambda f: (1, 0, 0, 0)),
+            pl.BlockSpec((depth, rows, cols), lambda f: (0, 0, 0)),
+        ],
+        out_specs=pl.BlockSpec((1, depth, rows, cols), lambda f: (f, 0, 0, 0)),
+    )(padded, padded, padded, heat)
 
 
 def fire_halo(level):
@@ -243,6 +303,8 @@
     atmos_rows, atmos_cols = (atmos.shape[2], atmos.shape[3])
     padded_atm = extended(atmos, (("gx", 2), ("gy", 3)), 3)
     surface = padded_atm[0:2, 0]
+    lanes = -(-padded_atm.shape[3] // 128) * 128
+    padded_atm = jnp.pad(padded_atm, ((0, 0), (0, 0), (0, 0), (0, lanes - padded_atm.shape[3])))
     slots = burn_tiles.reshape(-1)
     listed = burn_count.reshape(())
     tiles_dev = substep_count.size
@@ -263,9 +325,8 @@
     stacked = jnp.concatenate([room, stacked, room], axis=2)
     winds = surface_winds(surface, fire_rows, fire_cols, halo, HALO_Y)
     tables = jnp.concatenate([spread_rate, wind_factor, burn_time, heat_yield]).astype(jnp.float32)
-    level, remaining, heat_rows = fire_step(tables, stacked, winds, fuel_left)
-    heat_atm = heat_rows.reshape(atmos_rows, atmos_cols, RF).sum(axis=2) / (RF * RF)
-    return (atmos_step(padded_atm, heat_atm), level, remaining)
+    level, remaining, heat_atm = fire_step(tables, stacked, winds, fuel_left)
+    return (atmos_call(padded_atm, heat_atm), level, remaining)
 
 
 def solution(mesh):

time: 87.5 us -> 86.5 us (0.989)
  Pallas kernels: 11.9 us -> 22.9 us
  waiting for transfers between devices: 7.18 us -> 1.53 us
  other arithmetic: 14.5 us -> 10.2 us
  local copies, waits for them, and re-layouts: 22.2 us -> 18 us
  starting transfers between devices: 26.1 us -> 29.3 us
    pallas_call x0 -> x1, Pallas kernels: none -> 10.8 us  [atmos_call(): pl.pallas_call(atmos_kernel, grid=(fields,), out_shape=jax.ShapeDtypeStru...]
    add x1 -> x0, other arithmetic: 10.1 us -> none  [atmos_step(): centre - COURANT * (centre[0:1] * deriv_x + centre[1:2] * deriv_y)]
    ppermute x4, waiting for transfers between devices: 5.68 us -> 0.01 us  [extended(): lax.ppermute(tail, axis, [(i, (i + 1) % count) for i in range(ends)])]
    concatenate x2 -> x3, other arithmetic: 0.46 us -> 4.7 us  [extended(): jnp.concatenate([lax.ppermute(tail, axis, [(i, (i + 1) % count) for i in...]
    ppermute x4, starting transfers between devices: 11.5 us -> 15.3 us  [extended(): lax.ppermute(head, axis, [((i + 1) % count, i) for i in range(ends)])]
    slice x4 -> x2, local copies, waits for them, and re-layouts: 6 us -> 2.38 us  [extended(): head = lax.slice_in_dim(cells, 0, width, axis=dim)]
    unnamed x26 -> x16, local copies, waits for them, and re-layouts: 3.39 us -> 0.8 us
    pad x0 -> x1, local copies, waits for them, and re-layouts: none -> 2.33 us  [shards(): jnp.pad(padded_atm, ((0, 0), (0, 0), (0, 0), (0, lanes - padded_atm.shape...]
  transfers between devices with their start and end apart: 8 -> 8, of which waited for: 2 -> 1; matrix products, arithmetic and copies ran while one was open for 19% -> 15% of each run, Pallas kernels for 0% -> 0%
where the time goes in v4:
time: 86.5 us; the launch traced here: 85.9 us
  starting transfers between devices  29.3 us (34%)
  Pallas kernels  22.9 us (26%)
  local copies, waits for them, and re-layouts  18 us (21%)
  other arithmetic  10.2 us (12%)
  matrix products  2.43 us (3%)
  between operations  1.64 us (2%)
  waiting for transfers between devices  1.53 us (2%)
    ppermute x4, starting transfers between devices, extended(): lax.ppermute(head, axis, [((i + 1) % count, i) for i in range(ends)])  15.3 us
    ppermute x4, starting transfers between devices, extended(): lax.ppermute(tail, axis, [(i, (i + 1) % count) for i in range(ends)])  14 us
    pallas_call x1, Pallas kernels, fire_step(): pl.pallas_call(fire_kernel, out_shape=(jax.ShapeDtypeStruct((rows, cols),...  12.1 us
    pallas_call x1, Pallas kernels, atmos_call(): pl.pallas_call(atmos_kernel, grid=(fields,), out_shape=jax.ShapeDtypeStru...  10.8 us
    slice x3, local copies, waits for them, and re-layouts, extended(): lax.slice_in_dim(cells, cells.shape[dim] - width, cells.shape[dim], axis=...  5.14 us
    concatenate x3, other arithmetic, extended(): jnp.concatenate([lax.ppermute(tail, axis, [(i, (i + 1) % count) for i in...  4.7 us
    ppermute x1, local copies, waits for them, and re-layouts, extended(): lax.ppermute(head, axis, [((i + 1) % count, i) for i in range(ends)])  2.99 us
    slice x2, local copies, waits for them, and re-layouts, extended(): head = lax.slice_in_dim(cells, 0, width, axis=dim)  2.38 us
  transfers between devices with their start and end apart: 8, of which 1 were waited for; matrix products, arithmetic and copies ran while one was open for 15% of the time, Pallas kernels for 0%

profile of v4, /device:TPU:120, one launch (start us, length us, event | category | flops | bytes accessed | tf_op | source)
XLA Modules:
  0.0 85.9 jit_solution(1690269236317534120)
XLA Ops:
  1.4 0.7 fusion.20
  2.1 0.7 fusion.28
  2.8 0.1 broadcast_in_dim.29
  2.9 0.1 broadcast_in_dim.30
  2.9 1.0 %convert_bitcast_fusion = f32[1,64,1024]{2,1,0:T(8,128)S(1)} fusion(s32[64,1024]{1,0:T(8,128)} %param.14), kind=kLoop, calls=%fused_computation.16 | loop fusion | flops 65536 | bytes 524288 | tf_op jit(solution)/shard_map/stack | solution.py:322
  4.0 0.9 %pad_maximum_fusion.5 = (f32[3,16,1024]{2,1,0:T(8,128)S(1)}, f32[3,16,1024]{2,1,0:T(8,128)S(1)}) fusion(f32[1,64,1024]{2,1,0:T(8,128)S(1)} %broadcast_in_dim.52, f32[1,64,1024]{2,1,0:T(8,128)S(1)} %convert_bitcast_fusion, f32[1,64,1024]{2,1,0:T(8,128)} %bitcast.26), kind=kLoop, calls=%fused_computation.19 | loop fusion | flops 196608 | bytes 1179648 | tf_op jit(solution)/shard_map/slice | solution.py:22
  4.9 1.9 %collective-permute-start.4 = (f32[3,16,1024]{2,1,0:T(8,128)S(1)}, f32[3,16,1024]{2,1,0:T(8,128)S(1)}, u32[]{:S(2)}, u32[]{:S(2)}) collective-permute-start(f32[3,16,1024]{2,1,0:T(8,128)S(1)} %get-tuple-element.15), channel_id=1, source_target_pairs={{0,8},{8,16},{16,24},{24,32},{32,40},{40,48},{48,56},{56,64},{64,7... | collective-permute-start | bytes 589832 | tf_op jit(solution)/shard_map/ppermute | solution.py:25
  6.8 5.8 %collective-permute-start.5 = (f32[3,16,1024]{2,1,0:T(8,128)S(1)}, f32[3,16,1024]{2,1,0:T(8,128)S(1)}, u32[]{:S(2)}, u32[]{:S(2)}) collective-permute-start(f32[3,16,1024]{2,1,0:T(8,128)S(1)} %get-tuple-element.16), channel_id=1, source_target_pairs={{8,0},{16,8},{24,16},{32,24},{40,32},{48,40},{56,48},{64,56},{72,6... | collective-permute-start | bytes 589832 | tf_op jit(solution)/shard_map/ppermute | solution.py:27
  12.6 0.0 copy-done
  12.6 0.1 fusion.33
  12.7 1.9 %collective-permute-start = (f32[5,48,3,128]{3,2,1,0:T(4,128)S(1)}, f32[5,48,3,128]{3,2,1,0:T(4,128)S(1)}, u32[]{:S(2)}, u32[]{:S(2)}) collective-permute-start(f32[5,48,3,128]{3,2,1,0:T(4,128)S(1)} %get-tuple-element.13), channel_id=1, source_target_pairs={{0,8},{8,16},{16,24},{24,32},{32,40},{40,48},{48,56},{56,64},{64,7... | collective-permute-start | bytes 1105928 | tf_op jit(solution)/shard_map/ppermute | solution.py:25
  14.7 5.8 %collective-permute-start.1 = (f32[5,48,3,128]{3,2,1,0:T(4,128)S(1)}, f32[5,48,3,128]{3,2,1,0:T(4,128)S(1)}, u32[]{:S(2)}, u32[]{:S(2)}) collective-permute-start(f32[5,48,3,128]{3,2,1,0:T(4,128)S(1)} %get-tuple-element.14), channel_id=1, source_target_pairs={{8,0},{16,8},{24,16},{32,24},{40,32},{48,40},{56,48},{64,56},{72,6... | collective-permute-start | bytes 1105928 | tf_op jit(solution)/shard_map/ppermute | solution.py:27
  20.5 0.0 collective-permute-done.4
  20.5 0.0 collective-permute-done.5
  20.5 0.1 pad_maximum_fusion.2
  20.7 0.9 %fusion.32 = (f32[3,96,16]{2,1,0:T(8,128)}, f32[3,96,16]{2,1,0:T(8,128)}) fusion(f32[3,96,1024]{2,1,0:T(8,128)S(1)} %pad_maximum_fusion.2), kind=kLoop, calls=%fused_computation.75 | loop fusion | bytes 73728 | tf_op jit(solution)/shard_map/slice | solution.py:21
  21.6 5.0 %collective-permute-start.6 = (f32[3,96,16]{2,1,0:T(8,128)}, f32[3,96,16]{2,1,0:T(8,128)}, u32[]{:S(2)}, u32[]{:S(2)}) collective-permute-start(f32[3,96,16]{2,1,0:T(8,128)} %get-tuple-element.12), channel_id=1, source_target_pairs={{0,1},{1,2},{2,3},{3,4},{4,5},{5,6},{6,7},{8,9},{9,10},{10,11},{11... | collective-permute-start | bytes 55304 | tf_op jit(solution)/shard_map/ppermute | solution.py:25
  26.6 1.9 %collective-permute-start.7 = (f32[3,96,16]{2,1,0:T(8,128)}, f32[3,96,16]{2,1,0:T(8,128)}, u32[]{:S(2)}, u32[]{:S(2)}) collective-permute-start(f32[3,96,16]{2,1,0:T(8,128)} %get-tuple-element.11), channel_id=1, source_target_pairs={{1,0},{2,1},{3,2},{4,3},{5,4},{6,5},{7,6},{9,8},{10,9},{11,10},{12... | collective-permute-start | bytes 55304 | tf_op jit(solution)/shard_map/ppermute | solution.py:27
  28.5 0.0 collective-permute-done
  28.6 0.0 collective-permute-done.1
  28.6 0.0 copy-done.1
  28.6 0.0 copy-start.2
  28.6 0.8 copy-done.2
  29.4 0.4 pad_maximum_fusion.1
  29.7 2.0 %fusion.31 = (f32[5,48,14,3]{3,2,1,0:T(8,128)}, f32[5,48,14,3]{3,2,1,0:T(8,128)S(1)}) fusion(f32[5,48,14,128]{3,2,1,0:T(8,128)S(1)} %pad_maximum_fusion.1), kind=kLoop, calls=%fused_computation.74 | loop fusion | bytes 161280 | tf_op jit(solution)/shard_map/slice | solution.py:22
  31.7 3.0 %copy.18 = f32[5,48,14,3]{1,2,3,0:T(8,128)} copy(f32[5,48,14,3]{3,2,1,0:T(8,128)} %get-tuple-element.9) | data formatting | bytes 80640 | tf_op jit(solution)/shard_map/slice | solution.py:22
  34.7 5.1 %collective-permute-start.2 = (f32[5,48,14,3]{1,2,3,0:T(8,128)}, f32[5,48,14,3]{1,2,3,0:T(8,128)}, u32[]{:S(2)}, u32[]{:S(2)}) collective-permute-start(f32[5,48,14,3]{1,2,3,0:T(8,128)} %copy.18), channel_id=1, source_target_pairs={{0,1},{1,2},{2,3},{3,4},{4,5},{5,6},{6,7},{8,9},{9,10},{10,11},{11... | collective-permute-start | bytes 120968 | tf_op jit(solution)/shard_map/ppermute | solution.py:25
  39.9 1.5 %copy.19 = f32[5,48,14,3]{1,2,3,0:T(8,128)} copy(f32[5,48,14,3]{3,2,1,0:T(8,128)S(1)} %get-tuple-element.10) | data formatting | bytes 80640 | tf_op jit(solution)/shard_map/slice | solution.py:21
  41.3 1.9 %collective-permute-start.3 = (f32[5,48,14,3]{1,2,3,0:T(8,128)}, f32[5,48,14,3]{1,2,3,0:T(8,128)}, u32[]{:S(2)}, u32[]{:S(2)}) collective-permute-start(f32[5,48,14,3]{1,2,3,0:T(8,128)} %copy.19), channel_id=1, source_target_pairs={{1,0},{2,1},{3,2},{4,3},{5,4},{6,5},{7,6},{9,8},{10,9},{11,10},{12... | collective-permute-start | bytes 120968 | tf_op jit(solution)/shard_map/ppermute | solution.py:27
  43.3 0.0 copy-done.4
  43.3 0.0 copy-done.5
  43.3 0.0 copy-done.6
  43.3 0.0 copy-done.7
  43.3 0.6 pad_maximum_fusion.6.tab_ref
  43.9 0.0 collective-permute-done.6
  43.9 0.0 collective-permute-done.7
  44.0 2.3 %concatenate.19.ext_ref = f32[3,96,1280]{2,1,0:T(8,128)} concatenate(f32[3,96,112]{2,1,0:T(8,128)S(1)} %broadcast_in_dim.26, f32[3,96,16]{2,1,0:T(8,128)} %collective-permute-done.6, f32[3,96,1024]{2,1,0:T(8,128)} %copy-done.1, f32[3,96,16]{2,1,0:T(8,128)} %collective-permute-done.7, f32[3,96,112]{2,1,0:T(8,128)S(1)} %broadcast_in_dim.26), dimensions={2} | concatenate | bytes 2949120 | tf_op jit(solution)/shard_map/concatenate | solution.py:325
  46.3 0.0 collective-permute-done.2
  46.3 1.8 %copy.20 = f32[5,48,14,3]{3,2,1,0:T(8,128)S(1)} copy(f32[5,48,14,3]{1,2,3,0:T(8,128)} %collective-permute-done.2) | data formatting | bytes 80640 | tf_op jit(solution)/shard_map/ppermute | solution.py:25
  48.1 1.5 %collective-permute-done.3 = f32[5,48,14,3]{1,2,3,0:T(8,128)} collective-permute-done((f32[5,48,14,3]{1,2,3,0:T(8,128)}, f32[5,48,14,3]{1,2,3,0:T(8,128)}, u32[]{:S(2)}, u32[]{:S(2)}) %collective-permute-start.3) | collective-permute-done | bytes 40352 | tf_op jit(solution)/shard_map/ppermute | solution.py:27
  49.6 3.0 %copy.21 = f32[5,48,14,3]{3,2,1,0:T(8,128)} copy(f32[5,48,14,3]{1,2,3,0:T(8,128)} %collective-permute-done.3) | data formatting | bytes 80640 | tf_op jit(solution)/shard_map/ppermute | solution.py:27
  52.6 4.2 %pad_maximum_fusion = f32[5,48,14,134]{3,2,1,0:T(8,128)S(1)} fusion(f32[5,48,14,3]{3,2,1,0:T(8,128)} %copy.21, f32[5,48,3,128]{3,2,1,0:T(4,128)} %copy-done.2, f32[5,48,8,128]{3,2,1,0:T(8,128)S(1)} %copy-done, f32[5,48,3,128]{3,2,1,0:T(4,128)S(1)} %collective-permute-done, f32[5,48,14,3]{3,2,1,0:T(8,128)S(1)} %copy.20), kind=kLoop, calls=%fused_computation | loop fusion | flops 1800960 | bytes 3601920 | tf_op jit(solution)/shard_map/concatenate | solution.py:23
  56.9 2.3 %pad.4.q_ref.u_ref.v_ref = f32[5,48,14,256]{3,2,1,0:T(8,128)} pad(f32[5,48,14,134]{3,2,1,0:T(8,128)S(1)} %pad_maximum_fusion, f32[]{:T(128)} %constant.75.clone.1), padding=0_0x0_0x0_0x0_122 | pad | bytes 5241604 | tf_op jit(solution)/shard_map/jit(_pad)/pad | solution.py:307
  59.2 0.4 convolution_bitcast_fusion
  59.6 2.0 %fusion.wind_ref = f32[2,96,1280]{2,1,0:T(8,128)} fusion(f32[2,96,134]{1,2,0:T(8,128)S(1)} %convolution_bitcast_fusion, f32[1280]{0:T(1024)S(1)} %get-tuple-element.21, s32[1280]{0:T(1024)S(1)} %get-tuple-element.24, f32[1280]{0:T(1024)S(1)} %get-tuple-element.22, s32[1280]{0:T(1024)S(1)} %get-tuple-element.23), kind=kOutput, calls=%fused_computation.6 | convolution fusion | flops 396039680 | bytes 1106432 | tf_op jit(solution)/shard_map/kib,jb->kij/dot_general | solution.py:145
  61.6 12.1 %shard_map.130 = (f32[64,1024]{1,0:T(8,128)}, f32[64,1024]{1,0:T(8,128)}, f32[8,128]{1,0:T(8,128)}) custom-call(f32[52]{0:T(128)} %pad_maximum_fusion.6.tab_ref, f32[3,96,1280]{2,1,0:T(8,128)} %concatenate.19.ext_ref, f32[2,96,1280]{2,1,0:T(8,128)} %fusion.wind_ref, f32[64,1024]{1,0:T(8,128)} %fuel_ref.1), custom_call_target="tpu_custom_call" | custom-call | tf_op jit(solution)/shard_map/pallas_call | solution.py:219
  73.7 1.5 %broadcast_multiply_fusion.h_ref = f32[48,8,128]{2,1,0:T(8,128)} fusion(f32[48]{0:T(128)S(1)} %multiply_exponential_fusion, f32[8,128]{1,0:T(8,128)} %get-tuple-element.6), kind=kLoop, calls=%fused_computation.20 | loop fusion | flops 49152 | bytes 200896 | tf_op jit(solution)/shard_map/mul | solution.py:269
  75.2 10.8 %shard_map.131 = f32[5,48,8,128]{3,2,1,0:T(8,128)} custom-call(f32[5,48,14,256]{3,2,1,0:T(8,128)} %pad.4.q_ref.u_ref.v_ref, f32[5,48,14,256]{3,2,1,0:T(8,128)} %pad.4.q_ref.u_ref.v_ref, f32[5,48,14,256]{3,2,1,0:T(8,128)} %pad.4.q_ref.u_ref.v_ref, f32[48,8,128]{2,1,0:T(8,128)} %broadcast_multiply_fusion.h_ref), custom_call_target="tpu_custom_call" | custom-call | tf_op jit(solution)/shard_map/pallas_call | solution.py:271
  (16 shorter events, 0.1 us)
Async XLA Ops:
  0.6 11.9 %copy-start = (f32[5,48,8,128]{3,2,1,0:T(8,128)S(1)}, f32[5,48,8,128]{3,2,1,0:T(8,128)}, u32[]{:S(2)}) copy-start(f32[5,48,8,128]{3,2,1,0:T(8,128)} %param.11) | copy-start | bytes 2949124
  2.9 17.6 %copy-start.3 = (f32[64,1024]{1,0:T(8,128)S(1)}, f32[64,1024]{1,0:T(8,128)}, u32[]{:S(2)}) copy-start(f32[64,1024]{1,0:T(8,128)} %param.12) | copy-start | bytes 786436
  4.9 15.6 %collective-permute-start.4 = (f32[3,16,1024]{2,1,0:T(8,128)S(1)}, f32[3,16,1024]{2,1,0:T(8,128)S(1)}, u32[]{:S(2)}, u32[]{:S(2)}) collective-permute-start(f32[3,16,1024]{2,1,0:T(8,128)S(1)} %get-tuple-element.15), channel_id=1, source_target_pairs={{0,8},{8,16},{16,24},{24,32},{32,40},{40,48},{48,56},{56,64},{64,7... | collective-permute-start | bytes 589832 | tf_op jit(solution)/shard_map/ppermute | solution.py:25
  6.8 13.7 %collective-permute-start.5 = (f32[3,16,1024]{2,1,0:T(8,128)S(1)}, f32[3,16,1024]{2,1,0:T(8,128)S(1)}, u32[]{:S(2)}, u32[]{:S(2)}) collective-permute-start(f32[3,16,1024]{2,1,0:T(8,128)S(1)} %get-tuple-element.16), channel_id=1, source_target_pairs={{8,0},{16,8},{24,16},{32,24},{40,32},{48,40},{56,48},{64,56},{72,6... | collective-permute-start | bytes 589832 | tf_op jit(solution)/shard_map/ppermute | solution.py:27
  12.7 15.8 %collective-permute-start = (f32[5,48,3,128]{3,2,1,0:T(4,128)S(1)}, f32[5,48,3,128]{3,2,1,0:T(4,128)S(1)}, u32[]{:S(2)}, u32[]{:S(2)}) collective-permute-start(f32[5,48,3,128]{3,2,1,0:T(4,128)S(1)} %get-tuple-element.13), channel_id=1, source_target_pairs={{0,8},{8,16},{16,24},{24,32},{32,40},{40,48},{48,56},{56,64},{64,7... | collective-permute-start | bytes 1105928 | tf_op jit(solution)/shard_map/ppermute | solution.py:25
  14.7 13.9 %collective-permute-start.1 = (f32[5,48,3,128]{3,2,1,0:T(4,128)S(1)}, f32[5,48,3,128]{3,2,1,0:T(4,128)S(1)}, u32[]{:S(2)}, u32[]{:S(2)}) collective-permute-start(f32[5,48,3,128]{3,2,1,0:T(4,128)S(1)} %get-tuple-element.14), channel_id=1, source_target_pairs={{8,0},{16,8},{24,16},{32,24},{40,32},{48,40},{56,48},{64,56},{72,6... | collective-permute-start | bytes 1105928 | tf_op jit(solution)/shard_map/ppermute | solution.py:27
  20.7 7.9 %copy-start.1 = (f32[3,96,1024]{2,1,0:T(8,128)}, f32[3,96,1024]{2,1,0:T(8,128)S(1)}, u32[]{:S(2)}) copy-start(f32[3,96,1024]{2,1,0:T(8,128)S(1)} %pad_maximum_fusion.2) | copy-start | bytes 3538948
  21.6 22.4 %collective-permute-start.6 = (f32[3,96,16]{2,1,0:T(8,128)}, f32[3,96,16]{2,1,0:T(8,128)}, u32[]{:S(2)}, u32[]{:S(2)}) collective-permute-start(f32[3,96,16]{2,1,0:T(8,128)} %get-tuple-element.12), channel_id=1, source_target_pairs={{0,1},{1,2},{2,3},{3,4},{4,5},{5,6},{6,7},{8,9},{9,10},{10,11},{11... | collective-permute-start | bytes 55304 | tf_op jit(solution)/shard_map/ppermute | solution.py:25
  26.6 17.3 %collective-permute-start.7 = (f32[3,96,16]{2,1,0:T(8,128)}, f32[3,96,16]{2,1,0:T(8,128)}, u32[]{:S(2)}, u32[]{:S(2)}) collective-permute-start(f32[3,96,16]{2,1,0:T(8,128)} %get-tuple-element.11), channel_id=1, source_target_pairs={{1,0},{2,1},{3,2},{4,3},{5,4},{6,5},{7,6},{9,8},{10,9},{11,10},{12... | collective-permute-start | bytes 55304 | tf_op jit(solution)/shard_map/ppermute | solution.py:27
  28.6 0.8 copy-start.2
  31.7 11.6 %copy-start.4 = (f32[13]{0:T(128)S(1)}, f32[13]{0:T(128)}, u32[]{:S(2)}) copy-start(f32[13]{0:T(128)} %param.18) | copy-start | bytes 160
  31.7 11.6 %copy-start.5 = (f32[13]{0:T(128)S(1)}, f32[13]{0:T(128)}, u32[]{:S(2)}) copy-start(f32[13]{0:T(128)} %param.17) | copy-start | bytes 160
  31.7 11.6 %copy-start.6 = (f32[13]{0:T(128)S(1)}, f32[13]{0:T(128)}, u32[]{:S(2)}) copy-start(f32[13]{0:T(128)} %param.16) | copy-start | bytes 160
  31.7 11.6 %copy-start.7 = (f32[13]{0:T(128)S(1)}, f32[13]{0:T(128)}, u32[]{:S(2)}) copy-start(f32[13]{0:T(128)} %param.15) | copy-start | bytes 160
  34.7 11.6 %collective-permute-start.2 = (f32[5,48,14,3]{1,2,3,0:T(8,128)}, f32[5,48,14,3]{1,2,3,0:T(8,128)}, u32[]{:S(2)}, u32[]{:S(2)}) collective-permute-start(f32[5,48,14,3]{1,2,3,0:T(8,128)} %copy.18), channel_id=1, source_target_pairs={{0,1},{1,2},{2,3},{3,4},{4,5},{5,6},{6,7},{8,9},{9,10},{10,11},{11... | collective-permute-start | bytes 120968 | tf_op jit(solution)/shard_map/ppermute | solution.py:25
  41.3 8.3 %collective-permute-start.3 = (f32[5,48,14,3]{1,2,3,0:T(8,128)}, f32[5,48,14,3]{1,2,3,0:T(8,128)}, u32[]{:S(2)}, u32[]{:S(2)}) collective-permute-start(f32[5,48,14,3]{1,2,3,0:T(8,128)} %copy.19), channel_id=1, source_target_pairs={{1,0},{2,1},{3,2},{4,3},{5,4},{6,5},{7,6},{9,8},{10,9},{11,10},{12... | collective-permute-start | bytes 120968 | tf_op jit(solution)/shard_map/ppermute | solution.py:27

commit v5 on v2

--- a/solution.py
+++ b/solution.py
@@ -204,7 +204,13 @@
         level = jnp.where(float(substep) < nsteps, moved, level)
     level_out[...] = level[inner]
     fuel_out[...] = remaining
-    heat_out[...] = heating.reshape(rows // RF, RF, cols).sum(axis=1)
+    heat_rows = heating.reshape(rows // RF, RF, cols).sum(axis=1)
+    lane_in = lax.broadcasted_iota(jnp.int32, (cols, cols // RF), 0) // RF
+    lane_out = lax.broadcasted_iota(jnp.int32, (cols, cols // RF), 1)
+    blocks = (lane_in == lane_out).astype(jnp.float32)
+    heat_out[...] = jnp.dot(
+        heat_rows, blocks, precision=lax.Precision.HIGHEST, preferred_element_type=jnp.float32
+    ) / (RF * RF)
 
 
 def fire_step(tables, ext, winds, fuel_left):
@@ -215,7 +221,7 @@
         out_shape=(
             jax.ShapeDtypeStruct((rows, cols), jnp.float32),
             jax.ShapeDtypeStruct((rows, cols), jnp.float32),
-            jax.ShapeDtypeStruct((rows // RF, cols), jnp.float32),
+            jax.ShapeDtypeStruct((rows // RF, cols // RF), jnp.float32),
         ),
         in_specs=[pl.BlockSpec(memory_space=pltpu.SMEM), vmem, vmem, vmem],
         out_specs=(vmem, vmem, vmem),
@@ -263,8 +269,7 @@
     stacked = jnp.concatenate([room, stacked, room], axis=2)
     winds = surface_winds(surface, fire_rows, fire_cols, halo, HALO_Y)
     tables = jnp.concatenate([spread_rate, wind_factor, burn_time, heat_yield]).astype(jnp.float32)
-    level, remaining, heat_rows = fire_step(tables, stacked, winds, fuel_left)
-    heat_atm = heat_rows.reshape(atmos_rows, atmos_cols, RF).sum(axis=2) / (RF * RF)
+    level, remaining, heat_atm = fire_step(tables, stacked, winds, fuel_left)
     return (atmos_step(padded_atm, heat_atm), level, remaining)
 
 

time: 87.5 us -> 99.3 us (1.13)
  other arithmetic: 14.5 us -> 31.8 us
  waiting for transfers between devices: 7.18 us -> 0.02 us
  starting transfers between devices: 26.1 us -> 27.8 us
    concatenate x2 -> x3, other arithmetic: 0.46 us -> 11.5 us  [extended(): jnp.concatenate([lax.ppermute(tail, axis, [(i, (i + 1) % count) for i in...]
    ppermute x4, waiting for transfers between devices: 5.68 us -> 0.01 us  [extended(): lax.ppermute(tail, axis, [(i, (i + 1) % count) for i in range(ends)])]
    unnamed x26 -> x46, local copies, waits for them, and re-layouts: 3.39 us -> 7.94 us
    slice x4 -> x2, local copies, waits for them, and re-layouts: 6 us -> 2.49 us  [extended(): head = lax.slice_in_dim(cells, 0, width, axis=dim)]
    ppermute x4, starting transfers between devices: 11.5 us -> 13.9 us  [extended(): lax.ppermute(head, axis, [((i + 1) % count, i) for i in range(ends)])]
    scatter-add x1, other arithmetic: 0.12 us -> 2.03 us  [atmos_step(): return updated.at[3].add(heat_atm[None, :, :] * profile[:, None, None])]
    reshape x1 -> x0, local copies, waits for them, and re-layouts: 1.87 us -> none  [shards(): heat_rows.reshape(atmos_rows, atmos_cols, RF).sum(axis=2) / (RF * RF)]
    slice x0 -> x1, other arithmetic: none -> 1.65 us  [extended(): head = lax.slice_in_dim(cells, 0, width, axis=dim)]
  transfers between devices with their start and end apart: 8 -> 8, of which waited for: 2 -> 0; matrix products, arithmetic and copies ran while one was open for 19% -> 21% of each run, Pallas kernels for 0% -> 0%
where the time goes in v5:
time: 99.3 us; the launch traced here: 98.6 us
  other arithmetic  31.8 us (32%)
  starting transfers between devices  27.8 us (28%)
  local copies, waits for them, and re-layouts  22.7 us (23%)
  Pallas kernels  12.1 us (12%)
  matrix products  2.43 us (2%)
  between operations  1.67 us (2%)
    ppermute x4, starting transfers between devices, extended(): lax.ppermute(tail, axis, [(i, (i + 1) % count) for i in range(ends)])  14 us
    ppermute x4, starting transfers between devices, extended(): lax.ppermute(head, axis, [((i + 1) % count, i) for i in range(ends)])  13.9 us
    pallas_call x1, Pallas kernels, fire_step(): pl.pallas_call(fire_kernel, out_shape=(jax.ShapeDtypeStruct((rows, cols),...  12.1 us
    concatenate x3, other arithmetic, extended(): jnp.concatenate([lax.ppermute(tail, axis, [(i, (i + 1) % count) for i in...  11.5 us
    add x1, other arithmetic, atmos_step(): centre - COURANT * (centre[0:1] * deriv_x + centre[1:2] * deriv_y)  10.9 us
    unnamed x46, local copies, waits for them, and re-layouts  7.94 us
    slice x1, local copies, waits for them, and re-layouts, shards(): surface = padded_atm[0:2, 0]  2.72 us
    ppermute x1, local copies, waits for them, and re-layouts, extended(): lax.ppermute(head, axis, [((i + 1) % count, i) for i in range(ends)])  2.5 us
  transfers between devices with their start and end apart: 8, of which 0 were waited for; matrix products, arithmetic and copies ran while one was open for 21% of the time, Pallas kernels for 0%

profile of v5, /device:TPU:120, one launch (start us, length us, event | category | flops | bytes accessed | tf_op | source)
XLA Modules:
  0.0 98.6 jit_solution(12338901867343530165)
XLA Ops:
  0.7 1.7 %fusion.55 = (f32[5,48,3,128]{3,2,1,0:T(4,128)S(1)}, f32[5,48,3,128]{3,2,1,0:T(4,128)S(1)}) fusion(f32[5,48,8,128]{3,2,1,0:T(8,128)} %param.13), kind=kLoop, calls=%fused_computation.119 | loop fusion | bytes 1474560 | tf_op jit(solution)/shard_map/slice | solution.py:21
  2.4 0.8 copy.102
  3.2 4.3 %collective-permute-start = (f32[5,48,3,128]{3,1,2,0:T(8,128)}, f32[5,48,3,128]{3,1,2,0:T(8,128)}, u32[]{:S(2)}, u32[]{:S(2)}) collective-permute-start(f32[5,48,3,128]{3,1,2,0:T(8,128)} %copy.102), channel_id=1, source_target_pairs={{8,0},{16,8},{24,16},{32,24},{40,32},{48,40},{56,48},{64,56},{72,6... | collective-permute-start | bytes 1105928 | tf_op jit(solution)/shard_map/ppermute | solution.py:27
  7.5 0.8 copy.103
  8.2 1.9 %collective-permute-start.1 = (f32[5,48,3,128]{3,1,2,0:T(8,128)}, f32[5,48,3,128]{3,1,2,0:T(8,128)}, u32[]{:S(2)}, u32[]{:S(2)}) collective-permute-start(f32[5,48,3,128]{3,1,2,0:T(8,128)} %copy.103), channel_id=1, source_target_pairs={{0,8},{8,16},{16,24},{24,32},{32,40},{40,48},{48,56},{56,64},{64,7... | collective-permute-start | bytes 1105928 | tf_op jit(solution)/shard_map/ppermute | solution.py:25
  10.8 0.1 fusion.43
  10.9 0.1 broadcast_in_dim.29
  11.0 0.1 broadcast_in_dim.30
  11.1 0.8 pad_maximum_fusion.10
  11.9 1.9 %collective-permute-start.4 = (f32[3,16,1024]{2,1,0:T(8,128)}, f32[3,16,1024]{2,1,0:T(8,128)}, u32[]{:S(2)}, u32[]{:S(2)}) collective-permute-start(f32[3,16,1024]{2,1,0:T(8,128)} %get-tuple-element.46), channel_id=1, source_target_pairs={{0,8},{8,16},{16,24},{24,32},{32,40},{40,48},{48,56},{56,64},{64,7... | collective-permute-start | bytes 589832 | tf_op jit(solution)/shard_map/ppermute | solution.py:25
  13.8 5.8 %collective-permute-start.5 = (f32[3,16,1024]{2,1,0:T(8,128)}, f32[3,16,1024]{2,1,0:T(8,128)}, u32[]{:S(2)}, u32[]{:S(2)}) collective-permute-start(f32[3,16,1024]{2,1,0:T(8,128)} %get-tuple-element.47), channel_id=1, source_target_pairs={{8,0},{16,8},{24,16},{32,24},{40,32},{48,40},{56,48},{64,56},{72,6... | collective-permute-start | bytes 589832 | tf_op jit(solution)/shard_map/ppermute | solution.py:27
  19.6 2.2 %copy.96 = f32[5,48,8,128]{1,2,3,0:T(8,128)S(1)} copy(f32[5,48,8,128]{3,2,1,0:T(8,128)} %param.13) | data formatting | bytes 1966080 | tf_op args[0]
  21.9 0.6 fusion.49
  22.5 0.6 broadcast_add_fusion.2
  23.1 0.6 broadcast_add_fusion
  23.7 0.6 multiply_exponential_fusion
  24.3 1.8 %multiply_bitcast_fusion.1 = (f32[48,8,128]{2,1,0:T(8,128)}, f32[48,8,128]{2,1,0:T(8,128)}) fusion(f32[5,48,8,128]{3,2,1,0:T(8,128)} %param.13), kind=kLoop, calls=%fused_computation.61 | loop fusion | flops 98304 | bytes 786432 | tf_op jit(solution)/shard_map/mul | solution.py:123
  26.1 1.1 %pad_maximum_fusion.7 = f32[3,96,1024]{2,1,0:T(8,128)S(1)} fusion(f32[3,16,1024]{2,1,0:T(8,128)} %collective-permute-done.5, f32[1,64,1024]{2,1,0:T(8,128)S(1)} %broadcast_in_dim.52, f32[1,64,1024]{2,1,0:T(8,128)S(1)} %convert_bitcast_fusion, f32[1,64,1024]{2,1,0:T(8,128)S(1)} %bitcast.29, f32[3,16,1024]{2,1,0:T(8,128)} %collective-permute-done.4), kind=kLoop, calls=%fused_computation.40 | loop fusion | flops 1179648 | bytes 2359296 | tf_op jit(solution)/shard_map/concatenate | solution.py:23
  27.2 1.0 %copy-done.2 = f32[3,96,1024]{2,1,0:T(8,128)} copy-done((f32[3,96,1024]{2,1,0:T(8,128)}, f32[3,96,1024]{2,1,0:T(8,128)S(1)}, u32[]{:S(2)}) %copy-start.2) | copy-done | bytes 1179672
  28.2 0.8 fusion.54
  28.9 5.0 %collective-permute-start.6 = (f32[3,96,16]{2,1,0:T(8,128)}, f32[3,96,16]{2,1,0:T(8,128)}, u32[]{:S(2)}, u32[]{:S(2)}) collective-permute-start(f32[3,96,16]{2,1,0:T(8,128)} %get-tuple-element.41), channel_id=1, source_target_pairs={{0,1},{1,2},{2,3},{3,4},{4,5},{5,6},{6,7},{8,9},{9,10},{10,11},{11... | collective-permute-start | bytes 55304 | tf_op jit(solution)/shard_map/ppermute | solution.py:25
  34.0 1.9 %collective-permute-start.7 = (f32[3,96,16]{2,1,0:T(8,128)}, f32[3,96,16]{2,1,0:T(8,128)}, u32[]{:S(2)}, u32[]{:S(2)}) collective-permute-start(f32[3,96,16]{2,1,0:T(8,128)} %get-tuple-element.40), channel_id=1, source_target_pairs={{1,0},{2,1},{3,2},{4,3},{5,4},{6,5},{7,6},{9,8},{10,9},{11,10},{12... | collective-permute-start | bytes 55304 | tf_op jit(solution)/shard_map/ppermute | solution.py:27
  35.9 0.0 collective-permute-done
  35.9 2.5 %copy.87 = f32[5,48,3,128]{1,2,3,0:T(4,128)} copy(f32[5,48,3,128]{3,1,2,0:T(8,128)} %collective-permute-done) | data formatting | bytes 737280 | tf_op jit(solution)/shard_map/ppermute | solution.py:27
  38.4 0.0 collective-permute-done.1
  38.4 2.5 %copy.89 = f32[5,48,3,128]{1,2,3,0:T(4,128)} copy(f32[5,48,3,128]{3,1,2,0:T(8,128)} %collective-permute-done.1) | data formatting | bytes 737280 | tf_op jit(solution)/shard_map/ppermute | solution.py:25
  40.9 0.0 copy-start.6
  40.9 0.0 copy-start.5
  40.9 1.7 %pad_maximum_fusion.13 = (f32[5,48,14,3]{1,2,3,0:T(8,128)}, f32[5,48,14,3]{1,2,3,0:T(8,128)}) fusion(f32[5,48,3,128]{1,2,3,0:T(4,128)} %copy.87, f32[5,48,8,128]{1,2,3,0:T(8,128)S(1)} %copy.96, f32[5,48,3,128]{1,2,3,0:T(4,128)} %copy.89), kind=kLoop, calls=%fused_computation.64 | loop fusion | flops 40320 | bytes 1800960 | tf_op jit(solution)/shard_map/slice | solution.py:21
  42.6 1.9 %collective-permute-start.2 = (f32[5,48,14,3]{1,2,3,0:T(8,128)}, f32[5,48,14,3]{1,2,3,0:T(8,128)}, u32[]{:S(2)}, u32[]{:S(2)}) collective-permute-start(f32[5,48,14,3]{1,2,3,0:T(8,128)} %get-tuple-element.38), channel_id=1, source_target_pairs={{1,0},{2,1},{3,2},{4,3},{5,4},{6,5},{7,6},{9,8},{10,9},{11,10},{12... | collective-permute-start | bytes 120968 | tf_op jit(solution)/shard_map/ppermute | solution.py:27
  44.5 5.1 %collective-permute-start.3 = (f32[5,48,14,3]{1,2,3,0:T(8,128)}, f32[5,48,14,3]{1,2,3,0:T(8,128)}, u32[]{:S(2)}, u32[]{:S(2)}) collective-permute-start(f32[5,48,14,3]{1,2,3,0:T(8,128)} %get-tuple-element.39), channel_id=1, source_target_pairs={{0,1},{1,2},{2,3},{3,4},{4,5},{5,6},{6,7},{8,9},{9,10},{10,11},{11... | collective-permute-start | bytes 120968 | tf_op jit(solution)/shard_map/ppermute | solution.py:25
  49.7 0.6 pad_maximum_fusion.14.tab_ref
  50.3 0.3 copy.91
  50.6 1.1 %copy.95 = f32[48,8,128]{0,1,2:T(8,128)} copy(f32[48,8,128]{2,1,0:T(8,128)S(1)} %copy-done.5) | data formatting | bytes 393216 | tf_op jit(solution)/shard_map/mul | solution.py:123
  51.7 0.0 collective-permute-done.6
  51.7 0.0 collective-permute-done.7
  51.7 2.3 %concatenate.44.ext_ref = f32[3,96,1280]{2,1,0:T(8,128)} concatenate(f32[3,96,112]{2,1,0:T(8,128)S(1)} %broadcast_in_dim.26, f32[3,96,16]{2,1,0:T(8,128)} %collective-permute-done.6, f32[3,96,1024]{2,1,0:T(8,128)} %copy-done.2, f32[3,96,16]{2,1,0:T(8,128)} %collective-permute-done.7, f32[3,96,112]{2,1,0:T(8,128)S(1)} %broadcast_in_dim.26), dimensions={2} | concatenate | bytes 2949120 | tf_op jit(solution)/shard_map/concatenate | solution.py:269
  54.0 0.0 collective-permute-done.2
  54.1 3.1 %pad_maximum_fusion.3 = f32[2,1,14,134]{1,2,3,0:T(8,128)} fusion(f32[5,48,14,3]{1,2,3,0:T(8,128)} %collective-permute-done.2, f32[5,48,14,3]{1,2,3,0:T(8,128)} %collective-permute-done.3, f32[5,48,3,128]{1,2,3,0:T(4,128)} %copy.87, f32[5,48,8,128]{1,2,3,0:T(8,128)S(1)} %copy.96, f32[5,48,3,128]{1,2,3,0:T(4,128)} %copy.89), kind=kLoop, calls=%fused_computation.36 | loop fusion | flops 15008 | bytes 1815968 | tf_op jit(solution)/shard_map/concatenate | solution.py:23
  57.2 2.7 %copy.98 = f32[2,1,14,134]{3,0,2,1:T(2,128)S(1)} copy(f32[2,1,14,134]{1,2,3,0:T(8,128)} %pad_maximum_fusion.3) | data formatting | bytes 30016 | tf_op jit(solution)/shard_map/slice | solution.py:251
  59.9 0.4 convolution_bitcast_fusion
  60.4 2.0 %fusion.21.wind_ref = f32[2,96,1280]{2,1,0:T(8,128)} fusion(f32[2,96,134]{1,2,0:T(8,128)S(1)} %convolution_bitcast_fusion, f32[1280]{0:T(1024)S(1)} %get-tuple-element.52, s32[1280]{0:T(1024)S(1)} %copy-done.9, f32[1280]{0:T(1024)S(1)} %get-tuple-element.53, s32[1280]{0:T(1024)S(1)} %copy-done.8), kind=kOutput, calls=%fused_computation.44 | convolution fusion | flops 396039680 | bytes 1106432 | tf_op jit(solution)/shard_map/kib,jb->kij/dot_general | solution.py:145
  62.4 12.1 %shard_map.130 = (f32[64,1024]{1,0:T(8,128)}, f32[64,1024]{1,0:T(8,128)}, f32[8,128]{1,0:T(8,128)}) custom-call(f32[52]{0:T(128)} %pad_maximum_fusion.14.tab_ref, f32[3,96,1280]{2,1,0:T(8,128)} %concatenate.44.ext_ref, f32[2,96,1280]{2,1,0:T(8,128)} %fusion.21.wind_ref, f32[64,1024]{1,0:T(8,128)} %fuel_ref.1), custom_call_target="tpu_custom_call" | custom-call | tf_op jit(solution)/shard_map/pallas_call | solution.py:219
  74.5 0.8 copy.100
  75.3 7.3 %pad_maximum_fusion = (f32[5,48,14,131]{1,2,3,0:T(8,128)S(1)}, f32[5,48,14,131]{1,2,3,0:T(8,128)}) fusion(f32[5,48,14,3]{1,2,3,0:T(8,128)} %collective-permute-done.2, f32[5,48,3,128]{1,2,3,0:T(4,128)} %copy.87, f32[5,48,8,128]{1,2,3,0:T(8,128)S(1)} %copy.96, f32[5,48,3,128]{1,2,3,0:T(4,128)} %copy.89, f32[5,48,14,3]{1,2,3,0:T(8,128)} %collective-permute-done.3), kind=kLoop, calls=%fused_computation.8 | loop fusion | flops 2640960 | bytes 5322240 | tf_op jit(solution)/shard_map/concatenate | solution.py:23
  82.6 10.9 %fusion.8 = f32[5,48,8,128]{1,2,3,0:T(8,128)} fusion(f32[5,48,8,128]{1,2,3,0:T(8,128)S(1)} %copy.96, f32[5,48,3,128]{1,2,3,0:T(4,128)S(1)} %copy-done.1, f32[5,48,3,128]{1,2,3,0:T(4,128)S(1)} %copy-done, f32[5,48,14,131]{1,2,3,0:T(8,128)} %get-tuple-element.37, f32[5,48,14,131]{1,2,3,0:T(8,128)S(1)} %get-tuple-element.36, f32[48,8,128]{0,1,2:T(8,128)S(1)} %copy-done.3, ...), kind=kLoop, calls=%fused_computation.18 | loop fusion | flops 8847360 | bytes 8994816 | tf_op jit(solution)/shard_map/add | solution.py:123
  93.5 2.0 %fusion.26 = f32[5,48,8,128]{1,2,3,0:T(8,128)} fusion(f32[5,48,8,128]{1,2,3,0:T(8,128)} %fusion.8, f32[48]{0:T(128)S(1)} %copy-done.10, f32[8,128]{0,1:T(8,128)S(1)} %copy.100), kind=kLoop, calls=%fused_computation.50 | loop fusion | flops 98304 | bytes 1052864 | tf_op jit(solution)/shard_map/scatter-add | solution.py:126
  95.5 3.1 %copy.101 = f32[5,48,8,128]{3,2,1,0:T(8,128)} copy(f32[5,48,8,128]{1,2,3,0:T(8,128)} %fusion.26) | data formatting | bytes 1966080
  (48 shorter events, 0.2 us)
Async XLA Ops:
  0.6 10.2 %copy-start.19 = (s32[1,1,16]{2,1,0:T(1,128)S(1)}, s32[1,1,16]{2,1,0:T(1,128)}, u32[]{:S(2)}) copy-start(s32[1,1,16]{2,1,0:T(1,128)} %param.21) | copy-start | bytes 196
  0.6 10.3 %copy-start.20 = (s32[1,16]{1,0:T(1,128)S(1)}, s32[1,16]{1,0:T(1,128)}, u32[]{:S(2)}) copy-start(s32[1,16]{1,0:T(1,128)} %param.23) | copy-start | bytes 196
  0.7 10.4 %copy-start.7 = (s32[64,1024]{1,0:T(8,128)S(1)}, s32[64,1024]{1,0:T(8,128)}, u32[]{:S(2)}) copy-start(s32[64,1024]{1,0:T(8,128)} %param.16) | copy-start | bytes 786436
  0.7 10.5 %copy-start.4 = (f32[64,1024]{1,0:T(8,128)S(1)}, f32[64,1024]{1,0:T(8,128)}, u32[]{:S(2)}) copy-start(f32[64,1024]{1,0:T(8,128)} %param.14) | copy-start | bytes 786436
  3.2 32.7 %collective-permute-start = (f32[5,48,3,128]{3,1,2,0:T(8,128)}, f32[5,48,3,128]{3,1,2,0:T(8,128)}, u32[]{:S(2)}, u32[]{:S(2)}) collective-permute-start(f32[5,48,3,128]{3,1,2,0:T(8,128)} %copy.102), channel_id=1, source_target_pairs={{8,0},{16,8},{24,16},{32,24},{40,32},{48,40},{56,48},{64,56},{72,6... | collective-permute-start | bytes 1105928 | tf_op jit(solution)/shard_map/ppermute | solution.py:27
  8.2 30.2 %collective-permute-start.1 = (f32[5,48,3,128]{3,1,2,0:T(8,128)}, f32[5,48,3,128]{3,1,2,0:T(8,128)}, u32[]{:S(2)}, u32[]{:S(2)}) collective-permute-start(f32[5,48,3,128]{3,1,2,0:T(8,128)} %copy.103), channel_id=1, source_target_pairs={{0,8},{8,16},{16,24},{24,32},{32,40},{40,48},{48,56},{56,64},{64,7... | collective-permute-start | bytes 1105928 | tf_op jit(solution)/shard_map/ppermute | solution.py:25
  11.9 14.1 %collective-permute-start.4 = (f32[3,16,1024]{2,1,0:T(8,128)}, f32[3,16,1024]{2,1,0:T(8,128)}, u32[]{:S(2)}, u32[]{:S(2)}) collective-permute-start(f32[3,16,1024]{2,1,0:T(8,128)} %get-tuple-element.46), channel_id=1, source_target_pairs={{0,8},{8,16},{16,24},{24,32},{32,40},{40,48},{48,56},{56,64},{64,7... | collective-permute-start | bytes 589832 | tf_op jit(solution)/shard_map/ppermute | solution.py:25
  13.8 12.2 %collective-permute-start.5 = (f32[3,16,1024]{2,1,0:T(8,128)}, f32[3,16,1024]{2,1,0:T(8,128)}, u32[]{:S(2)}, u32[]{:S(2)}) collective-permute-start(f32[3,16,1024]{2,1,0:T(8,128)} %get-tuple-element.47), channel_id=1, source_target_pairs={{8,0},{16,8},{24,16},{32,24},{40,32},{48,40},{56,48},{64,56},{72,6... | collective-permute-start | bytes 589832 | tf_op jit(solution)/shard_map/ppermute | solution.py:27
  27.2 1.0 %copy-start.2 = (f32[3,96,1024]{2,1,0:T(8,128)}, f32[3,96,1024]{2,1,0:T(8,128)S(1)}, u32[]{:S(2)}) copy-start(f32[3,96,1024]{2,1,0:T(8,128)S(1)} %pad_maximum_fusion.7) | copy-start | bytes 3538948
  28.9 22.7 %collective-permute-start.6 = (f32[3,96,16]{2,1,0:T(8,128)}, f32[3,96,16]{2,1,0:T(8,128)}, u32[]{:S(2)}, u32[]{:S(2)}) collective-permute-start(f32[3,96,16]{2,1,0:T(8,128)} %get-tuple-element.41), channel_id=1, source_target_pairs={{0,1},{1,2},{2,3},{3,4},{4,5},{5,6},{6,7},{8,9},{9,10},{10,11},{11... | collective-permute-start | bytes 55304 | tf_op jit(solution)/shard_map/ppermute | solution.py:25
  34.0 17.7 %collective-permute-start.7 = (f32[3,96,16]{2,1,0:T(8,128)}, f32[3,96,16]{2,1,0:T(8,128)}, u32[]{:S(2)}, u32[]{:S(2)}) collective-permute-start(f32[3,96,16]{2,1,0:T(8,128)} %get-tuple-element.40), channel_id=1, source_target_pairs={{1,0},{2,1},{3,2},{4,3},{5,4},{6,5},{7,6},{9,8},{10,9},{11,10},{12... | collective-permute-start | bytes 55304 | tf_op jit(solution)/shard_map/ppermute | solution.py:27
  40.9 8.8 %copy-start.15 = (f32[13]{0:T(128)S(1)}, f32[13]{0:T(128)}, u32[]{:S(2)}) copy-start(f32[13]{0:T(128)} %param.20) | copy-start | bytes 160
  40.9 8.8 %copy-start.16 = (f32[13]{0:T(128)S(1)}, f32[13]{0:T(128)}, u32[]{:S(2)}) copy-start(f32[13]{0:T(128)} %param.19) | copy-start | bytes 160
  40.9 8.8 %copy-start.17 = (f32[13]{0:T(128)S(1)}, f32[13]{0:T(128)}, u32[]{:S(2)}) copy-start(f32[13]{0:T(128)} %param.18) | copy-start | bytes 160
  40.9 8.8 %copy-start.18 = (f32[13]{0:T(128)S(1)}, f32[13]{0:T(128)}, u32[]{:S(2)}) copy-start(f32[13]{0:T(128)} %param.17) | copy-start | bytes 160
  40.9 9.4 %copy-start.6 = (f32[48,8,128]{2,1,0:T(8,128)S(1)}, f32[48,8,128]{2,1,0:T(8,128)}, u32[]{:S(2)}) copy-start(f32[48,8,128]{2,1,0:T(8,128)} %get-tuple-element.42) | copy-start | bytes 589828
  40.9 9.7 %copy-start.5 = (f32[48,8,128]{2,1,0:T(8,128)S(1)}, f32[48,8,128]{2,1,0:T(8,128)}, u32[]{:S(2)}) copy-start(f32[48,8,128]{2,1,0:T(8,128)} %get-tuple-element.43) | copy-start | bytes 589828
  42.6 11.4 %collective-permute-start.2 = (f32[5,48,14,3]{1,2,3,0:T(8,128)}, f32[5,48,14,3]{1,2,3,0:T(8,128)}, u32[]{:S(2)}, u32[]{:S(2)}) collective-permute-start(f32[5,48,14,3]{1,2,3,0:T(8,128)} %get-tuple-element.38), channel_id=1, source_target_pairs={{1,0},{2,1},{3,2},{4,3},{5,4},{6,5},{7,6},{9,8},{10,9},{11,10},{12... | collective-permute-start | bytes 120968 | tf_op jit(solution)/shard_map/ppermute | solution.py:27
  44.5 9.5 %collective-permute-start.3 = (f32[5,48,14,3]{1,2,3,0:T(8,128)}, f32[5,48,14,3]{1,2,3,0:T(8,128)}, u32[]{:S(2)}, u32[]{:S(2)}) collective-permute-start(f32[5,48,14,3]{1,2,3,0:T(8,128)} %get-tuple-element.39), channel_id=1, source_target_pairs={{0,1},{1,2},{2,3},{3,4},{4,5},{5,6},{6,7},{8,9},{9,10},{10,11},{11... | collective-permute-start | bytes 120968 | tf_op jit(solution)/shard_map/ppermute | solution.py:25
  54.0 5.9 %copy-start.11 = (f32[96]{0:T(128)S(1)}, f32[96]{0:T(128)}, u32[]{:S(2)}) copy-start(f32[96]{0:T(128)} %get-tuple-element.48) | copy-start | bytes 1156
  54.0 5.9 %copy-start.12 = (f32[96]{0:T(128)S(1)}, f32[96]{0:T(128)}, u32[]{:S(2)}) copy-start(f32[96]{0:T(128)} %get-tuple-element.49) | copy-start | bytes 1156
  54.0 5.9 %copy-start.13 = (s32[96]{0:T(128)S(1)}, s32[96]{0:T(128)}, u32[]{:S(2)}) copy-start(s32[96]{0:T(128)} %get-tuple-element.50) | copy-start | bytes 1156
  54.0 5.9 %copy-start.14 = (s32[96]{0:T(128)S(1)}, s32[96]{0:T(128)}, u32[]{:S(2)}) copy-start(s32[96]{0:T(128)} %get-tuple-element.51) | copy-start | bytes 1156
  54.0 6.3 %copy-start.8 = (s32[1280]{0:T(1024)S(1)}, s32[1280]{0:T(1024)}, u32[]{:S(2)}) copy-start(s32[1280]{0:T(1024)} %get-tuple-element.54) | copy-start | bytes 15364
  54.0 6.3 %copy-start.9 = (s32[1280]{0:T(1024)S(1)}, s32[1280]{0:T(1024)}, u32[]{:S(2)}) copy-start(s32[1280]{0:T(1024)} %get-tuple-element.55) | copy-start | bytes 15364
  75.3 7.3 %copy-start = (f32[5,48,3,128]{1,2,3,0:T(4,128)S(1)}, f32[5,48,3,128]{1,2,3,0:T(4,128)}, u32[]{:S(2)}) copy-start(f32[5,48,3,128]{1,2,3,0:T(4,128)} %copy.87) | copy-start | bytes 1105924
  75.3 7.3 %copy-start.1 = (f32[5,48,3,128]{1,2,3,0:T(4,128)S(1)}, f32[5,48,3,128]{1,2,3,0:T(4,128)}, u32[]{:S(2)}) copy-start(f32[5,48,3,128]{1,2,3,0:T(4,128)} %copy.89) | copy-start | bytes 1105924
  75.3 7.3 %copy-start.3 = (f32[48,8,128]{0,1,2:T(8,128)S(1)}, f32[48,8,128]{0,1,2:T(8,128)}, u32[]{:S(2)}) copy-start(f32[48,8,128]{0,1,2:T(8,128)} %copy.95) | copy-start | bytes 589828
  82.6 10.9 %copy-start.10 = (f32[48]{0:T(128)S(1)}, f32[48]{0:T(128)}, u32[]{:S(2)}) copy-start(f32[48]{0:T(128)} %multiply_exponential_fusion) | copy-start | bytes 580

commit v6 on v4

--- a/solution.py
+++ b/solution.py
@@ -234,7 +234,9 @@
 
     def at(ref, dx, dy):
         band = ref[0, :, 3 + dx : 3 + dx + rows, :]
-        return pltpu.roll(band, (width - 3 - dy) % width, 2)[:, :, :cols]
+        if dy == 0:
+            return band[:, :, :cols]
+        return pltpu.roll(band, (width - dy) % width, 2)[:, :, :cols]
 
     centre = at(q_ref, 0, 0)
     deriv_x = (
@@ -301,10 +303,14 @@
 ):
     fire_rows, fire_cols = level_set.shape
     atmos_rows, atmos_cols = (atmos.shape[2], atmos.shape[3])
-    padded_atm = extended(atmos, (("gx", 2), ("gy", 3)), 3)
-    surface = padded_atm[0:2, 0]
-    lanes = -(-padded_atm.shape[3] // 128) * 128
-    padded_atm = jnp.pad(padded_atm, ((0, 0), (0, 0), (0, 0), (0, lanes - padded_atm.shape[3])))
+    along_x = extended(atmos, (("gx", 2),), 3)
+    count = lax.axis_size("gy")
+    from_lo = lax.ppermute(along_x[..., -3:], "gy", [(i, i + 1) for i in range(count - 1)])
+    from_hi = lax.ppermute(along_x[..., :3], "gy", [(i + 1, i) for i in range(count - 1)])
+    lanes = 2 * (-(-atmos_cols // 128) * 128)
+    room = jnp.zeros(along_x.shape[:3] + (lanes - atmos_cols - 6,), jnp.float32)
+    padded_atm = jnp.concatenate([along_x, from_hi, room, from_lo], axis=3)
+    surface = jnp.concatenate([from_lo[0:2, 0], along_x[0:2, 0], from_hi[0:2, 0]], axis=2)
     slots = burn_tiles.reshape(-1)
     listed = burn_count.reshape(())
     tiles_dev = substep_count.size

time: 86.5 us -> 95.4 us (1.10)
  waiting for transfers between devices: 1.53 us -> 16.2 us
  Pallas kernels: 22.9 us -> 19.5 us
  other arithmetic: 10.2 us -> 7.79 us
  starting transfers between devices: 29.3 us -> 27 us
  local copies, waits for them, and re-layouts: 18 us -> 19.4 us
    slice x0 -> x7, local copies, waits for them, and re-layouts: none -> 7.47 us  [the longest x2 3.44 us: shards(): along_x[..., :3]]
    ppermute x0 -> x2, starting transfers between devices: none -> 6 us  [the longest x1 4.09 us: shards(): lax.ppermute(along_x[..., :3], 'gy', [(i + 1, i) for i in range(count - 1)])]
    ppermute x4 -> x3, waiting for transfers between devices: 0.01 us -> 5.95 us  [extended(): lax.ppermute(tail, axis, [(i, (i + 1) % count) for i in range(ends)])]
    ppermute x4 -> x3, waiting for transfers between devices: 1.52 us -> 6.85 us  [extended(): lax.ppermute(head, axis, [((i + 1) % count, i) for i in range(ends)])]
    ppermute x4 -> x3, starting transfers between devices: 14 us -> 9.01 us  [extended(): lax.ppermute(tail, axis, [(i, (i + 1) % count) for i in range(ends)])]
    concatenate x0 -> x1, other arithmetic: none -> 4.4 us  [shards(): padded_atm = jnp.concatenate([along_x, from_hi, room, from_lo], axis=3)]
    concatenate x3 -> x2, other arithmetic: 4.7 us -> 0.42 us  [extended(): jnp.concatenate([lax.ppermute(tail, axis, [(i, (i + 1) % count) for i in...]
    ppermute x0 -> x2, waiting for transfers between devices: none -> 3.4 us  [the longest x1 3.39 us: shards(): lax.ppermute(along_x[..., :3], 'gy', [(i + 1, i) for i in range(count - 1)])]
  transfers between devices with their start and end apart: 8 -> 8, of which waited for: 1 -> 4; matrix products, arithmetic and copies ran while one was open for 15% -> 6% of each run, Pallas kernels for 0% -> 0%
where the time goes in v6:
time: 95.4 us; the launch traced here: 93.9 us
  starting transfers between devices  27 us (28%)
  Pallas kernels  19.5 us (20%)
  local copies, waits for them, and re-layouts  19.4 us (20%)
  waiting for transfers between devices  16.2 us (17%)
  other arithmetic  7.79 us (8%)
  matrix products  2.51 us (3%)
  between operations  1.57 us (2%)
    ppermute x3, starting transfers between devices, extended(): lax.ppermute(head, axis, [((i + 1) % count, i) for i in range(ends)])  11.9 us
    pallas_call x1, Pallas kernels, fire_step(): pl.pallas_call(fire_kernel, out_shape=(jax.ShapeDtypeStruct((rows, cols),...  11.9 us
    ppermute x3, starting transfers between devices, extended(): lax.ppermute(tail, axis, [(i, (i + 1) % count) for i in range(ends)])  9.01 us
    pallas_call x1, Pallas kernels, atmos_call(): pl.pallas_call(atmos_kernel, grid=(fields,), out_shape=jax.ShapeDtypeStru...  7.68 us
    ppermute x3, waiting for transfers between devices, extended(): lax.ppermute(head, axis, [((i + 1) % count, i) for i in range(ends)])  6.85 us
    ppermute x3, waiting for transfers between devices, extended(): lax.ppermute(tail, axis, [(i, (i + 1) % count) for i in range(ends)])  5.95 us
    concatenate x1, other arithmetic, shards(): padded_atm = jnp.concatenate([along_x, from_hi, room, from_lo], axis=3)  4.4 us
    ppermute x1, starting transfers between devices, shards(): lax.ppermute(along_x[..., :3], 'gy', [(i + 1, i) for i in range(count - 1)])  4.09 us
  transfers between devices with their start and end apart: 8, of which 4 were waited for; matrix products, arithmetic and copies ran while one was open for 6% of the time, Pallas kernels for 0%

profile of v6, /device:TPU:120, one launch (start us, length us, event | category | flops | bytes accessed | tf_op | source)
XLA Modules:
  0.0 93.9 jit_solution(4400798067898049969)
XLA Ops:
  0.7 2.7 %fusion.39 = (f32[5,48,3,128]{3,2,1,0:T(4,128)}, f32[5,48,3,128]{3,2,1,0:T(4,128)}) fusion(f32[5,48,8,128]{3,2,1,0:T(8,128)} %param.11), kind=kLoop, calls=%fused_computation.82 | loop fusion | bytes 1474560 | tf_op jit(solution)/shard_map/slice | solution.py:22
  3.4 4.3 %collective-permute-start.1 = (f32[5,48,3,128]{3,2,1,0:T(4,128)}, f32[5,48,3,128]{3,2,1,0:T(4,128)S(1)}, u32[]{:S(2)}, u32[]{:S(2)}) collective-permute-start(f32[5,48,3,128]{3,2,1,0:T(4,128)} %get-tuple-element.14), channel_id=1, source_target_pairs={{8,0},{16,8},{24,16},{32,24},{40,32},{48,40},{56,48},{64,56},{72,6... | collective-permute-start | bytes 1105928 | tf_op jit(solution)/shard_map/ppermute | solution.py:27
  7.6 1.9 %collective-permute-start = (f32[5,48,3,128]{3,2,1,0:T(4,128)}, f32[5,48,3,128]{3,2,1,0:T(4,128)S(1)}, u32[]{:S(2)}, u32[]{:S(2)}) collective-permute-start(f32[5,48,3,128]{3,2,1,0:T(4,128)} %get-tuple-element.13), channel_id=1, source_target_pairs={{0,8},{8,16},{16,24},{24,32},{32,40},{40,48},{48,56},{56,64},{64,7... | collective-permute-start | bytes 1105928 | tf_op jit(solution)/shard_map/ppermute | solution.py:25
  10.2 0.1 fusion.25
  10.3 0.1 broadcast_in_dim.54
  10.4 0.1 broadcast_in_dim.55
  10.6 0.0 copy-start.5
  10.6 0.0 copy-start.6
  10.6 0.0 copy-start.7
  10.6 0.0 copy-start.8
  10.6 5.8 %collective-permute-start.5 = (f32[3,16,1024]{2,1,0:T(8,128)S(1)}, f32[3,16,1024]{2,1,0:T(8,128)S(1)}, u32[]{:S(2)}, u32[]{:S(2)}) collective-permute-start(f32[3,16,1024]{2,1,0:T(8,128)S(1)} %get-tuple-element.16), channel_id=1, source_target_pairs={{8,0},{16,8},{24,16},{32,24},{40,32},{48,40},{56,48},{64,56},{72,6... | collective-permute-start | bytes 589832 | tf_op jit(solution)/shard_map/ppermute | solution.py:27
  16.4 1.9 %collective-permute-start.4 = (f32[3,16,1024]{2,1,0:T(8,128)S(1)}, f32[3,16,1024]{2,1,0:T(8,128)S(1)}, u32[]{:S(2)}, u32[]{:S(2)}) collective-permute-start(f32[3,16,1024]{2,1,0:T(8,128)S(1)} %get-tuple-element.15), channel_id=1, source_target_pairs={{0,8},{8,16},{16,24},{24,32},{32,40},{40,48},{48,56},{56,64},{64,7... | collective-permute-start | bytes 589832 | tf_op jit(solution)/shard_map/ppermute | solution.py:25
  18.4 1.2 %collective-permute-done.5 = f32[3,16,1024]{2,1,0:T(8,128)S(1)} collective-permute-done((f32[3,16,1024]{2,1,0:T(8,128)S(1)}, f32[3,16,1024]{2,1,0:T(8,128)S(1)}, u32[]{:S(2)}, u32[]{:S(2)}) %collective-permute-start.5) | collective-permute-done | bytes 196640 | tf_op jit(solution)/shard_map/ppermute | solution.py:27
  19.6 5.9 %collective-permute-done.4 = f32[3,16,1024]{2,1,0:T(8,128)S(1)} collective-permute-done((f32[3,16,1024]{2,1,0:T(8,128)S(1)}, f32[3,16,1024]{2,1,0:T(8,128)S(1)}, u32[]{:S(2)}, u32[]{:S(2)}) %collective-permute-start.4) | collective-permute-done | bytes 196640 | tf_op jit(solution)/shard_map/ppermute | solution.py:25
  25.5 0.1 pad_maximum_fusion.2
  25.6 0.0 copy-start
  25.6 0.1 fusion.38
  25.7 5.2 %collective-permute-start.6 = (f32[3,96,16]{2,1,0:T(8,128)S(1)}, f32[3,96,16]{2,1,0:T(8,128)S(1)}, u32[]{:S(2)}, u32[]{:S(2)}) collective-permute-start(f32[3,96,16]{2,1,0:T(8,128)S(1)} %get-tuple-element.12), channel_id=1, source_target_pairs={{0,1},{1,2},{2,3},{3,4},{4,5},{5,6},{6,7},{8,9},{9,10},{10,11},{11... | collective-permute-start | bytes 55304 | tf_op jit(solution)/shard_map/ppermute | solution.py:25
  30.9 1.9 %collective-permute-start.7 = (f32[3,96,16]{2,1,0:T(8,128)S(1)}, f32[3,96,16]{2,1,0:T(8,128)}, u32[]{:S(2)}, u32[]{:S(2)}) collective-permute-start(f32[3,96,16]{2,1,0:T(8,128)S(1)} %get-tuple-element.11), channel_id=1, source_target_pairs={{1,0},{2,1},{3,2},{4,3},{5,4},{6,5},{7,6},{9,8},{10,9},{11,10},{12... | collective-permute-start | bytes 55304 | tf_op jit(solution)/shard_map/ppermute | solution.py:27
  32.8 0.6 pad_maximum_fusion.6.tab_ref
  33.4 0.1 pad.19.clone
  33.5 0.0 collective-permute-done.6
  33.5 5.7 %collective-permute-done.7 = f32[3,96,16]{2,1,0:T(8,128)} collective-permute-done((f32[3,96,16]{2,1,0:T(8,128)S(1)}, f32[3,96,16]{2,1,0:T(8,128)}, u32[]{:S(2)}, u32[]{:S(2)}) %collective-permute-start.7) | collective-permute-done | bytes 18464 | tf_op jit(solution)/shard_map/ppermute | solution.py:27
  39.2 2.2 %concatenate.22.ext_ref = f32[3,96,1280]{2,1,0:T(8,128)} concatenate(f32[3,96,112]{2,1,0:T(8,128)S(1)} %broadcast_in_dim.29, f32[3,96,16]{2,1,0:T(8,128)S(1)} %collective-permute-done.6, f32[3,96,1024]{2,1,0:T(8,128)S(1)} %pad_maximum_fusion.2, f32[3,96,16]{2,1,0:T(8,128)} %collective-permute-done.7, f32[3,96,112]{2,1,0:T(8,128)S(1)} %broadcast_in_dim.29), dimensions={2} | concatenate | bytes 2949120 | tf_op jit(solution)/shard_map/concatenate | solution.py:331
  41.4 0.0 collective-permute-done.1
  41.4 0.8 copy-done.1
  42.2 0.3 pad_maximum_fusion.1
  42.6 2.0 %fusion.37 = (f32[5,48,14,3]{3,2,1,0:T(8,128)S(1)}, f32[5,48,14,3]{3,2,1,0:T(8,128)}) fusion(f32[5,48,14,128]{3,2,1,0:T(8,128)S(1)} %pad_maximum_fusion.1), kind=kLoop, calls=%fused_computation.80 | loop fusion | bytes 161280 | tf_op jit(solution)/shard_map/slice | solution.py:309
  44.5 3.0 %copy.27 = f32[5,48,14,3]{1,2,3,0:T(8,128)} copy(f32[5,48,14,3]{3,2,1,0:T(8,128)} %get-tuple-element.10) | data formatting | bytes 80640 | tf_op jit(solution)/shard_map/slice | solution.py:308
  47.5 1.9 %collective-permute-start.3 = (f32[5,48,14,3]{1,2,3,0:T(8,128)}, f32[5,48,14,3]{1,2,3,0:T(8,128)}, u32[]{:S(2)}, u32[]{:S(2)}) collective-permute-start(f32[5,48,14,3]{1,2,3,0:T(8,128)} %copy.27), channel_id=1, source_target_pairs={{0,1},{1,2},{2,3},{3,4},{4,5},{5,6},{6,7},{8,9},{9,10},{10,11},{11... | collective-permute-start | bytes 120968 | tf_op jit(solution)/shard_map/ppermute | solution.py:308
  49.4 1.5 %copy.26 = f32[5,48,14,3]{1,2,3,0:T(8,128)} copy(f32[5,48,14,3]{3,2,1,0:T(8,128)S(1)} %get-tuple-element.9) | data formatting | bytes 80640 | tf_op jit(solution)/shard_map/slice | solution.py:309
  50.9 4.1 %collective-permute-start.2 = (f32[5,48,14,3]{1,2,3,0:T(8,128)}, f32[5,48,14,3]{1,2,3,0:T(8,128)S(1)}, u32[]{:S(2)}, u32[]{:S(2)}) collective-permute-start(f32[5,48,14,3]{1,2,3,0:T(8,128)} %copy.26), channel_id=1, source_target_pairs={{1,0},{2,1},{3,2},{4,3},{5,4},{6,5},{7,6},{9,8},{10,9},{11,10},{12... | collective-permute-start | bytes 120968 | tf_op jit(solution)/shard_map/ppermute | solution.py:309
  55.0 0.7 maximum_bitcast_fusion
  55.7 3.4 %collective-permute-done.2 = f32[5,48,14,3]{1,2,3,0:T(8,128)S(1)} collective-permute-done((f32[5,48,14,3]{1,2,3,0:T(8,128)}, f32[5,48,14,3]{1,2,3,0:T(8,128)S(1)}, u32[]{:S(2)}, u32[]{:S(2)}) %collective-permute-start.2) | collective-permute-done | bytes 40352 | tf_op jit(solution)/shard_map/ppermute | solution.py:309
  59.1 0.6 copy-done.4
  59.7 0.1 copy.31
  59.9 0.1 copy.33
  60.0 0.8 slice.48
  60.8 0.1 copy.30
  60.9 0.1 copy.32
  61.0 0.5 convolution_bitcast_fusion
  61.5 2.0 %fusion.wind_ref = f32[2,96,1280]{2,1,0:T(8,128)} fusion(f32[2,96,134]{1,2,0:T(8,128)S(1)} %convolution_bitcast_fusion, f32[1280]{0:T(1024)S(1)} %get-tuple-element.21, s32[1280]{0:T(1024)S(1)} %get-tuple-element.24, f32[1280]{0:T(1024)S(1)} %get-tuple-element.22, s32[1280]{0:T(1024)S(1)} %get-tuple-element.23), kind=kOutput, calls=%fused_computation.6 | convolution fusion | flops 396039680 | bytes 1106432 | tf_op jit(solution)/shard_map/kib,jb->kij/dot_general | solution.py:145
  63.5 11.9 %shard_map.130 = (f32[64,1024]{1,0:T(8,128)}, f32[64,1024]{1,0:T(8,128)}, f32[8,128]{1,0:T(8,128)}) custom-call(f32[52]{0:T(128)} %pad_maximum_fusion.6.tab_ref, f32[3,96,1280]{2,1,0:T(8,128)} %concatenate.22.ext_ref, f32[2,96,1280]{2,1,0:T(8,128)} %fusion.wind_ref, f32[64,1024]{1,0:T(8,128)} %fuel_ref.1), custom_call_target="tpu_custom_call" | custom-call | tf_op jit(solution)/shard_map/pallas_call | solution.py:219
  75.4 1.5 %broadcast_multiply_fusion.h_ref = f32[48,8,128]{2,1,0:T(8,128)} fusion(f32[48]{0:T(128)S(1)} %multiply_exponential_fusion, f32[8,128]{1,0:T(8,128)} %get-tuple-element.6), kind=kLoop, calls=%fused_computation.20 | loop fusion | flops 49152 | bytes 200896 | tf_op jit(solution)/shard_map/mul | solution.py:271
  76.9 2.0 %copy.29 = f32[5,48,14,3]{3,2,1,0:T(8,128)S(1)} copy(f32[5,48,14,3]{1,2,3,0:T(8,128)} %collective-permute-done.3) | data formatting | bytes 80640 | tf_op jit(solution)/shard_map/ppermute | solution.py:308
  78.9 3.0 %copy.28 = f32[5,48,14,3]{3,2,1,0:T(8,128)} copy(f32[5,48,14,3]{1,2,3,0:T(8,128)} %copy-done.4) | data formatting | bytes 80640 | tf_op jit(solution)/shard_map/ppermute | solution.py:309
  81.9 4.4 %pad_maximum_fusion.q_ref.u_ref.v_ref = f32[5,48,14,256]{3,2,1,0:T(8,128)} fusion(f32[5,48,14,3]{3,2,1,0:T(8,128)S(1)} %copy.29, f32[5,48,14,3]{3,2,1,0:T(8,128)} %copy.28, f32[5,48,3,128]{3,2,1,0:T(4,128)S(1)} %collective-permute-done.1, f32[5,48,8,128]{3,2,1,0:T(8,128)S(1)} %copy-done, f32[5,48,3,128]{3,2,1,0:T(4,128)} %copy-done.1, f32[256]{0:T(256)S(1)} %pad.19.clone), kind=kLoop, calls=%fused_computation | loop fusion | flops 4300800 | bytes 5242624 | tf_op jit(solution)/shard_map/concatenate | solution.py:312
  86.3 7.7 %shard_map.131 = f32[5,48,8,128]{3,2,1,0:T(8,128)} custom-call(f32[5,48,14,256]{3,2,1,0:T(8,128)} %pad_maximum_fusion.q_ref.u_ref.v_ref, f32[5,48,14,256]{3,2,1,0:T(8,128)} %pad_maximum_fusion.q_ref.u_ref.v_ref, f32[5,48,14,256]{3,2,1,0:T(8,128)} %pad_maximum_fusion.q_ref.u_ref.v_ref, f32[48,8,128]{2,1,0:T(8,128)} %broadcast_multiply_fusion.h_ref), custom_call_target="tpu_custom_call" | custom-call | tf_op jit(solution)/shard_map/pallas_call | solution.py:273
  (30 shorter events, 0.2 us)
Async XLA Ops:
  0.6 9.6 %copy-start.9 = (s32[1,1,16]{2,1,0:T(1,128)S(1)}, s32[1,1,16]{2,1,0:T(1,128)}, u32[]{:S(2)}) copy-start(s32[1,1,16]{2,1,0:T(1,128)} %param.19) | copy-start | bytes 196
  0.6 9.7 %copy-start.10 = (s32[1,16]{1,0:T(1,128)S(1)}, s32[1,16]{1,0:T(1,128)}, u32[]{:S(2)}) copy-start(s32[1,16]{1,0:T(1,128)} %param.21) | copy-start | bytes 196
  0.7 9.8 %copy-start.3 = (s32[64,1024]{1,0:T(8,128)S(1)}, s32[64,1024]{1,0:T(8,128)}, u32[]{:S(2)}) copy-start(s32[64,1024]{1,0:T(8,128)} %param.14) | copy-start | bytes 786436
  0.7 9.9 %copy-start.2 = (f32[64,1024]{1,0:T(8,128)S(1)}, f32[64,1024]{1,0:T(8,128)}, u32[]{:S(2)}) copy-start(f32[64,1024]{1,0:T(8,128)} %param.12) | copy-start | bytes 786436
  3.4 38.1 %collective-permute-start.1 = (f32[5,48,3,128]{3,2,1,0:T(4,128)}, f32[5,48,3,128]{3,2,1,0:T(4,128)S(1)}, u32[]{:S(2)}, u32[]{:S(2)}) collective-permute-start(f32[5,48,3,128]{3,2,1,0:T(4,128)} %get-tuple-element.14), channel_id=1, source_target_pairs={{8,0},{16,8},{24,16},{32,24},{40,32},{48,40},{56,48},{64,56},{72,6... | collective-permute-start | bytes 1105928 | tf_op jit(solution)/shard_map/ppermute | solution.py:27
  7.6 33.8 %collective-permute-start = (f32[5,48,3,128]{3,2,1,0:T(4,128)}, f32[5,48,3,128]{3,2,1,0:T(4,128)S(1)}, u32[]{:S(2)}, u32[]{:S(2)}) collective-permute-start(f32[5,48,3,128]{3,2,1,0:T(4,128)} %get-tuple-element.13), channel_id=1, source_target_pairs={{0,8},{8,16},{16,24},{24,32},{32,40},{40,48},{48,56},{56,64},{64,7... | collective-permute-start | bytes 1105928 | tf_op jit(solution)/shard_map/ppermute | solution.py:25
  10.6 22.2 %copy-start.5 = (f32[13]{0:T(128)S(1)}, f32[13]{0:T(128)}, u32[]{:S(2)}) copy-start(f32[13]{0:T(128)} %param.18) | copy-start | bytes 160
  10.6 22.2 %copy-start.6 = (f32[13]{0:T(128)S(1)}, f32[13]{0:T(128)}, u32[]{:S(2)}) copy-start(f32[13]{0:T(128)} %param.17) | copy-start | bytes 160
  10.6 22.2 %copy-start.7 = (f32[13]{0:T(128)S(1)}, f32[13]{0:T(128)}, u32[]{:S(2)}) copy-start(f32[13]{0:T(128)} %param.16) | copy-start | bytes 160
  10.6 22.2 %copy-start.8 = (f32[13]{0:T(128)S(1)}, f32[13]{0:T(128)}, u32[]{:S(2)}) copy-start(f32[13]{0:T(128)} %param.15) | copy-start | bytes 160
  10.6 8.9 %collective-permute-start.5 = (f32[3,16,1024]{2,1,0:T(8,128)S(1)}, f32[3,16,1024]{2,1,0:T(8,128)S(1)}, u32[]{:S(2)}, u32[]{:S(2)}) collective-permute-start(f32[3,16,1024]{2,1,0:T(8,128)S(1)} %get-tuple-element.16), channel_id=1, source_target_pairs={{8,0},{16,8},{24,16},{32,24},{40,32},{48,40},{56,48},{64,56},{72,6... | collective-permute-start | bytes 589832 | tf_op jit(solution)/shard_map/ppermute | solution.py:27
  16.4 9.1 %collective-permute-start.4 = (f32[3,16,1024]{2,1,0:T(8,128)S(1)}, f32[3,16,1024]{2,1,0:T(8,128)S(1)}, u32[]{:S(2)}, u32[]{:S(2)}) collective-permute-start(f32[3,16,1024]{2,1,0:T(8,128)S(1)} %get-tuple-element.15), channel_id=1, source_target_pairs={{0,8},{8,16},{16,24},{24,32},{32,40},{40,48},{48,56},{56,64},{64,7... | collective-permute-start | bytes 589832 | tf_op jit(solution)/shard_map/ppermute | solution.py:25
  25.6 16.6 %copy-start = (f32[5,48,8,128]{3,2,1,0:T(8,128)S(1)}, f32[5,48,8,128]{3,2,1,0:T(8,128)}, u32[]{:S(2)}) copy-start(f32[5,48,8,128]{3,2,1,0:T(8,128)} %param.11) | copy-start | bytes 2949124
  25.7 7.8 %collective-permute-start.6 = (f32[3,96,16]{2,1,0:T(8,128)S(1)}, f32[3,96,16]{2,1,0:T(8,128)S(1)}, u32[]{:S(2)}, u32[]{:S(2)}) collective-permute-start(f32[3,96,16]{2,1,0:T(8,128)S(1)} %get-tuple-element.12), channel_id=1, source_target_pairs={{0,1},{1,2},{2,3},{3,4},{4,5},{5,6},{6,7},{8,9},{9,10},{10,11},{11... | collective-permute-start | bytes 55304 | tf_op jit(solution)/shard_map/ppermute | solution.py:25
  30.9 8.4 %collective-permute-start.7 = (f32[3,96,16]{2,1,0:T(8,128)S(1)}, f32[3,96,16]{2,1,0:T(8,128)}, u32[]{:S(2)}, u32[]{:S(2)}) collective-permute-start(f32[3,96,16]{2,1,0:T(8,128)S(1)} %get-tuple-element.11), channel_id=1, source_target_pairs={{1,0},{2,1},{3,2},{4,3},{5,4},{6,5},{7,6},{9,8},{10,9},{11,10},{12... | collective-permute-start | bytes 55304 | tf_op jit(solution)/shard_map/ppermute | solution.py:27
  41.4 0.8 copy-start.1
  47.5 12.5 %collective-permute-start.3 = (f32[5,48,14,3]{1,2,3,0:T(8,128)}, f32[5,48,14,3]{1,2,3,0:T(8,128)}, u32[]{:S(2)}, u32[]{:S(2)}) collective-permute-start(f32[5,48,14,3]{1,2,3,0:T(8,128)} %copy.27), channel_id=1, source_target_pairs={{0,1},{1,2},{2,3},{3,4},{4,5},{5,6},{6,7},{8,9},{9,10},{10,11},{11... | collective-permute-start | bytes 120968 | tf_op jit(solution)/shard_map/ppermute | solution.py:308
  50.9 8.2 %collective-permute-start.2 = (f32[5,48,14,3]{1,2,3,0:T(8,128)}, f32[5,48,14,3]{1,2,3,0:T(8,128)S(1)}, u32[]{:S(2)}, u32[]{:S(2)}) collective-permute-start(f32[5,48,14,3]{1,2,3,0:T(8,128)} %copy.26), channel_id=1, source_target_pairs={{1,0},{2,1},{3,2},{4,3},{5,4},{6,5},{7,6},{9,8},{10,9},{11,10},{12... | collective-permute-start | bytes 120968 | tf_op jit(solution)/shard_map/ppermute | solution.py:309
  59.1 0.7 copy-start.4

commit v7 on v6

--- a/solution.py
+++ b/solution.py
@@ -305,12 +305,15 @@
     atmos_rows, atmos_cols = (atmos.shape[2], atmos.shape[3])
     along_x = extended(atmos, (("gx", 2),), 3)
     count = lax.axis_size("gy")
-    from_lo = lax.ppermute(along_x[..., -3:], "gy", [(i, i + 1) for i in range(count - 1)])
-    from_hi = lax.ppermute(along_x[..., :3], "gy", [(i + 1, i) for i in range(count - 1)])
+    from_lo = lax.ppermute(atmos[..., -3:], "gy", [(i, i + 1) for i in range(count - 1)])
+    from_hi = lax.ppermute(atmos[..., :3], "gy", [(i + 1, i) for i in range(count - 1)])
+    rows_pad = ((0, 0), (0, 0), (3, 3), (0, 0))
     lanes = 2 * (-(-atmos_cols // 128) * 128)
     room = jnp.zeros(along_x.shape[:3] + (lanes - atmos_cols - 6,), jnp.float32)
-    padded_atm = jnp.concatenate([along_x, from_hi, room, from_lo], axis=3)
-    surface = jnp.concatenate([from_lo[0:2, 0], along_x[0:2, 0], from_hi[0:2, 0]], axis=2)
+    padded_atm = jnp.concatenate(
+        [along_x, jnp.pad(from_hi, rows_pad), room, jnp.pad(from_lo, rows_pad)], axis=3
+    )
+    surface = extended(along_x[0:2, 0], (("gy", 2),), 3)
     slots = burn_tiles.reshape(-1)
     listed = burn_count.reshape(())
     tiles_dev = substep_count.size

time: 95.4 us -> 85.7 us (0.90)
  waiting for transfers between devices: 16.2 us -> 3.65 us
  local copies, waits for them, and re-layouts: 19.4 us -> 10.4 us
  other arithmetic: 7.79 us -> 14.1 us
  starting transfers between devices: 27 us -> 33 us
    slice x7 -> x1, local copies, waits for them, and re-layouts: 7.47 us -> 0.32 us  [shards(): atmos[..., :3]]
    ppermute x3 -> x4, waiting for transfers between devices: 5.95 us -> 0.01 us  [extended(): lax.ppermute(tail, axis, [(i, (i + 1) % count) for i in range(ends)])]
    ppermute x3 -> x4, waiting for transfers between devices: 6.85 us -> 1.3 us  [extended(): lax.ppermute(head, axis, [((i + 1) % count, i) for i in range(ends)])]
    ppermute x3 -> x4, starting transfers between devices: 11.9 us -> 15.5 us  [extended(): lax.ppermute(head, axis, [((i + 1) % count, i) for i in range(ends)])]
    slice x1, other arithmetic: 0.03 us -> 1.64 us  [extended(): lax.slice_in_dim(cells, cells.shape[dim] - width, cells.shape[dim], axis=...]
    ppermute x2, local copies, waits for them, and re-layouts: 4.98 us -> 3.41 us  [the longest x1 2.17 us: shards(): lax.ppermute(atmos[..., -3:], 'gy', [(i, i + 1) for i in range(count - 1)])]
    ppermute x3 -> x4, starting transfers between devices: 9.01 us -> 10.5 us  [extended(): lax.ppermute(tail, axis, [(i, (i + 1) % count) for i in range(ends)])]
    add x2, other arithmetic: 0.03 us -> 1.23 us  [interp_table(): (within.astype(jnp.float32) + 0.5) / ratio]
  transfers between devices with their start and end apart: 8 -> 10, of which waited for: 4 -> 2; matrix products, arithmetic and copies ran while one was open for 6% -> 21% of each run, Pallas kernels for 0% -> 0%
where the time goes in v7:
time: 85.7 us; the launch traced here: 84.8 us
  starting transfers between devices  33 us (39%)
  Pallas kernels  19.6 us (23%)
  other arithmetic  14.1 us (16%)
  local copies, waits for them, and re-layouts  10.4 us (12%)
  waiting for transfers between devices  3.65 us (4%)
  matrix products  2.51 us (3%)
  between operations  1.61 us (2%)
    ppermute x4, starting transfers between devices, extended(): lax.ppermute(head, axis, [((i + 1) % count, i) for i in range(ends)])  15.5 us
    pallas_call x1, Pallas kernels, fire_step(): pl.pallas_call(fire_kernel, out_shape=(jax.ShapeDtypeStruct((rows, cols),...  11.9 us
    ppermute x4, starting transfers between devices, extended(): lax.ppermute(tail, axis, [(i, (i + 1) % count) for i in range(ends)])  10.5 us
    pallas_call x1, Pallas kernels, atmos_call(): pl.pallas_call(atmos_kernel, grid=(fields,), out_shape=jax.ShapeDtypeStru...  7.69 us
    ppermute x1, starting transfers between devices, shards(): lax.ppermute(atmos[..., -3:], 'gy', [(i, i + 1) for i in range(count - 1)])  5.04 us
    concatenate x1, other arithmetic, shards(): jnp.concatenate([along_x, jnp.pad(from_hi, rows_pad), room, jnp.pad(from_...  3.62 us
    slice x2, local copies, waits for them, and re-layouts, extended(): lax.slice_in_dim(cells, cells.shape[dim] - width, cells.shape[dim], axis=...  2.74 us
    ppermute x1, waiting for transfers between devices, shards(): lax.ppermute(atmos[..., :3], 'gy', [(i + 1, i) for i in range(count - 1)])  2.34 us
  transfers between devices with their start and end apart: 10, of which 2 were waited for; matrix products, arithmetic and copies ran while one was open for 21% of the time, Pallas kernels for 0%

profile of v7, /device:TPU:120, one launch (start us, length us, event | category | flops | bytes accessed | tf_op | source)
XLA Modules:
  0.0 84.8 jit_solution(12250026944255902820)
XLA Ops:
  0.6 0.0 copy-start
  1.4 0.7 fusion.28
  2.1 0.7 fusion.36
  2.8 0.1 broadcast_in_dim.54
  2.9 0.1 broadcast_in_dim.55
  2.9 1.0 %convert_bitcast_fusion = f32[1,64,1024]{2,1,0:T(8,128)S(1)} fusion(s32[64,1024]{1,0:T(8,128)} %param.14), kind=kLoop, calls=%fused_computation.21 | loop fusion | flops 65536 | bytes 524288 | tf_op jit(solution)/shard_map/stack | solution.py:331
  3.9 1.6 %pad_maximum_fusion.3 = (f32[3,16,1024]{2,1,0:T(8,128)}, f32[3,16,1024]{2,1,0:T(8,128)}) fusion(f32[1,64,1024]{2,1,0:T(8,128)S(1)} %broadcast_in_dim.56, f32[1,64,1024]{2,1,0:T(8,128)S(1)} %convert_bitcast_fusion, f32[1,64,1024]{2,1,0:T(8,128)} %bitcast.25), kind=kLoop, calls=%fused_computation.24 | loop fusion | flops 196608 | bytes 1179648 | tf_op jit(solution)/shard_map/slice | solution.py:22
  5.6 1.9 %collective-permute-start.4 = (f32[3,16,1024]{2,1,0:T(8,128)}, f32[3,16,1024]{2,1,0:T(8,128)}, u32[]{:S(2)}, u32[]{:S(2)}) collective-permute-start(f32[3,16,1024]{2,1,0:T(8,128)} %get-tuple-element.15), channel_id=1, source_target_pairs={{0,8},{8,16},{16,24},{24,32},{32,40},{40,48},{48,56},{56,64},{64,7... | collective-permute-start | bytes 589832 | tf_op jit(solution)/shard_map/ppermute | solution.py:25
  7.5 5.8 %collective-permute-start.5 = (f32[3,16,1024]{2,1,0:T(8,128)}, f32[3,16,1024]{2,1,0:T(8,128)}, u32[]{:S(2)}, u32[]{:S(2)}) collective-permute-start(f32[3,16,1024]{2,1,0:T(8,128)} %get-tuple-element.16), channel_id=1, source_target_pairs={{8,0},{16,8},{24,16},{32,24},{40,32},{48,40},{56,48},{64,56},{72,6... | collective-permute-start | bytes 589832 | tf_op jit(solution)/shard_map/ppermute | solution.py:27
  13.3 2.7 %fusion.41 = (f32[5,48,3,128]{3,2,1,0:T(4,128)}, f32[5,48,3,128]{3,2,1,0:T(4,128)}) fusion(f32[5,48,8,128]{3,2,1,0:T(8,128)} %param.11), kind=kLoop, calls=%fused_computation.88 | loop fusion | bytes 1474560 | tf_op jit(solution)/shard_map/slice | solution.py:22
  15.9 1.9 %collective-permute-start = (f32[5,48,3,128]{3,2,1,0:T(4,128)}, f32[5,48,3,128]{3,2,1,0:T(4,128)}, u32[]{:S(2)}, u32[]{:S(2)}) collective-permute-start(f32[5,48,3,128]{3,2,1,0:T(4,128)} %get-tuple-element.11), channel_id=1, source_target_pairs={{0,8},{8,16},{16,24},{24,32},{32,40},{40,48},{48,56},{56,64},{64,7... | collective-permute-start | bytes 1105928 | tf_op jit(solution)/shard_map/ppermute | solution.py:25
  17.8 5.8 %collective-permute-start.1 = (f32[5,48,3,128]{3,2,1,0:T(4,128)}, f32[5,48,3,128]{3,2,1,0:T(4,128)}, u32[]{:S(2)}, u32[]{:S(2)}) collective-permute-start(f32[5,48,3,128]{3,2,1,0:T(4,128)} %get-tuple-element.12), channel_id=1, source_target_pairs={{8,0},{16,8},{24,16},{32,24},{40,32},{48,40},{56,48},{64,56},{72,6... | collective-permute-start | bytes 1105928 | tf_op jit(solution)/shard_map/ppermute | solution.py:27
  23.6 0.3 fusion.42
  23.9 0.4 copy.23
  24.3 5.0 %collective-permute-start.3 = (f32[5,48,8,3]{1,2,3,0:T(8,128)S(1)}, f32[5,48,8,3]{1,2,3,0:T(8,128)}, u32[]{:S(2)}, u32[]{:S(2)}) collective-permute-start(f32[5,48,8,3]{1,2,3,0:T(8,128)S(1)} %copy.23), channel_id=1, source_target_pairs={{0,1},{1,2},{2,3},{3,4},{4,5},{5,6},{6,7},{8,9},{9,10},{10,11},{11... | collective-permute-start | bytes 69128 | tf_op jit(solution)/shard_map/ppermute | solution.py:308
  29.4 0.5 broadcast_add_fusion.2
  29.9 0.6 fusion.34
  30.5 0.4 copy.22
  30.9 0.6 select_add_fusion
  31.6 0.0 collective-permute-done.4
  31.6 1.9 %collective-permute-start.2 = (f32[5,48,8,3]{1,2,3,0:T(8,128)S(1)}, f32[5,48,8,3]{1,2,3,0:T(8,128)}, u32[]{:S(2)}, u32[]{:S(2)}) collective-permute-start(f32[5,48,8,3]{1,2,3,0:T(8,128)S(1)} %copy.22), channel_id=1, source_target_pairs={{1,0},{2,1},{3,2},{4,3},{5,4},{6,5},{7,6},{9,8},{10,9},{11,10},{12... | collective-permute-start | bytes 69128 | tf_op jit(solution)/shard_map/ppermute | solution.py:309
  33.5 0.0 collective-permute-done.5
  33.5 1.2 %pad_maximum_fusion = f32[3,96,1024]{2,1,0:T(8,128)S(1)} fusion(f32[3,16,1024]{2,1,0:T(8,128)} %collective-permute-done.5, f32[1,64,1024]{2,1,0:T(8,128)S(1)} %broadcast_in_dim.56, f32[1,64,1024]{2,1,0:T(8,128)S(1)} %convert_bitcast_fusion, f32[1,64,1024]{2,1,0:T(8,128)} %bitcast.26, f32[3,16,1024]{2,1,0:T(8,128)} %collective-permute-done.4), kind=kLoop, calls=%fused_computation.7 | loop fusion | flops 1179648 | bytes 2359296 | tf_op jit(solution)/shard_map/concatenate | solution.py:23
  34.7 0.7 fusion.40
  35.4 1.9 %collective-permute-start.7 = (f32[3,96,16]{2,1,0:T(8,128)}, f32[3,96,16]{2,1,0:T(8,128)S(1)}, u32[]{:S(2)}, u32[]{:S(2)}) collective-permute-start(f32[3,96,16]{2,1,0:T(8,128)} %get-tuple-element.9), channel_id=1, source_target_pairs={{1,0},{2,1},{3,2},{4,3},{5,4},{6,5},{7,6},{9,8},{10,9},{11,10},{12... | collective-permute-start | bytes 55304 | tf_op jit(solution)/shard_map/ppermute | solution.py:27
  37.3 2.3 %collective-permute-done.2 = f32[5,48,8,3]{1,2,3,0:T(8,128)} collective-permute-done((f32[5,48,8,3]{1,2,3,0:T(8,128)S(1)}, f32[5,48,8,3]{1,2,3,0:T(8,128)}, u32[]{:S(2)}, u32[]{:S(2)}) %collective-permute-start.2) | collective-permute-done | bytes 23072 | tf_op jit(solution)/shard_map/ppermute | solution.py:309
  39.6 2.8 %collective-permute-start.6 = (f32[3,96,16]{2,1,0:T(8,128)S(1)}, f32[3,96,16]{2,1,0:T(8,128)}, u32[]{:S(2)}, u32[]{:S(2)}) collective-permute-start(f32[3,96,16]{2,1,0:T(8,128)S(1)} %get-tuple-element.10), channel_id=1, source_target_pairs={{0,1},{1,2},{2,3},{3,4},{4,5},{5,6},{6,7},{8,9},{9,10},{10,11},{11... | collective-permute-start | bytes 55304 | tf_op jit(solution)/shard_map/ppermute | solution.py:25
  42.5 1.3 %pad_maximum_fusion.6.tab_ref = f32[52]{0:T(128)} fusion(f32[13]{0:T(128)} %param.18, f32[13]{0:T(128)} %param.17, f32[13]{0:T(128)} %param.16, f32[13]{0:T(128)} %param.15), kind=kLoop, calls=%fused_computation.77 | loop fusion | flops 156 | bytes 416 | tf_op jit(solution)/shard_map/concatenate | solution.py:336
  43.8 0.1 pad.28.clone
  43.8 1.2 %copy.19 = f32[5,48,8,3]{3,2,1,0:T(8,128)S(1)} copy(f32[5,48,8,3]{1,2,3,0:T(8,128)} %collective-permute-done.2) | data formatting | bytes 46080 | tf_op jit(solution)/shard_map/ppermute | solution.py:309
  45.1 0.0 collective-permute-done.3
  45.1 2.2 %copy.21 = f32[5,48,8,3]{3,2,1,0:T(8,128)} copy(f32[5,48,8,3]{1,2,3,0:T(8,128)} %collective-permute-done.3) | data formatting | bytes 46080 | tf_op jit(solution)/shard_map/ppermute | solution.py:308
  47.3 0.0 collective-permute-done.7
  47.3 0.0 collective-permute-done.6
  47.3 2.2 %concatenate.22.ext_ref = f32[3,96,1280]{2,1,0:T(8,128)} concatenate(f32[3,96,112]{2,1,0:T(8,128)S(1)} %broadcast_in_dim.29, f32[3,96,16]{2,1,0:T(8,128)} %collective-permute-done.6, f32[3,96,1024]{2,1,0:T(8,128)S(1)} %pad_maximum_fusion, f32[3,96,16]{2,1,0:T(8,128)S(1)} %collective-permute-done.7, f32[3,96,112]{2,1,0:T(8,128)S(1)} %broadcast_in_dim.29), dimensions={2} | concatenate | bytes 2949120 | tf_op jit(solution)/shard_map/concatenate | solution.py:334
  49.5 0.0 collective-permute-done
  49.5 0.0 collective-permute-done.1
  49.5 0.7 fusion.17
  50.2 0.1 fusion.43
  50.2 3.9 %collective-permute-start.8 = (f32[2,14,3]{2,1,0:T(8,128)S(1)}, f32[2,14,3]{2,1,0:T(8,128)S(1)}, u32[]{:S(2)}, u32[]{:S(2)}) collective-permute-start(f32[2,14,3]{2,1,0:T(8,128)S(1)} %get-tuple-element.17), channel_id=1, source_target_pairs={{0,1},{1,2},{2,3},{3,4},{4,5},{5,6},{6,7},{8,9},{9,10},{10,11},{11... | collective-permute-start | bytes 1016 | tf_op jit(solution)/shard_map/ppermute | solution.py:25
  54.2 2.1 %collective-permute-start.9 = (f32[2,14,3]{2,1,0:T(8,128)S(1)}, f32[2,14,3]{2,1,0:T(8,128)S(1)}, u32[]{:S(2)}, u32[]{:S(2)}) collective-permute-start(f32[2,14,3]{2,1,0:T(8,128)S(1)} %get-tuple-element.18), channel_id=1, source_target_pairs={{1,0},{2,1},{3,2},{4,3},{5,4},{6,5},{7,6},{9,8},{10,9},{11,10},{12... | collective-permute-start | bytes 1016 | tf_op jit(solution)/shard_map/ppermute | solution.py:27
  56.3 3.6 %select_maximum_fusion.q_ref.u_ref.v_ref = f32[5,48,14,256]{3,2,1,0:T(8,128)} fusion(f32[5,48,8,3]{3,2,1,0:T(8,128)} %copy.21, f32[5,48,8,3]{3,2,1,0:T(8,128)S(1)} %copy.19, f32[5,48,3,128]{3,2,1,0:T(4,128)} %collective-permute-done.1, f32[5,48,8,128]{3,2,1,0:T(8,128)S(1)} %copy-done, f32[5,48,3,128]{3,2,1,0:T(4,128)} %collective-permute-done, ...), kind=kLoop, calls=%fused_computation.2 | loop fusion | flops 9461760 | bytes 5208064 | tf_op jit(solution)/shard_map/concatenate | solution.py:313
  59.9 1.3 %collective-permute-done.9 = f32[2,14,3]{2,1,0:T(8,128)S(1)} collective-permute-done((f32[2,14,3]{2,1,0:T(8,128)S(1)}, f32[2,14,3]{2,1,0:T(8,128)S(1)}, u32[]{:S(2)}, u32[]{:S(2)}) %collective-permute-start.9) | collective-permute-done | bytes 368 | tf_op jit(solution)/shard_map/ppermute | solution.py:27
  61.2 0.5 convolution_bitcast_fusion
  61.7 2.0 %fusion.2.wind_ref = f32[2,96,1280]{2,1,0:T(8,128)} fusion(f32[2,96,134]{1,2,0:T(8,128)S(1)} %convolution_bitcast_fusion, f32[1280]{0:T(1024)S(1)} %copy-done.1, s32[1280]{0:T(1024)S(1)} %get-tuple-element.26, f32[1280]{0:T(1024)S(1)} %copy-done.2, s32[1280]{0:T(1024)S(1)} %get-tuple-element.25), kind=kOutput, calls=%fused_computation.11 | convolution fusion | flops 396039680 | bytes 1106432 | tf_op jit(solution)/shard_map/kib,jb->kij/dot_general | solution.py:145
  63.7 11.9 %shard_map.130 = (f32[64,1024]{1,0:T(8,128)}, f32[64,1024]{1,0:T(8,128)}, f32[8,128]{1,0:T(8,128)}) custom-call(f32[52]{0:T(128)} %pad_maximum_fusion.6.tab_ref, f32[3,96,1280]{2,1,0:T(8,128)} %concatenate.22.ext_ref, f32[2,96,1280]{2,1,0:T(8,128)} %fusion.2.wind_ref, f32[64,1024]{1,0:T(8,128)} %fuel_ref.1), custom_call_target="tpu_custom_call" | custom-call | tf_op jit(solution)/shard_map/pallas_call | solution.py:219
  75.6 1.5 %broadcast_multiply_fusion.h_ref = f32[48,8,128]{2,1,0:T(8,128)} fusion(f32[48]{0:T(128)S(1)} %multiply_exponential_fusion, f32[8,128]{1,0:T(8,128)} %get-tuple-element.6), kind=kLoop, calls=%fused_computation.25 | loop fusion | flops 49152 | bytes 200896 | tf_op jit(solution)/shard_map/mul | solution.py:271
  77.1 7.7 %shard_map.131 = f32[5,48,8,128]{3,2,1,0:T(8,128)} custom-call(f32[5,48,14,256]{3,2,1,0:T(8,128)} %select_maximum_fusion.q_ref.u_ref.v_ref, f32[5,48,14,256]{3,2,1,0:T(8,128)} %select_maximum_fusion.q_ref.u_ref.v_ref, f32[5,48,14,256]{3,2,1,0:T(8,128)} %select_maximum_fusion.q_ref.u_ref.v_ref, f32[48,8,128]{2,1,0:T(8,128)} %broadcast_multiply_fusion.h_ref), custom_call_target="tpu_custom_call" | custom-call | tf_op jit(solution)/shard_map/pallas_call | solution.py:273
  (20 shorter events, 0.1 us)
Async XLA Ops:
  0.6 23.0 %copy-start = (f32[5,48,8,128]{3,2,1,0:T(8,128)S(1)}, f32[5,48,8,128]{3,2,1,0:T(8,128)}, u32[]{:S(2)}) copy-start(f32[5,48,8,128]{3,2,1,0:T(8,128)} %param.11) | copy-start | bytes 2949124
  5.6 26.0 %collective-permute-start.4 = (f32[3,16,1024]{2,1,0:T(8,128)}, f32[3,16,1024]{2,1,0:T(8,128)}, u32[]{:S(2)}, u32[]{:S(2)}) collective-permute-start(f32[3,16,1024]{2,1,0:T(8,128)} %get-tuple-element.15), channel_id=1, source_target_pairs={{0,8},{8,16},{16,24},{24,32},{32,40},{40,48},{48,56},{56,64},{64,7... | collective-permute-start | bytes 589832 | tf_op jit(solution)/shard_map/ppermute | solution.py:25
  7.5 26.0 %collective-permute-start.5 = (f32[3,16,1024]{2,1,0:T(8,128)}, f32[3,16,1024]{2,1,0:T(8,128)}, u32[]{:S(2)}, u32[]{:S(2)}) collective-permute-start(f32[3,16,1024]{2,1,0:T(8,128)} %get-tuple-element.16), channel_id=1, source_target_pairs={{8,0},{16,8},{24,16},{32,24},{40,32},{48,40},{56,48},{64,56},{72,6... | collective-permute-start | bytes 589832 | tf_op jit(solution)/shard_map/ppermute | solution.py:27
  15.9 33.5 %collective-permute-start = (f32[5,48,3,128]{3,2,1,0:T(4,128)}, f32[5,48,3,128]{3,2,1,0:T(4,128)}, u32[]{:S(2)}, u32[]{:S(2)}) collective-permute-start(f32[5,48,3,128]{3,2,1,0:T(4,128)} %get-tuple-element.11), channel_id=1, source_target_pairs={{0,8},{8,16},{16,24},{24,32},{32,40},{40,48},{48,56},{56,64},{64,7... | collective-permute-start | bytes 1105928 | tf_op jit(solution)/shard_map/ppermute | solution.py:25
  17.8 31.6 %collective-permute-start.1 = (f32[5,48,3,128]{3,2,1,0:T(4,128)}, f32[5,48,3,128]{3,2,1,0:T(4,128)}, u32[]{:S(2)}, u32[]{:S(2)}) collective-permute-start(f32[5,48,3,128]{3,2,1,0:T(4,128)} %get-tuple-element.12), channel_id=1, source_target_pairs={{8,0},{16,8},{24,16},{32,24},{40,32},{48,40},{56,48},{64,56},{72,6... | collective-permute-start | bytes 1105928 | tf_op jit(solution)/shard_map/ppermute | solution.py:27
  24.3 20.8 %collective-permute-start.3 = (f32[5,48,8,3]{1,2,3,0:T(8,128)S(1)}, f32[5,48,8,3]{1,2,3,0:T(8,128)}, u32[]{:S(2)}, u32[]{:S(2)}) collective-permute-start(f32[5,48,8,3]{1,2,3,0:T(8,128)S(1)} %copy.23), channel_id=1, source_target_pairs={{0,1},{1,2},{2,3},{3,4},{4,5},{5,6},{6,7},{8,9},{9,10},{10,11},{11... | collective-permute-start | bytes 69128 | tf_op jit(solution)/shard_map/ppermute | solution.py:308
  31.6 8.1 %collective-permute-start.2 = (f32[5,48,8,3]{1,2,3,0:T(8,128)S(1)}, f32[5,48,8,3]{1,2,3,0:T(8,128)}, u32[]{:S(2)}, u32[]{:S(2)}) collective-permute-start(f32[5,48,8,3]{1,2,3,0:T(8,128)S(1)} %copy.22), channel_id=1, source_target_pairs={{1,0},{2,1},{3,2},{4,3},{5,4},{6,5},{7,6},{9,8},{10,9},{11,10},{12... | collective-permute-start | bytes 69128 | tf_op jit(solution)/shard_map/ppermute | solution.py:309
  35.4 11.9 %collective-permute-start.7 = (f32[3,96,16]{2,1,0:T(8,128)}, f32[3,96,16]{2,1,0:T(8,128)S(1)}, u32[]{:S(2)}, u32[]{:S(2)}) collective-permute-start(f32[3,96,16]{2,1,0:T(8,128)} %get-tuple-element.9), channel_id=1, source_target_pairs={{1,0},{2,1},{3,2},{4,3},{5,4},{6,5},{7,6},{9,8},{10,9},{11,10},{12... | collective-permute-start | bytes 55304 | tf_op jit(solution)/shard_map/ppermute | solution.py:27
  39.6 7.6 %collective-permute-start.6 = (f32[3,96,16]{2,1,0:T(8,128)S(1)}, f32[3,96,16]{2,1,0:T(8,128)}, u32[]{:S(2)}, u32[]{:S(2)}) collective-permute-start(f32[3,96,16]{2,1,0:T(8,128)S(1)} %get-tuple-element.10), channel_id=1, source_target_pairs={{0,1},{1,2},{2,3},{3,4},{4,5},{5,6},{6,7},{8,9},{9,10},{10,11},{11... | collective-permute-start | bytes 55304 | tf_op jit(solution)/shard_map/ppermute | solution.py:25
  50.2 9.7 %collective-permute-start.8 = (f32[2,14,3]{2,1,0:T(8,128)S(1)}, f32[2,14,3]{2,1,0:T(8,128)S(1)}, u32[]{:S(2)}, u32[]{:S(2)}) collective-permute-start(f32[2,14,3]{2,1,0:T(8,128)S(1)} %get-tuple-element.17), channel_id=1, source_target_pairs={{0,1},{1,2},{2,3},{3,4},{4,5},{5,6},{6,7},{8,9},{9,10},{10,11},{11... | collective-permute-start | bytes 1016 | tf_op jit(solution)/shard_map/ppermute | solution.py:25
  54.1 7.0 %copy-start.3 = (s32[96]{0:T(128)S(1)}, s32[96]{0:T(128)}, u32[]{:S(2)}) copy-start(s32[96]{0:T(128)} %get-tuple-element.21) | copy-start | bytes 1156
  54.2 7.0 %copy-start.4 = (s32[96]{0:T(128)S(1)}, s32[96]{0:T(128)}, u32[]{:S(2)}) copy-start(s32[96]{0:T(128)} %get-tuple-element.22) | copy-start | bytes 1156
  54.2 7.0 %copy-start.5 = (f32[96]{0:T(128)S(1)}, f32[96]{0:T(128)}, u32[]{:S(2)}) copy-start(f32[96]{0:T(128)} %get-tuple-element.19) | copy-start | bytes 1156
  54.2 7.0 %copy-start.6 = (f32[96]{0:T(128)S(1)}, f32[96]{0:T(128)}, u32[]{:S(2)}) copy-start(f32[96]{0:T(128)} %get-tuple-element.20) | copy-start | bytes 1156
  54.2 7.5 %copy-start.1 = (f32[1280]{0:T(1024)S(1)}, f32[1280]{0:T(1024)}, u32[]{:S(2)}) copy-start(f32[1280]{0:T(1024)} %get-tuple-element.23) | copy-start | bytes 15364
  54.2 7.5 %copy-start.2 = (f32[1280]{0:T(1024)S(1)}, f32[1280]{0:T(1024)}, u32[]{:S(2)}) copy-start(f32[1280]{0:T(1024)} %get-tuple-element.24) | copy-start | bytes 15364
  54.2 7.0 %collective-permute-start.9 = (f32[2,14,3]{2,1,0:T(8,128)S(1)}, f32[2,14,3]{2,1,0:T(8,128)S(1)}, u32[]{:S(2)}, u32[]{:S(2)}) collective-permute-start(f32[2,14,3]{2,1,0:T(8,128)S(1)} %get-tuple-element.18), channel_id=1, source_target_pairs={{1,0},{2,1},{3,2},{4,3},{5,4},{6,5},{7,6},{9,8},{10,9},{11,10},{12... | collective-permute-start | bytes 1016 | tf_op jit(solution)/shard_map/ppermute | solution.py:27

commit v8 on v7

--- a/solution.py
+++ b/solution.py
@@ -228,7 +228,7 @@
     )(tables, ext, winds, fuel_left)
 
 
-def atmos_kernel(q_ref, u_ref, v_ref, h_ref, o_ref):
+def atmos_kernel(p_ref, q_ref, u_ref, v_ref, h_ref, o_ref):
     rows, cols = o_ref.shape[2], o_ref.shape[3]
     width = q_ref.shape[3]
 
@@ -261,27 +261,29 @@
         - COURANT * (at(u_ref, 0, 0) * deriv_x + at(v_ref, 0, 0) * deriv_y)
         + DIFFUSE * laplace
     )
-    o_ref[0] = jnp.where(pl.program_id(0) == 3, updated + h_ref[...], updated)
+    heat = h_ref[...]
+    profile_heat = jnp.stack([heat * p_ref[k] for k in range(updated.shape[0])])
+    o_ref[0] = jnp.where(pl.program_id(0) == 3, updated + profile_heat, updated)
 
 
 def atmos_call(padded, heat_atm):
     fields, depth, ext_rows, width = padded.shape
     rows, cols = heat_atm.shape
     profile = jnp.exp(-4.0 * jnp.arange(depth).astype(jnp.float32) / depth)
-    heat = heat_atm[None, :, :] * profile[:, None, None]
     block = (1, depth, ext_rows, width)
     return pl.pallas_call(
         atmos_kernel,
         grid=(fields,),
         out_shape=jax.ShapeDtypeStruct((fields, depth, rows, cols), jnp.float32),
         in_specs=[
+            pl.BlockSpec(memory_space=pltpu.SMEM),
             pl.BlockSpec(block, lambda f: (f, 0, 0, 0)),
             pl.BlockSpec(block, lambda f: (0, 0, 0, 0)),
             pl.BlockSpec(block, lambda f: (1, 0, 0, 0)),
-            pl.BlockSpec((depth, rows, cols), lambda f: (0, 0, 0)),
+            pl.BlockSpec((rows, cols), lambda f: (0, 0)),
         ],
         out_specs=pl.BlockSpec((1, depth, rows, cols), lambda f: (f, 0, 0, 0)),
-    )(padded, padded, padded, heat)
+    )(profile, padded, padded, padded, heat_atm)
 
 
 def fire_halo(level):

time: 85.7 us -> 85.1 us (level)
  waiting for transfers between devices: 3.65 us -> 2.4 us
  starting transfers between devices: 33 us -> 34.2 us
  other arithmetic: 14.1 us -> 13.2 us
    ppermute x1, waiting for transfers between devices: 2.34 us -> 0.01 us  [shards(): lax.ppermute(atmos[..., :3], 'gy', [(i + 1, i) for i in range(count - 1)])]
    mul x1 -> x0, other arithmetic: 1.47 us -> none  [atmos_call(): heat = heat_atm[None, :, :] * profile[:, None, None]]
    ppermute x4, starting transfers between devices: 15.5 us -> 16.8 us  [extended(): lax.ppermute(head, axis, [((i + 1) % count, i) for i in range(ends)])]
    unnamed x16 -> x14, local copies, waits for them, and re-layouts: 0.81 us -> 2.03 us
    ppermute x4, waiting for transfers between devices: 1.3 us -> 2.38 us  [extended(): lax.ppermute(head, axis, [((i + 1) % count, i) for i in range(ends)])]
  transfers between devices with their start and end apart: 10 -> 10, of which waited for: 2 -> 1; matrix products, arithmetic and copies ran while one was open for 21% -> 23% of each run, Pallas kernels for 0% -> 0%
where the time goes in v8:
time: 85.1 us; the launch traced here: 84.3 us
  starting transfers between devices  34.2 us (40%)
  Pallas kernels  19.5 us (23%)
  other arithmetic  13.2 us (16%)
  local copies, waits for them, and re-layouts  10.9 us (13%)
  matrix products  2.51 us (3%)
  waiting for transfers between devices  2.4 us (3%)
  between operations  1.6 us (2%)
    ppermute x4, starting transfers between devices, extended(): lax.ppermute(head, axis, [((i + 1) % count, i) for i in range(ends)])  16.8 us
    pallas_call x1, Pallas kernels, fire_step(): pl.pallas_call(fire_kernel, out_shape=(jax.ShapeDtypeStruct((rows, cols),...  11.9 us
    ppermute x4, starting transfers between devices, extended(): lax.ppermute(tail, axis, [(i, (i + 1) % count) for i in range(ends)])  10.3 us
    pallas_call x1, Pallas kernels, atmos_call(): pl.pallas_call(atmos_kernel, grid=(fields,), out_shape=jax.ShapeDtypeStru...  7.67 us
    ppermute x1, starting transfers between devices, shards(): lax.ppermute(atmos[..., -3:], 'gy', [(i, i + 1) for i in range(count - 1)])  5.03 us
    concatenate x1, other arithmetic, shards(): jnp.concatenate([along_x, jnp.pad(from_hi, rows_pad), room, jnp.pad(from_...  3.66 us
    slice x2, local copies, waits for them, and re-layouts, extended(): lax.slice_in_dim(cells, cells.shape[dim] - width, cells.shape[dim], axis=...  2.71 us
    ppermute x4, waiting for transfers between devices, extended(): lax.ppermute(head, axis, [((i + 1) % count, i) for i in range(ends)])  2.38 us
  transfers between devices with their start and end apart: 10, of which 1 were waited for; matrix products, arithmetic and copies ran while one was open for 23% of the time, Pallas kernels for 0%

profile of v8, /device:TPU:120, one launch (start us, length us, event | category | flops | bytes accessed | tf_op | source)
XLA Modules:
  0.0 84.3 jit_solution(13028230867756159153)
XLA Ops:
  0.6 0.0 copy-start
  1.4 0.7 fusion.28
  2.1 0.7 fusion.36
  2.8 0.1 broadcast_in_dim.52
  2.9 0.1 broadcast_in_dim.53
  2.9 1.0 %convert_bitcast_fusion = f32[1,64,1024]{2,1,0:T(8,128)S(1)} fusion(s32[64,1024]{1,0:T(8,128)} %param.14), kind=kLoop, calls=%fused_computation.21 | loop fusion | flops 65536 | bytes 524288 | tf_op jit(solution)/shard_map/stack | solution.py:333
  3.9 1.6 %pad_maximum_fusion.3 = (f32[3,16,1024]{2,1,0:T(8,128)}, f32[3,16,1024]{2,1,0:T(8,128)}) fusion(f32[1,64,1024]{2,1,0:T(8,128)S(1)} %broadcast_in_dim.54, f32[1,64,1024]{2,1,0:T(8,128)S(1)} %convert_bitcast_fusion, f32[1,64,1024]{2,1,0:T(8,128)} %bitcast.25), kind=kLoop, calls=%fused_computation.24 | loop fusion | flops 196608 | bytes 1179648 | tf_op jit(solution)/shard_map/slice | solution.py:22
  5.6 1.9 %collective-permute-start.4 = (f32[3,16,1024]{2,1,0:T(8,128)}, f32[3,16,1024]{2,1,0:T(8,128)}, u32[]{:S(2)}, u32[]{:S(2)}) collective-permute-start(f32[3,16,1024]{2,1,0:T(8,128)} %get-tuple-element.15), channel_id=1, source_target_pairs={{0,8},{8,16},{16,24},{24,32},{32,40},{40,48},{48,56},{56,64},{64,7... | collective-permute-start | bytes 589832 | tf_op jit(solution)/shard_map/ppermute | solution.py:25
  7.5 5.8 %collective-permute-start.5 = (f32[3,16,1024]{2,1,0:T(8,128)}, f32[3,16,1024]{2,1,0:T(8,128)}, u32[]{:S(2)}, u32[]{:S(2)}) collective-permute-start(f32[3,16,1024]{2,1,0:T(8,128)} %get-tuple-element.16), channel_id=1, source_target_pairs={{8,0},{16,8},{24,16},{32,24},{40,32},{48,40},{56,48},{64,56},{72,6... | collective-permute-start | bytes 589832 | tf_op jit(solution)/shard_map/ppermute | solution.py:27
  13.3 2.6 %fusion.41 = (f32[5,48,3,128]{3,2,1,0:T(4,128)}, f32[5,48,3,128]{3,2,1,0:T(4,128)}) fusion(f32[5,48,8,128]{3,2,1,0:T(8,128)} %param.11), kind=kLoop, calls=%fused_computation.87 | loop fusion | bytes 1474560 | tf_op jit(solution)/shard_map/slice | solution.py:22
  15.9 1.9 %collective-permute-start = (f32[5,48,3,128]{3,2,1,0:T(4,128)}, f32[5,48,3,128]{3,2,1,0:T(4,128)}, u32[]{:S(2)}, u32[]{:S(2)}) collective-permute-start(f32[5,48,3,128]{3,2,1,0:T(4,128)} %get-tuple-element.11), channel_id=1, source_target_pairs={{0,8},{8,16},{16,24},{24,32},{32,40},{40,48},{48,56},{56,64},{64,7... | collective-permute-start | bytes 1105928 | tf_op jit(solution)/shard_map/ppermute | solution.py:25
  17.8 5.8 %collective-permute-start.1 = (f32[5,48,3,128]{3,2,1,0:T(4,128)}, f32[5,48,3,128]{3,2,1,0:T(4,128)}, u32[]{:S(2)}, u32[]{:S(2)}) collective-permute-start(f32[5,48,3,128]{3,2,1,0:T(4,128)} %get-tuple-element.12), channel_id=1, source_target_pairs={{8,0},{16,8},{24,16},{32,24},{40,32},{48,40},{56,48},{64,56},{72,6... | collective-permute-start | bytes 1105928 | tf_op jit(solution)/shard_map/ppermute | solution.py:27
  23.6 0.3 fusion.42
  23.9 1.0 %copy.22 = f32[5,48,8,3]{1,2,3,0:T(8,128)} copy(f32[5,48,8,3]{3,2,1,0:T(8,128)S(1)} %get-tuple-element.13) | data formatting | bytes 46080
  24.9 2.0 %collective-permute-start.2 = (f32[5,48,8,3]{1,2,3,0:T(8,128)}, f32[5,48,8,3]{1,2,3,0:T(8,128)S(1)}, u32[]{:S(2)}, u32[]{:S(2)}) collective-permute-start(f32[5,48,8,3]{1,2,3,0:T(8,128)} %copy.22), channel_id=1, source_target_pairs={{1,0},{2,1},{3,2},{4,3},{5,4},{6,5},{7,6},{9,8},{10,9},{11,10},{12... | collective-permute-start | bytes 69128 | tf_op jit(solution)/shard_map/ppermute | solution.py:311
  26.9 0.5 fusion.34
  27.5 0.6 broadcast_add_fusion.2
  28.1 1.0 %copy.23 = f32[5,48,8,3]{1,2,3,0:T(8,128)} copy(f32[5,48,8,3]{3,2,1,0:T(8,128)S(1)} %get-tuple-element.14) | data formatting | bytes 46080
  29.1 0.6 multiply_exponential_fusion.p_ref
  29.7 0.6 broadcast_add_fusion
  30.3 0.0 collective-permute-done.4
  30.3 5.0 %collective-permute-start.3 = (f32[5,48,8,3]{1,2,3,0:T(8,128)}, f32[5,48,8,3]{1,2,3,0:T(8,128)}, u32[]{:S(2)}, u32[]{:S(2)}) collective-permute-start(f32[5,48,8,3]{1,2,3,0:T(8,128)} %copy.23), channel_id=1, source_target_pairs={{0,1},{1,2},{2,3},{3,4},{4,5},{5,6},{6,7},{8,9},{9,10},{10,11},{11... | collective-permute-start | bytes 69128 | tf_op jit(solution)/shard_map/ppermute | solution.py:310
  35.3 0.0 collective-permute-done.5
  35.3 1.2 %pad_maximum_fusion = f32[3,96,1024]{2,1,0:T(8,128)S(1)} fusion(f32[3,16,1024]{2,1,0:T(8,128)} %collective-permute-done.5, f32[1,64,1024]{2,1,0:T(8,128)S(1)} %broadcast_in_dim.54, f32[1,64,1024]{2,1,0:T(8,128)S(1)} %convert_bitcast_fusion, f32[1,64,1024]{2,1,0:T(8,128)} %bitcast.26, f32[3,16,1024]{2,1,0:T(8,128)} %collective-permute-done.4), kind=kLoop, calls=%fused_computation.7 | loop fusion | flops 1179648 | bytes 2359296 | tf_op jit(solution)/shard_map/concatenate | solution.py:23
  36.5 0.8 fusion.40
  37.3 3.8 %collective-permute-start.6 = (f32[3,96,16]{2,1,0:T(8,128)}, f32[3,96,16]{2,1,0:T(8,128)S(1)}, u32[]{:S(2)}, u32[]{:S(2)}) collective-permute-start(f32[3,96,16]{2,1,0:T(8,128)} %get-tuple-element.10), channel_id=1, source_target_pairs={{0,1},{1,2},{2,3},{3,4},{4,5},{5,6},{6,7},{8,9},{9,10},{10,11},{11... | collective-permute-start | bytes 55304 | tf_op jit(solution)/shard_map/ppermute | solution.py:25
  41.1 0.0 collective-permute-done.2
  41.1 2.0 %collective-permute-start.7 = (f32[3,96,16]{2,1,0:T(8,128)S(1)}, f32[3,96,16]{2,1,0:T(8,128)}, u32[]{:S(2)}, u32[]{:S(2)}) collective-permute-start(f32[3,96,16]{2,1,0:T(8,128)S(1)} %get-tuple-element.9), channel_id=1, source_target_pairs={{1,0},{2,1},{3,2},{4,3},{5,4},{6,5},{7,6},{9,8},{10,9},{11,10},{12... | collective-permute-start | bytes 55304 | tf_op jit(solution)/shard_map/ppermute | solution.py:27
  43.2 1.3 %pad_maximum_fusion.6.tab_ref = f32[52]{0:T(128)} fusion(f32[13]{0:T(128)} %param.18, f32[13]{0:T(128)} %param.17, f32[13]{0:T(128)} %param.16, f32[13]{0:T(128)} %param.15), kind=kLoop, calls=%fused_computation.76 | loop fusion | flops 156 | bytes 416 | tf_op jit(solution)/shard_map/concatenate | solution.py:338
  44.4 0.1 pad.28.clone
  44.5 0.4 copy.19
  45.0 0.0 collective-permute-done.3
  45.0 2.2 %copy.21 = f32[5,48,8,3]{3,2,1,0:T(8,128)} copy(f32[5,48,8,3]{1,2,3,0:T(8,128)} %collective-permute-done.3) | data formatting | bytes 46080 | tf_op jit(solution)/shard_map/ppermute | solution.py:310
  47.1 0.0 collective-permute-done.6
  47.1 2.3 %collective-permute-done.7 = f32[3,96,16]{2,1,0:T(8,128)} collective-permute-done((f32[3,96,16]{2,1,0:T(8,128)S(1)}, f32[3,96,16]{2,1,0:T(8,128)}, u32[]{:S(2)}, u32[]{:S(2)}) %collective-permute-start.7) | collective-permute-done | bytes 18464 | tf_op jit(solution)/shard_map/ppermute | solution.py:27
  49.5 2.2 %concatenate.22.ext_ref = f32[3,96,1280]{2,1,0:T(8,128)} concatenate(f32[3,96,112]{2,1,0:T(8,128)S(1)} %broadcast_in_dim.29, f32[3,96,16]{2,1,0:T(8,128)S(1)} %collective-permute-done.6, f32[3,96,1024]{2,1,0:T(8,128)S(1)} %pad_maximum_fusion, f32[3,96,16]{2,1,0:T(8,128)} %collective-permute-done.7, f32[3,96,112]{2,1,0:T(8,128)S(1)} %broadcast_in_dim.29), dimensions={2} | concatenate | bytes 2949120 | tf_op jit(solution)/shard_map/concatenate | solution.py:336
  51.7 0.0 collective-permute-done
  51.7 0.0 collective-permute-done.1
  51.7 0.7 fusion.17
  52.4 0.1 fusion.43
  52.5 2.7 %collective-permute-start.8 = (f32[2,14,3]{2,1,0:T(8,128)S(1)}, f32[2,14,3]{2,1,0:T(8,128)S(1)}, u32[]{:S(2)}, u32[]{:S(2)}) collective-permute-start(f32[2,14,3]{2,1,0:T(8,128)S(1)} %get-tuple-element.17), channel_id=1, source_target_pairs={{0,1},{1,2},{2,3},{3,4},{4,5},{5,6},{6,7},{8,9},{9,10},{10,11},{11... | collective-permute-start | bytes 1016 | tf_op jit(solution)/shard_map/ppermute | solution.py:25
  55.2 3.3 %collective-permute-start.9 = (f32[2,14,3]{2,1,0:T(8,128)S(1)}, f32[2,14,3]{2,1,0:T(8,128)S(1)}, u32[]{:S(2)}, u32[]{:S(2)}) collective-permute-start(f32[2,14,3]{2,1,0:T(8,128)S(1)} %get-tuple-element.18), channel_id=1, source_target_pairs={{1,0},{2,1},{3,2},{4,3},{5,4},{6,5},{7,6},{9,8},{10,9},{11,10},{12... | collective-permute-start | bytes 1016 | tf_op jit(solution)/shard_map/ppermute | solution.py:27
  58.5 3.7 %select_maximum_fusion.q_ref.u_ref.v_ref = f32[5,48,14,256]{3,2,1,0:T(8,128)} fusion(f32[5,48,8,3]{3,2,1,0:T(8,128)} %copy.21, f32[5,48,8,3]{3,2,1,0:T(8,128)S(1)} %copy.19, f32[5,48,3,128]{3,2,1,0:T(4,128)} %collective-permute-done.1, f32[5,48,8,128]{3,2,1,0:T(8,128)S(1)} %copy-done, f32[5,48,3,128]{3,2,1,0:T(4,128)} %collective-permute-done, ...), kind=kLoop, calls=%fused_computation.2 | loop fusion | flops 9461760 | bytes 5208064 | tf_op jit(solution)/shard_map/concatenate | solution.py:315
  62.2 0.0 collective-permute-done.9
  62.2 0.5 convolution_bitcast_fusion
  62.7 2.0 %fusion.2.wind_ref = f32[2,96,1280]{2,1,0:T(8,128)} fusion(f32[2,96,134]{1,2,0:T(8,128)S(1)} %convolution_bitcast_fusion, f32[1280]{0:T(1024)S(1)} %get-tuple-element.23, s32[1280]{0:T(1024)S(1)} %copy-done.2, f32[1280]{0:T(1024)S(1)} %get-tuple-element.24, s32[1280]{0:T(1024)S(1)} %copy-done.1), kind=kOutput, calls=%fused_computation.11 | convolution fusion | flops 396039680 | bytes 1106432 | tf_op jit(solution)/shard_map/kib,jb->kij/dot_general | solution.py:145
  64.7 11.9 %shard_map.130 = (f32[64,1024]{1,0:T(8,128)}, f32[64,1024]{1,0:T(8,128)}, f32[8,128]{1,0:T(8,128)}) custom-call(f32[52]{0:T(128)} %pad_maximum_fusion.6.tab_ref, f32[3,96,1280]{2,1,0:T(8,128)} %concatenate.22.ext_ref, f32[2,96,1280]{2,1,0:T(8,128)} %fusion.2.wind_ref, f32[64,1024]{1,0:T(8,128)} %fuel_ref.1), custom_call_target="tpu_custom_call" | custom-call | tf_op jit(solution)/shard_map/pallas_call | solution.py:219
  76.6 7.7 %shard_map.131 = f32[5,48,8,128]{3,2,1,0:T(8,128)} custom-call(f32[48]{0:T(128)} %multiply_exponential_fusion.p_ref, f32[5,48,14,256]{3,2,1,0:T(8,128)} %select_maximum_fusion.q_ref.u_ref.v_ref, f32[5,48,14,256]{3,2,1,0:T(8,128)} %select_maximum_fusion.q_ref.u_ref.v_ref, f32[5,48,14,256]{3,2,1,0:T(8,128)} %select_maximum_fusion.q_ref.u_ref.v_ref, ...), custom_call_target="tpu_custom_call" | custom-call | tf_op jit(solution)/shard_map/pallas_call | solution.py:274
  (17 shorter events, 0.1 us)
Async XLA Ops:
  0.6 23.0 %copy-start = (f32[5,48,8,128]{3,2,1,0:T(8,128)S(1)}, f32[5,48,8,128]{3,2,1,0:T(8,128)}, u32[]{:S(2)}) copy-start(f32[5,48,8,128]{3,2,1,0:T(8,128)} %param.11) | copy-start | bytes 2949124
  5.6 24.7 %collective-permute-start.4 = (f32[3,16,1024]{2,1,0:T(8,128)}, f32[3,16,1024]{2,1,0:T(8,128)}, u32[]{:S(2)}, u32[]{:S(2)}) collective-permute-start(f32[3,16,1024]{2,1,0:T(8,128)} %get-tuple-element.15), channel_id=1, source_target_pairs={{0,8},{8,16},{16,24},{24,32},{32,40},{40,48},{48,56},{56,64},{64,7... | collective-permute-start | bytes 589832 | tf_op jit(solution)/shard_map/ppermute | solution.py:25
  7.5 27.8 %collective-permute-start.5 = (f32[3,16,1024]{2,1,0:T(8,128)}, f32[3,16,1024]{2,1,0:T(8,128)}, u32[]{:S(2)}, u32[]{:S(2)}) collective-permute-start(f32[3,16,1024]{2,1,0:T(8,128)} %get-tuple-element.16), channel_id=1, source_target_pairs={{8,0},{16,8},{24,16},{32,24},{40,32},{48,40},{56,48},{64,56},{72,6... | collective-permute-start | bytes 589832 | tf_op jit(solution)/shard_map/ppermute | solution.py:27
  15.9 35.8 %collective-permute-start = (f32[5,48,3,128]{3,2,1,0:T(4,128)}, f32[5,48,3,128]{3,2,1,0:T(4,128)}, u32[]{:S(2)}, u32[]{:S(2)}) collective-permute-start(f32[5,48,3,128]{3,2,1,0:T(4,128)} %get-tuple-element.11), channel_id=1, source_target_pairs={{0,8},{8,16},{16,24},{24,32},{32,40},{40,48},{48,56},{56,64},{64,7... | collective-permute-start | bytes 1105928 | tf_op jit(solution)/shard_map/ppermute | solution.py:25
  17.8 33.9 %collective-permute-start.1 = (f32[5,48,3,128]{3,2,1,0:T(4,128)}, f32[5,48,3,128]{3,2,1,0:T(4,128)}, u32[]{:S(2)}, u32[]{:S(2)}) collective-permute-start(f32[5,48,3,128]{3,2,1,0:T(4,128)} %get-tuple-element.12), channel_id=1, source_target_pairs={{8,0},{16,8},{24,16},{32,24},{40,32},{48,40},{56,48},{64,56},{72,6... | collective-permute-start | bytes 1105928 | tf_op jit(solution)/shard_map/ppermute | solution.py:27
  24.9 16.2 %collective-permute-start.2 = (f32[5,48,8,3]{1,2,3,0:T(8,128)}, f32[5,48,8,3]{1,2,3,0:T(8,128)S(1)}, u32[]{:S(2)}, u32[]{:S(2)}) collective-permute-start(f32[5,48,8,3]{1,2,3,0:T(8,128)} %copy.22), channel_id=1, source_target_pairs={{1,0},{2,1},{3,2},{4,3},{5,4},{6,5},{7,6},{9,8},{10,9},{11,10},{12... | collective-permute-start | bytes 69128 | tf_op jit(solution)/shard_map/ppermute | solution.py:311
  30.3 14.7 %collective-permute-start.3 = (f32[5,48,8,3]{1,2,3,0:T(8,128)}, f32[5,48,8,3]{1,2,3,0:T(8,128)}, u32[]{:S(2)}, u32[]{:S(2)}) collective-permute-start(f32[5,48,8,3]{1,2,3,0:T(8,128)} %copy.23), channel_id=1, source_target_pairs={{0,1},{1,2},{2,3},{3,4},{4,5},{5,6},{6,7},{8,9},{9,10},{10,11},{11... | collective-permute-start | bytes 69128 | tf_op jit(solution)/shard_map/ppermute | solution.py:310
  37.3 9.8 %collective-permute-start.6 = (f32[3,96,16]{2,1,0:T(8,128)}, f32[3,96,16]{2,1,0:T(8,128)S(1)}, u32[]{:S(2)}, u32[]{:S(2)}) collective-permute-start(f32[3,96,16]{2,1,0:T(8,128)} %get-tuple-element.10), channel_id=1, source_target_pairs={{0,1},{1,2},{2,3},{3,4},{4,5},{5,6},{6,7},{8,9},{9,10},{10,11},{11... | collective-permute-start | bytes 55304 | tf_op jit(solution)/shard_map/ppermute | solution.py:25
  41.1 8.4 %collective-permute-start.7 = (f32[3,96,16]{2,1,0:T(8,128)S(1)}, f32[3,96,16]{2,1,0:T(8,128)}, u32[]{:S(2)}, u32[]{:S(2)}) collective-permute-start(f32[3,96,16]{2,1,0:T(8,128)S(1)} %get-tuple-element.9), channel_id=1, source_target_pairs={{1,0},{2,1},{3,2},{4,3},{5,4},{6,5},{7,6},{9,8},{10,9},{11,10},{12... | collective-permute-start | bytes 55304 | tf_op jit(solution)/shard_map/ppermute | solution.py:27
  52.5 9.7 %collective-permute-start.8 = (f32[2,14,3]{2,1,0:T(8,128)S(1)}, f32[2,14,3]{2,1,0:T(8,128)S(1)}, u32[]{:S(2)}, u32[]{:S(2)}) collective-permute-start(f32[2,14,3]{2,1,0:T(8,128)S(1)} %get-tuple-element.17), channel_id=1, source_target_pairs={{0,1},{1,2},{2,3},{3,4},{4,5},{5,6},{6,7},{8,9},{9,10},{10,11},{11... | collective-permute-start | bytes 1016 | tf_op jit(solution)/shard_map/ppermute | solution.py:25
  55.2 7.0 %copy-start.3 = (f32[96]{0:T(128)S(1)}, f32[96]{0:T(128)}, u32[]{:S(2)}) copy-start(f32[96]{0:T(128)} %get-tuple-element.20) | copy-start | bytes 1156
  55.2 7.0 %copy-start.4 = (s32[96]{0:T(128)S(1)}, s32[96]{0:T(128)}, u32[]{:S(2)}) copy-start(s32[96]{0:T(128)} %get-tuple-element.21) | copy-start | bytes 1156
  55.2 7.0 %copy-start.5 = (s32[96]{0:T(128)S(1)}, s32[96]{0:T(128)}, u32[]{:S(2)}) copy-start(s32[96]{0:T(128)} %get-tuple-element.22) | copy-start | bytes 1156
  55.2 7.5 %copy-start.1 = (s32[1280]{0:T(1024)S(1)}, s32[1280]{0:T(1024)}, u32[]{:S(2)}) copy-start(s32[1280]{0:T(1024)} %get-tuple-element.25) | copy-start | bytes 15364
  55.2 7.5 %copy-start.2 = (s32[1280]{0:T(1024)S(1)}, s32[1280]{0:T(1024)}, u32[]{:S(2)}) copy-start(s32[1280]{0:T(1024)} %get-tuple-element.26) | copy-start | bytes 15364
  55.2 7.0 %collective-permute-start.9 = (f32[2,14,3]{2,1,0:T(8,128)S(1)}, f32[2,14,3]{2,1,0:T(8,128)S(1)}, u32[]{:S(2)}, u32[]{:S(2)}) collective-permute-start(f32[2,14,3]{2,1,0:T(8,128)S(1)} %get-tuple-element.18), channel_id=1, source_target_pairs={{1,0},{2,1},{3,2},{4,3},{5,4},{6,5},{7,6},{9,8},{10,9},{11,10},{12... | collective-permute-start | bytes 1016 | tf_op jit(solution)/shard_map/ppermute | solution.py:27

commit v9 on v5

--- a/solution.py
+++ b/solution.py
@@ -228,6 +228,63 @@
     )(tables, ext, winds, fuel_left)
 
 
+def atmos_kernel(p_ref, q_ref, lo_ref, hi_ref, y_ref, u_ref, v_ref, h_ref, o_ref, ext_ref):
+    rows, cols = o_ref.shape[2], o_ref.shape[3]
+    halo = lo_ref.shape[2]
+    centre = q_ref[0]
+    ext_ref[:, 0:halo, :] = lo_ref[0]
+    ext_ref[:, halo : halo + rows, :] = centre
+    ext_ref[:, halo + rows : 2 * halo + rows, :] = hi_ref[0]
+    ends = y_ref[0]
+    lane = lax.broadcasted_iota(jnp.int32, centre.shape, 2)
+
+    def ax(dx):
+        return ext_ref[:, halo + dx : halo + dx + rows, :]
+
+    def ay(dy):
+        if dy > 0:
+            turn = cols - dy
+            return jnp.where(lane >= turn, pltpu.roll(ends, turn, 2), pltpu.roll(centre, turn, 2))
+        return jnp.where(lane < -dy, pltpu.roll(ends, -dy, 2), pltpu.roll(centre, -dy, 2))
+
+    deriv_x = (
+        ax(3) - 9.0 * ax(2) + 45.0 * ax(1) - 45.0 * ax(-1) + 9.0 * ax(-2) - ax(-3)
+    ) / 60.0
+    deriv_y = (
+        ay(3) - 9.0 * ay(2) + 45.0 * ay(1) - 45.0 * ay(-1) + 9.0 * ay(-2) - ay(-3)
+    ) / 60.0
+    laplace = ax(1) + ax(-1) + ay(1) + ay(-1) - 4.0 * centre
+    updated = centre - COURANT * (u_ref[0] * deriv_x + v_ref[0] * deriv_y) + DIFFUSE * laplace
+    heat = h_ref[...]
+    profile_heat = jnp.stack([heat * p_ref[k] for k in range(updated.shape[0])])
+    o_ref[0] = jnp.where(pl.program_id(0) == 3, updated + profile_heat, updated)
+
+
+def atmos_call(atmos, x_lo, x_hi, y_ends, heat_atm):
+    fields, depth, rows, cols = atmos.shape
+    halo = x_lo.shape[2]
+    profile = jnp.exp(-4.0 * jnp.arange(depth).astype(jnp.float32) / depth)
+    block = (1, depth, rows, cols)
+    edge = (1, depth, halo, cols)
+    return pl.pallas_call(
+        atmos_kernel,
+        grid=(fields,),
+        out_shape=jax.ShapeDtypeStruct((fields, depth, rows, cols), jnp.float32),
+        in_specs=[
+            pl.BlockSpec(memory_space=pltpu.SMEM),
+            pl.BlockSpec(block, lambda f: (f, 0, 0, 0)),
+            pl.BlockSpec(edge, lambda f: (f, 0, 0, 0)),
+            pl.BlockSpec(edge, lambda f: (f, 0, 0, 0)),
+            pl.BlockSpec(block, lambda f: (f, 0, 0, 0)),
+            pl.BlockSpec(block, lambda f: (0, 0, 0, 0)),
+            pl.BlockSpec(block, lambda f: (1, 0, 0, 0)),
+            pl.BlockSpec((rows, cols), lambda f: (0, 0)),
+        ],
+        out_specs=pl.BlockSpec(block, lambda f: (f, 0, 0, 0)),
+        scratch_shapes=[pltpu.VMEM((depth, -(-(rows + 2 * halo) // 8) * 8, cols), jnp.float32)],
+    )(profile, atmos, x_lo, x_hi, y_ends, atmos, atmos, heat_atm)
+
+
 def fire_halo(level):
     return extended(level, (("gx", 0), ("gy", 1)), 2)
 
@@ -247,8 +304,16 @@
 ):
     fire_rows, fire_cols = level_set.shape
     atmos_rows, atmos_cols = (atmos.shape[2], atmos.shape[3])
-    padded_atm = extended(atmos, (("gx", 2), ("gy", 3)), 3)
-    surface = padded_atm[0:2, 0]
+    count_x = lax.axis_size("gx")
+    x_lo = lax.ppermute(atmos[:, :, -3:], "gx", [(i, i + 1) for i in range(count_x - 1)])
+    x_hi = lax.ppermute(atmos[:, :, :3], "gx", [(i + 1, i) for i in range(count_x - 1)])
+    count = lax.axis_size("gy")
+    from_lo = lax.ppermute(atmos[..., -3:], "gy", [(i, i + 1) for i in range(count - 1)])
+    from_hi = lax.ppermute(atmos[..., :3], "gy", [(i + 1, i) for i in range(count - 1)])
+    room = jnp.zeros(atmos.shape[:3] + (atmos_cols - 6,), jnp.float32)
+    y_ends = jnp.concatenate([from_hi, room, from_lo], axis=3)
+    along_x = jnp.concatenate([x_lo[0:2, 0:1], atmos[0:2, 0:1], x_hi[0:2, 0:1]], axis=2)
+    surface = extended(along_x[:, 0], (("gy", 2),), 3)
     slots = burn_tiles.reshape(-1)
     listed = burn_count.reshape(())
     tiles_dev = substep_count.size
@@ -270,7 +335,7 @@
     winds = surface_winds(surface, fire_rows, fire_cols, halo, HALO_Y)
     tables = jnp.concatenate([spread_rate, wind_factor, burn_time, heat_yield]).astype(jnp.float32)
     level, remaining, heat_atm = fire_step(tables, stacked, winds, fuel_left)
-    return (atmos_step(padded_atm, heat_atm), level, remaining)
+    return (atmos_call(atmos, x_lo, x_hi, y_ends, heat_atm), level, remaining)
 
 
 def solution(mesh):

time: 99.3 us -> 76 us (0.77)
  other arithmetic: 31.8 us -> 10.1 us
  local copies, waits for them, and re-layouts: 22.7 us -> 8.99 us
  Pallas kernels: 12.1 us -> 18.6 us
  waiting for transfers between devices: 0.02 us -> 2.77 us
  starting transfers between devices: 27.8 us -> 30.5 us
    ppermute x0 -> x4, starting transfers between devices: none -> 11 us  [the longest x1 5.03 us: shards(): lax.ppermute(atmos[..., -3:], 'gy', [(i, i + 1) for i in range(count - 1)])]
    add x1 -> x0, other arithmetic: 10.9 us -> none  [atmos_step(): centre - COURANT * (centre[0:1] * deriv_x + centre[1:2] * deriv_y)]
    concatenate x3 -> x1, other arithmetic: 11.5 us -> 1.27 us  [extended(): jnp.concatenate([lax.ppermute(tail, axis, [(i, (i + 1) % count) for i in...]
    pallas_call x0 -> x1, Pallas kernels: none -> 6.78 us  [atmos_call(): pl.pallas_call(atmos_kernel, grid=(fields,), out_shape=jax.ShapeDtypeStru...]
    unnamed x46 -> x35, local copies, waits for them, and re-layouts: 7.94 us -> 2.15 us
    ppermute x4 -> x3, starting transfers between devices: 14 us -> 9.44 us  [extended(): lax.ppermute(tail, axis, [(i, (i + 1) % count) for i in range(ends)])]
    ppermute x2, local copies, waits for them, and re-layouts: 4.99 us -> 0.85 us  [the longest x1 0.43 us: shards(): lax.ppermute(atmos[..., -3:], 'gy', [(i, i + 1) for i in range(count - 1)])]
    ppermute x4 -> x3, starting transfers between devices: 13.9 us -> 10.1 us  [extended(): lax.ppermute(head, axis, [((i + 1) % count, i) for i in range(ends)])]
  transfers between devices with their start and end apart: 8 -> 10, of which waited for: 0 -> 2; matrix products, arithmetic and copies ran while one was open for 21% -> 19% of each run, Pallas kernels for 0% -> 0%
where the time goes in v9:
time: 76 us; the launch traced here: 75.3 us
  starting transfers between devices  30.5 us (40%)
  Pallas kernels  18.6 us (24%)
  other arithmetic  10.1 us (13%)
  local copies, waits for them, and re-layouts  8.99 us (12%)
  waiting for transfers between devices  2.77 us (4%)
  matrix products  2.51 us (3%)
  between operations  1.74 us (2%)
    pallas_call x1, Pallas kernels, fire_step(): pl.pallas_call(fire_kernel, out_shape=(jax.ShapeDtypeStruct((rows, cols),...  11.9 us
    ppermute x3, starting transfers between devices, extended(): lax.ppermute(head, axis, [((i + 1) % count, i) for i in range(ends)])  10.1 us
    ppermute x3, starting transfers between devices, extended(): lax.ppermute(tail, axis, [(i, (i + 1) % count) for i in range(ends)])  9.44 us
    pallas_call x1, Pallas kernels, atmos_call(): pl.pallas_call(atmos_kernel, grid=(fields,), out_shape=jax.ShapeDtypeStru...  6.78 us
    ppermute x1, starting transfers between devices, shards(): lax.ppermute(atmos[..., -3:], 'gy', [(i, i + 1) for i in range(count - 1)])  5.03 us
    concatenate x1, local copies, waits for them, and re-layouts, shards(): stacked = jnp.concatenate([room, stacked, room], axis=2)  2.19 us
    unnamed x35, local copies, waits for them, and re-layouts  2.15 us
    ppermute x1, starting transfers between devices, shards(): lax.ppermute(atmos[:, :, -3:], 'gx', [(i, i + 1) for i in range(count_x -...  2.02 us
  transfers between devices with their start and end apart: 10, of which 2 were waited for; matrix products, arithmetic and copies ran while one was open for 19% of the time, Pallas kernels for 0%

profile of v9, /device:TPU:120, one launch (start us, length us, event | category | flops | bytes accessed | tf_op | source)
XLA Modules:
  0.0 75.3 jit_solution(4503102702205264735)
XLA Ops:
  0.6 0.0 copy-start
  1.4 0.7 fusion.25
  2.1 0.7 fusion.33
  2.8 0.1 broadcast_in_dim.52
  2.9 0.1 broadcast_in_dim.53
  2.9 1.0 %convert_bitcast_fusion = f32[1,64,1024]{2,1,0:T(8,128)S(1)} fusion(s32[64,1024]{1,0:T(8,128)} %param.14), kind=kLoop, calls=%fused_computation.15 | loop fusion | flops 65536 | bytes 524288 | tf_op jit(solution)/shard_map/stack | solution.py:331
  3.9 0.0 copy-start.1
  4.0 0.7 copy-done.1
  4.6 1.6 %pad_maximum_fusion.4 = (f32[3,16,1024]{2,1,0:T(8,128)}, f32[3,16,1024]{2,1,0:T(8,128)}) fusion(f32[1,64,1024]{2,1,0:T(8,128)S(1)} %broadcast_in_dim.54, f32[1,64,1024]{2,1,0:T(8,128)S(1)} %convert_bitcast_fusion, f32[1,64,1024]{2,1,0:T(8,128)} %bitcast.31), kind=kLoop, calls=%fused_computation.18 | loop fusion | flops 196608 | bytes 1179648 | tf_op jit(solution)/shard_map/slice | solution.py:22
  6.3 1.9 %collective-permute-start.4 = (f32[3,16,1024]{2,1,0:T(8,128)}, f32[3,16,1024]{2,1,0:T(8,128)}, u32[]{:S(2)}, u32[]{:S(2)}) collective-permute-start(f32[3,16,1024]{2,1,0:T(8,128)} %get-tuple-element.15), channel_id=1, source_target_pairs={{0,8},{8,16},{16,24},{24,32},{32,40},{40,48},{48,56},{56,64},{64,7... | collective-permute-start | bytes 589832 | tf_op jit(solution)/shard_map/ppermute | solution.py:25
  8.2 5.8 %collective-permute-start.5 = (f32[3,16,1024]{2,1,0:T(8,128)}, f32[3,16,1024]{2,1,0:T(8,128)}, u32[]{:S(2)}, u32[]{:S(2)}) collective-permute-start(f32[3,16,1024]{2,1,0:T(8,128)} %get-tuple-element.16), channel_id=1, source_target_pairs={{8,0},{16,8},{24,16},{32,24},{40,32},{48,40},{56,48},{64,56},{72,6... | collective-permute-start | bytes 589832 | tf_op jit(solution)/shard_map/ppermute | solution.py:27
  14.0 1.1 %fusion.39 = (f32[5,48,3,128]{3,2,1,0:T(4,128)}, f32[5,48,3,128]{3,2,1,0:T(4,128)}) fusion(f32[5,48,8,128]{3,2,1,0:T(8,128)S(1)} %copy-done), kind=kLoop, calls=%fused_computation.83 | loop fusion | bytes 1474560 | tf_op jit(solution)/shard_map/slice | solution.py:309
  15.1 1.9 %collective-permute-start.1 = (f32[5,48,3,128]{3,2,1,0:T(4,128)}, f32[5,48,3,128]{3,2,1,0:T(4,128)}, u32[]{:S(2)}, u32[]{:S(2)}) collective-permute-start(f32[5,48,3,128]{3,2,1,0:T(4,128)} %get-tuple-element.13), channel_id=1, source_target_pairs={{8,0},{16,8},{24,16},{32,24},{40,32},{48,40},{56,48},{64,56},{72,6... | collective-permute-start | bytes 1105928 | tf_op jit(solution)/shard_map/ppermute | solution.py:309
  17.0 0.3 fusion.38
  17.3 0.0 copy-start.14
  17.4 0.0 copy-start.15
  17.4 0.4 copy.25
  17.8 2.0 %collective-permute-start.2 = (f32[5,48,8,3]{1,2,3,0:T(8,128)S(1)}, f32[5,48,8,3]{1,2,3,0:T(8,128)S(1)}, u32[]{:S(2)}, u32[]{:S(2)}) collective-permute-start(f32[5,48,8,3]{1,2,3,0:T(8,128)S(1)} %copy.25), channel_id=1, source_target_pairs={{1,0},{2,1},{3,2},{4,3},{5,4},{6,5},{7,6},{9,8},{10,9},{11,10},{12... | collective-permute-start | bytes 69128 | tf_op jit(solution)/shard_map/ppermute | solution.py:312
  19.8 0.4 copy.26
  20.2 5.0 %collective-permute-start.3 = (f32[5,48,8,3]{1,2,3,0:T(8,128)S(1)}, f32[5,48,8,3]{1,2,3,0:T(8,128)S(1)}, u32[]{:S(2)}, u32[]{:S(2)}) collective-permute-start(f32[5,48,8,3]{1,2,3,0:T(8,128)S(1)} %copy.26), channel_id=1, source_target_pairs={{0,1},{1,2},{2,3},{3,4},{4,5},{5,6},{6,7},{8,9},{9,10},{10,11},{11... | collective-permute-start | bytes 69128 | tf_op jit(solution)/shard_map/ppermute | solution.py:311
  25.2 0.6 slice_bitcast_fusion
  25.8 0.5 fusion.31
  26.3 0.6 broadcast_add_fusion.2
  26.9 0.6 select_add_fusion
  27.5 0.6 broadcast_add_fusion
  28.2 0.6 multiply_exponential_fusion.p_ref
  28.7 0.7 pad_maximum_fusion.5.tab_ref
  29.4 0.7 pad.19.clone
  30.1 2.0 %collective-permute-start = (f32[5,48,3,128]{3,2,1,0:T(4,128)}, f32[5,48,3,128]{3,2,1,0:T(4,128)}, u32[]{:S(2)}, u32[]{:S(2)}) collective-permute-start(f32[5,48,3,128]{3,2,1,0:T(4,128)} %get-tuple-element.14), channel_id=1, source_target_pairs={{0,8},{8,16},{16,24},{24,32},{32,40},{40,48},{48,56},{56,64},{64,7... | collective-permute-start | bytes 1105928 | tf_op jit(solution)/shard_map/ppermute | solution.py:308
  32.1 0.4 copy.20
  32.5 0.4 copy.21
  33.0 1.3 %pad_maximum_fusion = f32[3,96,1024]{2,1,0:T(8,128)S(1)} fusion(f32[3,16,1024]{2,1,0:T(8,128)} %collective-permute-done.5, f32[1,64,1024]{2,1,0:T(8,128)} %copy-done.1, f32[1,64,1024]{2,1,0:T(8,128)S(1)} %convert_bitcast_fusion, f32[1,64,1024]{2,1,0:T(8,128)} %bitcast.32, f32[3,16,1024]{2,1,0:T(8,128)} %collective-permute-done.4), kind=kLoop, calls=%fused_computation | loop fusion | flops 1179648 | bytes 2359296 | tf_op jit(solution)/shard_map/concatenate | solution.py:23
  34.3 0.1 fusion.37
  34.4 3.7 %collective-permute-start.6 = (f32[3,96,16]{2,1,0:T(8,128)S(1)}, f32[3,96,16]{2,1,0:T(8,128)S(1)}, u32[]{:S(2)}, u32[]{:S(2)}) collective-permute-start(f32[3,96,16]{2,1,0:T(8,128)S(1)} %get-tuple-element.10), channel_id=1, source_target_pairs={{0,1},{1,2},{2,3},{3,4},{4,5},{5,6},{6,7},{8,9},{9,10},{10,11},{11... | collective-permute-start | bytes 55304 | tf_op jit(solution)/shard_map/ppermute | solution.py:25
  38.1 2.1 %collective-permute-start.7 = (f32[3,96,16]{2,1,0:T(8,128)S(1)}, f32[3,96,16]{2,1,0:T(8,128)}, u32[]{:S(2)}, u32[]{:S(2)}) collective-permute-start(f32[3,96,16]{2,1,0:T(8,128)S(1)} %get-tuple-element.9), channel_id=1, source_target_pairs={{1,0},{2,1},{3,2},{4,3},{5,4},{6,5},{7,6},{9,8},{10,9},{11,10},{12... | collective-permute-start | bytes 55304 | tf_op jit(solution)/shard_map/ppermute | solution.py:27
  40.3 0.7 slice_bitcast_fusion.1
  40.9 1.7 %collective-permute-done.lo_ref = f32[5,48,3,128]{3,2,1,0:T(4,128)} collective-permute-done((f32[5,48,3,128]{3,2,1,0:T(4,128)}, f32[5,48,3,128]{3,2,1,0:T(4,128)}, u32[]{:S(2)}, u32[]{:S(2)}) %collective-permute-start) | collective-permute-done | bytes 368672 | tf_op jit(solution)/shard_map/ppermute | solution.py:308
  42.6 0.7 slice_bitcast_fusion.2
  43.3 0.1 fusion.40
  43.4 3.8 %collective-permute-start.8 = (f32[2,14,3]{2,1,0:T(8,128)S(1)}, f32[2,14,3]{2,1,0:T(8,128)S(1)}, u32[]{:S(2)}, u32[]{:S(2)}) collective-permute-start(f32[2,14,3]{2,1,0:T(8,128)S(1)} %get-tuple-element.17), channel_id=1, source_target_pairs={{0,1},{1,2},{2,3},{3,4},{4,5},{5,6},{6,7},{8,9},{9,10},{10,11},{11... | collective-permute-start | bytes 1016 | tf_op jit(solution)/shard_map/ppermute | solution.py:25
  47.2 2.2 %collective-permute-start.9 = (f32[2,14,3]{2,1,0:T(8,128)S(1)}, f32[2,14,3]{2,1,0:T(8,128)S(1)}, u32[]{:S(2)}, u32[]{:S(2)}) collective-permute-start(f32[2,14,3]{2,1,0:T(8,128)S(1)} %get-tuple-element.18), channel_id=1, source_target_pairs={{1,0},{2,1},{3,2},{4,3},{5,4},{6,5},{7,6},{9,8},{10,9},{11,10},{12... | collective-permute-start | bytes 1016 | tf_op jit(solution)/shard_map/ppermute | solution.py:27
  49.4 1.3 %pad_maximum_fusion.1.y_ref = f32[5,48,8,128]{3,2,1,0:T(8,128)} fusion(f32[5,48,8,3]{3,2,1,0:T(8,128)S(1)} %copy.21, f32[5,48,8,3]{3,2,1,0:T(8,128)S(1)} %copy.20, f32[128]{0:T(128)S(1)} %copy-done.11), kind=kLoop, calls=%fused_computation.4 | loop fusion | flops 491520 | bytes 1029632 | tf_op jit(solution)/shard_map/concatenate | solution.py:314
  50.8 2.2 %concatenate.21.ext_ref = f32[3,96,1280]{2,1,0:T(8,128)} concatenate(f32[3,96,112]{2,1,0:T(8,128)S(1)} %broadcast_in_dim.29, f32[3,96,16]{2,1,0:T(8,128)S(1)} %collective-permute-done.6, f32[3,96,1024]{2,1,0:T(8,128)S(1)} %pad_maximum_fusion, f32[3,96,16]{2,1,0:T(8,128)} %collective-permute-done.7, f32[3,96,112]{2,1,0:T(8,128)S(1)} %broadcast_in_dim.29), dimensions={2} | concatenate | bytes 2949120 | tf_op jit(solution)/shard_map/concatenate | solution.py:334
  53.0 1.1 %collective-permute-done.9 = f32[2,14,3]{2,1,0:T(8,128)S(1)} collective-permute-done((f32[2,14,3]{2,1,0:T(8,128)S(1)}, f32[2,14,3]{2,1,0:T(8,128)S(1)}, u32[]{:S(2)}, u32[]{:S(2)}) %collective-permute-start.9) | collective-permute-done | bytes 368 | tf_op jit(solution)/shard_map/ppermute | solution.py:27
  54.1 0.5 convolution_bitcast_fusion
  54.6 2.0 %fusion.wind_ref = f32[2,96,1280]{2,1,0:T(8,128)} fusion(f32[2,96,134]{1,2,0:T(8,128)S(1)} %convolution_bitcast_fusion, f32[1280]{0:T(1024)S(1)} %copy-done.2, s32[1280]{0:T(1024)S(1)} %copy-done.5, f32[1280]{0:T(1024)S(1)} %copy-done.3, s32[1280]{0:T(1024)S(1)} %copy-done.4), kind=kOutput, calls=%fused_computation.5 | convolution fusion | flops 396039680 | bytes 1106432 | tf_op jit(solution)/shard_map/kib,jb->kij/dot_general | solution.py:145
  56.6 11.9 %shard_map.130 = (f32[64,1024]{1,0:T(8,128)}, f32[64,1024]{1,0:T(8,128)}, f32[8,128]{1,0:T(8,128)}) custom-call(f32[52]{0:T(128)} %pad_maximum_fusion.5.tab_ref, f32[3,96,1280]{2,1,0:T(8,128)} %concatenate.21.ext_ref, f32[2,96,1280]{2,1,0:T(8,128)} %fusion.wind_ref, f32[64,1024]{1,0:T(8,128)} %fuel_ref.1), custom_call_target="tpu_custom_call" | custom-call | tf_op jit(solution)/shard_map/pallas_call | solution.py:219
  68.5 6.8 %shard_map.131 = f32[5,48,8,128]{3,2,1,0:T(8,128)} custom-call(f32[48]{0:T(128)} %multiply_exponential_fusion.p_ref, f32[5,48,8,128]{3,2,1,0:T(8,128)} %v_ref.1, f32[5,48,3,128]{3,2,1,0:T(4,128)} %collective-permute-done.lo_ref, f32[5,48,3,128]{3,2,1,0:T(4,128)} %collective-permute-done.1.hi_ref, f32[5,48,8,128]{3,2,1,0:T(8,128)} %pad_maximum_fusion.1.y_ref, ...), custom_call_target="tpu_custom_call" | custom-call | tf_op jit(solution)/shard_map/pallas_call | solution.py:269
  (40 shorter events, 0.1 us)
Async XLA Ops:
  0.6 13.3 %copy-start = (f32[5,48,8,128]{3,2,1,0:T(8,128)S(1)}, f32[5,48,8,128]{3,2,1,0:T(8,128)}, u32[]{:S(2)}) copy-start(f32[5,48,8,128]{3,2,1,0:T(8,128)} %v_ref.1) | copy-start | bytes 2949124
  3.9 0.7 copy-start.1
  6.3 26.7 %collective-permute-start.4 = (f32[3,16,1024]{2,1,0:T(8,128)}, f32[3,16,1024]{2,1,0:T(8,128)}, u32[]{:S(2)}, u32[]{:S(2)}) collective-permute-start(f32[3,16,1024]{2,1,0:T(8,128)} %get-tuple-element.15), channel_id=1, source_target_pairs={{0,8},{8,16},{16,24},{24,32},{32,40},{40,48},{48,56},{56,64},{64,7... | collective-permute-start | bytes 589832 | tf_op jit(solution)/shard_map/ppermute | solution.py:25
  8.2 24.8 %collective-permute-start.5 = (f32[3,16,1024]{2,1,0:T(8,128)}, f32[3,16,1024]{2,1,0:T(8,128)}, u32[]{:S(2)}, u32[]{:S(2)}) collective-permute-start(f32[3,16,1024]{2,1,0:T(8,128)} %get-tuple-element.16), channel_id=1, source_target_pairs={{8,0},{16,8},{24,16},{32,24},{40,32},{48,40},{56,48},{64,56},{72,6... | collective-permute-start | bytes 589832 | tf_op jit(solution)/shard_map/ppermute | solution.py:27
  15.1 25.2 %collective-permute-start.1 = (f32[5,48,3,128]{3,2,1,0:T(4,128)}, f32[5,48,3,128]{3,2,1,0:T(4,128)}, u32[]{:S(2)}, u32[]{:S(2)}) collective-permute-start(f32[5,48,3,128]{3,2,1,0:T(4,128)} %get-tuple-element.13), channel_id=1, source_target_pairs={{8,0},{16,8},{24,16},{32,24},{40,32},{48,40},{56,48},{64,56},{72,6... | collective-permute-start | bytes 1105928 | tf_op jit(solution)/shard_map/ppermute | solution.py:309
  17.3 11.4 %copy-start.12 = (f32[13]{0:T(128)S(1)}, f32[13]{0:T(128)}, u32[]{:S(2)}) copy-start(f32[13]{0:T(128)} %param.18) | copy-start | bytes 160
  17.3 11.4 %copy-start.13 = (f32[13]{0:T(128)S(1)}, f32[13]{0:T(128)}, u32[]{:S(2)}) copy-start(f32[13]{0:T(128)} %param.17) | copy-start | bytes 160
  17.3 11.4 %copy-start.14 = (f32[13]{0:T(128)S(1)}, f32[13]{0:T(128)}, u32[]{:S(2)}) copy-start(f32[13]{0:T(128)} %param.16) | copy-start | bytes 160
  17.4 11.4 %copy-start.15 = (f32[13]{0:T(128)S(1)}, f32[13]{0:T(128)}, u32[]{:S(2)}) copy-start(f32[13]{0:T(128)} %param.15) | copy-start | bytes 160
  17.8 12.3 %collective-permute-start.2 = (f32[5,48,8,3]{1,2,3,0:T(8,128)S(1)}, f32[5,48,8,3]{1,2,3,0:T(8,128)S(1)}, u32[]{:S(2)}, u32[]{:S(2)}) collective-permute-start(f32[5,48,8,3]{1,2,3,0:T(8,128)S(1)} %copy.25), channel_id=1, source_target_pairs={{1,0},{2,1},{3,2},{4,3},{5,4},{6,5},{7,6},{9,8},{10,9},{11,10},{12... | collective-permute-start | bytes 69128 | tf_op jit(solution)/shard_map/ppermute | solution.py:312
  20.2 12.4 %collective-permute-start.3 = (f32[5,48,8,3]{1,2,3,0:T(8,128)S(1)}, f32[5,48,8,3]{1,2,3,0:T(8,128)S(1)}, u32[]{:S(2)}, u32[]{:S(2)}) collective-permute-start(f32[5,48,8,3]{1,2,3,0:T(8,128)S(1)} %copy.26), channel_id=1, source_target_pairs={{0,1},{1,2},{2,3},{3,4},{4,5},{5,6},{6,7},{8,9},{9,10},{10,11},{11... | collective-permute-start | bytes 69128 | tf_op jit(solution)/shard_map/ppermute | solution.py:311
  30.1 12.6 %collective-permute-start = (f32[5,48,3,128]{3,2,1,0:T(4,128)}, f32[5,48,3,128]{3,2,1,0:T(4,128)}, u32[]{:S(2)}, u32[]{:S(2)}) collective-permute-start(f32[5,48,3,128]{3,2,1,0:T(4,128)} %get-tuple-element.14), channel_id=1, source_target_pairs={{0,8},{8,16},{16,24},{24,32},{32,40},{40,48},{48,56},{56,64},{64,7... | collective-permute-start | bytes 1105928 | tf_op jit(solution)/shard_map/ppermute | solution.py:308
  33.0 10.3 %copy-start.6 = (f32[2,1,8,128]{3,2,0,1:T(8,128)S(1)}, f32[2,1,8,128]{3,2,0,1:T(8,128)}, u32[]{:S(2)}) copy-start(f32[2,1,8,128]{3,2,0,1:T(8,128)} %slice_bitcast_fusion) | copy-start | bytes 24580
  33.0 16.5 %copy-start.11 = (f32[128]{0:T(128)S(1)}, f32[128]{0:T(128)}, u32[]{:S(2)}) copy-start(f32[128]{0:T(128)} %pad.19.clone) | copy-start | bytes 1540
  34.4 16.3 %collective-permute-start.6 = (f32[3,96,16]{2,1,0:T(8,128)S(1)}, f32[3,96,16]{2,1,0:T(8,128)S(1)}, u32[]{:S(2)}, u32[]{:S(2)}) collective-permute-start(f32[3,96,16]{2,1,0:T(8,128)S(1)} %get-tuple-element.10), channel_id=1, source_target_pairs={{0,1},{1,2},{2,3},{3,4},{4,5},{5,6},{6,7},{8,9},{9,10},{10,11},{11... | collective-permute-start | bytes 55304 | tf_op jit(solution)/shard_map/ppermute | solution.py:25
  38.1 12.6 %collective-permute-start.7 = (f32[3,96,16]{2,1,0:T(8,128)S(1)}, f32[3,96,16]{2,1,0:T(8,128)}, u32[]{:S(2)}, u32[]{:S(2)}) collective-permute-start(f32[3,96,16]{2,1,0:T(8,128)S(1)} %get-tuple-element.9), channel_id=1, source_target_pairs={{1,0},{2,1},{3,2},{4,3},{5,4},{6,5},{7,6},{9,8},{10,9},{11,10},{12... | collective-permute-start | bytes 55304 | tf_op jit(solution)/shard_map/ppermute | solution.py:27
  43.4 9.6 %collective-permute-start.8 = (f32[2,14,3]{2,1,0:T(8,128)S(1)}, f32[2,14,3]{2,1,0:T(8,128)S(1)}, u32[]{:S(2)}, u32[]{:S(2)}) collective-permute-start(f32[2,14,3]{2,1,0:T(8,128)S(1)} %get-tuple-element.17), channel_id=1, source_target_pairs={{0,1},{1,2},{2,3},{3,4},{4,5},{5,6},{6,7},{8,9},{9,10},{10,11},{11... | collective-permute-start | bytes 1016 | tf_op jit(solution)/shard_map/ppermute | solution.py:25
  47.2 6.8 %collective-permute-start.9 = (f32[2,14,3]{2,1,0:T(8,128)S(1)}, f32[2,14,3]{2,1,0:T(8,128)S(1)}, u32[]{:S(2)}, u32[]{:S(2)}) collective-permute-start(f32[2,14,3]{2,1,0:T(8,128)S(1)} %get-tuple-element.18), channel_id=1, source_target_pairs={{1,0},{2,1},{3,2},{4,3},{5,4},{6,5},{7,6},{9,8},{10,9},{11,10},{12... | collective-permute-start | bytes 1016 | tf_op jit(solution)/shard_map/ppermute | solution.py:27
  50.7 3.3 %copy-start.7 = (f32[96]{0:T(128)S(1)}, f32[96]{0:T(128)}, u32[]{:S(2)}) copy-start(f32[96]{0:T(128)} %get-tuple-element.19) | copy-start | bytes 1156
  50.7 3.3 %copy-start.8 = (f32[96]{0:T(128)S(1)}, f32[96]{0:T(128)}, u32[]{:S(2)}) copy-start(f32[96]{0:T(128)} %get-tuple-element.20) | copy-start | bytes 1156
  50.8 3.3 %copy-start.9 = (s32[96]{0:T(128)S(1)}, s32[96]{0:T(128)}, u32[]{:S(2)}) copy-start(s32[96]{0:T(128)} %get-tuple-element.21) | copy-start | bytes 1156
  50.8 3.3 %copy-start.10 = (s32[96]{0:T(128)S(1)}, s32[96]{0:T(128)}, u32[]{:S(2)}) copy-start(s32[96]{0:T(128)} %get-tuple-element.22) | copy-start | bytes 1156
  50.8 3.8 %copy-start.2 = (f32[1280]{0:T(1024)S(1)}, f32[1280]{0:T(1024)}, u32[]{:S(2)}) copy-start(f32[1280]{0:T(1024)} %get-tuple-element.23) | copy-start | bytes 15364
  50.8 3.8 %copy-start.3 = (f32[1280]{0:T(1024)S(1)}, f32[1280]{0:T(1024)}, u32[]{:S(2)}) copy-start(f32[1280]{0:T(1024)} %get-tuple-element.24) | copy-start | bytes 15364
  50.8 3.8 %copy-start.4 = (s32[1280]{0:T(1024)S(1)}, s32[1280]{0:T(1024)}, u32[]{:S(2)}) copy-start(s32[1280]{0:T(1024)} %get-tuple-element.25) | copy-start | bytes 15364
  50.8 3.8 %copy-start.5 = (s32[1280]{0:T(1024)S(1)}, s32[1280]{0:T(1024)}, u32[]{:S(2)}) copy-start(s32[1280]{0:T(1024)} %get-tuple-element.26) | copy-start | bytes 15364

commit v10 on v9

--- a/solution.py
+++ b/solution.py
@@ -313,7 +313,6 @@
     room = jnp.zeros(atmos.shape[:3] + (atmos_cols - 6,), jnp.float32)
     y_ends = jnp.concatenate([from_hi, room, from_lo], axis=3)
     along_x = jnp.concatenate([x_lo[0:2, 0:1], atmos[0:2, 0:1], x_hi[0:2, 0:1]], axis=2)
-    surface = extended(along_x[:, 0], (("gy", 2),), 3)
     slots = burn_tiles.reshape(-1)
     listed = burn_count.reshape(())
     tiles_dev = substep_count.size
@@ -329,7 +328,33 @@
         fire_rows, fire_cols
     )
     stacked = jnp.stack([level_set, fuel_map.astype(jnp.float32), nsteps])
-    stacked = extended(stacked, (("gx", 1), ("gy", 2)), halo)
+    stacked = extended(stacked, (("gx", 1),), halo)
+    surf = along_x[:, 0]
+    fire_count = stacked.shape[0]
+
+    def with_surface(fire_part, surf_part):
+        room = (
+            (0, 0),
+            (0, fire_part.shape[1] - surf_part.shape[1]),
+            (0, fire_part.shape[2] - surf_part.shape[2]),
+        )
+        return jnp.concatenate([fire_part, jnp.pad(surf_part, room)], axis=0)
+
+    got_lo = lax.ppermute(
+        with_surface(stacked[..., -halo:], surf[..., -3:]),
+        "gy",
+        [(i, i + 1) for i in range(count - 1)],
+    )
+    got_hi = lax.ppermute(
+        with_surface(stacked[..., :halo], surf[..., :3]),
+        "gy",
+        [(i + 1, i) for i in range(count - 1)],
+    )
+    srows = surf.shape[1]
+    stacked = jnp.concatenate([got_lo[:fire_count], stacked, got_hi[:fire_count]], axis=2)
+    surface = jnp.concatenate(
+        [got_lo[fire_count:, :srows, :3], surf, got_hi[fire_count:, :srows, :3]], axis=2
+    )
     room = jnp.zeros(stacked.shape[:2] + (HALO_Y - halo,), jnp.float32)
     stacked = jnp.concatenate([room, stacked, room], axis=2)
     winds = surface_winds(surface, fire_rows, fire_cols, halo, HALO_Y)

time: 76 us -> 81.3 us (1.070)
  waiting for transfers between devices: 2.77 us -> 15.7 us
  starting transfers between devices: 30.5 us -> 24.5 us
  other arithmetic: 10.1 us -> 7.82 us
    ppermute x3 -> x1, starting transfers between devices: 9.44 us -> 1.91 us  [extended(): lax.ppermute(tail, axis, [(i, (i + 1) % count) for i in range(ends)])]
    ppermute x0 -> x2, starting transfers between devices: none -> 6.02 us  [the longest x1 4.1 us: shards(): lax.ppermute(with_surface(stacked[..., :halo], surf[..., :3]), 'gy', [(i...]
    ppermute x1, waiting for transfers between devices: 1.69 us -> 7.68 us  [shards(): lax.ppermute(atmos[:, :, -3:], 'gx', [(i, i + 1) for i in range(count_x -...]
    ppermute x3 -> x1, starting transfers between devices: 10.1 us -> 5.75 us  [extended(): lax.ppermute(head, axis, [((i + 1) % count, i) for i in range(ends)])]
    ppermute x1, waiting for transfers between devices: 0.01 us -> 4.08 us  [shards(): lax.ppermute(atmos[..., :3], 'gy', [(i + 1, i) for i in range(count - 1)])]
    ppermute x0 -> x2, waiting for transfers between devices: none -> 3.89 us  [the longest x1 3.15 us: shards(): lax.ppermute(with_surface(stacked[..., :halo], surf[..., :3]), 'gy', [(i...]
    slice x2 -> x6, local copies, waits for them, and re-layouts: 0.17 us -> 1.63 us  [the longest x1 0.72 us: shards(): got_lo[fire_count:, :srows, :3]]
    add x2, other arithmetic: 1.21 us -> 0.03 us  [interp_table(): lower = jnp.where(within < ratio // 2, coarse, coarse + 1) + 2]
  transfers between devices with their start and end apart: 10 -> 8, of which waited for: 2 -> 4; matrix products, arithmetic and copies ran while one was open for 19% -> 10% of each run, Pallas kernels for 0% -> 0%
where the time goes in v10:
time: 81.3 us; the launch traced here: 79.9 us
  starting transfers between devices  24.5 us (30%)
  Pallas kernels  18.7 us (23%)
  waiting for transfers between devices  15.7 us (19%)
  local copies, waits for them, and re-layouts  9.1 us (11%)
  other arithmetic  7.82 us (10%)
  matrix products  2.51 us (3%)
  between operations  1.63 us (2%)
    pallas_call x1, Pallas kernels, fire_step(): pl.pallas_call(fire_kernel, out_shape=(jax.ShapeDtypeStruct((rows, cols),...  11.9 us
    ppermute x1, waiting for transfers between devices, shards(): lax.ppermute(atmos[:, :, -3:], 'gx', [(i, i + 1) for i in range(count_x -...  7.68 us
    pallas_call x1, Pallas kernels, atmos_call(): pl.pallas_call(atmos_kernel, grid=(fields,), out_shape=jax.ShapeDtypeStru...  6.81 us
    ppermute x1, starting transfers between devices, extended(): lax.ppermute(head, axis, [((i + 1) % count, i) for i in range(ends)])  5.75 us
    ppermute x1, starting transfers between devices, shards(): lax.ppermute(atmos[..., -3:], 'gy', [(i, i + 1) for i in range(count - 1)])  5.03 us
    ppermute x1, starting transfers between devices, shards(): lax.ppermute(with_surface(stacked[..., :halo], surf[..., :3]), 'gy', [(i...  4.1 us
    ppermute x1, waiting for transfers between devices, shards(): lax.ppermute(atmos[..., :3], 'gy', [(i + 1, i) for i in range(count - 1)])  4.08 us
    ppermute x1, waiting for transfers between devices, shards(): lax.ppermute(with_surface(stacked[..., :halo], surf[..., :3]), 'gy', [(i...  3.15 us
  transfers between devices with their start and end apart: 8, of which 4 were waited for; matrix products, arithmetic and copies ran while one was open for 10% of the time, Pallas kernels for 0%

profile of v10, /device:TPU:120, one launch (start us, length us, event | category | flops | bytes accessed | tf_op | source)
XLA Modules:
  0.0 79.9 jit_solution(11810606086152743480)
XLA Ops:
  0.6 0.0 copy-start
  1.4 0.7 fusion.25
  2.1 0.7 fusion.33
  2.8 0.1 broadcast_in_dim.52
  2.9 0.1 broadcast_in_dim.53
  2.9 1.0 %convert_bitcast_fusion = f32[1,64,1024]{2,1,0:T(8,128)S(1)} fusion(s32[64,1024]{1,0:T(8,128)} %param.14), kind=kLoop, calls=%fused_computation.15 | loop fusion | flops 65536 | bytes 524288 | tf_op jit(solution)/shard_map/stack | solution.py:330
  3.9 0.0 copy-start.1
  4.0 0.7 copy-done.1
  4.6 1.6 %pad_maximum_fusion.4 = (f32[3,16,1024]{2,1,0:T(8,128)}, f32[3,16,1024]{2,1,0:T(8,128)}) fusion(f32[1,64,1024]{2,1,0:T(8,128)S(1)} %broadcast_in_dim.54, f32[1,64,1024]{2,1,0:T(8,128)S(1)} %convert_bitcast_fusion, f32[1,64,1024]{2,1,0:T(8,128)} %bitcast.31), kind=kLoop, calls=%fused_computation.21 | loop fusion | flops 196608 | bytes 1179648 | tf_op jit(solution)/shard_map/slice | solution.py:22
  6.3 1.9 %collective-permute-start.4 = (f32[3,16,1024]{2,1,0:T(8,128)}, f32[3,16,1024]{2,1,0:T(8,128)}, u32[]{:S(2)}, u32[]{:S(2)}) collective-permute-start(f32[3,16,1024]{2,1,0:T(8,128)} %get-tuple-element.15), channel_id=1, source_target_pairs={{0,8},{8,16},{16,24},{24,32},{32,40},{40,48},{48,56},{56,64},{64,7... | collective-permute-start | bytes 589832 | tf_op jit(solution)/shard_map/ppermute | solution.py:25
  8.2 5.8 %collective-permute-start.5 = (f32[3,16,1024]{2,1,0:T(8,128)}, f32[3,16,1024]{2,1,0:T(8,128)}, u32[]{:S(2)}, u32[]{:S(2)}) collective-permute-start(f32[3,16,1024]{2,1,0:T(8,128)} %get-tuple-element.16), channel_id=1, source_target_pairs={{8,0},{16,8},{24,16},{32,24},{40,32},{48,40},{56,48},{64,56},{72,6... | collective-permute-start | bytes 589832 | tf_op jit(solution)/shard_map/ppermute | solution.py:27
  14.0 1.1 %fusion.39 = (f32[5,48,3,128]{3,2,1,0:T(4,128)}, f32[5,48,3,128]{3,2,1,0:T(4,128)}) fusion(f32[5,48,8,128]{3,2,1,0:T(8,128)S(1)} %copy-done), kind=kLoop, calls=%fused_computation.86 | loop fusion | bytes 1474560 | tf_op jit(solution)/shard_map/slice | solution.py:309
  15.1 1.9 %collective-permute-start.1 = (f32[5,48,3,128]{3,2,1,0:T(4,128)}, f32[5,48,3,128]{3,2,1,0:T(4,128)}, u32[]{:S(2)}, u32[]{:S(2)}) collective-permute-start(f32[5,48,3,128]{3,2,1,0:T(4,128)} %get-tuple-element.13), channel_id=1, source_target_pairs={{8,0},{16,8},{24,16},{32,24},{40,32},{48,40},{56,48},{64,56},{72,6... | collective-permute-start | bytes 1105928 | tf_op jit(solution)/shard_map/ppermute | solution.py:309
  17.0 0.3 fusion.38
  17.3 0.0 copy-start.5
  17.3 0.0 copy-start.6
  17.3 0.0 copy-start.7
  17.4 0.4 copy.62
  17.7 5.0 %collective-permute-start.3 = (f32[5,48,8,3]{1,2,3,0:T(8,128)S(1)}, f32[5,48,8,3]{1,2,3,0:T(8,128)S(1)}, u32[]{:S(2)}, u32[]{:S(2)}) collective-permute-start(f32[5,48,8,3]{1,2,3,0:T(8,128)S(1)} %copy.62), channel_id=1, source_target_pairs={{0,1},{1,2},{2,3},{3,4},{4,5},{5,6},{6,7},{8,9},{9,10},{10,11},{11... | collective-permute-start | bytes 69128 | tf_op jit(solution)/shard_map/ppermute | solution.py:311
  22.8 0.4 copy.61
  23.2 1.9 %collective-permute-start.2 = (f32[5,48,8,3]{1,2,3,0:T(8,128)S(1)}, f32[5,48,8,3]{1,2,3,0:T(8,128)S(1)}, u32[]{:S(2)}, u32[]{:S(2)}) collective-permute-start(f32[5,48,8,3]{1,2,3,0:T(8,128)S(1)} %copy.61), channel_id=1, source_target_pairs={{1,0},{2,1},{3,2},{4,3},{5,4},{6,5},{7,6},{9,8},{10,9},{11,10},{12... | collective-permute-start | bytes 69128 | tf_op jit(solution)/shard_map/ppermute | solution.py:312
  25.2 0.5 multiply_exponential_fusion.p_ref
  25.7 0.6 pad_maximum_fusion.5.tab_ref
  26.3 0.1 pad.32.clone
  26.4 4.1 %collective-permute-done.2 = f32[5,48,8,3]{1,2,3,0:T(8,128)S(1)} collective-permute-done((f32[5,48,8,3]{1,2,3,0:T(8,128)S(1)}, f32[5,48,8,3]{1,2,3,0:T(8,128)S(1)}, u32[]{:S(2)}, u32[]{:S(2)}) %collective-permute-start.2) | collective-permute-done | bytes 23072 | tf_op jit(solution)/shard_map/ppermute | solution.py:312
  30.5 1.9 %collective-permute-start = (f32[5,48,3,128]{3,2,1,0:T(4,128)}, f32[5,48,3,128]{3,2,1,0:T(4,128)}, u32[]{:S(2)}, u32[]{:S(2)}) collective-permute-start(f32[5,48,3,128]{3,2,1,0:T(4,128)} %get-tuple-element.14), channel_id=1, source_target_pairs={{0,8},{8,16},{16,24},{24,32},{32,40},{40,48},{48,56},{56,64},{64,7... | collective-permute-start | bytes 1105928 | tf_op jit(solution)/shard_map/ppermute | solution.py:308
  32.4 0.4 copy.56
  32.9 0.4 copy.57
  33.3 0.0 collective-permute-done.4
  33.3 1.3 %pad_maximum_fusion = f32[3,96,1024]{2,1,0:T(8,128)S(1)} fusion(f32[3,16,1024]{2,1,0:T(8,128)} %collective-permute-done.5, f32[1,64,1024]{2,1,0:T(8,128)} %copy-done.1, f32[1,64,1024]{2,1,0:T(8,128)S(1)} %convert_bitcast_fusion, f32[1,64,1024]{2,1,0:T(8,128)} %bitcast.32, f32[3,16,1024]{2,1,0:T(8,128)} %collective-permute-done.4), kind=kLoop, calls=%fused_computation | loop fusion | flops 1179648 | bytes 2359296 | tf_op jit(solution)/shard_map/concatenate | solution.py:23
  34.6 0.1 fusion.37
  34.7 0.7 slice_bitcast_fusion.1
  35.4 7.7 %collective-permute-done.lo_ref = f32[5,48,3,128]{3,2,1,0:T(4,128)} collective-permute-done((f32[5,48,3,128]{3,2,1,0:T(4,128)}, f32[5,48,3,128]{3,2,1,0:T(4,128)}, u32[]{:S(2)}, u32[]{:S(2)}) %collective-permute-start) | collective-permute-done | bytes 368672 | tf_op jit(solution)/shard_map/ppermute | solution.py:308
  43.1 0.7 slice_bitcast_fusion.2
  43.8 0.1 fusion.40
  43.9 1.9 %collective-permute-start.6 = (f32[5,96,16]{2,1,0:T(8,128)S(1)}, f32[5,96,16]{2,1,0:T(8,128)S(1)}, u32[]{:S(2)}, u32[]{:S(2)}) collective-permute-start(f32[5,96,16]{2,1,0:T(8,128)S(1)} %select_maximum_fusion.1), channel_id=1, source_target_pairs={{0,1},{1,2},{2,3},{3,4},{4,5},{5,6},{6,7},{8,9},{9,10},{10,11},{11... | collective-permute-start | bytes 92168 | tf_op jit(solution)/shard_map/ppermute | solution.py:343
  45.8 4.1 %collective-permute-start.7 = (f32[5,96,16]{2,1,0:T(8,128)S(1)}, f32[5,96,16]{2,1,0:T(8,128)S(1)}, u32[]{:S(2)}, u32[]{:S(2)}) collective-permute-start(f32[5,96,16]{2,1,0:T(8,128)S(1)} %select_maximum_fusion), channel_id=1, source_target_pairs={{1,0},{2,1},{3,2},{4,3},{5,4},{6,5},{7,6},{9,8},{10,9},{11,10},{12... | collective-permute-start | bytes 92168 | tf_op jit(solution)/shard_map/ppermute | solution.py:348
  49.9 1.3 %pad_maximum_fusion.1.y_ref = f32[5,48,8,128]{3,2,1,0:T(8,128)} fusion(f32[5,48,8,3]{3,2,1,0:T(8,128)S(1)} %copy.57, f32[5,48,8,3]{3,2,1,0:T(8,128)S(1)} %copy.56, f32[128]{0:T(128)S(1)} %pad.32.clone), kind=kLoop, calls=%fused_computation.4 | loop fusion | flops 491520 | bytes 1029632 | tf_op jit(solution)/shard_map/concatenate | solution.py:314
  51.2 0.7 collective-permute-done.6
  52.0 3.1 %collective-permute-done.7 = f32[5,96,16]{2,1,0:T(8,128)S(1)} collective-permute-done((f32[5,96,16]{2,1,0:T(8,128)S(1)}, f32[5,96,16]{2,1,0:T(8,128)S(1)}, u32[]{:S(2)}, u32[]{:S(2)}) %collective-permute-start.7) | collective-permute-done | bytes 30752 | tf_op jit(solution)/shard_map/ppermute | solution.py:348
  55.1 0.7 copy-done.3
  55.8 1.4 %concatenate.30.ext_ref = f32[3,96,1280]{2,1,0:T(8,128)} concatenate(f32[3,96,112]{2,1,0:T(8,128)S(1)} %broadcast_in_dim.29, f32[3,96,16]{2,1,0:T(8,128)S(1)} %slice.72, f32[3,96,1024]{2,1,0:T(8,128)S(1)} %pad_maximum_fusion, f32[3,96,16]{2,1,0:T(8,128)S(1)} %slice.75, f32[3,96,112]{2,1,0:T(8,128)S(1)} %broadcast_in_dim.29), dimensions={2} | concatenate | bytes 2949120 | tf_op jit(solution)/shard_map/concatenate | solution.py:359
  57.2 0.7 slice.76
  57.9 0.7 slice.77
  58.7 0.5 convolution_bitcast_fusion
  59.2 2.0 %fusion.wind_ref = f32[2,96,1280]{2,1,0:T(8,128)} fusion(f32[2,96,134]{1,2,0:T(8,128)S(1)} %convolution_bitcast_fusion, f32[1280]{0:T(1024)S(1)} %get-tuple-element.23, s32[1280]{0:T(1024)S(1)} %get-tuple-element.26, f32[1280]{0:T(1024)S(1)} %get-tuple-element.24, s32[1280]{0:T(1024)S(1)} %get-tuple-element.25), kind=kOutput, calls=%fused_computation.5 | convolution fusion | flops 396039680 | bytes 1106432 | tf_op jit(solution)/shard_map/kib,jb->kij/dot_general | solution.py:145
  61.2 11.9 %shard_map.130 = (f32[64,1024]{1,0:T(8,128)}, f32[64,1024]{1,0:T(8,128)}, f32[8,128]{1,0:T(8,128)}) custom-call(f32[52]{0:T(128)} %pad_maximum_fusion.5.tab_ref, f32[3,96,1280]{2,1,0:T(8,128)} %concatenate.30.ext_ref, f32[2,96,1280]{2,1,0:T(8,128)} %fusion.wind_ref, f32[64,1024]{1,0:T(8,128)} %fuel_ref.1), custom_call_target="tpu_custom_call" | custom-call | tf_op jit(solution)/shard_map/pallas_call | solution.py:219
  73.0 6.8 %shard_map.131 = f32[5,48,8,128]{3,2,1,0:T(8,128)} custom-call(f32[48]{0:T(128)} %multiply_exponential_fusion.p_ref, f32[5,48,8,128]{3,2,1,0:T(8,128)} %v_ref.1, f32[5,48,3,128]{3,2,1,0:T(4,128)} %collective-permute-done.lo_ref, f32[5,48,3,128]{3,2,1,0:T(4,128)} %collective-permute-done.1.hi_ref, f32[5,48,8,128]{3,2,1,0:T(8,128)} %pad_maximum_fusion.1.y_ref, ...), custom_call_target="tpu_custom_call" | custom-call | tf_op jit(solution)/shard_map/pallas_call | solution.py:269
  (26 shorter events, 0.2 us)
Async XLA Ops:
  0.6 13.3 %copy-start = (f32[5,48,8,128]{3,2,1,0:T(8,128)S(1)}, f32[5,48,8,128]{3,2,1,0:T(8,128)}, u32[]{:S(2)}) copy-start(f32[5,48,8,128]{3,2,1,0:T(8,128)} %v_ref.1) | copy-start | bytes 2949124
  3.9 0.7 copy-start.1
  6.3 27.0 %collective-permute-start.4 = (f32[3,16,1024]{2,1,0:T(8,128)}, f32[3,16,1024]{2,1,0:T(8,128)}, u32[]{:S(2)}, u32[]{:S(2)}) collective-permute-start(f32[3,16,1024]{2,1,0:T(8,128)} %get-tuple-element.15), channel_id=1, source_target_pairs={{0,8},{8,16},{16,24},{24,32},{32,40},{40,48},{48,56},{56,64},{64,7... | collective-permute-start | bytes 589832 | tf_op jit(solution)/shard_map/ppermute | solution.py:25
  8.2 25.1 %collective-permute-start.5 = (f32[3,16,1024]{2,1,0:T(8,128)}, f32[3,16,1024]{2,1,0:T(8,128)}, u32[]{:S(2)}, u32[]{:S(2)}) collective-permute-start(f32[3,16,1024]{2,1,0:T(8,128)} %get-tuple-element.16), channel_id=1, source_target_pairs={{8,0},{16,8},{24,16},{32,24},{40,32},{48,40},{56,48},{64,56},{72,6... | collective-permute-start | bytes 589832 | tf_op jit(solution)/shard_map/ppermute | solution.py:27
  15.1 19.6 %collective-permute-start.1 = (f32[5,48,3,128]{3,2,1,0:T(4,128)}, f32[5,48,3,128]{3,2,1,0:T(4,128)}, u32[]{:S(2)}, u32[]{:S(2)}) collective-permute-start(f32[5,48,3,128]{3,2,1,0:T(4,128)} %get-tuple-element.13), channel_id=1, source_target_pairs={{8,0},{16,8},{24,16},{32,24},{40,32},{48,40},{56,48},{64,56},{72,6... | collective-permute-start | bytes 1105928 | tf_op jit(solution)/shard_map/ppermute | solution.py:309
  17.3 8.4 %copy-start.4 = (f32[13]{0:T(128)S(1)}, f32[13]{0:T(128)}, u32[]{:S(2)}) copy-start(f32[13]{0:T(128)} %param.18) | copy-start | bytes 160
  17.3 8.4 %copy-start.5 = (f32[13]{0:T(128)S(1)}, f32[13]{0:T(128)}, u32[]{:S(2)}) copy-start(f32[13]{0:T(128)} %param.17) | copy-start | bytes 160
  17.3 8.4 %copy-start.6 = (f32[13]{0:T(128)S(1)}, f32[13]{0:T(128)}, u32[]{:S(2)}) copy-start(f32[13]{0:T(128)} %param.16) | copy-start | bytes 160
  17.3 8.4 %copy-start.7 = (f32[13]{0:T(128)S(1)}, f32[13]{0:T(128)}, u32[]{:S(2)}) copy-start(f32[13]{0:T(128)} %param.15) | copy-start | bytes 160
  17.7 15.1 %collective-permute-start.3 = (f32[5,48,8,3]{1,2,3,0:T(8,128)S(1)}, f32[5,48,8,3]{1,2,3,0:T(8,128)S(1)}, u32[]{:S(2)}, u32[]{:S(2)}) collective-permute-start(f32[5,48,8,3]{1,2,3,0:T(8,128)S(1)} %copy.62), channel_id=1, source_target_pairs={{0,1},{1,2},{2,3},{3,4},{4,5},{5,6},{6,7},{8,9},{9,10},{10,11},{11... | collective-permute-start | bytes 69128 | tf_op jit(solution)/shard_map/ppermute | solution.py:311
  23.2 7.3 %collective-permute-start.2 = (f32[5,48,8,3]{1,2,3,0:T(8,128)S(1)}, f32[5,48,8,3]{1,2,3,0:T(8,128)S(1)}, u32[]{:S(2)}, u32[]{:S(2)}) collective-permute-start(f32[5,48,8,3]{1,2,3,0:T(8,128)S(1)} %copy.61), channel_id=1, source_target_pairs={{1,0},{2,1},{3,2},{4,3},{5,4},{6,5},{7,6},{9,8},{10,9},{11,10},{12... | collective-permute-start | bytes 69128 | tf_op jit(solution)/shard_map/ppermute | solution.py:312
  30.5 12.6 %collective-permute-start = (f32[5,48,3,128]{3,2,1,0:T(4,128)}, f32[5,48,3,128]{3,2,1,0:T(4,128)}, u32[]{:S(2)}, u32[]{:S(2)}) collective-permute-start(f32[5,48,3,128]{3,2,1,0:T(4,128)} %get-tuple-element.14), channel_id=1, source_target_pairs={{0,8},{8,16},{16,24},{24,32},{32,40},{40,48},{48,56},{56,64},{64,7... | collective-permute-start | bytes 1105928 | tf_op jit(solution)/shard_map/ppermute | solution.py:308
  43.9 8.1 %collective-permute-start.6 = (f32[5,96,16]{2,1,0:T(8,128)S(1)}, f32[5,96,16]{2,1,0:T(8,128)S(1)}, u32[]{:S(2)}, u32[]{:S(2)}) collective-permute-start(f32[5,96,16]{2,1,0:T(8,128)S(1)} %select_maximum_fusion.1), channel_id=1, source_target_pairs={{0,1},{1,2},{2,3},{3,4},{4,5},{5,6},{6,7},{8,9},{9,10},{10,11},{11... | collective-permute-start | bytes 92168 | tf_op jit(solution)/shard_map/ppermute | solution.py:343
  45.8 9.3 %collective-permute-start.7 = (f32[5,96,16]{2,1,0:T(8,128)S(1)}, f32[5,96,16]{2,1,0:T(8,128)S(1)}, u32[]{:S(2)}, u32[]{:S(2)}) collective-permute-start(f32[5,96,16]{2,1,0:T(8,128)S(1)} %select_maximum_fusion), channel_id=1, source_target_pairs={{1,0},{2,1},{3,2},{4,3},{5,4},{6,5},{7,6},{9,8},{10,9},{11,10},{12... | collective-permute-start | bytes 92168 | tf_op jit(solution)/shard_map/ppermute | solution.py:348
  52.0 3.2 %copy-start.2 = (f32[5,96,16]{2,1,0:T(8,128)}, f32[5,96,16]{2,1,0:T(8,128)S(1)}, u32[]{:S(2)}) copy-start(f32[5,96,16]{2,1,0:T(8,128)S(1)} %collective-permute-done.6) | copy-start | bytes 92164
  55.1 0.7 copy-start.3

commit v11 on v9

--- a/solution.py
+++ b/solution.py
@@ -160,8 +160,18 @@
     return out
 
 
-def fire_kernel(tab_ref, ext_ref, wind_ref, fuel_ref, level_out, fuel_out, heat_out):
+def fire_kernel(
+    tab_ref, mid_ref, xlo_ref, xhi_ref, ylo_ref, yhi_ref, wind_ref, fuel_ref,
+    level_out, fuel_out, heat_out, ext_ref,
+):
     rows, cols = fuel_ref.shape
+    edge_x = xlo_ref.shape[1]
+    edge_y = ylo_ref.shape[2]
+    ext_ref[:, 0:edge_x, edge_y : edge_y + cols] = xlo_ref[...]
+    ext_ref[:, edge_x : edge_x + rows, edge_y : edge_y + cols] = mid_ref[...]
+    ext_ref[:, edge_x + rows :, edge_y : edge_y + cols] = xhi_ref[...]
+    ext_ref[:, :, 0:edge_y] = ylo_ref[...]
+    ext_ref[:, :, edge_y + cols :] = yhi_ref[...]
     hx = (ext_ref.shape[1] - rows) // 2
     hy = (ext_ref.shape[2] - cols) // 2
     inner = (slice(hx, hx + rows), slice(hy, hy + cols))
@@ -213,7 +223,7 @@
     ) / (RF * RF)
 
 
-def fire_step(tables, ext, winds, fuel_left):
+def fire_step(tables, mid, x_lo, x_hi, y_lo, y_hi, winds, fuel_left):
     rows, cols = fuel_left.shape
     vmem = pl.BlockSpec(memory_space=pltpu.VMEM)
     return pl.pallas_call(
@@ -223,9 +233,10 @@
             jax.ShapeDtypeStruct((rows, cols), jnp.float32),
             jax.ShapeDtypeStruct((rows // RF, cols // RF), jnp.float32),
         ),
-        in_specs=[pl.BlockSpec(memory_space=pltpu.SMEM), vmem, vmem, vmem],
+        in_specs=[pl.BlockSpec(memory_space=pltpu.SMEM)] + [vmem] * 7,
+        scratch_shapes=[pltpu.VMEM(mid.shape[:1] + winds.shape[1:], jnp.float32)],
         out_specs=(vmem, vmem, vmem),
-    )(tables, ext, winds, fuel_left)
+    )(tables, mid, x_lo, x_hi, y_lo, y_hi, winds, fuel_left)
 
 
 def atmos_kernel(p_ref, q_ref, lo_ref, hi_ref, y_ref, u_ref, v_ref, h_ref, o_ref, ext_ref):
@@ -329,12 +340,21 @@
         fire_rows, fire_cols
     )
     stacked = jnp.stack([level_set, fuel_map.astype(jnp.float32), nsteps])
-    stacked = extended(stacked, (("gx", 1), ("gy", 2)), halo)
-    room = jnp.zeros(stacked.shape[:2] + (HALO_Y - halo,), jnp.float32)
-    stacked = jnp.concatenate([room, stacked, room], axis=2)
+    f_lo = lax.ppermute(stacked[:, -halo:], "gx", [(i, i + 1) for i in range(count_x - 1)])
+    f_hi = lax.ppermute(stacked[:, :halo], "gx", [(i + 1, i) for i in range(count_x - 1)])
+
+    def column(lo, hi):
+        return jnp.concatenate([f_lo[..., lo:hi], stacked[..., lo:hi], f_hi[..., lo:hi]], axis=1)
+
+    y_lo = lax.ppermute(
+        column(fire_cols - halo, fire_cols), "gy", [(i, i + 1) for i in range(count - 1)]
+    )
+    y_hi = lax.ppermute(column(0, halo), "gy", [(i + 1, i) for i in range(count - 1)])
+    y_lo = jnp.pad(y_lo, ((0, 0), (0, 0), (HALO_Y - halo, 0)))
+    y_hi = jnp.pad(y_hi, ((0, 0), (0, 0), (0, HALO_Y - halo)))
     winds = surface_winds(surface, fire_rows, fire_cols, halo, HALO_Y)
     tables = jnp.concatenate([spread_rate, wind_factor, burn_time, heat_yield]).astype(jnp.float32)
-    level, remaining, heat_atm = fire_step(tables, stacked, winds, fuel_left)
+    level, remaining, heat_atm = fire_step(tables, stacked, f_lo, f_hi, y_lo, y_hi, winds, fuel_left)
     return (atmos_call(atmos, x_lo, x_hi, y_ends, heat_atm), level, remaining)
 
 

time: 76 us -> 78.3 us (1.030)
  other arithmetic: 10.1 us -> 2.78 us
  local copies, waits for them, and re-layouts: 8.99 us -> 14.5 us
  starting transfers between devices: 30.5 us -> 33.3 us
  waiting for transfers between devices: 2.77 us -> 4.22 us
    ppermute x0 -> x4, starting transfers between devices: none -> 13.1 us  [the longest x1 5.36 us: shards(): lax.ppermute(stacked[:, :halo], 'gx', [(i + 1, i) for i in range(count_x...]
    ppermute x3 -> x1, starting transfers between devices: 10.1 us -> 2.1 us  [extended(): lax.ppermute(head, axis, [((i + 1) % count, i) for i in range(ends)])]
    ppermute x3 -> x1, starting transfers between devices: 9.44 us -> 4.84 us  [extended(): lax.ppermute(tail, axis, [(i, (i + 1) % count) for i in range(ends)])]
    unnamed x35 -> x31, local copies, waits for them, and re-layouts: 2.15 us -> 6.03 us
    ppermute x1, starting transfers between devices: 1.91 us -> 4.27 us  [shards(): lax.ppermute(atmos[:, :, :3], 'gx', [(i + 1, i) for i in range(count_x -...]
    ppermute x0 -> x4, waiting for transfers between devices: none -> 2.2 us  [the longest x1 2.19 us: shards(): lax.ppermute(stacked[:, :halo], 'gx', [(i + 1, i) for i in range(count_x...]
    concatenate x1 -> x0, local copies, waits for them, and re-layouts: 2.19 us -> none  [shards(): stacked = jnp.concatenate([room, stacked, room], axis=2)]
    slice x1, local copies, waits for them, and re-layouts: 1.1 us -> 2.91 us  [shards(): atmos[:, :, :3]]
  transfers between devices with their start and end apart: 10 -> 10, of which waited for: 2 -> 2; matrix products, arithmetic and copies ran while one was open for 19% -> 15% of each run, Pallas kernels for 0% -> 0%
where the time goes in v11:
time: 78.3 us; the launch traced here: 77.6 us
  starting transfers between devices  33.3 us (43%)
  Pallas kernels  18.7 us (24%)
  local copies, waits for them, and re-layouts  14.5 us (19%)
  waiting for transfers between devices  4.22 us (5%)
  other arithmetic  2.78 us (4%)
  matrix products  2.51 us (3%)
  between operations  1.61 us (2%)
    pallas_call x1, Pallas kernels, fire_step(): pl.pallas_call(fire_kernel, out_shape=(jax.ShapeDtypeStruct((rows, cols),...  11.9 us
    pallas_call x1, Pallas kernels, atmos_call(): pl.pallas_call(atmos_kernel, grid=(fields,), out_shape=jax.ShapeDtypeStru...  6.78 us
    unnamed x31, local copies, waits for them, and re-layouts  6.03 us
    ppermute x1, starting transfers between devices, shards(): lax.ppermute(stacked[:, :halo], 'gx', [(i + 1, i) for i in range(count_x...  5.36 us
    ppermute x1, starting transfers between devices, shards(): lax.ppermute(atmos[..., -3:], 'gy', [(i, i + 1) for i in range(count - 1)])  5.02 us
    ppermute x1, starting transfers between devices, extended(): lax.ppermute(tail, axis, [(i, (i + 1) % count) for i in range(ends)])  4.84 us
    ppermute x1, starting transfers between devices, shards(): lax.ppermute(atmos[:, :, :3], 'gx', [(i + 1, i) for i in range(count_x -...  4.27 us
    ppermute x1, starting transfers between devices, shards(): lax.ppermute(column(fire_cols - halo, fire_cols), 'gy', [(i, i + 1) for i...  3.63 us
  transfers between devices with their start and end apart: 10, of which 2 were waited for; matrix products, arithmetic and copies ran while one was open for 15% of the time, Pallas kernels for 0%

profile of v11, /device:TPU:120, one launch (start us, length us, event | category | flops | bytes accessed | tf_op | source)
XLA Modules:
  0.0 77.6 jit_solution(15764780858310609658)
XLA Ops:
  0.6 2.9 %fusion.38 = (f32[5,48,3,128]{3,2,1,0:T(4,128)}, f32[5,48,3,128]{3,2,1,0:T(4,128)}) fusion(f32[5,48,8,128]{3,2,1,0:T(8,128)} %v_ref.1), kind=kLoop, calls=%fused_computation.81 | loop fusion | bytes 1474560 | tf_op jit(solution)/shard_map/slice | solution.py:320
  3.5 4.3 %collective-permute-start.1 = (f32[5,48,3,128]{3,2,1,0:T(4,128)}, f32[5,48,3,128]{3,2,1,0:T(4,128)S(1)}, u32[]{:S(2)}, u32[]{:S(2)}) collective-permute-start(f32[5,48,3,128]{3,2,1,0:T(4,128)} %get-tuple-element.11), channel_id=1, source_target_pairs={{8,0},{16,8},{24,16},{32,24},{40,32},{48,40},{56,48},{64,56},{72,6... | collective-permute-start | bytes 1105928 | tf_op jit(solution)/shard_map/ppermute | solution.py:320
  7.8 1.9 %collective-permute-start = (f32[5,48,3,128]{3,2,1,0:T(4,128)}, f32[5,48,3,128]{3,2,1,0:T(4,128)}, u32[]{:S(2)}, u32[]{:S(2)}) collective-permute-start(f32[5,48,3,128]{3,2,1,0:T(4,128)} %get-tuple-element.12), channel_id=1, source_target_pairs={{0,8},{8,16},{16,24},{24,32},{32,40},{40,48},{48,56},{56,64},{64,7... | collective-permute-start | bytes 1105928 | tf_op jit(solution)/shard_map/ppermute | solution.py:319
  10.4 0.0 copy-start.12
  10.4 0.6 copy-done.12
  11.1 0.1 fusion.25
  11.2 0.6 copy-done.13
  11.7 0.1 broadcast_in_dim.48
  11.8 0.1 broadcast_in_dim.49
  11.9 0.0 copy-start.6
  12.0 0.9 %copy-done.6 = f32[64,1024]{1,0:T(8,128)S(1)} copy-done((f32[64,1024]{1,0:T(8,128)S(1)}, f32[64,1024]{1,0:T(8,128)}, u32[]{:S(2)}) %copy-start.6) | copy-done | bytes 262168
  12.9 0.1 pad_maximum_fusion.1.mid_ref
  12.9 0.8 fusion.40
  13.7 1.9 %collective-permute-start.4 = (f32[3,16,1024]{2,1,0:T(8,128)}, f32[3,16,1024]{2,1,0:T(8,128)S(1)}, u32[]{:S(2)}, u32[]{:S(2)}) collective-permute-start(f32[3,16,1024]{2,1,0:T(8,128)} %get-tuple-element.16), channel_id=1, source_target_pairs={{0,8},{8,16},{16,24},{24,32},{32,40},{40,48},{48,56},{56,64},{64,7... | collective-permute-start | bytes 589832 | tf_op jit(solution)/shard_map/ppermute | solution.py:343
  15.6 1.2 %fusion.37 = (f32[5,48,8,3]{3,2,1,0:T(8,128)}, f32[5,48,8,3]{3,2,1,0:T(8,128)S(1)}) fusion(f32[5,48,8,128]{3,2,1,0:T(8,128)S(1)} %copy-done), kind=kLoop, calls=%fused_computation.80 | loop fusion | bytes 92160 | tf_op jit(solution)/shard_map/slice | solution.py:323
  16.9 2.2 %copy.33 = f32[5,48,8,3]{1,2,3,0:T(8,128)} copy(f32[5,48,8,3]{3,2,1,0:T(8,128)} %get-tuple-element.9) | data formatting | bytes 46080
  19.1 2.0 %collective-permute-start.2 = (f32[5,48,8,3]{1,2,3,0:T(8,128)}, f32[5,48,8,3]{1,2,3,0:T(8,128)S(1)}, u32[]{:S(2)}, u32[]{:S(2)}) collective-permute-start(f32[5,48,8,3]{1,2,3,0:T(8,128)} %copy.33), channel_id=1, source_target_pairs={{1,0},{2,1},{3,2},{4,3},{5,4},{6,5},{7,6},{9,8},{10,9},{11,10},{12... | collective-permute-start | bytes 69128 | tf_op jit(solution)/shard_map/ppermute | solution.py:323
  21.1 1.0 %copy.34 = f32[5,48,8,3]{1,2,3,0:T(8,128)} copy(f32[5,48,8,3]{3,2,1,0:T(8,128)S(1)} %get-tuple-element.10) | data formatting | bytes 46080
  22.1 5.0 %collective-permute-start.3 = (f32[5,48,8,3]{1,2,3,0:T(8,128)}, f32[5,48,8,3]{1,2,3,0:T(8,128)S(1)}, u32[]{:S(2)}, u32[]{:S(2)}) collective-permute-start(f32[5,48,8,3]{1,2,3,0:T(8,128)} %copy.34), channel_id=1, source_target_pairs={{0,1},{1,2},{2,3},{3,4},{4,5},{5,6},{6,7},{8,9},{9,10},{10,11},{11... | collective-permute-start | bytes 69128 | tf_op jit(solution)/shard_map/ppermute | solution.py:322
  27.3 0.1 fusion.39
  27.3 0.0 copy-start.8
  27.4 0.6 multiply_exponential_fusion.p_ref
  28.0 0.0 copy-done.8
  28.0 0.0 copy-done.9
  28.0 0.0 copy-done.10
  28.0 0.7 pad_maximum_fusion.4.tab_ref
  28.7 0.1 pad.30.clone
  28.8 5.4 %collective-permute-start.5 = (f32[3,16,1024]{2,1,0:T(8,128)S(1)}, f32[3,16,1024]{2,1,0:T(8,128)S(1)}, u32[]{:S(2)}, u32[]{:S(2)}) collective-permute-start(f32[3,16,1024]{2,1,0:T(8,128)S(1)} %copy-done.7), channel_id=1, source_target_pairs={{8,0},{16,8},{24,16},{32,24},{40,32},{48,40},{56,48},{64,56},{72,6... | collective-permute-start | bytes 589832 | tf_op jit(solution)/shard_map/ppermute | solution.py:344
  34.2 0.4 copy.28
  34.6 0.4 copy.29
  35.0 0.1 fusion.41
  35.1 2.2 %collective-permute-done.5.xhi_ref = f32[3,16,1024]{2,1,0:T(8,128)S(1)} collective-permute-done((f32[3,16,1024]{2,1,0:T(8,128)S(1)}, f32[3,16,1024]{2,1,0:T(8,128)S(1)}, u32[]{:S(2)}, u32[]{:S(2)}) %collective-permute-start.5) | collective-permute-done | bytes 196640 | tf_op jit(solution)/shard_map/ppermute | solution.py:344
  37.3 0.1 fusion.42
  37.4 0.6 copy-done.4
  38.0 3.6 %collective-permute-start.6 = (f32[3,96,16]{2,1,0:T(8,128)S(1)}, f32[3,96,16]{2,1,0:T(8,128)S(1)}, u32[]{:S(2)}, u32[]{:S(2)}) collective-permute-start(f32[3,96,16]{2,1,0:T(8,128)S(1)} %pad_maximum_fusion.2), channel_id=1, source_target_pairs={{0,1},{1,2},{2,3},{3,4},{4,5},{5,6},{6,7},{8,9},{9,10},{10,11},{11... | collective-permute-start | bytes 55304 | tf_op jit(solution)/shard_map/ppermute | solution.py:349
  41.6 2.2 %collective-permute-start.7 = (f32[3,96,16]{2,1,0:T(8,128)S(1)}, f32[3,96,16]{2,1,0:T(8,128)S(1)}, u32[]{:S(2)}, u32[]{:S(2)}) collective-permute-start(f32[3,96,16]{2,1,0:T(8,128)S(1)} %pad_maximum_fusion.3), channel_id=1, source_target_pairs={{1,0},{2,1},{3,2},{4,3},{5,4},{6,5},{7,6},{9,8},{10,9},{11,10},{12... | collective-permute-start | bytes 55304 | tf_op jit(solution)/shard_map/ppermute | solution.py:352
  43.9 0.7 slice_bitcast_fusion.2
  44.6 0.1 fusion.43
  44.7 4.8 %collective-permute-start.8 = (f32[2,14,3]{2,1,0:T(8,128)S(1)}, f32[2,14,3]{2,1,0:T(8,128)S(1)}, u32[]{:S(2)}, u32[]{:S(2)}) collective-permute-start(f32[2,14,3]{2,1,0:T(8,128)S(1)} %get-tuple-element.21), channel_id=1, source_target_pairs={{0,1},{1,2},{2,3},{3,4},{4,5},{5,6},{6,7},{8,9},{9,10},{10,11},{11... | collective-permute-start | bytes 1016 | tf_op jit(solution)/shard_map/ppermute | solution.py:25
  49.5 2.1 %collective-permute-start.9 = (f32[2,14,3]{2,1,0:T(8,128)S(1)}, f32[2,14,3]{2,1,0:T(8,128)S(1)}, u32[]{:S(2)}, u32[]{:S(2)}) collective-permute-start(f32[2,14,3]{2,1,0:T(8,128)S(1)} %get-tuple-element.22), channel_id=1, source_target_pairs={{1,0},{2,1},{3,2},{4,3},{5,4},{6,5},{7,6},{9,8},{10,9},{11,10},{12... | collective-permute-start | bytes 1016 | tf_op jit(solution)/shard_map/ppermute | solution.py:27
  51.6 1.3 %pad_maximum_fusion.y_ref = f32[5,48,8,128]{3,2,1,0:T(8,128)} fusion(f32[5,48,8,3]{3,2,1,0:T(8,128)S(1)} %copy.29, f32[5,48,8,3]{3,2,1,0:T(8,128)S(1)} %copy.28, f32[128]{0:T(128)S(1)} %pad.30.clone), kind=kLoop, calls=%fused_computation.3 | loop fusion | flops 491520 | bytes 1029632 | tf_op jit(solution)/shard_map/concatenate | solution.py:325
  52.9 0.8 pad.8.ylo_ref
  53.7 0.7 pad.9.yhi_ref
  54.4 2.0 %collective-permute-done.9 = f32[2,14,3]{2,1,0:T(8,128)S(1)} collective-permute-done((f32[2,14,3]{2,1,0:T(8,128)S(1)}, f32[2,14,3]{2,1,0:T(8,128)S(1)}, u32[]{:S(2)}, u32[]{:S(2)}) %collective-permute-start.9) | collective-permute-done | bytes 368 | tf_op jit(solution)/shard_map/ppermute | solution.py:27
  56.4 0.5 convolution_bitcast_fusion
  56.9 2.0 %fusion.wind_ref = f32[2,96,1280]{2,1,0:T(8,128)} fusion(f32[2,96,134]{1,2,0:T(8,128)S(1)} %convolution_bitcast_fusion, f32[1280]{0:T(1024)S(1)} %get-tuple-element.27, s32[1280]{0:T(1024)S(1)} %get-tuple-element.30, f32[1280]{0:T(1024)S(1)} %get-tuple-element.28, s32[1280]{0:T(1024)S(1)} %get-tuple-element.29), kind=kOutput, calls=%fused_computation.5 | convolution fusion | flops 396039680 | bytes 1106432 | tf_op jit(solution)/shard_map/kib,jb->kij/dot_general | solution.py:145
  58.9 11.9 %shard_map.130 = (f32[64,1024]{1,0:T(8,128)}, f32[64,1024]{1,0:T(8,128)}, f32[8,128]{1,0:T(8,128)}) custom-call(f32[52]{0:T(128)} %pad_maximum_fusion.4.tab_ref, f32[3,64,1024]{2,1,0:T(8,128)} %copy-done.1, f32[3,16,1024]{2,1,0:T(8,128)} %copy-done.3, f32[3,16,1024]{2,1,0:T(8,128)} %copy-done.4, f32[3,96,128]{2,1,0:T(8,128)} %pad.8.ylo_ref, ...), custom_call_target="tpu_custom_call" | custom-call | tf_op jit(solution)/shard_map/pallas_call | solution.py:229
  70.8 6.8 %shard_map.131 = f32[5,48,8,128]{3,2,1,0:T(8,128)} custom-call(f32[48]{0:T(128)} %multiply_exponential_fusion.p_ref, f32[5,48,8,128]{3,2,1,0:T(8,128)} %v_ref.1, f32[5,48,3,128]{3,2,1,0:T(4,128)} %collective-permute-done.lo_ref, f32[5,48,3,128]{3,2,1,0:T(4,128)} %copy-done.2, f32[5,48,8,128]{3,2,1,0:T(8,128)} %pad_maximum_fusion.y_ref, ...), custom_call_target="tpu_custom_call" | custom-call | tf_op jit(solution)/shard_map/pallas_call | solution.py:280
  (40 shorter events, 0.2 us)
Async XLA Ops:
  0.6 11.3 %copy-start.5 = (s32[64,1024]{1,0:T(8,128)S(1)}, s32[64,1024]{1,0:T(8,128)}, u32[]{:S(2)}) copy-start(s32[64,1024]{1,0:T(8,128)} %param.14) | copy-start | bytes 786436
  3.5 40.3 %collective-permute-start.1 = (f32[5,48,3,128]{3,2,1,0:T(4,128)}, f32[5,48,3,128]{3,2,1,0:T(4,128)S(1)}, u32[]{:S(2)}, u32[]{:S(2)}) collective-permute-start(f32[5,48,3,128]{3,2,1,0:T(4,128)} %get-tuple-element.11), channel_id=1, source_target_pairs={{8,0},{16,8},{24,16},{32,24},{40,32},{48,40},{56,48},{64,56},{72,6... | collective-permute-start | bytes 1105928 | tf_op jit(solution)/shard_map/ppermute | solution.py:320
  7.8 36.1 %collective-permute-start = (f32[5,48,3,128]{3,2,1,0:T(4,128)}, f32[5,48,3,128]{3,2,1,0:T(4,128)}, u32[]{:S(2)}, u32[]{:S(2)}) collective-permute-start(f32[5,48,3,128]{3,2,1,0:T(4,128)} %get-tuple-element.12), channel_id=1, source_target_pairs={{0,8},{8,16},{16,24},{24,32},{32,40},{40,48},{48,56},{56,64},{64,7... | collective-permute-start | bytes 1105928 | tf_op jit(solution)/shard_map/ppermute | solution.py:319
  10.4 0.7 copy-start.12
  11.1 0.7 copy-start.13
  11.9 1.0 %copy-start.6 = (f32[64,1024]{1,0:T(8,128)S(1)}, f32[64,1024]{1,0:T(8,128)}, u32[]{:S(2)}) copy-start(f32[64,1024]{1,0:T(8,128)} %param.12) | copy-start | bytes 786436
  12.9 2.8 %copy-start = (f32[5,48,8,128]{3,2,1,0:T(8,128)S(1)}, f32[5,48,8,128]{3,2,1,0:T(8,128)}, u32[]{:S(2)}) copy-start(f32[5,48,8,128]{3,2,1,0:T(8,128)} %v_ref.1) | copy-start | bytes 2949124
  12.9 14.3 %copy-start.1 = (f32[3,64,1024]{2,1,0:T(8,128)}, f32[3,64,1024]{2,1,0:T(8,128)S(1)}, u32[]{:S(2)}) copy-start(f32[3,64,1024]{2,1,0:T(8,128)S(1)} %pad_maximum_fusion.1.mid_ref) | copy-start | bytes 2359300
  13.7 21.3 %collective-permute-start.4 = (f32[3,16,1024]{2,1,0:T(8,128)}, f32[3,16,1024]{2,1,0:T(8,128)S(1)}, u32[]{:S(2)}, u32[]{:S(2)}) collective-permute-start(f32[3,16,1024]{2,1,0:T(8,128)} %get-tuple-element.16), channel_id=1, source_target_pairs={{0,8},{8,16},{16,24},{24,32},{32,40},{40,48},{48,56},{56,64},{64,7... | collective-permute-start | bytes 589832 | tf_op jit(solution)/shard_map/ppermute | solution.py:343
  19.1 9.7 %collective-permute-start.2 = (f32[5,48,8,3]{1,2,3,0:T(8,128)}, f32[5,48,8,3]{1,2,3,0:T(8,128)S(1)}, u32[]{:S(2)}, u32[]{:S(2)}) collective-permute-start(f32[5,48,8,3]{1,2,3,0:T(8,128)} %copy.33), channel_id=1, source_target_pairs={{1,0},{2,1},{3,2},{4,3},{5,4},{6,5},{7,6},{9,8},{10,9},{11,10},{12... | collective-permute-start | bytes 69128 | tf_op jit(solution)/shard_map/ppermute | solution.py:323
  22.1 12.5 %collective-permute-start.3 = (f32[5,48,8,3]{1,2,3,0:T(8,128)}, f32[5,48,8,3]{1,2,3,0:T(8,128)S(1)}, u32[]{:S(2)}, u32[]{:S(2)}) collective-permute-start(f32[5,48,8,3]{1,2,3,0:T(8,128)} %copy.34), channel_id=1, source_target_pairs={{0,1},{1,2},{2,3},{3,4},{4,5},{5,6},{6,7},{8,9},{9,10},{10,11},{11... | collective-permute-start | bytes 69128 | tf_op jit(solution)/shard_map/ppermute | solution.py:322
  27.2 0.7 copy-start.11
  27.2 1.5 %copy-start.7 = (f32[3,16,1024]{2,1,0:T(8,128)S(1)}, f32[3,16,1024]{2,1,0:T(8,128)}, u32[]{:S(2)}) copy-start(f32[3,16,1024]{2,1,0:T(8,128)} %get-tuple-element.15) | copy-start | bytes 589828
  27.3 0.7 copy-start.8
  27.4 0.7 copy-start.9
  27.4 0.7 copy-start.10
  28.8 8.5 %collective-permute-start.5 = (f32[3,16,1024]{2,1,0:T(8,128)S(1)}, f32[3,16,1024]{2,1,0:T(8,128)S(1)}, u32[]{:S(2)}, u32[]{:S(2)}) collective-permute-start(f32[3,16,1024]{2,1,0:T(8,128)S(1)} %copy-done.7), channel_id=1, source_target_pairs={{8,0},{16,8},{24,16},{32,24},{40,32},{48,40},{56,48},{64,56},{72,6... | collective-permute-start | bytes 589832 | tf_op jit(solution)/shard_map/ppermute | solution.py:344
  35.0 2.4 %copy-start.3 = (f32[3,16,1024]{2,1,0:T(8,128)}, f32[3,16,1024]{2,1,0:T(8,128)S(1)}, u32[]{:S(2)}) copy-start(f32[3,16,1024]{2,1,0:T(8,128)S(1)} %collective-permute-done.4.xlo_ref) | copy-start | bytes 589828
  37.3 0.7 copy-start.4
  38.0 14.9 %collective-permute-start.6 = (f32[3,96,16]{2,1,0:T(8,128)S(1)}, f32[3,96,16]{2,1,0:T(8,128)S(1)}, u32[]{:S(2)}, u32[]{:S(2)}) collective-permute-start(f32[3,96,16]{2,1,0:T(8,128)S(1)} %pad_maximum_fusion.2), channel_id=1, source_target_pairs={{0,1},{1,2},{2,3},{3,4},{4,5},{5,6},{6,7},{8,9},{9,10},{10,11},{11... | collective-permute-start | bytes 55304 | tf_op jit(solution)/shard_map/ppermute | solution.py:349
  41.6 12.0 %collective-permute-start.7 = (f32[3,96,16]{2,1,0:T(8,128)S(1)}, f32[3,96,16]{2,1,0:T(8,128)S(1)}, u32[]{:S(2)}, u32[]{:S(2)}) collective-permute-start(f32[3,96,16]{2,1,0:T(8,128)S(1)} %pad_maximum_fusion.3), channel_id=1, source_target_pairs={{1,0},{2,1},{3,2},{4,3},{5,4},{6,5},{7,6},{9,8},{10,9},{11,10},{12... | collective-permute-start | bytes 55304 | tf_op jit(solution)/shard_map/ppermute | solution.py:352
  43.9 9.1 %copy-start.2 = (f32[5,48,3,128]{3,2,1,0:T(4,128)}, f32[5,48,3,128]{3,2,1,0:T(4,128)S(1)}, u32[]{:S(2)}) copy-start(f32[5,48,3,128]{3,2,1,0:T(4,128)S(1)} %collective-permute-done.1.hi_ref) | copy-start | bytes 1105924
  44.7 9.7 %collective-permute-start.8 = (f32[2,14,3]{2,1,0:T(8,128)S(1)}, f32[2,14,3]{2,1,0:T(8,128)S(1)}, u32[]{:S(2)}, u32[]{:S(2)}) collective-permute-start(f32[2,14,3]{2,1,0:T(8,128)S(1)} %get-tuple-element.21), channel_id=1, source_target_pairs={{0,1},{1,2},{2,3},{3,4},{4,5},{5,6},{6,7},{8,9},{9,10},{10,11},{11... | collective-permute-start | bytes 1016 | tf_op jit(solution)/shard_map/ppermute | solution.py:25
  49.5 6.8 %collective-permute-start.9 = (f32[2,14,3]{2,1,0:T(8,128)S(1)}, f32[2,14,3]{2,1,0:T(8,128)S(1)}, u32[]{:S(2)}, u32[]{:S(2)}) collective-permute-start(f32[2,14,3]{2,1,0:T(8,128)S(1)} %get-tuple-element.22), channel_id=1, source_target_pairs={{1,0},{2,1},{3,2},{4,3},{5,4},{6,5},{7,6},{9,8},{10,9},{11,10},{12... | collective-permute-start | bytes 1016 | tf_op jit(solution)/shard_map/ppermute | solution.py:27

commit v12 on v9

--- a/solution.py
+++ b/solution.py
@@ -145,7 +145,7 @@
     return jnp.einsum("kib,jb->kij", along, table_y, precision=lax.Precision.HIGHEST)
 
 
-HALO_Y = 128
+HALO_Y = 64
 
 
 def shift(a, d, axis):
@@ -164,16 +164,19 @@
     rows, cols = fuel_ref.shape
     hx = (ext_ref.shape[1] - rows) // 2
     hy = (ext_ref.shape[2] - cols) // 2
-    inner = (slice(hx, hx + rows), slice(hy, hy + cols))
+    width = ext_ref.shape[2]
+
+    def interior(a):
+        return pltpu.roll(a[hx : hx + rows], (width - hy) % width, 1)[:, :cols]
     level = ext_ref[0]
     cat = ext_ref[1]
     nsteps = ext_ref[2]
     spread = lookup(tab_ref, cat, 0, 0.0)
     gain = lookup(tab_ref, cat, 1, 0.0)
-    cat_in = cat[inner]
+    cat_in = interior(cat)
     burnout = lookup(tab_ref, cat_in, 2, 1.0)
     yields = lookup(tab_ref, cat_in, 3, 0.0)
-    nsteps_in = nsteps[inner]
+    nsteps_in = interior(nsteps)
     wind_u = wind_ref[0]
     wind_v = wind_ref[1]
     remaining = fuel_ref[...]
@@ -197,12 +200,12 @@
         slope_y = (shift(level, -2, 1) - 8.0 * ym1 + 8.0 * yp1 - shift(level, 2, 1)) / 12.0
         pushing = jnp.maximum(wind_u * slope_x + wind_v * slope_y, 0.0)
         moved = level - spread * (upwind + gain * pushing)
-        burned = remaining / (1.0 + jnp.exp(moved[inner])) / burnout
+        burned = remaining / (1.0 + jnp.exp(interior(moved))) / burnout
         active = float(substep) < nsteps_in
         remaining = jnp.where(active, remaining - burned, remaining)
         heating = heating + jnp.where(active, yields * burned, 0.0)
         level = jnp.where(float(substep) < nsteps, moved, level)
-    level_out[...] = level[inner]
+    level_out[...] = interior(level)
     fuel_out[...] = remaining
     heat_rows = heating.reshape(rows // RF, RF, cols).sum(axis=1)
     lane_in = lax.broadcasted_iota(jnp.int32, (cols, cols // RF), 0) // RF

time: 76 us -> 75.9 us (level)
  no operation moved by 1% of the time
where the time goes in v12:
time: 75.9 us; the launch traced here: 75.1 us
  starting transfers between devices  30.5 us (40%)
  Pallas kernels  18.5 us (24%)
  other arithmetic  10.2 us (13%)
  local copies, waits for them, and re-layouts  9.22 us (12%)
  waiting for transfers between devices  2.53 us (3%)
  matrix products  2.47 us (3%)
  between operations  1.74 us (2%)
    pallas_call x1, Pallas kernels, fire_step(): pl.pallas_call(fire_kernel, out_shape=(jax.ShapeDtypeStruct((rows, cols),...  11.7 us
    ppermute x3, starting transfers between devices, extended(): lax.ppermute(head, axis, [((i + 1) % count, i) for i in range(ends)])  10.1 us
    ppermute x3, starting transfers between devices, extended(): lax.ppermute(tail, axis, [(i, (i + 1) % count) for i in range(ends)])  9.44 us
    pallas_call x1, Pallas kernels, atmos_call(): pl.pallas_call(atmos_kernel, grid=(fields,), out_shape=jax.ShapeDtypeStru...  6.8 us
    ppermute x1, starting transfers between devices, shards(): lax.ppermute(atmos[..., -3:], 'gy', [(i, i + 1) for i in range(count - 1)])  5.03 us
    concatenate x1, local copies, waits for them, and re-layouts, shards(): stacked = jnp.concatenate([room, stacked, room], axis=2)  2.41 us
    unnamed x35, local copies, waits for them, and re-layouts  2.15 us
    ppermute x1, starting transfers between devices, shards(): lax.ppermute(atmos[:, :, -3:], 'gx', [(i, i + 1) for i in range(count_x -...  2.02 us
  transfers between devices with their start and end apart: 10, of which 2 were waited for; matrix products, arithmetic and copies ran while one was open for 19% of the time, Pallas kernels for 0%

profile of v12, /device:TPU:120, one launch (start us, length us, event | category | flops | bytes accessed | tf_op | source)
XLA Modules:
  0.0 75.1 jit_solution(2192732924548974729)
XLA Ops:
  0.6 0.0 copy-start
  1.4 0.7 fusion.25
  2.1 0.7 fusion.33
  2.8 0.1 broadcast_in_dim.52
  2.9 0.1 broadcast_in_dim.53
  2.9 1.0 %convert_bitcast_fusion = f32[1,64,1024]{2,1,0:T(8,128)S(1)} fusion(s32[64,1024]{1,0:T(8,128)} %param.14), kind=kLoop, calls=%fused_computation.15 | loop fusion | flops 65536 | bytes 524288 | tf_op jit(solution)/shard_map/stack | solution.py:334
  3.9 0.0 copy-start.1
  4.0 0.7 copy-done.1
  4.6 1.6 %pad_maximum_fusion.4 = (f32[3,16,1024]{2,1,0:T(8,128)}, f32[3,16,1024]{2,1,0:T(8,128)}) fusion(f32[1,64,1024]{2,1,0:T(8,128)S(1)} %broadcast_in_dim.54, f32[1,64,1024]{2,1,0:T(8,128)S(1)} %convert_bitcast_fusion, f32[1,64,1024]{2,1,0:T(8,128)} %bitcast.31), kind=kLoop, calls=%fused_computation.18 | loop fusion | flops 196608 | bytes 1179648 | tf_op jit(solution)/shard_map/slice | solution.py:22
  6.3 1.9 %collective-permute-start.4 = (f32[3,16,1024]{2,1,0:T(8,128)}, f32[3,16,1024]{2,1,0:T(8,128)}, u32[]{:S(2)}, u32[]{:S(2)}) collective-permute-start(f32[3,16,1024]{2,1,0:T(8,128)} %get-tuple-element.15), channel_id=1, source_target_pairs={{0,8},{8,16},{16,24},{24,32},{32,40},{40,48},{48,56},{56,64},{64,7... | collective-permute-start | bytes 589832 | tf_op jit(solution)/shard_map/ppermute | solution.py:25
  8.2 5.8 %collective-permute-start.5 = (f32[3,16,1024]{2,1,0:T(8,128)}, f32[3,16,1024]{2,1,0:T(8,128)}, u32[]{:S(2)}, u32[]{:S(2)}) collective-permute-start(f32[3,16,1024]{2,1,0:T(8,128)} %get-tuple-element.16), channel_id=1, source_target_pairs={{8,0},{16,8},{24,16},{32,24},{40,32},{48,40},{56,48},{64,56},{72,6... | collective-permute-start | bytes 589832 | tf_op jit(solution)/shard_map/ppermute | solution.py:27
  14.0 1.1 %fusion.39 = (f32[5,48,3,128]{3,2,1,0:T(4,128)}, f32[5,48,3,128]{3,2,1,0:T(4,128)}) fusion(f32[5,48,8,128]{3,2,1,0:T(8,128)S(1)} %copy-done), kind=kLoop, calls=%fused_computation.83 | loop fusion | bytes 1474560 | tf_op jit(solution)/shard_map/slice | solution.py:312
  15.1 1.9 %collective-permute-start.1 = (f32[5,48,3,128]{3,2,1,0:T(4,128)}, f32[5,48,3,128]{3,2,1,0:T(4,128)}, u32[]{:S(2)}, u32[]{:S(2)}) collective-permute-start(f32[5,48,3,128]{3,2,1,0:T(4,128)} %get-tuple-element.13), channel_id=1, source_target_pairs={{8,0},{16,8},{24,16},{32,24},{40,32},{48,40},{56,48},{64,56},{72,6... | collective-permute-start | bytes 1105928 | tf_op jit(solution)/shard_map/ppermute | solution.py:312
  17.0 0.3 fusion.38
  17.3 0.0 copy-start.14
  17.4 0.0 copy-start.15
  17.4 0.4 copy.25
  17.8 2.0 %collective-permute-start.2 = (f32[5,48,8,3]{1,2,3,0:T(8,128)S(1)}, f32[5,48,8,3]{1,2,3,0:T(8,128)S(1)}, u32[]{:S(2)}, u32[]{:S(2)}) collective-permute-start(f32[5,48,8,3]{1,2,3,0:T(8,128)S(1)} %copy.25), channel_id=1, source_target_pairs={{1,0},{2,1},{3,2},{4,3},{5,4},{6,5},{7,6},{9,8},{10,9},{11,10},{12... | collective-permute-start | bytes 69128 | tf_op jit(solution)/shard_map/ppermute | solution.py:315
  19.8 0.4 copy.26
  20.2 5.0 %collective-permute-start.3 = (f32[5,48,8,3]{1,2,3,0:T(8,128)S(1)}, f32[5,48,8,3]{1,2,3,0:T(8,128)S(1)}, u32[]{:S(2)}, u32[]{:S(2)}) collective-permute-start(f32[5,48,8,3]{1,2,3,0:T(8,128)S(1)} %copy.26), channel_id=1, source_target_pairs={{0,1},{1,2},{2,3},{3,4},{4,5},{5,6},{6,7},{8,9},{9,10},{10,11},{11... | collective-permute-start | bytes 69128 | tf_op jit(solution)/shard_map/ppermute | solution.py:314
  25.2 0.6 slice_bitcast_fusion
  25.8 0.6 fusion.31
  26.4 0.6 broadcast_add_fusion.2
  27.0 0.6 select_add_fusion
  27.6 0.6 broadcast_add_fusion
  28.2 0.6 multiply_exponential_fusion.p_ref
  28.8 0.6 pad_maximum_fusion.5.tab_ref
  29.5 0.7 pad.19.clone
  30.1 2.0 %collective-permute-start = (f32[5,48,3,128]{3,2,1,0:T(4,128)}, f32[5,48,3,128]{3,2,1,0:T(4,128)}, u32[]{:S(2)}, u32[]{:S(2)}) collective-permute-start(f32[5,48,3,128]{3,2,1,0:T(4,128)} %get-tuple-element.14), channel_id=1, source_target_pairs={{0,8},{8,16},{16,24},{24,32},{32,40},{40,48},{48,56},{56,64},{64,7... | collective-permute-start | bytes 1105928 | tf_op jit(solution)/shard_map/ppermute | solution.py:311
  32.2 0.4 copy.20
  32.6 0.4 copy.21
  33.1 1.3 %pad_maximum_fusion = f32[3,96,1024]{2,1,0:T(8,128)S(1)} fusion(f32[3,16,1024]{2,1,0:T(8,128)} %collective-permute-done.5, f32[1,64,1024]{2,1,0:T(8,128)} %copy-done.1, f32[1,64,1024]{2,1,0:T(8,128)S(1)} %convert_bitcast_fusion, f32[1,64,1024]{2,1,0:T(8,128)} %bitcast.32, f32[3,16,1024]{2,1,0:T(8,128)} %collective-permute-done.4), kind=kLoop, calls=%fused_computation | loop fusion | flops 1179648 | bytes 2359296 | tf_op jit(solution)/shard_map/concatenate | solution.py:23
  34.4 0.1 fusion.37
  34.5 3.7 %collective-permute-start.6 = (f32[3,96,16]{2,1,0:T(8,128)S(1)}, f32[3,96,16]{2,1,0:T(8,128)S(1)}, u32[]{:S(2)}, u32[]{:S(2)}) collective-permute-start(f32[3,96,16]{2,1,0:T(8,128)S(1)} %get-tuple-element.10), channel_id=1, source_target_pairs={{0,1},{1,2},{2,3},{3,4},{4,5},{5,6},{6,7},{8,9},{9,10},{10,11},{11... | collective-permute-start | bytes 55304 | tf_op jit(solution)/shard_map/ppermute | solution.py:25
  38.2 2.1 %collective-permute-start.7 = (f32[3,96,16]{2,1,0:T(8,128)S(1)}, f32[3,96,16]{2,1,0:T(8,128)}, u32[]{:S(2)}, u32[]{:S(2)}) collective-permute-start(f32[3,96,16]{2,1,0:T(8,128)S(1)} %get-tuple-element.9), channel_id=1, source_target_pairs={{1,0},{2,1},{3,2},{4,3},{5,4},{6,5},{7,6},{9,8},{10,9},{11,10},{12... | collective-permute-start | bytes 55304 | tf_op jit(solution)/shard_map/ppermute | solution.py:27
  40.3 0.7 slice_bitcast_fusion.1
  41.0 1.7 %collective-permute-done.lo_ref = f32[5,48,3,128]{3,2,1,0:T(4,128)} collective-permute-done((f32[5,48,3,128]{3,2,1,0:T(4,128)}, f32[5,48,3,128]{3,2,1,0:T(4,128)}, u32[]{:S(2)}, u32[]{:S(2)}) %collective-permute-start) | collective-permute-done | bytes 368672 | tf_op jit(solution)/shard_map/ppermute | solution.py:311
  42.7 0.7 slice_bitcast_fusion.2
  43.4 0.1 fusion.40
  43.5 3.8 %collective-permute-start.8 = (f32[2,14,3]{2,1,0:T(8,128)S(1)}, f32[2,14,3]{2,1,0:T(8,128)S(1)}, u32[]{:S(2)}, u32[]{:S(2)}) collective-permute-start(f32[2,14,3]{2,1,0:T(8,128)S(1)} %get-tuple-element.17), channel_id=1, source_target_pairs={{0,1},{1,2},{2,3},{3,4},{4,5},{5,6},{6,7},{8,9},{9,10},{10,11},{11... | collective-permute-start | bytes 1016 | tf_op jit(solution)/shard_map/ppermute | solution.py:25
  47.3 2.2 %collective-permute-start.9 = (f32[2,14,3]{2,1,0:T(8,128)S(1)}, f32[2,14,3]{2,1,0:T(8,128)S(1)}, u32[]{:S(2)}, u32[]{:S(2)}) collective-permute-start(f32[2,14,3]{2,1,0:T(8,128)S(1)} %get-tuple-element.18), channel_id=1, source_target_pairs={{1,0},{2,1},{3,2},{4,3},{5,4},{6,5},{7,6},{9,8},{10,9},{11,10},{12... | collective-permute-start | bytes 1016 | tf_op jit(solution)/shard_map/ppermute | solution.py:27
  49.5 1.3 %pad_maximum_fusion.1.y_ref = f32[5,48,8,128]{3,2,1,0:T(8,128)} fusion(f32[5,48,8,3]{3,2,1,0:T(8,128)S(1)} %copy.21, f32[5,48,8,3]{3,2,1,0:T(8,128)S(1)} %copy.20, f32[128]{0:T(128)S(1)} %copy-done.11), kind=kLoop, calls=%fused_computation.2 | loop fusion | flops 491520 | bytes 1029632 | tf_op jit(solution)/shard_map/concatenate | solution.py:317
  50.9 2.4 %concatenate.21.ext_ref = f32[3,96,1152]{2,1,0:T(8,128)} concatenate(f32[3,96,48]{2,1,0:T(8,128)S(1)} %broadcast_in_dim.29, f32[3,96,16]{2,1,0:T(8,128)S(1)} %collective-permute-done.6, f32[3,96,1024]{2,1,0:T(8,128)S(1)} %pad_maximum_fusion, f32[3,96,16]{2,1,0:T(8,128)} %collective-permute-done.7, f32[3,96,48]{2,1,0:T(8,128)S(1)} %broadcast_in_dim.29), dimensions={2} | concatenate | bytes 2654208 | tf_op jit(solution)/shard_map/concatenate | solution.py:337
  53.3 0.8 %collective-permute-done.9 = f32[2,14,3]{2,1,0:T(8,128)S(1)} collective-permute-done((f32[2,14,3]{2,1,0:T(8,128)S(1)}, f32[2,14,3]{2,1,0:T(8,128)S(1)}, u32[]{:S(2)}, u32[]{:S(2)}) %collective-permute-start.9) | collective-permute-done | bytes 368 | tf_op jit(solution)/shard_map/ppermute | solution.py:27
  54.1 0.5 convolution_bitcast_fusion
  54.7 2.0 %fusion.wind_ref = f32[2,96,1152]{2,1,0:T(8,128)} fusion(f32[2,96,134]{1,2,0:T(8,128)S(1)} %convolution_bitcast_fusion, f32[1152]{0:T(1024)S(1)} %copy-done.2, s32[1152]{0:T(1024)S(1)} %copy-done.5, f32[1152]{0:T(1024)S(1)} %copy-done.3, s32[1152]{0:T(1024)S(1)} %copy-done.4), kind=kOutput, calls=%fused_computation.5 | convolution fusion | flops 356435712 | bytes 1006080 | tf_op jit(solution)/shard_map/kib,jb->kij/dot_general | solution.py:145
  56.7 11.7 %shard_map.130 = (f32[64,1024]{1,0:T(8,128)}, f32[64,1024]{1,0:T(8,128)}, f32[8,128]{1,0:T(8,128)}) custom-call(f32[52]{0:T(128)} %pad_maximum_fusion.5.tab_ref, f32[3,96,1152]{2,1,0:T(8,128)} %concatenate.21.ext_ref, f32[2,96,1152]{2,1,0:T(8,128)} %fusion.wind_ref, f32[64,1024]{1,0:T(8,128)} %fuel_ref.1), custom_call_target="tpu_custom_call" | custom-call | tf_op jit(solution)/shard_map/pallas_call | solution.py:222
  68.3 6.8 %shard_map.131 = f32[5,48,8,128]{3,2,1,0:T(8,128)} custom-call(f32[48]{0:T(128)} %multiply_exponential_fusion.p_ref, f32[5,48,8,128]{3,2,1,0:T(8,128)} %v_ref.1, f32[5,48,3,128]{3,2,1,0:T(4,128)} %collective-permute-done.lo_ref, f32[5,48,3,128]{3,2,1,0:T(4,128)} %collective-permute-done.1.hi_ref, f32[5,48,8,128]{3,2,1,0:T(8,128)} %pad_maximum_fusion.1.y_ref, ...), custom_call_target="tpu_custom_call" | custom-call | tf_op jit(solution)/shard_map/pallas_call | solution.py:272
  (40 shorter events, 0.1 us)
Async XLA Ops:
  0.6 13.3 %copy-start = (f32[5,48,8,128]{3,2,1,0:T(8,128)S(1)}, f32[5,48,8,128]{3,2,1,0:T(8,128)}, u32[]{:S(2)}) copy-start(f32[5,48,8,128]{3,2,1,0:T(8,128)} %v_ref.1) | copy-start | bytes 2949124
  3.9 0.7 copy-start.1
  6.3 26.8 %collective-permute-start.4 = (f32[3,16,1024]{2,1,0:T(8,128)}, f32[3,16,1024]{2,1,0:T(8,128)}, u32[]{:S(2)}, u32[]{:S(2)}) collective-permute-start(f32[3,16,1024]{2,1,0:T(8,128)} %get-tuple-element.15), channel_id=1, source_target_pairs={{0,8},{8,16},{16,24},{24,32},{32,40},{40,48},{48,56},{56,64},{64,7... | collective-permute-start | bytes 589832 | tf_op jit(solution)/shard_map/ppermute | solution.py:25
  8.2 24.9 %collective-permute-start.5 = (f32[3,16,1024]{2,1,0:T(8,128)}, f32[3,16,1024]{2,1,0:T(8,128)}, u32[]{:S(2)}, u32[]{:S(2)}) collective-permute-start(f32[3,16,1024]{2,1,0:T(8,128)} %get-tuple-element.16), channel_id=1, source_target_pairs={{8,0},{16,8},{24,16},{32,24},{40,32},{48,40},{56,48},{64,56},{72,6... | collective-permute-start | bytes 589832 | tf_op jit(solution)/shard_map/ppermute | solution.py:27
  15.1 25.2 %collective-permute-start.1 = (f32[5,48,3,128]{3,2,1,0:T(4,128)}, f32[5,48,3,128]{3,2,1,0:T(4,128)}, u32[]{:S(2)}, u32[]{:S(2)}) collective-permute-start(f32[5,48,3,128]{3,2,1,0:T(4,128)} %get-tuple-element.13), channel_id=1, source_target_pairs={{8,0},{16,8},{24,16},{32,24},{40,32},{48,40},{56,48},{64,56},{72,6... | collective-permute-start | bytes 1105928 | tf_op jit(solution)/shard_map/ppermute | solution.py:312
  17.3 11.5 %copy-start.12 = (f32[13]{0:T(128)S(1)}, f32[13]{0:T(128)}, u32[]{:S(2)}) copy-start(f32[13]{0:T(128)} %param.18) | copy-start | bytes 160
  17.3 11.5 %copy-start.13 = (f32[13]{0:T(128)S(1)}, f32[13]{0:T(128)}, u32[]{:S(2)}) copy-start(f32[13]{0:T(128)} %param.17) | copy-start | bytes 160
  17.3 11.5 %copy-start.14 = (f32[13]{0:T(128)S(1)}, f32[13]{0:T(128)}, u32[]{:S(2)}) copy-start(f32[13]{0:T(128)} %param.16) | copy-start | bytes 160
  17.4 11.5 %copy-start.15 = (f32[13]{0:T(128)S(1)}, f32[13]{0:T(128)}, u32[]{:S(2)}) copy-start(f32[13]{0:T(128)} %param.15) | copy-start | bytes 160
  17.8 12.4 %collective-permute-start.2 = (f32[5,48,8,3]{1,2,3,0:T(8,128)S(1)}, f32[5,48,8,3]{1,2,3,0:T(8,128)S(1)}, u32[]{:S(2)}, u32[]{:S(2)}) collective-permute-start(f32[5,48,8,3]{1,2,3,0:T(8,128)S(1)} %copy.25), channel_id=1, source_target_pairs={{1,0},{2,1},{3,2},{4,3},{5,4},{6,5},{7,6},{9,8},{10,9},{11,10},{12... | collective-permute-start | bytes 69128 | tf_op jit(solution)/shard_map/ppermute | solution.py:315
  20.2 12.4 %collective-permute-start.3 = (f32[5,48,8,3]{1,2,3,0:T(8,128)S(1)}, f32[5,48,8,3]{1,2,3,0:T(8,128)S(1)}, u32[]{:S(2)}, u32[]{:S(2)}) collective-permute-start(f32[5,48,8,3]{1,2,3,0:T(8,128)S(1)} %copy.26), channel_id=1, source_target_pairs={{0,1},{1,2},{2,3},{3,4},{4,5},{5,6},{6,7},{8,9},{9,10},{10,11},{11... | collective-permute-start | bytes 69128 | tf_op jit(solution)/shard_map/ppermute | solution.py:314
  30.1 12.6 %collective-permute-start = (f32[5,48,3,128]{3,2,1,0:T(4,128)}, f32[5,48,3,128]{3,2,1,0:T(4,128)}, u32[]{:S(2)}, u32[]{:S(2)}) collective-permute-start(f32[5,48,3,128]{3,2,1,0:T(4,128)} %get-tuple-element.14), channel_id=1, source_target_pairs={{0,8},{8,16},{16,24},{24,32},{32,40},{40,48},{48,56},{56,64},{64,7... | collective-permute-start | bytes 1105928 | tf_op jit(solution)/shard_map/ppermute | solution.py:311
  33.0 10.3 %copy-start.6 = (f32[2,1,8,128]{3,2,0,1:T(8,128)S(1)}, f32[2,1,8,128]{3,2,0,1:T(8,128)}, u32[]{:S(2)}) copy-start(f32[2,1,8,128]{3,2,0,1:T(8,128)} %slice_bitcast_fusion) | copy-start | bytes 24580
  33.0 16.4 %copy-start.11 = (f32[128]{0:T(128)S(1)}, f32[128]{0:T(128)}, u32[]{:S(2)}) copy-start(f32[128]{0:T(128)} %pad.19.clone) | copy-start | bytes 1540
  34.5 16.3 %collective-permute-start.6 = (f32[3,96,16]{2,1,0:T(8,128)S(1)}, f32[3,96,16]{2,1,0:T(8,128)S(1)}, u32[]{:S(2)}, u32[]{:S(2)}) collective-permute-start(f32[3,96,16]{2,1,0:T(8,128)S(1)} %get-tuple-element.10), channel_id=1, source_target_pairs={{0,1},{1,2},{2,3},{3,4},{4,5},{5,6},{6,7},{8,9},{9,10},{10,11},{11... | collective-permute-start | bytes 55304 | tf_op jit(solution)/shard_map/ppermute | solution.py:25
  38.2 12.6 %collective-permute-start.7 = (f32[3,96,16]{2,1,0:T(8,128)S(1)}, f32[3,96,16]{2,1,0:T(8,128)}, u32[]{:S(2)}, u32[]{:S(2)}) collective-permute-start(f32[3,96,16]{2,1,0:T(8,128)S(1)} %get-tuple-element.9), channel_id=1, source_target_pairs={{1,0},{2,1},{3,2},{4,3},{5,4},{6,5},{7,6},{9,8},{10,9},{11,10},{12... | collective-permute-start | bytes 55304 | tf_op jit(solution)/shard_map/ppermute | solution.py:27
  43.5 9.8 %collective-permute-start.8 = (f32[2,14,3]{2,1,0:T(8,128)S(1)}, f32[2,14,3]{2,1,0:T(8,128)S(1)}, u32[]{:S(2)}, u32[]{:S(2)}) collective-permute-start(f32[2,14,3]{2,1,0:T(8,128)S(1)} %get-tuple-element.17), channel_id=1, source_target_pairs={{0,1},{1,2},{2,3},{3,4},{4,5},{5,6},{6,7},{8,9},{9,10},{10,11},{11... | collective-permute-start | bytes 1016 | tf_op jit(solution)/shard_map/ppermute | solution.py:25
  47.3 6.8 %collective-permute-start.9 = (f32[2,14,3]{2,1,0:T(8,128)S(1)}, f32[2,14,3]{2,1,0:T(8,128)S(1)}, u32[]{:S(2)}, u32[]{:S(2)}) collective-permute-start(f32[2,14,3]{2,1,0:T(8,128)S(1)} %get-tuple-element.18), channel_id=1, source_target_pairs={{1,0},{2,1},{3,2},{4,3},{5,4},{6,5},{7,6},{9,8},{10,9},{11,10},{12... | collective-permute-start | bytes 1016 | tf_op jit(solution)/shard_map/ppermute | solution.py:27
  50.8 3.3 %copy-start.7 = (f32[96]{0:T(128)S(1)}, f32[96]{0:T(128)}, u32[]{:S(2)}) copy-start(f32[96]{0:T(128)} %get-tuple-element.19) | copy-start | bytes 1156
  50.8 3.3 %copy-start.8 = (f32[96]{0:T(128)S(1)}, f32[96]{0:T(128)}, u32[]{:S(2)}) copy-start(f32[96]{0:T(128)} %get-tuple-element.20) | copy-start | bytes 1156
  50.8 3.3 %copy-start.9 = (s32[96]{0:T(128)S(1)}, s32[96]{0:T(128)}, u32[]{:S(2)}) copy-start(s32[96]{0:T(128)} %get-tuple-element.21) | copy-start | bytes 1156
  50.8 3.3 %copy-start.10 = (s32[96]{0:T(128)S(1)}, s32[96]{0:T(128)}, u32[]{:S(2)}) copy-start(s32[96]{0:T(128)} %get-tuple-element.22) | copy-start | bytes 1156
  50.8 3.8 %copy-start.2 = (f32[1152]{0:T(1024)S(1)}, f32[1152]{0:T(1024)}, u32[]{:S(2)}) copy-start(f32[1152]{0:T(1024)} %get-tuple-element.23) | copy-start | bytes 13828
  50.8 3.8 %copy-start.3 = (f32[1152]{0:T(1024)S(1)}, f32[1152]{0:T(1024)}, u32[]{:S(2)}) copy-start(f32[1152]{0:T(1024)} %get-tuple-element.24) | copy-start | bytes 13828
  50.9 3.8 %copy-start.4 = (s32[1152]{0:T(1024)S(1)}, s32[1152]{0:T(1024)}, u32[]{:S(2)}) copy-start(s32[1152]{0:T(1024)} %get-tuple-element.25) | copy-start | bytes 13828
  50.9 3.8 %copy-start.5 = (s32[1152]{0:T(1024)S(1)}, s32[1152]{0:T(1024)}, u32[]{:S(2)}) copy-start(s32[1152]{0:T(1024)} %get-tuple-element.26) | copy-start | bytes 13828

commit v13 on v12

--- a/solution.py
+++ b/solution.py
@@ -166,8 +166,8 @@
     hy = (ext_ref.shape[2] - cols) // 2
     width = ext_ref.shape[2]
 
-    def interior(a):
-        return pltpu.roll(a[hx : hx + rows], (width - hy) % width, 1)[:, :cols]
+    def interior(a, off=hx):
+        return pltpu.roll(a[off : off + rows], (width - hy) % width, 1)[:, :cols]
     level = ext_ref[0]
     cat = ext_ref[1]
     nsteps = ext_ref[2]
@@ -181,7 +181,14 @@
     wind_v = wind_ref[1]
     remaining = fuel_ref[...]
     heating = jnp.zeros_like(remaining)
+    off = hx
     for substep in range(SUBSTEPS):
+        trim = (off - 2 * (SUBSTEPS - substep)) // 8 * 8
+        if trim > 0:
+            level, spread, gain, wind_u, wind_v, nsteps = (
+                a[trim : a.shape[0] - trim] for a in (level, spread, gain, wind_u, wind_v, nsteps)
+            )
+            off -= trim
         xm1 = shift(level, -1, 0)
         xp1 = shift(level, 1, 0)
         ym1 = shift(level, -1, 1)
@@ -200,12 +207,12 @@
         slope_y = (shift(level, -2, 1) - 8.0 * ym1 + 8.0 * yp1 - shift(level, 2, 1)) / 12.0
         pushing = jnp.maximum(wind_u * slope_x + wind_v * slope_y, 0.0)
         moved = level - spread * (upwind + gain * pushing)
-        burned = remaining / (1.0 + jnp.exp(interior(moved))) / burnout
+        burned = remaining / (1.0 + jnp.exp(interior(moved, off))) / burnout
         active = float(substep) < nsteps_in
         remaining = jnp.where(active, remaining - burned, remaining)
         heating = heating + jnp.where(active, yields * burned, 0.0)
         level = jnp.where(float(substep) < nsteps, moved, level)
-    level_out[...] = interior(level)
+    level_out[...] = interior(level, off)
     fuel_out[...] = remaining
     heat_rows = heating.reshape(rows // RF, RF, cols).sum(axis=1)
     lane_in = lax.broadcasted_iota(jnp.int32, (cols, cols // RF), 0) // RF

time: 75.9 us -> 75.5 us (level)
  transfers between devices with their start and end apart: 10 -> 10, of which waited for: 2 -> 2; matrix products, arithmetic and copies ran while one was open for 19% -> 20% of each run, Pallas kernels for 0% -> 0%
where the time goes in v13:
time: 75.5 us; the launch traced here: 74.7 us
  starting transfers between devices  30.3 us (40%)
  Pallas kernels  18.1 us (24%)
  other arithmetic  10.2 us (14%)
  local copies, waits for them, and re-layouts  9.4 us (12%)
  waiting for transfers between devices  2.53 us (3%)
  matrix products  2.47 us (3%)
  between operations  1.74 us (2%)
    pallas_call x1, Pallas kernels, fire_step(): pl.pallas_call(fire_kernel, out_shape=(jax.ShapeDtypeStruct((rows, cols),...  11.3 us
    ppermute x3, starting transfers between devices, extended(): lax.ppermute(head, axis, [((i + 1) % count, i) for i in range(ends)])  9.9 us
    ppermute x3, starting transfers between devices, extended(): lax.ppermute(tail, axis, [(i, (i + 1) % count) for i in range(ends)])  9.44 us
    pallas_call x1, Pallas kernels, atmos_call(): pl.pallas_call(atmos_kernel, grid=(fields,), out_shape=jax.ShapeDtypeStru...  6.8 us
    ppermute x1, starting transfers between devices, shards(): lax.ppermute(atmos[..., -3:], 'gy', [(i, i + 1) for i in range(count - 1)])  5.03 us
    concatenate x1, local copies, waits for them, and re-layouts, shards(): stacked = jnp.concatenate([room, stacked, room], axis=2)  2.59 us
    unnamed x35, local copies, waits for them, and re-layouts  2.15 us
    ppermute x1, starting transfers between devices, shards(): lax.ppermute(atmos[:, :, -3:], 'gx', [(i, i + 1) for i in range(count_x -...  2.02 us
  transfers between devices with their start and end apart: 10, of which 2 were waited for; matrix products, arithmetic and copies ran while one was open for 20% of the time, Pallas kernels for 0%

profile of v13, /device:TPU:120, one launch (start us, length us, event | category | flops | bytes accessed | tf_op | source)
XLA Modules:
  0.0 74.7 jit_solution(948706046857079968)
XLA Ops:
  0.6 0.0 copy-start
  1.4 0.7 %fusion.25 = pred[16]{0:T(512)(128)(4,1)S(1)} fusion(s32[16]{0:T(128)} %bitcast.33, pred[16]{0:T(512)(128)(4,1)S(1)} %iota_compare_fusion.9), kind=kLoop, calls=%fused_computation.48 | loop fusion | flops 752 | bytes 96 | tf_op jit(solution)/shard_map/reduce_or | solution.py:331
  2.1 0.7 fusion.33
  2.8 0.1 broadcast_in_dim.52
  2.9 0.1 broadcast_in_dim.53
  2.9 1.0 %convert_bitcast_fusion = f32[1,64,1024]{2,1,0:T(8,128)S(1)} fusion(s32[64,1024]{1,0:T(8,128)} %param.14), kind=kLoop, calls=%fused_computation.15 | loop fusion | flops 65536 | bytes 524288 | tf_op jit(solution)/shard_map/stack | solution.py:341
  3.9 0.0 copy-start.1
  4.0 0.7 copy-done.1
  4.6 1.6 %pad_maximum_fusion.4 = (f32[3,16,1024]{2,1,0:T(8,128)}, f32[3,16,1024]{2,1,0:T(8,128)}) fusion(f32[1,64,1024]{2,1,0:T(8,128)S(1)} %broadcast_in_dim.54, f32[1,64,1024]{2,1,0:T(8,128)S(1)} %convert_bitcast_fusion, f32[1,64,1024]{2,1,0:T(8,128)} %bitcast.31), kind=kLoop, calls=%fused_computation.18 | loop fusion | flops 196608 | bytes 1179648 | tf_op jit(solution)/shard_map/slice | solution.py:22
  6.3 1.9 %collective-permute-start.4 = (f32[3,16,1024]{2,1,0:T(8,128)}, f32[3,16,1024]{2,1,0:T(8,128)}, u32[]{:S(2)}, u32[]{:S(2)}) collective-permute-start(f32[3,16,1024]{2,1,0:T(8,128)} %get-tuple-element.15), channel_id=1, source_target_pairs={{0,8},{8,16},{16,24},{24,32},{32,40},{40,48},{48,56},{56,64},{64,7... | collective-permute-start | bytes 589832 | tf_op jit(solution)/shard_map/ppermute | solution.py:25
  8.2 5.8 %collective-permute-start.5 = (f32[3,16,1024]{2,1,0:T(8,128)}, f32[3,16,1024]{2,1,0:T(8,128)}, u32[]{:S(2)}, u32[]{:S(2)}) collective-permute-start(f32[3,16,1024]{2,1,0:T(8,128)} %get-tuple-element.16), channel_id=1, source_target_pairs={{8,0},{16,8},{24,16},{32,24},{40,32},{48,40},{56,48},{64,56},{72,6... | collective-permute-start | bytes 589832 | tf_op jit(solution)/shard_map/ppermute | solution.py:27
  14.0 1.1 %fusion.39 = (f32[5,48,3,128]{3,2,1,0:T(4,128)}, f32[5,48,3,128]{3,2,1,0:T(4,128)}) fusion(f32[5,48,8,128]{3,2,1,0:T(8,128)S(1)} %copy-done), kind=kLoop, calls=%fused_computation.83 | loop fusion | bytes 1474560 | tf_op jit(solution)/shard_map/slice | solution.py:319
  15.1 1.9 %collective-permute-start.1 = (f32[5,48,3,128]{3,2,1,0:T(4,128)}, f32[5,48,3,128]{3,2,1,0:T(4,128)}, u32[]{:S(2)}, u32[]{:S(2)}) collective-permute-start(f32[5,48,3,128]{3,2,1,0:T(4,128)} %get-tuple-element.13), channel_id=1, source_target_pairs={{8,0},{16,8},{24,16},{32,24},{40,32},{48,40},{56,48},{64,56},{72,6... | collective-permute-start | bytes 1105928 | tf_op jit(solution)/shard_map/ppermute | solution.py:319
  17.0 0.3 fusion.38
  17.3 0.0 copy-start.13
  17.3 0.0 copy-start.14
  17.4 0.4 copy.25
  17.8 2.0 %collective-permute-start.2 = (f32[5,48,8,3]{1,2,3,0:T(8,128)S(1)}, f32[5,48,8,3]{1,2,3,0:T(8,128)S(1)}, u32[]{:S(2)}, u32[]{:S(2)}) collective-permute-start(f32[5,48,8,3]{1,2,3,0:T(8,128)S(1)} %copy.25), channel_id=1, source_target_pairs={{1,0},{2,1},{3,2},{4,3},{5,4},{6,5},{7,6},{9,8},{10,9},{11,10},{12... | collective-permute-start | bytes 69128 | tf_op jit(solution)/shard_map/ppermute | solution.py:322
  19.8 0.4 copy.26
  20.2 5.0 %collective-permute-start.3 = (f32[5,48,8,3]{1,2,3,0:T(8,128)S(1)}, f32[5,48,8,3]{1,2,3,0:T(8,128)S(1)}, u32[]{:S(2)}, u32[]{:S(2)}) collective-permute-start(f32[5,48,8,3]{1,2,3,0:T(8,128)S(1)} %copy.26), channel_id=1, source_target_pairs={{0,1},{1,2},{2,3},{3,4},{4,5},{5,6},{6,7},{8,9},{9,10},{10,11},{11... | collective-permute-start | bytes 69128 | tf_op jit(solution)/shard_map/ppermute | solution.py:321
  25.2 0.6 slice_bitcast_fusion
  25.8 0.6 fusion.31
  26.4 0.6 broadcast_add_fusion.2
  27.0 0.6 select_add_fusion
  27.6 0.6 broadcast_add_fusion
  28.2 0.6 multiply_exponential_fusion.p_ref
  28.8 0.6 pad_maximum_fusion.5.tab_ref
  29.5 0.7 pad.19.clone
  30.1 2.0 %collective-permute-start = (f32[5,48,3,128]{3,2,1,0:T(4,128)}, f32[5,48,3,128]{3,2,1,0:T(4,128)}, u32[]{:S(2)}, u32[]{:S(2)}) collective-permute-start(f32[5,48,3,128]{3,2,1,0:T(4,128)} %get-tuple-element.14), channel_id=1, source_target_pairs={{0,8},{8,16},{16,24},{24,32},{32,40},{40,48},{48,56},{56,64},{64,7... | collective-permute-start | bytes 1105928 | tf_op jit(solution)/shard_map/ppermute | solution.py:318
  32.2 0.4 copy.20
  32.6 0.4 copy.21
  33.1 1.3 %pad_maximum_fusion = f32[3,96,1024]{2,1,0:T(8,128)S(1)} fusion(f32[3,16,1024]{2,1,0:T(8,128)} %collective-permute-done.5, f32[1,64,1024]{2,1,0:T(8,128)} %copy-done.1, f32[1,64,1024]{2,1,0:T(8,128)S(1)} %convert_bitcast_fusion, f32[1,64,1024]{2,1,0:T(8,128)} %bitcast.32, f32[3,16,1024]{2,1,0:T(8,128)} %collective-permute-done.4), kind=kLoop, calls=%fused_computation | loop fusion | flops 1179648 | bytes 2359296 | tf_op jit(solution)/shard_map/concatenate | solution.py:23
  34.4 0.1 fusion.37
  34.5 3.7 %collective-permute-start.6 = (f32[3,96,16]{2,1,0:T(8,128)S(1)}, f32[3,96,16]{2,1,0:T(8,128)S(1)}, u32[]{:S(2)}, u32[]{:S(2)}) collective-permute-start(f32[3,96,16]{2,1,0:T(8,128)S(1)} %get-tuple-element.10), channel_id=1, source_target_pairs={{0,1},{1,2},{2,3},{3,4},{4,5},{5,6},{6,7},{8,9},{9,10},{10,11},{11... | collective-permute-start | bytes 55304 | tf_op jit(solution)/shard_map/ppermute | solution.py:25
  38.2 2.1 %collective-permute-start.7 = (f32[3,96,16]{2,1,0:T(8,128)S(1)}, f32[3,96,16]{2,1,0:T(8,128)}, u32[]{:S(2)}, u32[]{:S(2)}) collective-permute-start(f32[3,96,16]{2,1,0:T(8,128)S(1)} %get-tuple-element.9), channel_id=1, source_target_pairs={{1,0},{2,1},{3,2},{4,3},{5,4},{6,5},{7,6},{9,8},{10,9},{11,10},{12... | collective-permute-start | bytes 55304 | tf_op jit(solution)/shard_map/ppermute | solution.py:27
  40.3 0.7 slice_bitcast_fusion.1
  41.0 1.7 %collective-permute-done.lo_ref = f32[5,48,3,128]{3,2,1,0:T(4,128)} collective-permute-done((f32[5,48,3,128]{3,2,1,0:T(4,128)}, f32[5,48,3,128]{3,2,1,0:T(4,128)}, u32[]{:S(2)}, u32[]{:S(2)}) %collective-permute-start) | collective-permute-done | bytes 368672 | tf_op jit(solution)/shard_map/ppermute | solution.py:318
  42.7 0.7 slice_bitcast_fusion.2
  43.4 0.1 fusion.40
  43.5 3.8 %collective-permute-start.8 = (f32[2,14,3]{2,1,0:T(8,128)S(1)}, f32[2,14,3]{2,1,0:T(8,128)S(1)}, u32[]{:S(2)}, u32[]{:S(2)}) collective-permute-start(f32[2,14,3]{2,1,0:T(8,128)S(1)} %get-tuple-element.17), channel_id=1, source_target_pairs={{0,1},{1,2},{2,3},{3,4},{4,5},{5,6},{6,7},{8,9},{9,10},{10,11},{11... | collective-permute-start | bytes 1016 | tf_op jit(solution)/shard_map/ppermute | solution.py:25
  47.3 2.0 %collective-permute-start.9 = (f32[2,14,3]{2,1,0:T(8,128)S(1)}, f32[2,14,3]{2,1,0:T(8,128)S(1)}, u32[]{:S(2)}, u32[]{:S(2)}) collective-permute-start(f32[2,14,3]{2,1,0:T(8,128)S(1)} %get-tuple-element.18), channel_id=1, source_target_pairs={{1,0},{2,1},{3,2},{4,3},{5,4},{6,5},{7,6},{9,8},{10,9},{11,10},{12... | collective-permute-start | bytes 1016 | tf_op jit(solution)/shard_map/ppermute | solution.py:27
  49.3 1.3 %pad_maximum_fusion.1.y_ref = f32[5,48,8,128]{3,2,1,0:T(8,128)} fusion(f32[5,48,8,3]{3,2,1,0:T(8,128)S(1)} %copy.21, f32[5,48,8,3]{3,2,1,0:T(8,128)S(1)} %copy.20, f32[128]{0:T(128)S(1)} %copy-done.11), kind=kLoop, calls=%fused_computation.2 | loop fusion | flops 491520 | bytes 1029632 | tf_op jit(solution)/shard_map/concatenate | solution.py:324
  50.7 2.6 %concatenate.21.ext_ref = f32[3,96,1152]{2,1,0:T(8,128)} concatenate(f32[3,96,48]{2,1,0:T(8,128)S(1)} %broadcast_in_dim.29, f32[3,96,16]{2,1,0:T(8,128)S(1)} %collective-permute-done.6, f32[3,96,1024]{2,1,0:T(8,128)S(1)} %pad_maximum_fusion, f32[3,96,16]{2,1,0:T(8,128)} %collective-permute-done.7, f32[3,96,48]{2,1,0:T(8,128)S(1)} %broadcast_in_dim.29), dimensions={2} | concatenate | bytes 2654208 | tf_op jit(solution)/shard_map/concatenate | solution.py:344
  53.3 0.8 %collective-permute-done.9 = f32[2,14,3]{2,1,0:T(8,128)S(1)} collective-permute-done((f32[2,14,3]{2,1,0:T(8,128)S(1)}, f32[2,14,3]{2,1,0:T(8,128)S(1)}, u32[]{:S(2)}, u32[]{:S(2)}) %collective-permute-start.9) | collective-permute-done | bytes 368 | tf_op jit(solution)/shard_map/ppermute | solution.py:27
  54.1 0.5 convolution_bitcast_fusion
  54.7 2.0 %fusion.wind_ref = f32[2,96,1152]{2,1,0:T(8,128)} fusion(f32[2,96,134]{1,2,0:T(8,128)S(1)} %convolution_bitcast_fusion, f32[1152]{0:T(1024)S(1)} %copy-done.2, s32[1152]{0:T(1024)S(1)} %copy-done.5, f32[1152]{0:T(1024)S(1)} %copy-done.3, s32[1152]{0:T(1024)S(1)} %copy-done.4), kind=kOutput, calls=%fused_computation.5 | convolution fusion | flops 356435712 | bytes 1006080 | tf_op jit(solution)/shard_map/kib,jb->kij/dot_general | solution.py:145
  56.7 11.3 %shard_map.130 = (f32[64,1024]{1,0:T(8,128)}, f32[64,1024]{1,0:T(8,128)}, f32[8,128]{1,0:T(8,128)}) custom-call(f32[52]{0:T(128)} %pad_maximum_fusion.5.tab_ref, f32[3,96,1152]{2,1,0:T(8,128)} %concatenate.21.ext_ref, f32[2,96,1152]{2,1,0:T(8,128)} %fusion.wind_ref, f32[64,1024]{1,0:T(8,128)} %fuel_ref.1), custom_call_target="tpu_custom_call" | custom-call | tf_op jit(solution)/shard_map/pallas_call | solution.py:229
  67.9 6.8 %shard_map.131 = f32[5,48,8,128]{3,2,1,0:T(8,128)} custom-call(f32[48]{0:T(128)} %multiply_exponential_fusion.p_ref, f32[5,48,8,128]{3,2,1,0:T(8,128)} %v_ref.1, f32[5,48,3,128]{3,2,1,0:T(4,128)} %collective-permute-done.lo_ref, f32[5,48,3,128]{3,2,1,0:T(4,128)} %collective-permute-done.1.hi_ref, f32[5,48,8,128]{3,2,1,0:T(8,128)} %pad_maximum_fusion.1.y_ref, ...), custom_call_target="tpu_custom_call" | custom-call | tf_op jit(solution)/shard_map/pallas_call | solution.py:279
  (40 shorter events, 0.1 us)
Async XLA Ops:
  0.6 13.3 %copy-start = (f32[5,48,8,128]{3,2,1,0:T(8,128)S(1)}, f32[5,48,8,128]{3,2,1,0:T(8,128)}, u32[]{:S(2)}) copy-start(f32[5,48,8,128]{3,2,1,0:T(8,128)} %v_ref.1) | copy-start | bytes 2949124
  3.9 0.7 copy-start.1
  6.3 26.8 %collective-permute-start.4 = (f32[3,16,1024]{2,1,0:T(8,128)}, f32[3,16,1024]{2,1,0:T(8,128)}, u32[]{:S(2)}, u32[]{:S(2)}) collective-permute-start(f32[3,16,1024]{2,1,0:T(8,128)} %get-tuple-element.15), channel_id=1, source_target_pairs={{0,8},{8,16},{16,24},{24,32},{32,40},{40,48},{48,56},{56,64},{64,7... | collective-permute-start | bytes 589832 | tf_op jit(solution)/shard_map/ppermute | solution.py:25
  8.2 24.9 %collective-permute-start.5 = (f32[3,16,1024]{2,1,0:T(8,128)}, f32[3,16,1024]{2,1,0:T(8,128)}, u32[]{:S(2)}, u32[]{:S(2)}) collective-permute-start(f32[3,16,1024]{2,1,0:T(8,128)} %get-tuple-element.16), channel_id=1, source_target_pairs={{8,0},{16,8},{24,16},{32,24},{40,32},{48,40},{56,48},{64,56},{72,6... | collective-permute-start | bytes 589832 | tf_op jit(solution)/shard_map/ppermute | solution.py:27
  15.1 25.2 %collective-permute-start.1 = (f32[5,48,3,128]{3,2,1,0:T(4,128)}, f32[5,48,3,128]{3,2,1,0:T(4,128)}, u32[]{:S(2)}, u32[]{:S(2)}) collective-permute-start(f32[5,48,3,128]{3,2,1,0:T(4,128)} %get-tuple-element.13), channel_id=1, source_target_pairs={{8,0},{16,8},{24,16},{32,24},{40,32},{48,40},{56,48},{64,56},{72,6... | collective-permute-start | bytes 1105928 | tf_op jit(solution)/shard_map/ppermute | solution.py:319
  17.3 11.5 %copy-start.12 = (f32[13]{0:T(128)S(1)}, f32[13]{0:T(128)}, u32[]{:S(2)}) copy-start(f32[13]{0:T(128)} %param.18) | copy-start | bytes 160
  17.3 11.5 %copy-start.13 = (f32[13]{0:T(128)S(1)}, f32[13]{0:T(128)}, u32[]{:S(2)}) copy-start(f32[13]{0:T(128)} %param.17) | copy-start | bytes 160
  17.3 11.5 %copy-start.14 = (f32[13]{0:T(128)S(1)}, f32[13]{0:T(128)}, u32[]{:S(2)}) copy-start(f32[13]{0:T(128)} %param.16) | copy-start | bytes 160
  17.4 11.5 %copy-start.15 = (f32[13]{0:T(128)S(1)}, f32[13]{0:T(128)}, u32[]{:S(2)}) copy-start(f32[13]{0:T(128)} %param.15) | copy-start | bytes 160
  17.8 12.4 %collective-permute-start.2 = (f32[5,48,8,3]{1,2,3,0:T(8,128)S(1)}, f32[5,48,8,3]{1,2,3,0:T(8,128)S(1)}, u32[]{:S(2)}, u32[]{:S(2)}) collective-permute-start(f32[5,48,8,3]{1,2,3,0:T(8,128)S(1)} %copy.25), channel_id=1, source_target_pairs={{1,0},{2,1},{3,2},{4,3},{5,4},{6,5},{7,6},{9,8},{10,9},{11,10},{12... | collective-permute-start | bytes 69128 | tf_op jit(solution)/shard_map/ppermute | solution.py:322
  20.2 12.4 %collective-permute-start.3 = (f32[5,48,8,3]{1,2,3,0:T(8,128)S(1)}, f32[5,48,8,3]{1,2,3,0:T(8,128)S(1)}, u32[]{:S(2)}, u32[]{:S(2)}) collective-permute-start(f32[5,48,8,3]{1,2,3,0:T(8,128)S(1)} %copy.26), channel_id=1, source_target_pairs={{0,1},{1,2},{2,3},{3,4},{4,5},{5,6},{6,7},{8,9},{9,10},{10,11},{11... | collective-permute-start | bytes 69128 | tf_op jit(solution)/shard_map/ppermute | solution.py:321
  30.1 12.6 %collective-permute-start = (f32[5,48,3,128]{3,2,1,0:T(4,128)}, f32[5,48,3,128]{3,2,1,0:T(4,128)}, u32[]{:S(2)}, u32[]{:S(2)}) collective-permute-start(f32[5,48,3,128]{3,2,1,0:T(4,128)} %get-tuple-element.14), channel_id=1, source_target_pairs={{0,8},{8,16},{16,24},{24,32},{32,40},{40,48},{48,56},{56,64},{64,7... | collective-permute-start | bytes 1105928 | tf_op jit(solution)/shard_map/ppermute | solution.py:318
  33.0 10.3 %copy-start.6 = (f32[2,1,8,128]{3,2,0,1:T(8,128)S(1)}, f32[2,1,8,128]{3,2,0,1:T(8,128)}, u32[]{:S(2)}) copy-start(f32[2,1,8,128]{3,2,0,1:T(8,128)} %slice_bitcast_fusion) | copy-start | bytes 24580
  33.0 16.3 %copy-start.11 = (f32[128]{0:T(128)S(1)}, f32[128]{0:T(128)}, u32[]{:S(2)}) copy-start(f32[128]{0:T(128)} %pad.19.clone) | copy-start | bytes 1540
  34.5 16.1 %collective-permute-start.6 = (f32[3,96,16]{2,1,0:T(8,128)S(1)}, f32[3,96,16]{2,1,0:T(8,128)S(1)}, u32[]{:S(2)}, u32[]{:S(2)}) collective-permute-start(f32[3,96,16]{2,1,0:T(8,128)S(1)} %get-tuple-element.10), channel_id=1, source_target_pairs={{0,1},{1,2},{2,3},{3,4},{4,5},{5,6},{6,7},{8,9},{9,10},{10,11},{11... | collective-permute-start | bytes 55304 | tf_op jit(solution)/shard_map/ppermute | solution.py:25
  38.2 12.4 %collective-permute-start.7 = (f32[3,96,16]{2,1,0:T(8,128)S(1)}, f32[3,96,16]{2,1,0:T(8,128)}, u32[]{:S(2)}, u32[]{:S(2)}) collective-permute-start(f32[3,96,16]{2,1,0:T(8,128)S(1)} %get-tuple-element.9), channel_id=1, source_target_pairs={{1,0},{2,1},{3,2},{4,3},{5,4},{6,5},{7,6},{9,8},{10,9},{11,10},{12... | collective-permute-start | bytes 55304 | tf_op jit(solution)/shard_map/ppermute | solution.py:27
  43.5 9.8 %collective-permute-start.8 = (f32[2,14,3]{2,1,0:T(8,128)S(1)}, f32[2,14,3]{2,1,0:T(8,128)S(1)}, u32[]{:S(2)}, u32[]{:S(2)}) collective-permute-start(f32[2,14,3]{2,1,0:T(8,128)S(1)} %get-tuple-element.17), channel_id=1, source_target_pairs={{0,1},{1,2},{2,3},{3,4},{4,5},{5,6},{6,7},{8,9},{9,10},{10,11},{11... | collective-permute-start | bytes 1016 | tf_op jit(solution)/shard_map/ppermute | solution.py:25
  47.3 6.8 %collective-permute-start.9 = (f32[2,14,3]{2,1,0:T(8,128)S(1)}, f32[2,14,3]{2,1,0:T(8,128)S(1)}, u32[]{:S(2)}, u32[]{:S(2)}) collective-permute-start(f32[2,14,3]{2,1,0:T(8,128)S(1)} %get-tuple-element.18), channel_id=1, source_target_pairs={{1,0},{2,1},{3,2},{4,3},{5,4},{6,5},{7,6},{9,8},{10,9},{11,10},{12... | collective-permute-start | bytes 1016 | tf_op jit(solution)/shard_map/ppermute | solution.py:27
  50.6 3.5 %copy-start.7 = (f32[96]{0:T(128)S(1)}, f32[96]{0:T(128)}, u32[]{:S(2)}) copy-start(f32[96]{0:T(128)} %get-tuple-element.19) | copy-start | bytes 1156
  50.6 3.5 %copy-start.8 = (f32[96]{0:T(128)S(1)}, f32[96]{0:T(128)}, u32[]{:S(2)}) copy-start(f32[96]{0:T(128)} %get-tuple-element.20) | copy-start | bytes 1156
  50.6 3.5 %copy-start.9 = (s32[96]{0:T(128)S(1)}, s32[96]{0:T(128)}, u32[]{:S(2)}) copy-start(s32[96]{0:T(128)} %get-tuple-element.21) | copy-start | bytes 1156
  50.6 3.5 %copy-start.10 = (s32[96]{0:T(128)S(1)}, s32[96]{0:T(128)}, u32[]{:S(2)}) copy-start(s32[96]{0:T(128)} %get-tuple-element.22) | copy-start | bytes 1156
  50.7 4.0 %copy-start.2 = (f32[1152]{0:T(1024)S(1)}, f32[1152]{0:T(1024)}, u32[]{:S(2)}) copy-start(f32[1152]{0:T(1024)} %get-tuple-element.23) | copy-start | bytes 13828
  50.7 4.0 %copy-start.3 = (f32[1152]{0:T(1024)S(1)}, f32[1152]{0:T(1024)}, u32[]{:S(2)}) copy-start(f32[1152]{0:T(1024)} %get-tuple-element.24) | copy-start | bytes 13828
  50.7 4.0 %copy-start.4 = (s32[1152]{0:T(1024)S(1)}, s32[1152]{0:T(1024)}, u32[]{:S(2)}) copy-start(s32[1152]{0:T(1024)} %get-tuple-element.25) | copy-start | bytes 13828
  50.7 4.0 %copy-start.5 = (s32[1152]{0:T(1024)S(1)}, s32[1152]{0:T(1024)}, u32[]{:S(2)}) copy-start(s32[1152]{0:T(1024)} %get-tuple-element.26) | copy-start | bytes 13828
